TPU v7x, 32 devices: a whole 2x2x4 slice. The times are simulated.
32 devices in a mesh: dp: 8 (over y, x, core), tensor: 4 (over z).
Axes of the slice: x: 2, y: 2, z: 4, core: 2. Of those that a mesh axis runs over, the one named last changes fastest.
Arguments:
- block_in: bfloat16 [8192, 768], P(('dp', 'tensor')), may hold values from -6 to 6
- source: bfloat16 [32768, 768], P(('dp', 'tensor')), may hold values from -6 to 6
- target_len: int32 [16], P('dp'), may hold values from 256 to 512, as said below
- source_len: int32 [16], P('dp'), may hold values from 512 to 2048, as said below
- targets: int32 [8192], P('dp'), may hold values from 0 to 32127
- gain_self: float32 [768], replicated, may hold values from 0.5 to 1.5
- gain_cross: float32 [768], replicated, may hold values from 0.5 to 1.5
- gain_ff: float32 [768], replicated, may hold values from 0.5 to 1.5
- gain_final: float32 [768], replicated, may hold values from 0.5 to 1.5
- self_q: bfloat16 [768, 768], P(None, 'tensor'), may hold values from -0.21875 to 0.21875
- self_k: bfloat16 [768, 768], P(None, 'tensor'), may hold values from -0.21875 to 0.21875
- self_v: bfloat16 [768, 768], P(None, 'tensor'), may hold values from -0.21875 to 0.21875
- self_o: bfloat16 [768, 768], P('tensor'), may hold values from -0.875 to 0.875
- cross_q: bfloat16 [768, 768], P(None, 'tensor'), may hold values from -0.21875 to 0.21875
- cross_k: bfloat16 [768, 768], P(None, 'tensor'), may hold values from -0.21875 to 0.21875
- cross_v: bfloat16 [768, 768], P(None, 'tensor'), may hold values from -0.21875 to 0.21875
- cross_o: bfloat16 [768, 768], P('tensor'), may hold values from -1.25 to 1.25
- ff_gate: bfloat16 [768, 2048], P(None, 'tensor'), may hold values from -0.21875 to 0.21875
- ff_up: bfloat16 [768, 2048], P(None, 'tensor'), may hold values from -0.21875 to 0.21875
- ff_down: bfloat16 [2048, 768], P('tensor'), may hold values from -0.125 to 0.125
- embed_table: bfloat16 [32128, 768], P('tensor'), may hold values from -6 to 6
Outputs:
- block_out: float32 [8192, 768], P(('dp', 'tensor'))
- token_loss: float32 [8192], P('dp')
- grad_block_in: float32 [8192, 768], P(('dp', 'tensor'))
- grad_source: float32 [32768, 768], P(('dp', 'tensor'))
- grad_gain_self: float32 [768], replicated
- grad_gain_cross: float32 [768], replicated
- grad_gain_ff: float32 [768], replicated
- grad_gain_final: float32 [768], replicated
- grad_self_q: float32 [768, 768], P('dp', 'tensor')
- grad_self_k: float32 [768, 768], P('dp', 'tensor')
- grad_self_v: float32 [768, 768], P('dp', 'tensor')
- grad_self_o: float32 [768, 768], P('tensor', 'dp')
- grad_cross_q: float32 [768, 768], P('dp', 'tensor')
- grad_cross_k: float32 [768, 768], P('dp', 'tensor')
- grad_cross_v: float32 [768, 768], P('dp', 'tensor')
- grad_cross_o: float32 [768, 768], P('tensor', 'dp')
- grad_ff_gate: float32 [768, 2048], P('dp', 'tensor')
- grad_ff_up: float32 [768, 2048], P('dp', 'tensor')
- grad_ff_down: float32 [2048, 768], P('tensor', 'dp')
- grad_embed: float32 [32128, 768], P('tensor', 'dp')
Inputs may be any that keep to these rules, and one draw needn't show every extreme that they name: `target_len`: among the 2 sequences of each index of dp one has exactly 512 live target positions. `source_len`: among the 2 sequences of each index of dp one has exactly 2048 live source positions.
All inputs are finite; a program needn't handle non-finite values.
Results may differ from a plain program's by a relative error of at most 0.019.
Values may be sent and summed in bfloat16 or wider, within the bound.
A program may use at most 256 MiB of HBM per device.

v0:
```python
import jax
import jax.numpy as jnp
from jax import lax
from jax.sharding import PartitionSpec as P

D = 768
HDIM = 64
TGT = 512
SRC = 2048


epsilon = 1e-06


def normalize(values, gain_vec):
    inv_scale = lax.rsqrt(jnp.mean(values * values, axis=-1, keepdims=True) + epsilon)
    return (values * inv_scale * gain_vec, inv_scale)


def norm_back(values, inv_scale, gain_vec, grad_out):
    weighted = gain_vec * grad_out
    grad_gain = jnp.sum(grad_out * values * inv_scale, axis=0)
    grad_values = inv_scale * weighted - values * inv_scale**3 * jnp.mean(
        weighted * values, axis=-1, keepdims=True
    )
    return (grad_values, grad_gain)


def gather_rows(local_rows):
    return lax.all_gather(local_rows, "tensor", axis=0, tiled=True)


def gather_grads(local_rows):
    return lax.all_gather(local_rows, "tensor", axis=0, tiled=True)


def scatter_rows(whole_rows, weight, transposed):

    def local_term():
        if transposed:
            return jnp.einsum("rc,dc->rd", whole_rows, weight, preferred_element_type=jnp.float32)
        return jnp.dot(whole_rows, weight, preferred_element_type=jnp.float32)

    return lax.psum_scatter(local_term(), "tensor", scatter_dimension=0, tiled=True)


def attend_scores(queries, key_rows, key_mask):
    scores = jnp.einsum(
        "sqhd,skhd->shqk", queries, key_rows, preferred_element_type=jnp.float32
    ) * HDIM ** (-0.5)
    return jnp.where(key_mask, scores, -1000000000.0)


def attend(queries, key_rows, value_rows, key_mask):
    scores = attend_scores(queries, key_rows, key_mask)
    row_top = jnp.max(scores, axis=-1, keepdims=True)
    log_total = row_top + jnp.log(jnp.sum(jnp.exp(scores - row_top), axis=-1, keepdims=True))
    attn_probs = jnp.exp(scores - log_total).astype(jnp.bfloat16)
    output = jnp.einsum(
        "shqk,skhd->sqhd", attn_probs, value_rows, preferred_element_type=jnp.float32
    )
    return (output.astype(jnp.bfloat16), log_total)


def attend_back(queries, key_rows, value_rows, key_mask, log_total, grad_output):
    scores = attend_scores(queries, key_rows, key_mask)
    attn_probs = jnp.exp(scores - log_total)
    grad_probs = jnp.einsum(
        "sqhd,skhd->shqk", grad_output, value_rows, preferred_element_type=jnp.float32
    )
    row_dot = jnp.sum(attn_probs * grad_probs, axis=-1, keepdims=True)
    grad_scores = (attn_probs * (grad_probs - row_dot)).astype(jnp.bfloat16)
    grad_queries = (
        jnp.einsum("shqk,skhd->sqhd", grad_scores, key_rows, preferred_element_type=jnp.float32)
        * HDIM ** (-0.5)
    ).astype(jnp.bfloat16)
    grad_keys = (
        jnp.einsum("shqk,sqhd->skhd", grad_scores, queries, preferred_element_type=jnp.float32)
        * HDIM ** (-0.5)
    ).astype(jnp.bfloat16)
    grad_values = jnp.einsum(
        "shqk,sqhd->skhd",
        attn_probs.astype(jnp.bfloat16),
        grad_output,
        preferred_element_type=jnp.float32,
    ).astype(jnp.bfloat16)
    return (grad_queries, grad_keys, grad_values)


def on_device(
    block_in,
    source,
    target_len,
    source_len,
    targets,
    gain_self,
    gain_cross,
    gain_ff,
    gain_final,
    self_q,
    self_k,
    self_v,
    self_o,
    cross_q,
    cross_k,
    cross_v,
    cross_o,
    ff_gate,
    ff_up,
    ff_down,
    embed_table,
):
    seq_count = target_len.shape[0]
    head_count = self_q.shape[1] // HDIM

    def split_heads(matrix):
        return matrix.reshape(seq_count, -1, head_count, HDIM)

    def join_heads(stacked):
        return stacked.reshape(-1, head_count * HDIM)

    def project(row_block, weight):
        return jnp.dot(row_block, weight, preferred_element_type=jnp.float32).astype(jnp.bfloat16)

    x_in = block_in.astype(jnp.float32)
    positions = jnp.arange(TGT)
    self_mask = (positions[None, :] <= positions[:, None])[None, None] & (
        positions[None, None, None, :] < target_len[:, None, None, None]
    )
    cross_mask = jnp.arange(SRC)[None, None, None, :] < source_len[:, None, None, None]
    valid_rows = (positions[None, :] < target_len[:, None]).reshape(-1)
    normed_one, scale_one = normalize(x_in, gain_self)
    rows_one = gather_rows(normed_one.astype(jnp.bfloat16))
    query_one = project(rows_one, self_q)
    keys_one = project(rows_one, self_k)
    values_one = project(rows_one, self_v)
    att_one, log_one = attend(
        split_heads(query_one), split_heads(keys_one), split_heads(values_one), self_mask
    )
    att_one = join_heads(att_one)
    hidden_one = x_in + scatter_rows(att_one, self_o, False)
    normed_two, scale_two = normalize(hidden_one, gain_cross)
    rows_two = gather_rows(normed_two.astype(jnp.bfloat16))
    source_rows = gather_rows(source)
    query_two = project(rows_two, cross_q)
    keys_two = project(source_rows, cross_k)
    values_two = project(source_rows, cross_v)
    att_two, log_two = attend(
        split_heads(query_two), split_heads(keys_two), split_heads(values_two), cross_mask
    )
    att_two = join_heads(att_two)
    hidden_two = hidden_one + scatter_rows(att_two, cross_o, False)
    normed_three, scale_three = normalize(hidden_two, gain_ff)
    rows_three = gather_rows(normed_three.astype(jnp.bfloat16))
    gate_pre = jnp.dot(rows_three, ff_gate, preferred_element_type=jnp.float32)
    up_pre = jnp.dot(rows_three, ff_up, preferred_element_type=jnp.float32)
    gelu_gate, gelu_back = jax.vjp(lambda pre_act: jax.nn.gelu(pre_act, approximate=True), gate_pre)
    mixed_rows = (gelu_gate * up_pre).astype(jnp.bfloat16)
    block_out = hidden_two + scatter_rows(mixed_rows, ff_down, False)
    normed_final, scale_final = normalize(block_out, gain_final)
    final_rows = gather_rows((normed_final * D ** (-0.5)).astype(jnp.bfloat16))
    logits = jnp.einsum("rd,vd->rv", final_rows, embed_table, preferred_element_type=jnp.float32)
    vocab_local = embed_table.shape[0]
    row_top = lax.pmax(jnp.max(logits, axis=1), "tensor")
    columns = lax.axis_index("tensor") * vocab_local + jnp.arange(vocab_local)
    target_hit = (columns[None, :] == targets[:, None]).astype(jnp.float32)
    exp_total, picked = lax.psum(
        (jnp.sum(jnp.exp(logits - row_top[:, None]), axis=1), jnp.sum(target_hit * logits, axis=1)),
        "tensor",
    )
    log_total = row_top + jnp.log(exp_total)
    token_loss = jnp.where(valid_rows, log_total - picked, 0.0)
    grad_logits = jnp.where(
        valid_rows[:, None], jnp.exp(logits - log_total[:, None]) - target_hit, 0.0
    ).astype(jnp.bfloat16)
    grad_embed_local = jnp.einsum(
        "rv,rd->vd", grad_logits, final_rows, preferred_element_type=jnp.float32
    )
    grad_final = scatter_rows(grad_logits, embed_table, False) * D ** (-0.5)
    grad_res, grad_gain_final = norm_back(block_out, scale_final, gain_final, grad_final)
    grad_rows = gather_grads(grad_res.astype(jnp.bfloat16))
    grad_ff_down = jnp.einsum(
        "rf,rd->fd", mixed_rows, grad_rows, preferred_element_type=jnp.float32
    )
    grad_mixed = jnp.einsum("rd,fd->rf", grad_rows, ff_down, preferred_element_type=jnp.float32)
    grad_gate = gelu_back(grad_mixed * up_pre)[0].astype(jnp.bfloat16)
    grad_up = (grad_mixed * gelu_gate).astype(jnp.bfloat16)
    grad_ff_gate = jnp.einsum(
        "rd,rf->df", rows_three, grad_gate, preferred_element_type=jnp.float32
    )
    grad_ff_up = jnp.einsum("rd,rf->df", rows_three, grad_up, preferred_element_type=jnp.float32)
    grad_normed = scatter_rows(
        jnp.concatenate([grad_gate, grad_up], 1), jnp.concatenate([ff_gate, ff_up], 1), True
    )
    grad_step, grad_gain_ff = norm_back(hidden_two, scale_three, gain_ff, grad_normed)
    grad_res = grad_res + grad_step
    grad_rows = gather_grads(grad_res.astype(jnp.bfloat16))
    grad_cross_o = jnp.einsum("rh,rd->hd", att_two, grad_rows, preferred_element_type=jnp.float32)
    grad_att = jnp.einsum(
        "rd,hd->rh", grad_rows, cross_o, preferred_element_type=jnp.float32
    ).astype(jnp.bfloat16)
    grad_query, grad_keys, grad_values = attend_back(
        split_heads(query_two),
        split_heads(keys_two),
        split_heads(values_two),
        cross_mask,
        log_two,
        split_heads(grad_att),
    )
    grad_query = join_heads(grad_query)
    grad_keys = join_heads(grad_keys)
    grad_values = join_heads(grad_values)
    grad_cross_q = jnp.einsum("rd,rh->dh", rows_two, grad_query, preferred_element_type=jnp.float32)
    grad_cross_k = jnp.einsum(
        "rd,rh->dh", source_rows, grad_keys, preferred_element_type=jnp.float32
    )
    grad_cross_v = jnp.einsum(
        "rd,rh->dh", source_rows, grad_values, preferred_element_type=jnp.float32
    )
    grad_source = scatter_rows(
        jnp.concatenate([grad_keys, grad_values], 1), jnp.concatenate([cross_k, cross_v], 1), True
    )
    grad_normed = scatter_rows(grad_query, cross_q, True)
    grad_step, grad_gain_cross = norm_back(hidden_one, scale_two, gain_cross, grad_normed)
    grad_res = grad_res + grad_step
    grad_rows = gather_grads(grad_res.astype(jnp.bfloat16))
    grad_self_o = jnp.einsum("rh,rd->hd", att_one, grad_rows, preferred_element_type=jnp.float32)
    grad_att = jnp.einsum(
        "rd,hd->rh", grad_rows, self_o, preferred_element_type=jnp.float32
    ).astype(jnp.bfloat16)
    grad_query, grad_keys, grad_values = attend_back(
        split_heads(query_one),
        split_heads(keys_one),
        split_heads(values_one),
        self_mask,
        log_one,
        split_heads(grad_att),
    )
    grad_query = join_heads(grad_query)
    grad_keys = join_heads(grad_keys)
    grad_values = join_heads(grad_values)
    grad_self_q = jnp.einsum("rd,rh->dh", rows_one, grad_query, preferred_element_type=jnp.float32)
    grad_self_k = jnp.einsum("rd,rh->dh", rows_one, grad_keys, preferred_element_type=jnp.float32)
    grad_self_v = jnp.einsum("rd,rh->dh", rows_one, grad_values, preferred_element_type=jnp.float32)
    grad_normed = scatter_rows(
        jnp.concatenate([grad_query, grad_keys, grad_values], 1),
        jnp.concatenate([self_q, self_k, self_v], 1),
        True,
    )
    grad_step, grad_gain_self = norm_back(x_in, scale_one, gain_self, grad_normed)
    grad_block_in = grad_res + grad_step
    (
        grad_self_q,
        grad_self_k,
        grad_self_v,
        grad_cross_q,
        grad_cross_k,
        grad_cross_v,
        grad_ff_gate,
        grad_ff_up,
    ) = (
        lax.psum_scatter(grad_self_q, "dp", scatter_dimension=0, tiled=True),
        lax.psum_scatter(grad_self_k, "dp", scatter_dimension=0, tiled=True),
        lax.psum_scatter(grad_self_v, "dp", scatter_dimension=0, tiled=True),
        lax.psum_scatter(grad_cross_q, "dp", scatter_dimension=0, tiled=True),
        lax.psum_scatter(grad_cross_k, "dp", scatter_dimension=0, tiled=True),
        lax.psum_scatter(grad_cross_v, "dp", scatter_dimension=0, tiled=True),
        lax.psum_scatter(grad_ff_gate, "dp", scatter_dimension=0, tiled=True),
        lax.psum_scatter(grad_ff_up, "dp", scatter_dimension=0, tiled=True),
    )
    grad_self_o, grad_cross_o, grad_ff_down, grad_embed = (
        lax.psum_scatter(grad_self_o, "dp", scatter_dimension=1, tiled=True),
        lax.psum_scatter(grad_cross_o, "dp", scatter_dimension=1, tiled=True),
        lax.psum_scatter(grad_ff_down, "dp", scatter_dimension=1, tiled=True),
        lax.psum_scatter(grad_embed_local, "dp", scatter_dimension=1, tiled=True),
    )
    grad_gain_self, grad_gain_cross, grad_gain_ff, grad_gain_final = lax.psum(
        (grad_gain_self, grad_gain_cross, grad_gain_ff, grad_gain_final), ("dp", "tensor")
    )
    return (
        block_out,
        token_loss,
        grad_block_in,
        grad_source,
        grad_gain_self,
        grad_gain_cross,
        grad_gain_ff,
        grad_gain_final,
        grad_self_q,
        grad_self_k,
        grad_self_v,
        grad_self_o,
        grad_cross_q,
        grad_cross_k,
        grad_cross_v,
        grad_cross_o,
        grad_ff_gate,
        grad_ff_up,
        grad_ff_down,
        grad_embed,
    )


def solution(mesh):
    in_specs = (
        P(("dp", "tensor"), None),
        P(("dp", "tensor"), None),
        P("dp"),
        P("dp"),
        P("dp"),
        P(),
        P(),
        P(),
        P(),
        P(None, "tensor"),
        P(None, "tensor"),
        P(None, "tensor"),
        P("tensor", None),
        P(None, "tensor"),
        P(None, "tensor"),
        P(None, "tensor"),
        P("tensor", None),
        P(None, "tensor"),
        P(None, "tensor"),
        P("tensor", None),
        P("tensor", None),
    )
    out_specs = (
        P(("dp", "tensor"), None),
        P("dp"),
        P(("dp", "tensor"), None),
        P(("dp", "tensor"), None),
        P(),
        P(),
        P(),
        P(),
        P("dp", "tensor"),
        P("dp", "tensor"),
        P("dp", "tensor"),
        P("tensor", "dp"),
        P("dp", "tensor"),
        P("dp", "tensor"),
        P("dp", "tensor"),
        P("tensor", "dp"),
        P("dp", "tensor"),
        P("dp", "tensor"),
        P("tensor", "dp"),
        P("tensor", "dp"),
    )
    return jax.shard_map(
        on_device, mesh=mesh, in_specs=in_specs, out_specs=out_specs, check_vma=False
    )
```

profile of v0, /device:TPU:0, one launch (start us, length us, event | category | flops | bytes accessed | tf_op | source)
XLA Modules:
  0.0 1879.7 jit_solution(15588969528157292377)
XLA Ops:
  13.3 38.2 %all-gather.9.cloned.1.call-done = bf16[1024,768]{1,0:T(8,128)(2,1)} async-done(((bf16[256,768]{1,0:T(8,128)(2,1)}), bf16[1024,768]{1,0:T(8,128)(2,1)}) %all-gather.9.cloned.1.call-update) | async-done | bytes 1572880 | tf_op jit(solution)/shard_map/all_gather | solution.py:30
  74.2 58.5 %reduce-scatter.29.cloned.1.call-done = f32[256,768]{1,0:T(8,128)} async-done(((f32[1024,768]{1,0:T(8,128)}), f32[256,768]{1,0:T(8,128)}) %reduce-scatter.29.cloned.1.call-update) | async-done | bytes 786448 | tf_op jit(solution)/shard_map/reduce_scatter | solution.py:44
  135.7 113.9 %all-gather.11.cloned.1.call-done = bf16[4096,768]{1,0:T(8,128)(2,1)} async-done(((bf16[1024,768]{1,0:T(8,128)(2,1)}), bf16[4096,768]{1,0:T(8,128)(2,1)}) %all-gather.11.cloned.1.call-update) | async-done | bytes 6291472 | tf_op jit(solution)/shard_map/all_gather | solution.py:30
  249.6 6.1 convolution_convert_fusion
  259.6 6.1 convolution_convert_fusion.1
  269.6 17.3 all-gather.13.cloned.1.call-done
  289.3 12.6 fusion.4
  302.0 11.2 exponential_reduce_fusion.1
  313.2 11.1 fusion.47
  327.1 59.2 %reduce-scatter.31.cloned.1.call-done = f32[256,768]{1,0:T(8,128)} async-done(((f32[1024,768]{1,0:T(8,128)}), f32[256,768]{1,0:T(8,128)}) %reduce-scatter.31.cloned.1.call-update) | async-done | bytes 786448 | tf_op jit(solution)/shard_map/reduce_scatter | solution.py:44
  389.4 37.0 %all-gather.15.cloned.1.call-done = bf16[1024,768]{1,0:T(8,128)(2,1)} async-done(((bf16[256,768]{1,0:T(8,128)(2,1)}), bf16[1024,768]{1,0:T(8,128)(2,1)}) %all-gather.15.cloned.1.call-update) | async-done | bytes 1572880 | tf_op jit(solution)/shard_map/all_gather | solution.py:30
  435.5 59.2 %reduce-scatter.33.cloned.1.call-done = f32[256,768]{1,0:T(8,128)} async-done(((f32[1024,768]{1,0:T(8,128)}), f32[256,768]{1,0:T(8,128)}) %reduce-scatter.33.cloned.1.call-update) | async-done | bytes 786448 | tf_op jit(solution)/shard_map/reduce_scatter | solution.py:44
  500.2 35.3 %all-gather.17.cloned.1.call-done = bf16[1024,768]{1,0:T(8,128)(2,1)} async-done(((bf16[256,768]{1,0:T(8,128)(2,1)}), bf16[1024,768]{1,0:T(8,128)(2,1)}) %all-gather.17.cloned.1.call-update) | async-done | bytes 1572880 | tf_op jit(solution)/shard_map/all_gather | solution.py:30
  535.6 22.7 %fusion.108 = (f32[1024]{0:T(1024)}, f32[1024,8032]{0,1:T(8,128)}) fusion(bf16[1024,768]{1,0:T(8,128)(2,1)} %all-gather.17.cloned.1.call-done, bf16[8032,768]{1,0:T(8,128)(2,1)} %param.41), kind=kOutput, calls=%fused_computation.173 | convolution fusion | flops 12641467392 | bytes 46813184 | tf_op jit(solution)/shard_map/rd,vd->rv/dot_general | solution.py:162
  558.3 9.7 pmax.7
  568.0 15.4 fusion
  583.4 10.3 all-reduce.1
  595.1 15.1 fusion.3
  610.2 5.6 copy-done.5
  615.7 17.1 fusion.113
  633.6 58.5 %reduce-scatter.35.cloned.1.call-done = f32[256,768]{1,0:T(8,128)} async-done(((f32[1024,768]{1,0:T(8,128)}), f32[256,768]{1,0:T(8,128)}) %reduce-scatter.35.cloned.1.call-update) | async-done | bytes 786448 | tf_op jit(solution)/shard_map/reduce_scatter | solution.py:44
  696.8 37.2 %all-gather.19.cloned.1.call-done = bf16[1024,768]{1,0:T(8,128)(2,1)} async-done(((bf16[256,768]{1,0:T(8,128)(2,1)}), bf16[1024,768]{1,0:T(8,128)(2,1)}) %all-gather.19.cloned.1.call-update) | async-done | bytes 1572880 | tf_op jit(solution)/shard_map/all_gather | solution.py:34
  744.0 59.2 %reduce-scatter.37.cloned.1.call-done = f32[256,768]{1,0:T(8,128)} async-done(((f32[1024,768]{1,0:T(8,128)}), f32[256,768]{1,0:T(8,128)}) %reduce-scatter.37.cloned.1.call-update) | async-done | bytes 786448 | tf_op jit(solution)/shard_map/reduce_scatter | solution.py:44
  807.9 37.1 %all-gather.21.cloned.1.call-done = bf16[1024,768]{1,0:T(8,128)(2,1)} async-done(((bf16[256,768]{1,0:T(8,128)(2,1)}), bf16[1024,768]{1,0:T(8,128)(2,1)}) %all-gather.21.cloned.1.call-update) | async-done | bytes 1572880 | tf_op jit(solution)/shard_map/all_gather | solution.py:34
  847.4 21.3 %multiply_reduce_fusion = (f32[2,3,512]{2,1,0:T(4,128)S(1)}, f32[2,3,512,2048]{3,2,1,0:T(8,128)}) fusion(f32[2,3,512,2048]{3,2,1,0:T(8,128)} %get-tuple-element.121, f32[2,3,512]{2,1,0:T(4,128)S(1)} %copy-done.48, pred[2,2048]{1,0:T(4,128)(4,1)S(1)} %iota_compare_fusion.1, bf16[2,2048,3,64]{1,0,3,2:T(2,128)(2,1)} %reshape.279, ...), kind=kOutput, calls=%fused_computation.8 | convolution fusion | flops 836760576 | bytes 52326400 | tf_op jit(solution)/shard_map/sqhd,skhd->shqk/dot_general | solution.py:68
  868.7 21.5 %multiply_convert_fusion = bf16[2,3,512,2048]{3,2,1,0:T(8,128)(2,1)} fusion(f32[2,3,512,2048]{3,2,1,0:T(8,128)} %get-tuple-element.127, f32[2,3,512,2048]{3,2,1,0:T(8,128)} %get-tuple-element.121, f32[2,3,512]{2,1,0:T(4,128)S(1)} %get-tuple-element.126, f32[2,3,512]{2,1,0:T(4,128)S(1)} %copy-done.48, pred[2,2048]{1,0:T(4,128)(4,1)S(1)} %iota_compare_fusion.1), kind=kLoop, calls=%fused_computation.7 | loop fusion | flops 37748736 | bytes 62943232 | tf_op jit(solution)/shard_map/convert_element_type | solution.py:72
  890.2 8.6 fusion.54
  901.6 59.2 %reduce-scatter.39.cloned.1.call-done = f32[256,768]{1,0:T(8,128)} async-done(((f32[1024,768]{1,0:T(8,128)}), f32[256,768]{1,0:T(8,128)}) %reduce-scatter.39.cloned.1.call-update) | async-done | bytes 786448 | tf_op jit(solution)/shard_map/reduce_scatter | solution.py:44
  968.1 33.8 %all-gather.23.cloned.1.call-done = bf16[1024,768]{1,0:T(8,128)(2,1)} async-done(((bf16[256,768]{1,0:T(8,128)(2,1)}), bf16[1024,768]{1,0:T(8,128)(2,1)}) %all-gather.23.cloned.1.call-update) | async-done | bytes 1572880 | tf_op jit(solution)/shard_map/all_gather | solution.py:34
  1008.6 6.2 multiply_reduce_fusion.1
  1014.9 6.4 multiply_convert_fusion.1
  1042.5 11.3 fusion.12
  1057.3 5.2 convolution_bitcast_fusion.2
  1066.6 6.9 fusion.13
  1087.6 21.3 %fusion.122 = f32[8032,768]{0,1:T(8,128)} fusion(bf16[1024,8032]{0,1:T(8,128)(2,1)} %copy-done.5, bf16[1024,768]{1,0:T(8,128)(2,1)} %all-gather.17.cloned.1.call-done), kind=kOutput, calls=%fused_computation.187 | convolution fusion | flops 12633243648 | bytes 42696704 | tf_op jit(solution)/shard_map/rv,rd->vd/dot_general | solution.py:176
  1110.4 9.5 fusion.8
  1123.4 15.9 reduce-scatter.41.cloned.1.call-done
  1140.8 40.6 %all-reduce = (f32[768]{0:T(1024)}, f32[768]{0:T(1024)}, f32[768]{0:T(1024)}, f32[768]{0:T(1024)}) all-reduce(f32[768]{0:T(1024)S(1)} %get-tuple-element.88, f32[768]{0:T(1024)S(1)} %get-tuple-element.86, f32[768]{0:T(1024)S(1)} %copy-done.59, f32[768]{0:T(1024)S(1)} %copy-done.58), channel_id=1, replica_groups=mesh['dp'=8,'tensor'=4] {'dp','tensor'}, use_global_device_ids=true, to_apply=%region_29.30 | all-reduce | flops 3072 | bytes 24576 | tf_op jit(solution)/shard_map/psum | solution.py:277
  1183.6 40.7 %reduce-scatter.55.cloned.1.call-done = f32[96,512]{1,0:T(8,128)} async-done(((f32[768,512]{1,0:T(8,128)}), f32[96,512]{1,0:T(8,128)}) %reduce-scatter.55.cloned.1.call-update) | async-done | bytes 196624 | tf_op jit(solution)/shard_map/reduce_scatter | solution.py:269
  1224.3 42.2 %reduce-scatter.53.cloned.1.call-done = f32[96,512]{1,0:T(8,128)} async-done(((f32[768,512]{1,0:T(8,128)}), f32[96,512]{1,0:T(8,128)}) %reduce-scatter.53.cloned.1.call-update) | async-done | bytes 196624 | tf_op jit(solution)/shard_map/reduce_scatter | solution.py:268
  1266.5 38.7 %reduce-scatter.65.cloned.1.call-done = f32[96,192]{1,0:T(8,128)} async-done(((f32[768,192]{1,0:T(8,128)}), f32[96,192]{1,0:T(8,128)}) %reduce-scatter.65.cloned.1.call-update) | async-done | bytes 73744
  1305.2 38.7 %reduce-scatter.51.cloned.1.call-done = f32[96,192]{1,0:T(8,128)} async-done(((f32[768,192]{1,0:T(8,128)}), f32[96,192]{1,0:T(8,128)}) %reduce-scatter.51.cloned.1.call-update) | async-done | bytes 73744 | tf_op jit(solution)/shard_map/reduce_scatter | solution.py:265
  1344.0 38.8 %reduce-scatter.63.cloned.1.call-done = f32[96,192]{1,0:T(8,128)} async-done(((f32[768,192]{1,0:T(8,128)}), f32[96,192]{1,0:T(8,128)}) %reduce-scatter.63.cloned.1.call-update) | async-done | bytes 73744
  1382.7 38.6 %reduce-scatter.49.cloned.1.call-done = f32[96,192]{1,0:T(8,128)} async-done(((f32[768,192]{1,0:T(8,128)}), f32[96,192]{1,0:T(8,128)}) %reduce-scatter.49.cloned.1.call-update) | async-done | bytes 73744 | tf_op jit(solution)/shard_map/reduce_scatter | solution.py:264
  1421.3 38.7 %reduce-scatter.45.cloned.1.call-done = f32[96,192]{1,0:T(8,128)} async-done(((f32[768,192]{1,0:T(8,128)}), f32[96,192]{1,0:T(8,128)}) %reduce-scatter.45.cloned.1.call-update) | async-done | bytes 73744 | tf_op jit(solution)/shard_map/reduce_scatter | solution.py:262
  1460.1 38.6 %reduce-scatter.47.cloned.1.call-done = f32[96,192]{1,0:T(8,128)} async-done(((f32[768,192]{1,0:T(8,128)}), f32[96,192]{1,0:T(8,128)}) %reduce-scatter.47.cloned.1.call-update) | async-done | bytes 73744 | tf_op jit(solution)/shard_map/reduce_scatter | solution.py:263
  1498.7 159.0 %reduce-scatter.59.cloned.1.call-done = f32[8032,96]{0,1:T(8,128)} async-done(((f32[8032,768]{0,1:T(8,128)}), f32[8032,96]{0,1:T(8,128)}) %reduce-scatter.59.cloned.1.call-update) | async-done | bytes 3084304 | tf_op jit(solution)/shard_map/reduce_scatter | solution.py:275
  1657.7 214.9 %reduce-scatter.43.cloned.1.call-done = f32[1024,768]{1,0:T(8,128)} async-done(((f32[4096,768]{1,0:T(8,128)}), f32[1024,768]{1,0:T(8,128)}) %reduce-scatter.43.cloned.1.call-update) | async-done | bytes 3145744 | tf_op jit(solution)/shard_map/reduce_scatter | solution.py:44
  (314 shorter events, 153.6 us)
Async XLA Ops:
  7.2 425.6 %copy-start = (bf16[512,768]{1,0:T(8,128)(2,1)S(1)}, bf16[512,768]{1,0:T(8,128)(2,1)}, u32[]{:S(2)}) copy-start(bf16[512,768]{1,0:T(8,128)(2,1)} %param.40) | copy-start | bytes 2359300
  7.2 44.3 %all-gather.9.cloned.1.call-start = ((), (), s32[]{:S(2)}) async-start(), calls=%async_computation.20 | async-start | bytes 1966080 | tf_op jit(solution)/shard_map/all_gather | solution.py:30
  11.6 121.0 %reduce-scatter.29.cloned.1.call-start = ((), (), s32[]{:S(2)}) async-start(), calls=%async_computation.21 | async-start | bytes 3932160 | tf_op jit(solution)/shard_map/reduce_scatter | solution.py:44
  13.3 53.4 %copy-start.10 = (pred[2,512,512]{1,2,0:T(8,128)(4,1)}, pred[2,512,512]{1,2,0:T(8,128)(4,1)S(1)}, u32[]{:S(2)}) copy-start(pred[2,512,512]{1,2,0:T(8,128)(4,1)S(1)} %broadcast_and_fusion) | copy-start | bytes 1572868
  73.3 59.3 %copy-start.8 = (bf16[256,768]{1,0:T(8,128)(2,1)S(1)}, bf16[256,768]{1,0:T(8,128)(2,1)}, u32[]{:S(2)}) copy-start(bf16[256,768]{1,0:T(8,128)(2,1)} %param.21) | copy-start | bytes 1179652
  73.3 61.2 %copy-start.52 = (f32[768]{0:T(1024)S(1)}, f32[768]{0:T(1024)}, u32[]{:S(2)}) copy-start(f32[768]{0:T(1024)} %param.27) | copy-start | bytes 9220
  73.3 62.3 %copy-start.66 = (s32[2]{0:T(128)S(1)}, s32[2]{0:T(128)}, u32[]{:S(2)}) copy-start(s32[2]{0:T(128)} %param.24) | copy-start | bytes 28
  73.4 176.2 %copy-start.43 = (bf16[768,192]{0,1:T(8,128)(2,1)S(1)}, bf16[768,192]{0,1:T(8,128)(2,1)}, u32[]{:S(2)}) copy-start(bf16[768,192]{0,1:T(8,128)(2,1)} %param.35) | copy-start | bytes 884740
  73.4 176.2 %all-gather.11.cloned.1.call-start = ((), (), s32[]{:S(2)}) async-start(), calls=%async_computation.22 | async-start | bytes 7864320 | tf_op jit(solution)/shard_map/all_gather | solution.py:30
  74.1 212.8 %all-gather.13.cloned.1.call-start = ((), (), s32[]{:S(2)}) async-start(), calls=%async_computation.23 | async-start | bytes 1966080 | tf_op jit(solution)/shard_map/all_gather | solution.py:30
  134.5 121.2 %copy-start.60 = (f32[256]{0:T(256)}, f32[256]{0:T(256)S(1)}, u32[]{:S(2)}) copy-start(f32[256]{0:T(256)S(1)} %get-tuple-element.113) | copy-start | bytes 3076
  135.4 251.0 %reduce-scatter.31.cloned.1.call-start = ((), (), s32[]{:S(2)}) async-start(), calls=%async_computation.24 | async-start | bytes 3932160 | tf_op jit(solution)/shard_map/reduce_scatter | solution.py:44
  327.1 61.2 %copy-start.50 = (f32[768]{0:T(1024)S(1)}, f32[768]{0:T(1024)}, u32[]{:S(2)}) copy-start(f32[768]{0:T(1024)} %param.28) | copy-start | bytes 9220
  327.1 99.4 %copy-start.69 = (bf16[768,512]{1,0:T(8,128)(2,1)S(1)}, bf16[768,512]{1,0:T(8,128)(2,1)}, u32[]{:S(2)}) copy-start(bf16[768,512]{1,0:T(8,128)(2,1)} %param.38) | copy-start | bytes 2359300
  327.1 99.3 %all-gather.15.cloned.1.call-start = ((), (), s32[]{:S(2)}) async-start(), calls=%async_computation.25 | async-start | bytes 1966080 | tf_op jit(solution)/shard_map/all_gather | solution.py:30
  389.1 105.6 %reduce-scatter.33.cloned.1.call-start = ((), (), s32[]{:S(2)}) async-start(), calls=%async_computation.26 | async-start | bytes 3932160 | tf_op jit(solution)/shard_map/reduce_scatter | solution.py:44
  435.5 100.1 %all-gather.17.cloned.1.call-start = ((), (), s32[]{:S(2)}) async-start(), calls=%async_computation.27 | async-start | bytes 1966080 | tf_op jit(solution)/shard_map/all_gather | solution.py:30
  496.1 309.1 %copy-start.3 = (f32[256,768]{1,0:T(8,128)}, f32[256,768]{1,0:T(8,128)S(1)}, u32[]{:S(2)}) copy-start(f32[256,768]{1,0:T(8,128)S(1)} %get-tuple-element.103) | copy-start | bytes 2359300
  496.7 61.6 %copy-start.54 = (f32[256]{0:T(256)}, f32[256]{0:T(256)S(1)}, u32[]{:S(2)}) copy-start(f32[256]{0:T(256)S(1)} %get-tuple-element.117) | copy-start | bytes 3076
  498.3 193.8 %reduce-scatter.35.cloned.1.call-start = ((), (), s32[]{:S(2)}) async-start(), calls=%async_computation.28 | async-start | bytes 3932160 | tf_op jit(solution)/shard_map/reduce_scatter | solution.py:44
  632.9 101.1 %all-gather.19.cloned.1.call-start = ((), (), s32[]{:S(2)}) async-start(), calls=%async_computation.29 | async-start | bytes 1966080 | tf_op jit(solution)/shard_map/all_gather | solution.py:34
  696.8 106.5 %reduce-scatter.37.cloned.1.call-start = ((), (), s32[]{:S(2)}) async-start(), calls=%async_computation.30 | async-start | bytes 3932160 | tf_op jit(solution)/shard_map/reduce_scatter | solution.py:44
  743.9 61.2 %copy-start.12 = (f32[256,768]{1,0:T(8,128)S(1)}, f32[256,768]{1,0:T(8,128)}, u32[]{:S(2)}) copy-start(f32[256,768]{1,0:T(8,128)} %reduce-scatter.35.cloned.1.call-done) | copy-start | bytes 2359300
  744.0 101.0 %all-gather.21.cloned.1.call-start = ((), (), s32[]{:S(2)}) async-start(), calls=%async_computation.31 | async-start | bytes 1966080 | tf_op jit(solution)/shard_map/all_gather | solution.py:34
  807.7 153.1 %reduce-scatter.39.cloned.1.call-start = ((), (), s32[]{:S(2)}) async-start(), calls=%async_computation.32 | async-start | bytes 3932160 | tf_op jit(solution)/shard_map/reduce_scatter | solution.py:44
  899.2 61.6 %copy-start.53 = (f32[768]{0:T(1024)S(1)}, f32[768]{0:T(1024)}, u32[]{:S(2)}) copy-start(f32[768]{0:T(1024)} %param.27) | copy-start | bytes 9220
  899.3 61.6 %copy-start.61 = (f32[256]{0:T(256)S(1)}, f32[256]{0:T(256)}, u32[]{:S(2)}) copy-start(f32[256]{0:T(256)} %copy-done.60) | copy-start | bytes 3076
  901.6 60.7 %copy-start.23 = (f32[256,768]{1,0:T(8,128)S(1)}, f32[256,768]{1,0:T(8,128)}, u32[]{:S(2)}) copy-start(f32[256,768]{1,0:T(8,128)} %get-tuple-element.99) | copy-start | bytes 2359300
  901.6 60.7 %copy-start.65 = (f32[256]{0:T(256)S(1)}, f32[256]{0:T(256)}, u32[]{:S(2)}) copy-start(f32[256]{0:T(256)} %get-tuple-element.112) | copy-start | bytes 3076
  901.6 100.3 %all-gather.23.cloned.1.call-start = ((), (), s32[]{:S(2)}) async-start(), calls=%async_computation.33 | async-start | bytes 1966080 | tf_op jit(solution)/shard_map/all_gather | solution.py:34
  964.7 42.3 %copy-start.20 = (bf16[24,8,2,512]{3,1,2,0:T(8,128)(2,1)S(1)}, bf16[24,8,2,512]{3,1,2,0:T(8,128)(2,1)}, u32[]{:S(2)}) copy-start(bf16[24,8,2,512]{3,1,2,0:T(8,128)(2,1)} %copy-done.19) | copy-start | bytes 1179652
  964.7 155.3 %reduce-scatter.67.cloned.1.call-start = ((), (), s32[]{:S(2)}) async-start(), calls=%async_computation.47 | async-start | bytes 884736
  967.8 154.0 %reduce-scatter.61.cloned.1.call-start = ((), (), s32[]{:S(2)}) async-start(), calls=%async_computation.44 | async-start | bytes 884736
  1014.8 124.5 %reduce-scatter.41.cloned.1.call-start = ((), (), s32[]{:S(2)}) async-start(), calls=%async_computation.34 | async-start | bytes 3932160 | tf_op jit(solution)/shard_map/reduce_scatter | solution.py:44
  1029.7 153.9 %reduce-scatter.57.cloned.1.call-start = ((), (), s32[]{:S(2)}) async-start(), calls=%async_computation.42 | async-start | bytes 1769472 | tf_op jit(solution)/shard_map/reduce_scatter | solution.py:274
  1034.5 189.8 %reduce-scatter.55.cloned.1.call-start = ((), (), s32[]{:S(2)}) async-start(), calls=%async_computation.41 | async-start | bytes 1769472 | tf_op jit(solution)/shard_map/reduce_scatter | solution.py:269
  1038.6 228.0 %reduce-scatter.53.cloned.1.call-start = ((), (), s32[]{:S(2)}) async-start(), calls=%async_computation.40 | async-start | bytes 1769472 | tf_op jit(solution)/shard_map/reduce_scatter | solution.py:268
  1042.5 262.8 %reduce-scatter.65.cloned.1.call-start = ((), (), s32[]{:S(2)}) async-start(), calls=%async_computation.46 | async-start | bytes 884736
  1064.8 279.2 %reduce-scatter.51.cloned.1.call-start = ((), (), s32[]{:S(2)}) async-start(), calls=%async_computation.39 | async-start | bytes 884736 | tf_op jit(solution)/shard_map/reduce_scatter | solution.py:265
  1066.4 316.3 %reduce-scatter.63.cloned.1.call-start = ((), (), s32[]{:S(2)}) async-start(), calls=%async_computation.45 | async-start | bytes 884736
  1082.5 338.8 %reduce-scatter.49.cloned.1.call-start = ((), (), s32[]{:S(2)}) async-start(), calls=%async_computation.38 | async-start | bytes 884736 | tf_op jit(solution)/shard_map/reduce_scatter | solution.py:264
  1084.1 376.0 %reduce-scatter.45.cloned.1.call-start = ((), (), s32[]{:S(2)}) async-start(), calls=%async_computation.36 | async-start | bytes 884736 | tf_op jit(solution)/shard_map/reduce_scatter | solution.py:262
  1085.7 413.0 %reduce-scatter.47.cloned.1.call-start = ((), (), s32[]{:S(2)}) async-start(), calls=%async_computation.37 | async-start | bytes 884736 | tf_op jit(solution)/shard_map/reduce_scatter | solution.py:263
  1087.3 570.4 %reduce-scatter.59.cloned.1.call-start = ((), (), s32[]{:S(2)}) async-start(), calls=%async_computation.43 | async-start | bytes 27869184 | tf_op jit(solution)/shard_map/reduce_scatter | solution.py:275
  1108.9 763.7 %reduce-scatter.43.cloned.1.call-start = ((), (), s32[]{:S(2)}) async-start(), calls=%async_computation.35 | async-start | bytes 15728640 | tf_op jit(solution)/shard_map/reduce_scatter | solution.py:44
  1119.9 61.4 %copy-start.24 = (f32[256,768]{1,0:T(8,128)S(1)}, f32[256,768]{1,0:T(8,128)}, u32[]{:S(2)}) copy-start(f32[256,768]{1,0:T(8,128)} %get-tuple-element.97) | copy-start | bytes 2359300
  1119.9 61.4 %copy-start.64 = (f32[256]{0:T(256)S(1)}, f32[256]{0:T(256)}, u32[]{:S(2)}) copy-start(f32[256]{0:T(256)} %get-tuple-element.110) | copy-start | bytes 3076
  1120.0 752.7 %copy-start.1 = (bf16[512,768]{1,0:T(8,128)(2,1)S(1)}, bf16[512,768]{1,0:T(8,128)(2,1)}, u32[]{:S(2)}) copy-start(bf16[512,768]{1,0:T(8,128)(2,1)} %param.40) | copy-start | bytes 2359300
  (61 other events, 570.4 us)
Sparse Core Ops, SparseCore 0:
  11.7 39.7 all-gather.8
  73.5 59.0 reduce-scatter.28
  134.2 115.3 all-gather.10
  251.6 35.3 all-gather.12
  327.2 59.0 reduce-scatter.30
  389.3 37.1 all-gather.14
  435.6 59.0 reduce-scatter.32
  498.4 37.1 all-gather.16
  633.0 59.0 reduce-scatter.34
  696.9 37.0 all-gather.18
  744.1 59.0 reduce-scatter.36
  807.8 37.1 all-gather.20
  901.7 59.1 reduce-scatter.38
  964.8 37.1 all-gather.22
  1004.9 33.8 reduce-scatter.66
  1041.9 35.0 reduce-scatter.60
  1079.1 60.2 reduce-scatter.40
  1143.1 38.8 reduce-scatter.56
  1185.9 38.3 reduce-scatter.54
  1228.0 38.4 reduce-scatter.52
  1270.2 34.9 reduce-scatter.64
  1309.0 34.9 reduce-scatter.50
  1347.7 34.9 reduce-scatter.62
  1386.3 34.9 reduce-scatter.48
  1425.1 34.9 reduce-scatter.44
  1463.7 34.9 reduce-scatter.46
  1502.9 154.7 reduce-scatter.58
  1660.8 211.8 reduce-scatter.42
where the time goes:
time: 1890 us; the launch traced here: 1880 us
  waiting for transfers between devices  1410 us (75%)
  matrix products  241 us (13%)
  other arithmetic  104 us (6%)
  blocking collectives  60.6 us (3%)
  local copies, waits for them, and re-layouts  46.1 us (2%)
    reduce_scatter x8, waiting for transfers between devices, scatter_rows(): lax.psum_scatter(local_term(), 'tensor', scatter_dimension=0, tiled=True)  585 us
    all_gather x5, waiting for transfers between devices, gather_rows(): return lax.all_gather(local_rows, 'tensor', axis=0, tiled=True)  242 us
    reduce_scatter x1, waiting for transfers between devices, on_device(): lax.psum_scatter(grad_embed_local, 'dp', scatter_dimension=1, tiled=True)  159 us
    all_gather x3, waiting for transfers between devices, gather_grads(): return lax.all_gather(local_rows, 'tensor', axis=0, tiled=True)  108 us
    unnamed x32, waiting for transfers between devices  78.6 us
    reduce_scatter x1, waiting for transfers between devices, on_device(): lax.psum_scatter(grad_ff_gate, 'dp', scatter_dimension=0, tiled=True)  42.2 us
    reduce_scatter x1, waiting for transfers between devices, on_device(): lax.psum_scatter(grad_ff_up, 'dp', scatter_dimension=0, tiled=True)  40.7 us
    psum x1, blocking collectives, on_device(): lax.psum((grad_gain_self, grad_gain_cross, grad_gain_ff, grad_gain_final)...  40.6 us
  transfers between devices with their start and end apart: 28, of which 25 were waited for; matrix products, arithmetic and copies ran while one was open for 8% of the time, Pallas kernels for 0%

commit v1 on v0

v1 whole, which is shorter than its diff:
```python
import jax
import jax.numpy as jnp
from jax import lax
from jax.sharding import PartitionSpec as P
from jax.experimental import pallas as pl
from jax.experimental.pallas import tpu as pltpu

D = 768
HDIM = 64
TGT = 512
SRC = 2048
F32 = jnp.float32
BF16 = jnp.bfloat16
MESH_ID = pl.DeviceIdType.MESH

epsilon = 1e-06


def normalize(values, gain_vec):
    inv_scale = lax.rsqrt(jnp.mean(values * values, axis=-1, keepdims=True) + epsilon)
    return (values * inv_scale * gain_vec, inv_scale)


def norm_back(values, inv_scale, gain_vec, grad_out):
    weighted = gain_vec * grad_out
    grad_gain = jnp.sum(grad_out * values * inv_scale, axis=0)
    grad_values = inv_scale * weighted - values * inv_scale**3 * jnp.mean(
        weighted * values, axis=-1, keepdims=True
    )
    return (grad_values, grad_gain)


def dot_nt(left, right):
    return lax.dot_general(left, right, (((1,), (1,)), ((), ())), preferred_element_type=F32)


def dot_nn(left, right):
    return lax.dot_general(left, right, (((1,), (0,)), ((), ())), preferred_element_type=F32)


def dot_tn(left, right):
    return lax.dot_general(left, right, (((0,), (0,)), ((), ())), preferred_element_type=F32)


def swap(value, axis_name, size, bit):
    return lax.ppermute(value, axis_name, [(i, i ^ bit) for i in range(size)])


def gather_kernel(*refs):
    groups = (len(refs) - 4) // 2
    ins, outs = refs[:groups], refs[groups : 2 * groups]
    send_sem, recv_sem, local_sem, core_sem = refs[2 * groups :]
    dp = lax.axis_index("dp")
    z = lax.axis_index("tensor")
    core_peer, x_peer, y_peer = (
        dp + 1 - 2 * lax.rem(dp, 2),
        dp + 2 - 4 * lax.rem(dp // 2, 2),
        dp + 4 - 8 * (dp // 4),
    )
    xy_peer = x_peer + y_peer - dp
    z_peers = []
    for j in (1, 2, 3):
        low, high = lax.rem(z, 2), z // 2
        new_low = 1 - low if j % 2 else low
        new_high = 1 - high if j // 2 else high
        z_peers.append(new_high * 2 + new_low)
    barrier = pltpu.get_barrier_semaphore()
    for other in (core_peer, x_peer, y_peer):
        pl.semaphore_signal(
            barrier, inc=1, device_id={"dp": other, "tensor": z}, device_id_type=MESH_ID
        )
    for other in z_peers:
        pl.semaphore_signal(
            barrier, inc=1, device_id={"dp": dp, "tensor": other}, device_id_type=MESH_ID
        )
    pl.semaphore_wait(barrier, 6)

    def piece(ref, shard, index, rows, start=0, count=None):
        offset = pl.multiple_of(index * rows + start, 16)
        return ref.at[shard, pl.ds(offset, rows if count is None else count)]

    def remote(src, dst, sem, target_dp, target_z):
        copy = pltpu.make_async_remote_copy(
            src_ref=src,
            dst_ref=dst,
            send_sem=send_sem.at[sem],
            recv_sem=recv_sem.at[sem],
            device_id={"dp": target_dp, "tensor": target_z},
            device_id_type=MESH_ID,
        )
        copy.start()
        return copy

    slots = 24
    z_copies, x_copies, y_copies, dx_copies, dy_copies, c_copies, own = [], [], [], [], [], [], []
    for g in range(groups):
        rows = ins[g].shape[0] // 8
        offset = pl.multiple_of(dp * rows, 16)
        z_copies.append(
            [
                remote(
                    ins[g].at[pl.ds(offset, rows)],
                    piece(outs[g], z, dp, rows),
                    g * slots + j,
                    dp,
                    z_peers[j],
                )
                for j in range(3)
            ]
        )
        copy = pltpu.make_async_copy(ins[g], outs[g].at[z], local_sem.at[g])
        copy.start()
        own.append(copy)
    for g in range(groups):
        rows = ins[g].shape[0] // 8
        xs, ys = [], []
        for j in range(3):
            z_copies[g][j].wait()
            part = piece(outs[g], z_peers[j], dp, rows)
            xs.append(remote(part, part, g * slots + 3 + j, x_peer, z))
            ys.append(remote(part, part, g * slots + 6 + j, y_peer, z))
        x_copies.append(xs)
        y_copies.append(ys)
    for g in range(groups):
        rows = ins[g].shape[0] // 8
        dxs, dys, cs = [], [], []
        for j in range(3):
            part = piece(outs[g], z_peers[j], dp, rows)
            cs.append(remote(part, part, g * slots + 15 + j, core_peer, z))
            x_copies[g][j].wait()
            part = piece(outs[g], z_peers[j], x_peer, rows, 0, rows // 2)
            dys.append(remote(part, part, g * slots + 9 + j, y_peer, z))
            y_copies[g][j].wait()
            part = piece(outs[g], z_peers[j], y_peer, rows, rows // 2, rows // 2)
            dxs.append(remote(part, part, g * slots + 12 + j, x_peer, z))
            for n, owner in enumerate((x_peer, y_peer)):
                part = piece(outs[g], z_peers[j], owner, rows)
                cs.append(remote(part, part, g * slots + 18 + 2 * j + n, core_peer, z))
        dx_copies.append(dxs)
        dy_copies.append(dys)
        c_copies.append(cs)
    for g in range(groups):
        rows = ins[g].shape[0] // 8
        for j in range(3):
            dy_copies[g][j].wait()
            dx_copies[g][j].wait()
            part = piece(outs[g], z_peers[j], xy_peer, rows)
            copy = pltpu.make_async_remote_copy(
                src_ref=part,
                dst_ref=part,
                send_sem=core_sem.at[g * 3 + j, 0],
                recv_sem=core_sem.at[g * 3 + j, 1],
                device_id={"dp": core_peer, "tensor": z},
                device_id_type=MESH_ID,
            )
            copy.start()
            c_copies[g].append(copy)
    for g in range(groups):
        own[g].wait()
        for copy in c_copies[g]:
            copy.wait()


def gather_weights(shards, dp_size):
    if dp_size != 8:
        outs = []
        for shard in shards:
            rows = shard.shape[0] // dp_size
            part = lax.dynamic_slice_in_dim(shard, lax.axis_index("dp") * rows, rows, 0)
            outs.append(
                lax.all_gather(part, ("tensor", "dp"), axis=0, tiled=True).reshape(4, -1, D)
            )
        return outs
    groups = len(shards)
    return pl.pallas_call(
        gather_kernel,
        out_shape=[jax.ShapeDtypeStruct((4,) + shard.shape, shard.dtype) for shard in shards],
        in_specs=[pl.BlockSpec(memory_space=pl.ANY)] * groups,
        out_specs=[pl.BlockSpec(memory_space=pl.ANY)] * groups,
        scratch_shapes=[
            pltpu.SemaphoreType.DMA((24 * groups,)),
            pltpu.SemaphoreType.DMA((24 * groups,)),
            pltpu.SemaphoreType.DMA((groups,)),
            pltpu.SemaphoreType.DMA((3 * groups, 2)),
        ],
        compiler_params=pltpu.CompilerParams(collective_id=0, has_side_effects=True),
    )(*shards)


def reduce_dp(grads, dp_size):
    rows = D // dp_size
    if dp_size != 8:
        return lax.psum_scatter(
            grads.astype(F32), "dp", scatter_dimension=0, tiled=True
        ).astype(BF16)
    dp = lax.axis_index("dp")
    c, x, y = lax.rem(dp, 2), lax.rem(dp // 2, 2), dp // 4

    def fold(value, axis, position, bit):
        mine = lax.dynamic_index_in_dim(value, position, axis, keepdims=False)
        other = lax.dynamic_index_in_dim(value, 1 - position, axis, keepdims=False)
        got = swap(other, "dp", dp_size, bit)
        return (mine.astype(F32) + got.astype(F32)).astype(BF16)

    value = grads.reshape((2, 2, 2, rows) + grads.shape[1:])
    value = fold(value, 2, c, 1)
    width = value.shape[-1]
    half = (width // 2 + 127) // 128 * 128
    first = fold(fold(value[..., :half], 1, x, 2), 0, y, 4)
    second = fold(fold(value[..., half:], 0, y, 4), 0, x, 2)
    return jnp.concatenate([first, second], axis=-1)


def reduce_weights(grads, dp_size):
    z = lax.axis_index("tensor")
    part = reduce_dp(grads, dp_size)
    total = lax.dynamic_index_in_dim(part, z, 1, keepdims=False).astype(F32)
    for j in (1, 2, 3):
        piece = lax.dynamic_index_in_dim(part, z ^ j, 1, keepdims=False)
        total = total + swap(piece, "tensor", 4, j).astype(F32)
    return total


def heads(rows):
    return rows.reshape(rows.shape[0], -1, HDIM)


def scores_of(queries, keys, mask):
    scores = jnp.einsum("qhd,khd->hqk", heads(queries), heads(keys), preferred_element_type=F32)
    return jnp.where(mask, scores * HDIM ** (-0.5), -1000000000.0)


def attend(queries, keys, values, mask):
    scores = scores_of(queries, keys, mask)
    top = jnp.max(scores, axis=-1, keepdims=True)
    lse = top + jnp.log(jnp.sum(jnp.exp(scores - top), axis=-1, keepdims=True))
    probs = jnp.exp(scores - lse).astype(BF16)
    out = jnp.einsum("hqk,khd->qhd", probs, heads(values), preferred_element_type=F32)
    return out.reshape(queries.shape), lse


def attend_back(queries, keys, values, mask, lse, grad_out, row_dot):
    probs = jnp.exp(scores_of(queries, keys, mask) - lse)
    grad_probs = jnp.einsum(
        "qhd,khd->hqk", heads(grad_out), heads(values), preferred_element_type=F32
    )
    if row_dot is None:
        row_dot = jnp.sum(probs * grad_probs, axis=-1, keepdims=True)
    grad_scores = (probs * (grad_probs - row_dot)).astype(BF16)
    scale = HDIM ** (-0.5)
    grad_q = jnp.einsum("hqk,khd->qhd", grad_scores, heads(keys), preferred_element_type=F32)
    grad_k = jnp.einsum("hqk,qhd->khd", grad_scores, heads(queries), preferred_element_type=F32)
    grad_v = jnp.einsum(
        "hqk,qhd->khd", probs.astype(BF16), heads(grad_out), preferred_element_type=F32
    )
    return (
        grad_q.reshape(queries.shape) * scale,
        (grad_k.reshape(keys.shape) * scale).astype(BF16),
        grad_v.reshape(values.shape).astype(BF16),
    )


def make(mesh):
    dp_size = mesh.shape["dp"]

    def on_device(
        block_in,
        source,
        target_len,
        source_len,
        targets,
        gain_self,
        gain_cross,
        gain_ff,
        gain_final,
        self_q,
        self_k,
        self_v,
        self_o,
        cross_q,
        cross_k,
        cross_v,
        cross_o,
        ff_gate,
        ff_up,
        ff_down,
        embed_table,
    ):
        z = lax.axis_index("tensor")
        half = lax.rem(z, 2)
        seq = z // 2
        rows = block_in.shape[0]
        srcs = source.shape[0]

        def pair_swap(value):
            return swap(value, "tensor", 4, 1)

        def pair_rows(own):
            other = pair_swap(own)
            return jnp.where(
                half == 0,
                jnp.concatenate([own, other], 0),
                jnp.concatenate([other, own], 0),
            )

        def own_rows(both, axis=0):
            return lax.dynamic_slice_in_dim(both, half * rows, rows, axis)

        def other_rows(both, axis=0):
            return lax.dynamic_slice_in_dim(both, (1 - half) * rows, rows, axis)

        w_self, w_cross, w_ff = gather_weights(
            [
                jnp.concatenate([self_q.T, self_k.T, self_v.T, self_o], 0),
                jnp.concatenate([cross_q.T, cross_k.T, cross_v.T, cross_o], 0),
                jnp.concatenate([ff_gate.T, ff_up.T, ff_down], 0),
            ],
            dp_size,
        )

        def part(stack, index, size):
            return stack[:, index * size : (index + 1) * size].reshape(-1, D)

        hid = self_q.shape[1]
        fhid = ff_gate.shape[1]
        sq, sk, sv, so = (part(w_self, i, hid) for i in range(4))
        cq, ck, cv, co = (part(w_cross, i, hid) for i in range(4))
        wg, wu, wd = (part(w_ff, i, fhid) for i in range(3))

        my_len = lax.dynamic_index_in_dim(target_len, seq, keepdims=False)
        my_src = lax.dynamic_index_in_dim(source_len, seq, keepdims=False)
        pos = jnp.arange(TGT)
        self_mask = ((pos[None, :] <= pos[:, None]) & (pos[None, :] < my_len))[None]
        cross_mask = (half * srcs + jnp.arange(srcs) < my_src)[None, None, :]

        x_pair = pair_rows(block_in).astype(F32)
        n1, r1 = normalize(x_pair, gain_self)
        n1 = n1.astype(BF16)
        q1 = dot_nt(n1, sq).astype(BF16)
        k1 = dot_nt(n1, sk).astype(BF16)
        v1 = dot_nt(n1, sv).astype(BF16)
        a1, lse1 = attend(q1, k1, v1, self_mask)
        a1 = a1.astype(BF16)
        h1 = x_pair + dot_nn(a1, so)
        n2, r2 = normalize(h1, gain_cross)
        n2 = n2.astype(BF16)
        q2 = dot_nt(n2, cq).astype(BF16)
        k2 = dot_nt(source, ck).astype(BF16)
        v2 = dot_nt(source, cv).astype(BF16)
        o2, lse_own = attend(q2, k2, v2, cross_mask)
        o2_other = pair_swap(other_rows(o2).astype(BF16)).astype(F32)
        lse_other = pair_swap(lse_own)
        lse2 = jnp.logaddexp(lse_own, lse_other)

        def weigh(lse_part, out_part):
            weight = own_rows(jnp.exp(lse_part - lse2), 1)[:, :, 0].T
            return (heads(out_part) * weight[:, :, None]).reshape(out_part.shape)

        a2 = weigh(lse_own, own_rows(o2)) + weigh(lse_other, o2_other)
        a2b = a2.astype(BF16)
        h1o = own_rows(h1)
        r2o = own_rows(r2)
        h2 = h1o + dot_nn(a2b, co)
        n3, r3 = normalize(h2, gain_ff)
        n3 = n3.astype(BF16)
        gate_pre = dot_nt(n3, wg)
        up_pre = dot_nt(n3, wu)
        gelu_gate, gelu_back = jax.vjp(lambda v: jax.nn.gelu(v, approximate=True), gate_pre)
        mixed = (gelu_gate * up_pre).astype(BF16)
        block_out = h2 + dot_nn(mixed, wd)
        nf, rf = normalize(block_out, gain_final)
        fin = (nf * D ** (-0.5)).astype(BF16)

        vocab = embed_table.shape[0]
        fin_all = jnp.concatenate([fin] + [swap(fin, "tensor", 4, j) for j in (1, 2, 3)], 0)

        def relative(by_block):
            return jnp.concatenate(
                [lax.dynamic_index_in_dim(by_block, z ^ j, 0, keepdims=False) for j in range(4)], 0
            )

        tgt_rel = relative(targets.reshape(4, rows))
        pos_all = jnp.arange(4 * rows)
        live = lax.rem(pos_all, TGT) < jnp.repeat(target_len, TGT, total_repeat_length=4 * rows)
        live_rel = relative(live.reshape(4, rows))
        logits = dot_nt(fin_all, embed_table)
        columns = z * vocab + jnp.arange(vocab)
        hit = columns[None, :] == tgt_rel[:, None]
        top = jnp.max(logits, axis=1)
        total = jnp.sum(jnp.exp(logits - top[:, None]), axis=1)
        picked = jnp.sum(jnp.where(hit, logits, 0.0), axis=1)
        stats = jnp.stack([top, total, picked]).reshape(3, 4, rows)
        stats = jnp.stack(
            [lax.dynamic_index_in_dim(stats, z ^ j, 1, keepdims=False) for j in range(4)], 1
        )
        gathered = jnp.stack(
            [stats] + [swap(stats, "tensor", 4, j) for j in (1, 2, 3)], 0
        ).reshape(4, 3, 4 * rows)
        g_top = jnp.max(gathered[:, 0], axis=0)
        g_total = jnp.sum(gathered[:, 1] * jnp.exp(gathered[:, 0] - g_top), axis=0)
        g_lse = g_top + jnp.log(g_total)
        token_loss = jnp.where(live, g_lse - jnp.sum(gathered[:, 2], axis=0), 0.0)
        lse_rel = relative(g_lse.reshape(4, rows))
        grad_logits = jnp.where(
            live_rel[:, None],
            jnp.exp(logits - lse_rel[:, None]) - hit.astype(F32),
            0.0,
        ).astype(BF16)
        gf_all = dot_nn(grad_logits, embed_table)
        grad_final = gf_all[:rows]
        for j in (1, 2, 3):
            grad_final = grad_final + swap(
                gf_all[j * rows : (j + 1) * rows].astype(BF16), "tensor", 4, j
            ).astype(F32)
        grad_embed = dot_tn(fin_all, grad_logits).astype(BF16)
        grad_embed = reduce_dp(grad_embed, dp_size).astype(F32).T

        def by_shard(grad):
            return grad.astype(BF16).reshape(D, 4, -1)

        g_res, gg_final = norm_back(block_out, rf, gain_final, grad_final * D ** (-0.5))
        gr = g_res.astype(BF16)
        grad_mixed = dot_nt(gr, wd)
        g_gate = gelu_back(grad_mixed * up_pre)[0].astype(BF16)
        g_up = (grad_mixed * gelu_gate).astype(BF16)
        gn3 = dot_nn(g_gate, wg) + dot_nn(g_up, wu)
        step, gg_ff = norm_back(h2, r3, gain_ff, gn3)
        g_res = g_res + step
        ff_grads = reduce_weights(
            jnp.concatenate(
                [
                    by_shard(dot_tn(n3, g_gate)),
                    by_shard(dot_tn(n3, g_up)),
                    by_shard(dot_tn(gr, mixed)),
                ],
                2,
            ),
            dp_size,
        )
        gr_own = g_res.astype(BF16)
        gr = pair_rows(gr_own)
        g_att = dot_nt(gr, co).astype(BF16)
        dot_own = jnp.sum(heads(own_rows(g_att).astype(F32)) * heads(a2), axis=-1).T[:, :, None]
        dot_other = pair_swap(dot_own)
        row_dot = jnp.where(
            half == 0,
            jnp.concatenate([dot_own, dot_other], 1),
            jnp.concatenate([dot_other, dot_own], 1),
        )
        gq, gk, gv = attend_back(q2, k2, v2, cross_mask, lse2, g_att, row_dot)
        gq = (own_rows(gq) + pair_swap(other_rows(gq).astype(BF16)).astype(F32)).astype(BF16)
        grad_source = dot_nn(gk, ck) + dot_nn(gv, cv)
        n2o = own_rows(n2)
        cross_grads = reduce_weights(
            jnp.concatenate(
                [
                    by_shard(dot_tn(n2o, gq)),
                    by_shard(dot_tn(source, gk)),
                    by_shard(dot_tn(source, gv)),
                    by_shard(dot_tn(gr_own, a2b)),
                ],
                2,
            ),
            dp_size,
        )
        step, gg_cross = norm_back(h1o, r2o, gain_cross, dot_nn(gq, cq))
        g_res = g_res + step
        gr_own = g_res.astype(BF16)
        gr = pair_rows(gr_own)
        g_att = dot_nt(gr, so).astype(BF16)
        gq, gk, gv = attend_back(q1, k1, v1, self_mask, lse1, g_att, None)
        gq, gk, gv = own_rows(gq.astype(BF16)), own_rows(gk), own_rows(gv)
        n1o = own_rows(n1)
        self_grads = reduce_weights(
            jnp.concatenate(
                [
                    by_shard(dot_tn(n1o, gq)),
                    by_shard(dot_tn(n1o, gk)),
                    by_shard(dot_tn(n1o, gv)),
                    by_shard(dot_tn(gr_own, own_rows(a1))),
                ],
                2,
            ),
            dp_size,
        )
        gn1 = dot_nn(gq, sq) + dot_nn(gk, sk) + dot_nn(gv, sv)
        step, gg_self = norm_back(own_rows(x_pair), own_rows(r1), gain_self, gn1)
        grad_block_in = g_res + step
        gains = lax.psum(jnp.stack([gg_self, gg_cross, gg_ff, gg_final]), ("dp", "tensor"))

        def cols(grads, index, size):
            return grads[:, index * size : (index + 1) * size]

        return (
            block_out,
            token_loss,
            grad_block_in,
            grad_source,
            gains[0],
            gains[1],
            gains[2],
            gains[3],
            cols(self_grads, 0, hid),
            cols(self_grads, 1, hid),
            cols(self_grads, 2, hid),
            cols(self_grads, 3, hid).T,
            cols(cross_grads, 0, hid),
            cols(cross_grads, 1, hid),
            cols(cross_grads, 2, hid),
            cols(cross_grads, 3, hid).T,
            cols(ff_grads, 0, fhid),
            cols(ff_grads, 1, fhid),
            cols(ff_grads, 2, fhid).T,
            grad_embed,
        )

    return on_device


def solution(mesh):
    rows = P(("dp", "tensor"), None)
    wide, tall = P(None, "tensor"), P("tensor", None)
    in_specs = (rows, rows) + (P("dp"),) * 3 + (P(),) * 4
    in_specs += (wide, wide, wide, tall) * 2 + (wide, wide, tall, tall)
    g_in, g_out = P("dp", "tensor"), P("tensor", "dp")
    out_specs = (rows, P("dp"), rows, rows) + (P(),) * 4
    out_specs += (g_in, g_in, g_in, g_out) * 2 + (g_in, g_in, g_out, g_out)
    return jax.shard_map(
        make(mesh), mesh=mesh, in_specs=in_specs, out_specs=out_specs, check_vma=False
    )
```

time: 1890 us -> 952 us (0.50)
  waiting for transfers between devices: 1410 us -> 140 us
  local copies, waits for them, and re-layouts: 46.1 us -> 202 us
  Pallas kernels: 0 us -> 148 us
  starting transfers between devices: 2.72 us -> 70.8 us
  blocking collectives: 60.6 us -> 41.3 us
    reduce_scatter x16 -> x0, waiting for transfers between devices: 981 us -> none  [the longest x8 585 us: scatter_rows(): lax.psum_scatter(local_term(), 'tensor', scatter_dimension=0, tiled=True)]
    all_gather x8 -> x0, waiting for transfers between devices: 350 us -> none  [the longest x5 242 us: gather_rows(): return lax.all_gather(local_rows, 'tensor', axis=0, tiled=True)]
    pallas_call x0 -> x1, Pallas kernels: none -> 148 us  [gather_weights(): pl.pallas_call(gather_kernel, out_shape=[jax.ShapeDtypeStruct((4,) + shar...]
    ppermute x0 -> x45, waiting for transfers between devices: none -> 140 us  [swap(): return lax.ppermute(value, axis_name, [(i, i ^ bit) for i in range(size)])]
    concatenate x0 -> x20, local copies, waits for them, and re-layouts: none -> 82.9 us  [the longest x8 35.9 us: on_device(): jnp.concatenate([by_shard(dot_tn(n2o, gq)), by_shard(dot_tn(source, gk)),...]
    unnamed x32 -> x0, waiting for transfers between devices: 78.6 us -> none
    ppermute x0 -> x45, starting transfers between devices: none -> 70.8 us  [swap(): return lax.ppermute(value, axis_name, [(i, i ^ bit) for i in range(size)])]
    slice x0 -> x9, local copies, waits for them, and re-layouts: none -> 21 us  [the longest x2 13.6 us: part(): return stack[:, index * size:(index + 1) * size].reshape(-1, D)]
  transfers between devices with their start and end apart: 28 -> 45, of which waited for: 25 -> 26; matrix products, arithmetic and copies ran while one was open for 8% -> 35% of each run, Pallas kernels for 0% -> 16%
where the time goes in v1:
time: 952 us; the launch traced here: 946 us
  matrix products  225 us (24%)
  local copies, waits for them, and re-layouts  202 us (21%)
  Pallas kernels  148 us (16%)
  waiting for transfers between devices  140 us (15%)
  other arithmetic  116 us (12%)
  starting transfers between devices  70.8 us (7%)
  blocking collectives  41.3 us (4%)
    pallas_call x1, Pallas kernels, gather_weights(): pl.pallas_call(gather_kernel, out_shape=[jax.ShapeDtypeStruct((4,) + shar...  148 us
    ppermute x45, waiting for transfers between devices, swap(): return lax.ppermute(value, axis_name, [(i, i ^ bit) for i in range(size)])  140 us
    ppermute x45, starting transfers between devices, swap(): return lax.ppermute(value, axis_name, [(i, i ^ bit) for i in range(size)])  70.8 us
    dot_general x12, matrix products, dot_nt(): lax.dot_general(left, right, (((1,), (1,)), ((), ())), preferred_element_...  47.9 us
    dot_general x12, matrix products, dot_tn(): lax.dot_general(left, right, (((0,), (0,)), ((), ())), preferred_element_...  42.7 us
    psum x1, blocking collectives, on_device(): lax.psum(jnp.stack([gg_self, gg_cross, gg_ff, gg_final]), ('dp', 'tensor'))  41.3 us
    unnamed x275, local copies, waits for them, and re-layouts  41.1 us
    dot_general x12, matrix products, dot_nn(): lax.dot_general(left, right, (((1,), (0,)), ((), ())), preferred_element_...  37.7 us
  transfers between devices with their start and end apart: 45, of which 26 were waited for; matrix products, arithmetic and copies ran while one was open for 35% of the time, Pallas kernels for 16%

profile of v1, /device:TPU:0, one launch (start us, length us, event | category | flops | bytes accessed | tf_op | source)
XLA Modules:
  0.0 945.5 jit_solution(8770166183315453208)
XLA Ops:
  16.1 148.1 %shard_map.356 = (bf16[4,768,768]{2,1,0:T(8,128)(2,1)}, bf16[4,768,768]{2,1,0:T(8,128)(2,1)}, bf16[4,1536,768]{2,1,0:T(8,128)(2,1)}) custom-call(bf16[768,768]{1,0:T(8,128)(2,1)} %pad_maximum_fusion.4.refs_0_, bf16[768,768]{1,0:T(8,128)(2,1)} %pad_maximum_fusion.5.refs_1_, bf16[1536,768]{1,0:T(8,128)(2,1)} %pad_maximum_fusion.2.refs_2_), custom_call_target="tpu_custom_call" | custom-call | tf_op jit(solution)/shard_map/pallas_call | solution.py:175
  164.3 6.7 fusion.151
  173.6 6.8 fusion.153
  207.1 8.2 convolution_convert_fusion.21
  219.7 11.9 %fusion.5 = (f32[12,512]{1,0:T(8,128)S(1)}, f32[12,512,1024]{2,1,0:T(8,128)}) fusion(pred[1024]{0:T(1024)(128)(4,1)S(1)} %add_compare_fusion, bf16[512,12,64]{0,2,1:T(8,128)(2,1)S(1)} %bitcast.342, bf16[1024,12,64]{0,2,1:T(8,128)(2,1)} %bitcast.351), kind=kOutput, calls=%fused_computation.14 | convolution fusion | flops 824174592 | bytes 27550720 | tf_op jit(solution)/shard_map/qhd,khd->hqk/dot_general | solution.py:229
  231.6 11.3 %exponential_reduce_fusion.1 = f32[12,512]{1,0:T(8,128)S(1)} fusion(f32[12,512,1024]{2,1,0:T(8,128)} %get-tuple-element.195, f32[12,512]{1,0:T(8,128)S(1)} %get-tuple-element.194, pred[1024]{0:T(1024)(128)(4,1)S(1)} %add_compare_fusion), kind=kLoop, calls=%fused_computation.10 | loop fusion | flops 25159680 | bytes 25216000 | tf_op jit(solution)/shard_map/reduce_sum | solution.py:236
  243.6 11.0 %fusion.8 = f32[12,64,512]{2,1,0:T(8,128)S(1)} fusion(bf16[1024,12,64]{0,2,1:T(8,128)(2,1)S(1)} %bitcast.416, f32[12,512,1024]{2,1,0:T(8,128)} %get-tuple-element.195, f32[12,512]{1,0:T(8,128)} %log_add_fusion, pred[1024]{0:T(1024)(128)(4,1)S(1)} %add_compare_fusion), kind=kOutput, calls=%fused_computation.21 | convolution fusion | flops 830472192 | bytes 28337152 | tf_op jit(solution)/shard_map/hqk,khd->qhd/dot_general | solution.py:238
  260.9 7.2 collective-permute-done.1
  289.8 9.1 collective-permute-done.3
  299.0 14.2 %collective-permute-done.4 = bf16[256,768]{1,0:T(8,128)(2,1)S(1)} collective-permute-done((bf16[256,768]{1,0:T(8,128)(2,1)S(1)}, bf16[256,768]{1,0:T(8,128)(2,1)S(1)}, u32[]{:S(2)}, u32[]{:S(2)}) %collective-permute-start.4) | collective-permute-done | bytes 393248 | tf_op jit(solution)/shard_map/ppermute | solution.py:46
  313.9 22.1 %fusion.159 = (f32[1024]{0:T(1024)S(1)}, f32[1024,8032]{0,1:T(8,128)}) fusion(bf16[8032,768]{1,0:T(8,128)(2,1)} %param.43, bf16[256,768]{1,0:T(8,128)(2,1)} %collective-permute-done.5, bf16[256,768]{1,0:T(8,128)(2,1)} %copy-done.120, bf16[256,768]{1,0:T(8,128)(2,1)} %copy-done.118, bf16[256,768]{1,0:T(8,128)(2,1)} %copy-done.73), kind=kOutput, calls=%fused_computation.379 | convolution fusion | flops 12647758848 | bytes 46813184 | tf_op jit(solution)/shard_map/dot_general | solution.py:34
  336.6 15.0 %fusion = (f32[1024]{0:T(1024)S(1)}, f32[1024]{0:T(1024)S(1)}) fusion(f32[1024,8032]{0,1:T(8,128)} %get-tuple-element.203, s32[1024]{0:T(1024)S(1)} %copy-done.96, s32[8032]{0:T(1024)} %iota_add_fusion, f32[1024]{0:T(1024)S(1)} %get-tuple-element.202), kind=kLoop, calls=%fused_computation.2 | loop fusion | flops 41121792 | bytes 32947584 | tf_op jit(solution)/shard_map/reduce_sum | solution.py:391
  356.2 5.4 collective-permute-start.6
  373.3 15.1 %fusion.3 = bf16[1024,8032]{0,1:T(8,128)(2,1)S(1)} fusion(f32[1024,8032]{0,1:T(8,128)} %get-tuple-element.203, f32[1024]{0:T(1024)S(1)} %pad_maximum_fusion.10, s32[1024]{0:T(1024)} %pad_add_fusion, s32[8032]{0:T(1024)} %iota_add_fusion, pred[1024]{0:T(1024)(128)(4,1)} %pad_add_fusion.1), kind=kLoop, calls=%fused_computation.5 | loop fusion | flops 49348608 | bytes 49389952 | tf_op jit(solution)/shard_map/convert_element_type | solution.py:408
  388.4 5.7 copy-done.4
  394.1 17.4 %fusion.160 = (bf16[1024,768]{1,0:T(8,128)(2,1)}, f32[1024,768]{1,0:T(8,128)}) fusion(bf16[1024,8032]{0,1:T(8,128)(2,1)S(1)} %fusion.3, bf16[8032,768]{1,0:T(8,128)(2,1)} %param.43), kind=kOutput, calls=%fused_computation.380 | convolution fusion | flops 12634030080 | bytes 33505280 | tf_op jit(solution)/shard_map/dot_general | solution.py:38
  411.5 19.6 %convolution_convert_fusion = bf16[768,8032]{0,1:T(8,128)(2,1)} fusion(bf16[1024,8032]{0,1:T(8,128)(2,1)} %copy-done.4, bf16[256,768]{1,0:T(8,128)(2,1)} %collective-permute-done.5, bf16[256,768]{1,0:T(8,128)(2,1)S(1)} %copy-done.121, bf16[256,768]{1,0:T(8,128)(2,1)S(1)} %copy-done.119, bf16[256,768]{1,0:T(8,128)(2,1)S(1)} %copy-done.74), kind=kOutput, calls=%fused_computation.13 | convolution fusion | flops 12645703680 | bytes 30359552 | tf_op jit(solution)/shard_map/dot_general | solution.py:42
  431.1 16.3 %copy.148 = bf16[768,8032]{1,0:T(8,128)(2,1)} copy(bf16[768,8032]{0,1:T(8,128)(2,1)} %convolution_convert_fusion) | data formatting | bytes 24674304 | tf_op jit(solution)/shard_map/convert_element_type | solution.py:415
  452.3 5.8 dynamic-slice_bitcast_fusion
  458.1 15.2 %collective-permute-done.10 = bf16[256,768]{1,0:T(8,128)(2,1)S(1)} collective-permute-done((bf16[256,768]{1,0:T(8,128)(2,1)S(1)}, bf16[256,768]{1,0:T(8,128)(2,1)S(1)}, u32[]{:S(2)}, u32[]{:S(2)}) %collective-permute-start.10) | collective-permute-done | bytes 393248 | tf_op jit(solution)/shard_map/ppermute | solution.py:46
  488.7 6.5 concatenate.140
  502.6 6.1 concatenate.141
  508.7 6.2 concatenate.142
  519.9 7.6 collective-permute-start.12
  532.5 5.1 dynamic-slice_bitcast_fusion.1
  554.9 11.5 %fusion.28 = bf16[12,64,1024]{2,1,0:T(8,128)(2,1)S(1)} fusion(bf16[512,12,64]{0,2,1:T(8,128)(2,1)} %bitcast.386, f32[12,512,1024]{2,1,0:T(8,128)} %get-tuple-element.195, f32[12,512]{1,0:T(8,128)S(1)} %bitcast.398, pred[1024]{0:T(1024)(128)(4,1)S(1)} %copy-done.111), kind=kOutput, calls=%fused_computation.70 | convolution fusion | flops 831258624 | bytes 27550720 | tf_op jit(solution)/shard_map/hqk,qhd->khd/dot_general | solution.py:253
  570.1 5.5 concatenate.136
  579.7 16.0 %multiply_convert_fusion = bf16[12,512,1024]{2,1,0:T(8,128)(2,1)} fusion(f32[12,512,1024]{2,1,0:T(8,128)} %get-tuple-element.195, f32[12,512]{1,0:T(8,128)S(1)} %maximum_select_fusion.5, f32[12,512]{1,0:T(8,128)S(1)} %bitcast.399, pred[1024]{0:T(1024)(128)(4,1)S(1)} %copy-done.111, bf16[512,12,64]{0,2,1:T(8,128)(2,1)} %bitcast.387, ...), kind=kOutput, calls=%fused_computation.7 | convolution fusion | flops 843055104 | bytes 40158208 | tf_op jit(solution)/shard_map/qhd,khd->hqk/dot_general | solution.py:244
  595.7 9.0 convolution_multiply_fusion
  604.8 7.4 multiply_convert_fusion.2
  619.6 6.2 concatenate.135
  625.8 5.9 copy.141
  631.7 5.9 convolution_add_fusion
  639.2 4.9 concatenate.134
  666.4 6.5 convolution_convert_fusion.20
  672.9 9.7 %multiply_reduce_fusion = (f32[12,512]{1,0:T(8,128)S(1)}, f32[12,512,512]{1,2,0:T(8,128)}) fusion(f32[12,512,512]{1,2,0:T(8,128)} %copy-done.1, f32[12,512]{1,0:T(8,128)S(1)} %copy-done.84, pred[512,512]{0,1:T(8,128)(4,1)S(1)} %copy-done.26, bf16[512,12,64]{0,2,1:T(8,128)(2,1)S(1)} %bitcast.366, bf16[512,12,64]{0,2,1:T(8,128)(2,1)S(1)} %bitcast.364), kind=kOutput, calls=%fused_computation.16 | convolution fusion | flops 418375680 | bytes 27049984 | tf_op jit(solution)/shard_map/qhd,khd->hqk/dot_general | solution.py:244
  682.7 7.2 multiply_convert_fusion.1
  730.4 41.3 %psum.7 = f32[4,768]{1,0:T(4,128)S(1)} all-reduce(f32[4,768]{1,0:T(4,128)S(1)} %pad_maximum_fusion.9), channel_id=1, replica_groups=mesh['dp'=8,'tensor'=4] {'dp','tensor'}, use_global_device_ids=true, to_apply=%region_24.25 | all-reduce | flops 3072 | bytes 24576 | tf_op jit(solution)/shard_map/psum | solution.py:489
  785.8 9.3 collective-permute-done.27
  798.2 6.2 collective-permute-done.28
  825.9 5.9 collective-permute-done.18
  843.1 5.3 fusion.13
  854.4 8.5 fusion.11
  885.7 11.3 %collective-permute-done.34 = bf16[96,4,768]{2,0,1:T(8,128)(2,1)S(1)} collective-permute-done((bf16[96,4,768]{2,0,1:T(8,128)(2,1)S(1)}, bf16[96,4,768]{2,0,1:T(8,128)(2,1)S(1)}, u32[]{:S(2)}, u32[]{:S(2)}) %collective-permute-start.34) | collective-permute-done | bytes 589856 | tf_op jit(solution)/shard_map/ppermute | solution.py:46
  906.2 7.1 collective-permute-done.38
  914.3 9.1 collective-permute-done.43
  925.7 4.9 collective-permute-done.41
  931.8 6.9 collective-permute-done.44
  (541 shorter events, 327.6 us)
Async XLA Ops:
  0.7 180.5 %copy-start = (bf16[1024,768]{1,0:T(8,128)(2,1)S(1)}, bf16[1024,768]{1,0:T(8,128)(2,1)}, u32[]{:S(2)}) copy-start(bf16[1024,768]{1,0:T(8,128)(2,1)} %param.24) | copy-start | bytes 4718596
  0.7 188.1 %collective-permute-start = (bf16[256,768]{1,0:T(8,128)(2,1)}, bf16[256,768]{1,0:T(8,128)(2,1)S(1)}, u32[]{:S(2)}, u32[]{:S(2)}) collective-permute-start(bf16[256,768]{1,0:T(8,128)(2,1)} %param.23), channel_id=1, source_target_pairs={{0,1},{1,0},{2,3},{3,2},{4,5},{5,4},{6,7},{7,6},{8,9},{9,8},{10,11... | collective-permute-start | bytes 1179656 | tf_op jit(solution)/shard_map/ppermute | solution.py:46
  5.9 201.1 %copy-start.25 = (pred[512,512]{0,1:T(8,128)(4,1)}, pred[512,512]{0,1:T(8,128)(4,1)S(1)}, u32[]{:S(2)}) copy-start(pred[512,512]{0,1:T(8,128)(4,1)S(1)} %fusion.41) | copy-start | bytes 786436
  181.1 62.5 %copy-start.110 = (pred[1024]{0:T(1024)(128)(4,1)}, pred[1024]{0:T(1024)(128)(4,1)S(1)}, u32[]{:S(2)}) copy-start(pred[1024]{0:T(1024)(128)(4,1)S(1)} %add_compare_fusion) | copy-start | bytes 3076
  256.8 15.3 %collective-permute-start.2 = (bf16[256,768]{1,0:T(8,128)(2,1)}, bf16[256,768]{1,0:T(8,128)(2,1)S(1)}, u32[]{:S(2)}, u32[]{:S(2)}) collective-permute-start(bf16[256,768]{1,0:T(8,128)(2,1)} %copy.157), channel_id=1, source_target_pairs={{0,1},{1,0},{2,3},{3,2},{4,5},{5,4},{6,7},{7,6},{8,9},{9,8},{10,11... | collective-permute-start | bytes 1179656 | tf_op jit(solution)/shard_map/ppermute | solution.py:46
  257.3 10.8 %collective-permute-start.1 = (f32[12,512,1]{1,0,2:T(8,128)}, f32[12,512,1]{1,0,2:T(8,128)}, u32[]{:S(2)}, u32[]{:S(2)}) collective-permute-start(f32[12,512,1]{1,0,2:T(8,128)} %bitcast.29), channel_id=1, source_target_pairs={{0,1},{1,0},{2,3},{3,2},{4,5},{5,4},{6,7},{7,6},{8,9},{9,8},{10,11... | collective-permute-start | bytes 73736 | tf_op jit(solution)/shard_map/ppermute | solution.py:46
  282.7 16.3 %collective-permute-start.3 = (bf16[256,768]{1,0:T(8,128)(2,1)S(1)}, bf16[256,768]{1,0:T(8,128)(2,1)S(1)}, u32[]{:S(2)}, u32[]{:S(2)}) collective-permute-start(bf16[256,768]{1,0:T(8,128)(2,1)S(1)} %multiply_convert_fusion.9), channel_id=1, source_target_pairs={{0,1},{1,0},{2,3},{3,2},{4,5},{5,4},{6,7},{7,6},{8,9},{9,8},{10,11... | collective-permute-start | bytes 1179656 | tf_op jit(solution)/shard_map/ppermute | solution.py:46
  283.3 29.8 %collective-permute-start.4 = (bf16[256,768]{1,0:T(8,128)(2,1)S(1)}, bf16[256,768]{1,0:T(8,128)(2,1)S(1)}, u32[]{:S(2)}, u32[]{:S(2)}) collective-permute-start(bf16[256,768]{1,0:T(8,128)(2,1)S(1)} %multiply_convert_fusion.9), channel_id=1, source_target_pairs={{0,2},{1,3},{2,0},{3,1},{4,6},{5,7},{6,4},{7,5},{8,10},{9,11},{10,... | collective-permute-start | bytes 1179656 | tf_op jit(solution)/shard_map/ppermute | solution.py:46
  284.8 29.1 %collective-permute-start.5 = (bf16[256,768]{1,0:T(8,128)(2,1)S(1)}, bf16[256,768]{1,0:T(8,128)(2,1)}, u32[]{:S(2)}, u32[]{:S(2)}) collective-permute-start(bf16[256,768]{1,0:T(8,128)(2,1)S(1)} %multiply_convert_fusion.9), channel_id=1, source_target_pairs={{0,3},{1,2},{2,1},{3,0},{4,7},{5,6},{6,5},{7,4},{8,11},{9,10},{10,... | collective-permute-start | bytes 1179656 | tf_op jit(solution)/shard_map/ppermute | solution.py:46
  356.2 8.4 collective-permute-start.6
  361.6 4.9 collective-permute-start.7
  362.6 5.8 collective-permute-start.8
  448.7 24.6 %collective-permute-start.10 = (bf16[256,768]{1,0:T(8,128)(2,1)S(1)}, bf16[256,768]{1,0:T(8,128)(2,1)S(1)}, u32[]{:S(2)}, u32[]{:S(2)}) collective-permute-start(bf16[256,768]{1,0:T(8,128)(2,1)S(1)} %get-tuple-element.146), channel_id=1, source_target_pairs={{0,2},{1,3},{2,0},{3,1},{4,6},{5,7},{6,4},{7,5},{8,10},{9,11},{10,... | collective-permute-start | bytes 1179656 | tf_op jit(solution)/shard_map/ppermute | solution.py:46
  449.7 23.6 %collective-permute-start.11 = (bf16[256,768]{1,0:T(8,128)(2,1)S(1)}, bf16[256,768]{1,0:T(8,128)(2,1)S(1)}, u32[]{:S(2)}, u32[]{:S(2)}) collective-permute-start(bf16[256,768]{1,0:T(8,128)(2,1)S(1)} %get-tuple-element.145), channel_id=1, source_target_pairs={{0,3},{1,2},{2,1},{3,0},{4,7},{5,6},{6,5},{7,4},{8,11},{9,10},{10,... | collective-permute-start | bytes 1179656 | tf_op jit(solution)/shard_map/ppermute | solution.py:46
  451.3 23.3 %collective-permute-start.9 = (bf16[256,768]{1,0:T(8,128)(2,1)S(1)}, bf16[256,768]{1,0:T(8,128)(2,1)S(1)}, u32[]{:S(2)}, u32[]{:S(2)}) collective-permute-start(bf16[256,768]{1,0:T(8,128)(2,1)S(1)} %get-tuple-element.144), channel_id=1, source_target_pairs={{0,1},{1,0},{2,3},{3,2},{4,5},{5,4},{6,7},{7,6},{8,9},{9,8},{10,11... | collective-permute-start | bytes 1179656 | tf_op jit(solution)/shard_map/ppermute | solution.py:46
  458.1 396.3 %collective-permute-start.40 = (bf16[2,2,96,8032]{3,2,1,0:T(8,128)(2,1)}, bf16[2,2,96,8032]{3,2,1,0:T(8,128)(2,1)}, u32[]{:S(2)}, u32[]{:S(2)}) collective-permute-start(bf16[2,2,96,8032]{3,2,1,0:T(8,128)(2,1)} %dynamic-slice_bitcast_fusion), channel_id=1, source_target_pairs={{0,4},{4,0},{8,12},{12,8},{16,20},{20,16},{24,28},{28,24},{1,5},{5... | collective-permute-start | bytes 18505736 | tf_op jit(solution)/shard_map/ppermute | solution.py:46
  519.9 28.2 %collective-permute-start.12 = (bf16[256,768]{1,0:T(8,128)(2,1)}, bf16[256,768]{1,0:T(8,128)(2,1)}, u32[]{:S(2)}, u32[]{:S(2)}) collective-permute-start(bf16[256,768]{1,0:T(8,128)(2,1)} %get-tuple-element.120), channel_id=1, source_target_pairs={{0,1},{1,0},{2,3},{3,2},{4,5},{5,4},{6,7},{7,6},{8,9},{9,8},{10,11... | collective-permute-start | bytes 1179656 | tf_op jit(solution)/shard_map/ppermute | solution.py:46
  537.6 305.5 %collective-permute-start.32 = (bf16[2,2,96,4,1536]{4,2,3,1,0:T(8,128)(2,1)}, bf16[2,2,96,4,1536]{4,2,3,1,0:T(8,128)(2,1)}, u32[]{:S(2)}, u32[]{:S(2)}) collective-permute-start(bf16[2,2,96,4,1536]{4,2,3,1,0:T(8,128)(2,1)} %dynamic-slice_bitcast_fusion.1), channel_id=1, source_target_pairs={{0,4},{4,0},{8,12},{12,8},{16,20},{20,16},{24,28},{28,24},{1,5},{5... | collective-permute-start | bytes 14155784 | tf_op jit(solution)/shard_map/ppermute | solution.py:46
  553.8 25.9 %collective-permute-start.13 = (f32[12,256,1]{1,0,2:T(8,128)S(1)}, f32[12,256,1]{1,0,2:T(8,128)S(1)}, u32[]{:S(2)}, u32[]{:S(2)}) collective-permute-start(f32[12,256,1]{1,0,2:T(8,128)S(1)} %bitcast.400), channel_id=1, source_target_pairs={{0,1},{1,0},{2,3},{3,2},{4,5},{5,4},{6,7},{7,6},{8,9},{9,8},{10,11... | collective-permute-start | bytes 36872 | tf_op jit(solution)/shard_map/ppermute | solution.py:46
  618.6 19.0 %collective-permute-start.14 = (bf16[256,768]{0,1:T(8,128)(2,1)}, bf16[256,768]{0,1:T(8,128)(2,1)S(1)}, u32[]{:S(2)}, u32[]{:S(2)}) collective-permute-start(bf16[256,768]{0,1:T(8,128)(2,1)} %dynamic-slice_convert_fusion), channel_id=1, source_target_pairs={{0,1},{1,0},{2,3},{3,2},{4,5},{5,4},{6,7},{7,6},{8,9},{9,8},{10,11... | collective-permute-start | bytes 1179656 | tf_op jit(solution)/shard_map/ppermute | solution.py:46
  648.6 13.5 %collective-permute-start.15 = (bf16[256,768]{1,0:T(8,128)(2,1)S(1)}, bf16[256,768]{1,0:T(8,128)(2,1)}, u32[]{:S(2)}, u32[]{:S(2)}) collective-permute-start(bf16[256,768]{1,0:T(8,128)(2,1)S(1)} %get-tuple-element.118), channel_id=1, source_target_pairs={{0,1},{1,0},{2,3},{3,2},{4,5},{5,4},{6,7},{7,6},{8,9},{9,8},{10,11... | collective-permute-start | bytes 1179656 | tf_op jit(solution)/shard_map/ppermute | solution.py:46
  655.5 119.4 %collective-permute-start.24 = (bf16[2,2,96,4,768]{4,2,3,1,0:T(8,128)(2,1)}, bf16[2,2,96,4,768]{4,2,3,1,0:T(8,128)(2,1)}, u32[]{:S(2)}, u32[]{:S(2)}) collective-permute-start(bf16[2,2,96,4,768]{4,2,3,1,0:T(8,128)(2,1)} %dynamic-slice_bitcast_fusion.2), channel_id=1, source_target_pairs={{0,4},{4,0},{8,12},{12,8},{16,20},{20,16},{24,28},{28,24},{1,5},{5... | collective-permute-start | bytes 7077896 | tf_op jit(solution)/shard_map/ppermute | solution.py:46
  726.9 54.6 %collective-permute-start.16 = (bf16[2,2,96,4,768]{4,2,3,1,0:T(8,128)(2,1)}, bf16[2,2,96,4,768]{4,2,3,1,0:T(8,128)(2,1)}, u32[]{:S(2)}, u32[]{:S(2)}) collective-permute-start(bf16[2,2,96,4,768]{4,2,3,1,0:T(8,128)(2,1)} %dynamic-slice_bitcast_fusion.3), channel_id=1, source_target_pairs={{0,4},{4,0},{8,12},{12,8},{16,20},{20,16},{24,28},{28,24},{1,5},{5... | collective-permute-start | bytes 7077896 | tf_op jit(solution)/shard_map/ppermute | solution.py:46
  778.5 16.6 %collective-permute-start.27 = (bf16[2,96,4,384]{3,1,2,0:T(8,128)(2,1)S(1)}, bf16[2,96,4,384]{3,1,2,0:T(8,128)(2,1)S(1)}, u32[]{:S(2)}, u32[]{:S(2)}) collective-permute-start(bf16[2,96,4,384]{3,1,2,0:T(8,128)(2,1)S(1)} %dynamic-slice_bitcast_fusion.12), channel_id=1, source_target_pairs={{0,16},{4,20},{8,24},{12,28},{16,0},{20,4},{24,8},{28,12},{1,17},{... | collective-permute-start | bytes 1769480 | tf_op jit(solution)/shard_map/ppermute | solution.py:46
  780.9 16.4 %collective-permute-start.25 = (bf16[2,96,4,384]{3,1,2,0:T(8,128)(2,1)S(1)}, bf16[2,96,4,384]{3,1,2,0:T(8,128)(2,1)S(1)}, u32[]{:S(2)}, u32[]{:S(2)}) collective-permute-start(bf16[2,96,4,384]{3,1,2,0:T(8,128)(2,1)S(1)} %dynamic-slice_bitcast_fusion.13), channel_id=1, source_target_pairs={{0,8},{4,12},{8,0},{12,4},{16,24},{20,28},{24,16},{28,20},{1,9},{5... | collective-permute-start | bytes 1769480 | tf_op jit(solution)/shard_map/ppermute | solution.py:46
  784.3 28.7 %collective-permute-start.19 = (bf16[2,96,4,384]{3,1,2,0:T(8,128)(2,1)S(1)}, bf16[2,96,4,384]{3,1,2,0:T(8,128)(2,1)S(1)}, u32[]{:S(2)}, u32[]{:S(2)}) collective-permute-start(bf16[2,96,4,384]{3,1,2,0:T(8,128)(2,1)S(1)} %dynamic-slice_bitcast_fusion.14), channel_id=1, source_target_pairs={{0,16},{4,20},{8,24},{12,28},{16,0},{20,4},{24,8},{28,12},{1,17},{... | collective-permute-start | bytes 1769480 | tf_op jit(solution)/shard_map/ppermute | solution.py:46
  795.3 9.1 collective-permute-start.28
  797.6 14.2 %collective-permute-start.26 = (bf16[96,4,384]{2,0,1:T(8,128)(2,1)S(1)}, bf16[96,4,384]{2,0,1:T(8,128)(2,1)S(1)}, u32[]{:S(2)}, u32[]{:S(2)}) collective-permute-start(bf16[96,4,384]{2,0,1:T(8,128)(2,1)S(1)} %dynamic-slice_bitcast_fusion.17), channel_id=1, source_target_pairs={{0,16},{4,20},{8,24},{12,28},{16,0},{20,4},{24,8},{28,12},{1,17},{... | collective-permute-start | bytes 884744 | tf_op jit(solution)/shard_map/ppermute | solution.py:46
  804.4 10.6 %collective-permute-start.17 = (bf16[2,96,4,384]{3,1,2,0:T(8,128)(2,1)S(1)}, bf16[2,96,4,384]{3,1,2,0:T(8,128)(2,1)S(1)}, u32[]{:S(2)}, u32[]{:S(2)}) collective-permute-start(bf16[2,96,4,384]{3,1,2,0:T(8,128)(2,1)S(1)} %dynamic-slice_bitcast_fusion.15), channel_id=1, source_target_pairs={{0,8},{4,12},{8,0},{12,4},{16,24},{20,28},{24,16},{28,20},{1,9},{5... | collective-permute-start | bytes 1769480 | tf_op jit(solution)/shard_map/ppermute | solution.py:46
  811.9 6.4 collective-permute-start.29
  813.0 12.1 %collective-permute-start.30 = (bf16[96,768]{1,0:T(8,128)(2,1)S(1)}, bf16[96,768]{1,0:T(8,128)(2,1)S(1)}, u32[]{:S(2)}, u32[]{:S(2)}) collective-permute-start(bf16[96,768]{1,0:T(8,128)(2,1)S(1)} %get-tuple-element.154), channel_id=1, source_target_pairs={{0,2},{1,3},{2,0},{3,1},{4,6},{5,7},{6,4},{7,5},{8,10},{9,11},{10,... | collective-permute-start | bytes 442376 | tf_op jit(solution)/shard_map/ppermute | solution.py:46
  815.0 10.7 %collective-permute-start.31 = (bf16[96,768]{1,0:T(8,128)(2,1)S(1)}, bf16[96,768]{1,0:T(8,128)(2,1)S(1)}, u32[]{:S(2)}, u32[]{:S(2)}) collective-permute-start(bf16[96,768]{1,0:T(8,128)(2,1)S(1)} %get-tuple-element.155), channel_id=1, source_target_pairs={{0,3},{1,2},{2,1},{3,0},{4,7},{5,6},{6,5},{7,4},{8,11},{9,10},{10,... | collective-permute-start | bytes 442376 | tf_op jit(solution)/shard_map/ppermute | solution.py:46
  818.3 7.5 collective-permute-start.20
  825.1 6.7 collective-permute-start.18
  832.0 6.6 collective-permute-start.21
  832.0 7.7 collective-permute-start.22
  834.5 7.0 collective-permute-start.23
  850.1 21.7 %collective-permute-start.35 = (bf16[2,96,4,768]{3,1,2,0:T(8,128)(2,1)}, bf16[2,96,4,768]{3,1,2,0:T(8,128)(2,1)}, u32[]{:S(2)}, u32[]{:S(2)}) collective-permute-start(bf16[2,96,4,768]{3,1,2,0:T(8,128)(2,1)} %dynamic-slice_bitcast_fusion.6), channel_id=1, source_target_pairs={{0,16},{4,20},{8,24},{12,28},{16,0},{20,4},{24,8},{28,12},{1,17},{... | collective-permute-start | bytes 3538952 | tf_op jit(solution)/shard_map/ppermute | solution.py:46
  851.8 27.2 %collective-permute-start.33 = (bf16[2,96,4,768]{3,1,2,0:T(8,128)(2,1)}, bf16[2,96,4,768]{3,1,2,0:T(8,128)(2,1)}, u32[]{:S(2)}, u32[]{:S(2)}) collective-permute-start(bf16[2,96,4,768]{3,1,2,0:T(8,128)(2,1)} %dynamic-slice_bitcast_fusion.7), channel_id=1, source_target_pairs={{0,8},{4,12},{8,0},{12,4},{16,24},{20,28},{24,16},{28,20},{1,9},{5... | collective-permute-start | bytes 3538952 | tf_op jit(solution)/shard_map/ppermute | solution.py:46
  873.4 12.1 %collective-permute-start.36 = (bf16[96,4,768]{2,0,1:T(8,128)(2,1)S(1)}, bf16[96,4,768]{2,0,1:T(8,128)(2,1)S(1)}, u32[]{:S(2)}, u32[]{:S(2)}) collective-permute-start(bf16[96,4,768]{2,0,1:T(8,128)(2,1)S(1)} %dynamic-slice_bitcast_fusion.10), channel_id=1, source_target_pairs={{0,8},{4,12},{8,0},{12,4},{16,24},{20,28},{24,16},{28,20},{1,9},{5... | collective-permute-start | bytes 1769480 | tf_op jit(solution)/shard_map/ppermute | solution.py:46
  880.7 16.3 %collective-permute-start.34 = (bf16[96,4,768]{2,0,1:T(8,128)(2,1)S(1)}, bf16[96,4,768]{2,0,1:T(8,128)(2,1)S(1)}, u32[]{:S(2)}, u32[]{:S(2)}) collective-permute-start(bf16[96,4,768]{2,0,1:T(8,128)(2,1)S(1)} %dynamic-slice_bitcast_fusion.11), channel_id=1, source_target_pairs={{0,16},{4,20},{8,24},{12,28},{16,0},{20,4},{24,8},{28,12},{1,17},{... | collective-permute-start | bytes 1769480 | tf_op jit(solution)/shard_map/ppermute | solution.py:46
  881.0 42.4 %collective-permute-start.43 = (bf16[2,96,3936]{2,1,0:T(8,128)(2,1)S(1)}, bf16[2,96,3936]{2,1,0:T(8,128)(2,1)S(1)}, u32[]{:S(2)}, u32[]{:S(2)}) collective-permute-start(bf16[2,96,3936]{2,1,0:T(8,128)(2,1)S(1)} %dynamic-slice_bitcast_fusion.5), channel_id=1, source_target_pairs={{0,16},{4,20},{8,24},{12,28},{16,0},{20,4},{24,8},{28,12},{1,17},{... | collective-permute-start | bytes 4534280 | tf_op jit(solution)/shard_map/ppermute | solution.py:46
  897.2 9.0 collective-permute-start.37
  899.4 14.0 %collective-permute-start.38 = (bf16[96,1536]{1,0:T(8,128)(2,1)S(1)}, bf16[96,1536]{1,0:T(8,128)(2,1)S(1)}, u32[]{:S(2)}, u32[]{:S(2)}) collective-permute-start(bf16[96,1536]{1,0:T(8,128)(2,1)S(1)} %get-tuple-element.148), channel_id=1, source_target_pairs={{0,2},{1,3},{2,0},{3,1},{4,6},{5,7},{6,4},{7,5},{8,10},{9,11},{10,... | collective-permute-start | bytes 884744 | tf_op jit(solution)/shard_map/ppermute | solution.py:46
  899.8 13.5 %collective-permute-start.39 = (bf16[96,1536]{1,0:T(8,128)(2,1)S(1)}, bf16[96,1536]{1,0:T(8,128)(2,1)S(1)}, u32[]{:S(2)}, u32[]{:S(2)}) collective-permute-start(bf16[96,1536]{1,0:T(8,128)(2,1)S(1)} %get-tuple-element.149), channel_id=1, source_target_pairs={{0,3},{1,2},{2,1},{3,0},{4,7},{5,6},{6,5},{7,4},{8,11},{9,10},{10,... | collective-permute-start | bytes 884744 | tf_op jit(solution)/shard_map/ppermute | solution.py:46
  901.9 28.6 %collective-permute-start.41 = (bf16[2,96,4096]{2,1,0:T(8,128)(2,1)S(1)}, bf16[2,96,4096]{2,1,0:T(8,128)(2,1)S(1)}, u32[]{:S(2)}, u32[]{:S(2)}) collective-permute-start(bf16[2,96,4096]{2,1,0:T(8,128)(2,1)S(1)} %dynamic-slice_bitcast_fusion.4), channel_id=1, source_target_pairs={{0,8},{4,12},{8,0},{12,4},{16,24},{20,28},{24,16},{28,20},{1,9},{5... | collective-permute-start | bytes 4718600 | tf_op jit(solution)/shard_map/ppermute | solution.py:46
  923.9 14.8 %collective-permute-start.44 = (bf16[96,3936]{1,0:T(8,128)(2,1)S(1)}, bf16[96,3936]{1,0:T(8,128)(2,1)S(1)}, u32[]{:S(2)}, u32[]{:S(2)}) collective-permute-start(bf16[96,3936]{1,0:T(8,128)(2,1)S(1)} %dynamic-slice_bitcast_fusion.9), channel_id=1, source_target_pairs={{0,8},{4,12},{8,0},{12,4},{16,24},{20,28},{24,16},{28,20},{1,9},{5... | collective-permute-start | bytes 2267144 | tf_op jit(solution)/shard_map/ppermute | solution.py:46
  931.2 12.1 %collective-permute-start.42 = (bf16[96,4096]{1,0:T(8,128)(2,1)S(1)}, bf16[96,4096]{1,0:T(8,128)(2,1)S(1)}, u32[]{:S(2)}, u32[]{:S(2)}) collective-permute-start(bf16[96,4096]{1,0:T(8,128)(2,1)S(1)} %dynamic-slice_bitcast_fusion.8), channel_id=1, source_target_pairs={{0,16},{4,20},{8,24},{12,28},{16,0},{20,4},{24,8},{28,12},{1,17},{... | collective-permute-start | bytes 2359304 | tf_op jit(solution)/shard_map/ppermute | solution.py:46
  (128 other events, 835.5 us)

commit v2 on v1

v2 whole, which is shorter than its diff:
```python
import functools
import math

import jax
import jax.numpy as jnp
from jax import lax
from jax.sharding import PartitionSpec as P
from jax.experimental import pallas as pl
from jax.experimental.pallas import tpu as pltpu

D = 768
HDIM = 64
NHEAD = D // HDIM
PAIRS = NHEAD // 2
FF = 2048
TGT = 512
ROWS = 256
KEYS = 1024
CHUNK = 256
HALF_D = D // 2
VTILE = 512
F32 = jnp.float32
BF16 = jnp.bfloat16
MESH_ID = pl.DeviceIdType.MESH
VMEM_LIMIT = 56 * 2**20
NEG = -1000000000.0
SCALE = HDIM ** (-0.5)
EPS = 1e-06


def dot_nt(left, right):
    return lax.dot_general(left, right, (((1,), (1,)), ((), ())), preferred_element_type=F32)


def dot_nn(left, right):
    return lax.dot_general(left, right, (((1,), (0,)), ((), ())), preferred_element_type=F32)


def swap(value, axis_name, size, bit):
    return lax.ppermute(value, axis_name, [(i, i ^ bit) for i in range(size)])


def gather_kernel(groups, *refs):
    ins, outs = refs[:groups], refs[groups : 2 * groups]
    send_sem, recv_sem, local_sem = refs[2 * groups :]
    dp = lax.axis_index("dp")
    z = lax.axis_index("tensor")
    core_peer = dp + 1 - 2 * lax.rem(dp, 2)
    x_peer = dp + 2 - 4 * lax.rem(dp // 2, 2)
    y_peer = dp + 4 - 8 * (dp // 4)
    xy_peer = x_peer + y_peer - dp
    low, high = lax.rem(z, 2), z // 2
    z_peers = [high * 2 + 1 - low, (1 - high) * 2 + low, (1 - high) * 2 + 1 - low]
    barrier = pltpu.get_barrier_semaphore()
    for other in (core_peer, x_peer, y_peer):
        pl.semaphore_signal(
            barrier, inc=1, device_id={"dp": other, "tensor": z}, device_id_type=MESH_ID
        )
    for other in z_peers:
        pl.semaphore_signal(
            barrier, inc=1, device_id={"dp": dp, "tensor": other}, device_id_type=MESH_ID
        )
    pl.semaphore_wait(barrier, 6)

    rows, hid = 96, 192

    def piece(g, shard, owner, start=0, count=rows):
        offset = pl.multiple_of(shard * hid + lax.rem(owner, 2) * rows + start, 16)
        return outs[g].at[owner // 2, pl.ds(offset, count)]

    used = [0]

    def remote(src, dst, target_dp, target_z):
        sem = used[0]
        used[0] += 1
        copy = pltpu.make_async_remote_copy(
            src_ref=src,
            dst_ref=dst,
            send_sem=send_sem.at[sem],
            recv_sem=recv_sem.at[sem],
            device_id={"dp": target_dp, "tensor": target_z},
            device_id_type=MESH_ID,
        )
        copy.start()
        return copy

    def along_z(g):
        offset = pl.multiple_of(dp * rows, 16)
        return [
            remote(ins[g].at[pl.ds(offset, rows)], piece(g, z, dp), dp, z_peers[j])
            for j in range(3)
        ]

    z_copies, x_copies, y_copies, d_copies, c_copies, own = {}, {}, {}, {}, {}, []
    z_copies[0] = along_z(0)
    for g in range(groups):
        for m in range(4):
            copy = pltpu.make_async_copy(
                ins[g].at[pl.ds(m * hid, hid)],
                outs[g].at[m, pl.ds(pl.multiple_of(z * hid, 16), hid)],
                local_sem.at[4 * g + m],
            )
            copy.start()
            own.append(copy)
    for step in range(groups + 2):
        g = step
        if g < groups:
            for copy in z_copies[g]:
                copy.wait()
            if g + 1 < groups:
                z_copies[g + 1] = along_z(g + 1)
            x_copies[g], y_copies[g], c_copies[g] = [], [], []
            for peer in z_peers:
                part = piece(g, peer, dp)
                x_copies[g].append(remote(part, part, x_peer, z))
                y_copies[g].append(remote(part, part, y_peer, z))
                c_copies[g].append(remote(part, part, core_peer, z))
        g = step - 1
        if 0 <= g < groups:
            d_copies[g] = []
            for j, peer in enumerate(z_peers):
                x_copies[g][j].wait()
                part = piece(g, peer, x_peer, 0, rows // 2)
                d_copies[g].append(remote(part, part, y_peer, z))
                y_copies[g][j].wait()
                part = piece(g, peer, y_peer, rows // 2, rows // 2)
                d_copies[g].append(remote(part, part, x_peer, z))
                for owner in (x_peer, y_peer):
                    part = piece(g, peer, owner)
                    c_copies[g].append(remote(part, part, core_peer, z))
        g = step - 2
        if 0 <= g < groups:
            for j, peer in enumerate(z_peers):
                d_copies[g][2 * j].wait()
                d_copies[g][2 * j + 1].wait()
                part = piece(g, peer, xy_peer)
                c_copies[g].append(remote(part, part, core_peer, z))
    for copy in own:
        copy.wait()
    for g in range(groups):
        for copy in c_copies[g]:
            copy.wait()


def gather_wide(shard, dp_size):
    rows = shard.shape[0] // dp_size
    part = lax.dynamic_slice_in_dim(shard, lax.axis_index("dp") * rows, rows, 0)
    return lax.all_gather(part, ("tensor", "dp"), axis=0, tiled=True)


def gather_blocks(shards, dp_size):
    if dp_size != 8:
        return [
            gather_wide(shard, dp_size).reshape(4, 4, D // 4, D).swapaxes(0, 1).reshape(4, D, D)
            for shard in shards
        ]
    groups = len(shards)
    return pl.pallas_call(
        functools.partial(gather_kernel, groups),
        out_shape=[jax.ShapeDtypeStruct((4, D, D), BF16) for _ in shards],
        in_specs=[pl.BlockSpec(memory_space=pl.ANY)] * groups,
        out_specs=[pl.BlockSpec(memory_space=pl.ANY)] * groups,
        scratch_shapes=[
            pltpu.SemaphoreType.DMA((27 * groups,)),
            pltpu.SemaphoreType.DMA((27 * groups,)),
            pltpu.SemaphoreType.DMA((4 * groups,)),
        ],
        compiler_params=pltpu.CompilerParams(collective_id=0, has_side_effects=True),
    )(*shards)


def tile_of(width):
    return 512 if width % 512 == 0 else 384


def fold_call(body, xyz, ins, outs, width, out_specs=None):
    tile = tile_of(width)

    def spec(rows, dtype, index):
        return pl.BlockSpec((rows, tile), index)

    smem = pl.BlockSpec(memory_space=pltpu.SMEM)
    left, right = (lambda i: (0, i)), (lambda i: (0, i + width // tile))
    in_specs = [smem] + [
        spec(a.shape[0], a.dtype, right if second else left) for a, second in ins
    ]
    moved = sum(a.shape[0] * width * a.dtype.itemsize for a, _ in ins)
    moved += sum(o.size * jnp.dtype(o.dtype).itemsize for o in outs)
    rows = max(a.shape[0] for a, _ in ins)
    return pl.pallas_call(
        body,
        grid=(width // tile,),
        out_shape=outs,
        in_specs=in_specs,
        out_specs=out_specs or [spec(o.shape[0], o.dtype, left) for o in outs],
        scratch_shapes=[pltpu.VMEM((rows, tile), F32)],
        cost_estimate=pl.CostEstimate(flops=0, bytes_accessed=moved, transcendentals=0),
    )(xyz, *[a for a, _ in ins])


def block_rows(index):
    return pl.ds(pl.multiple_of(index * 96, 96), 96)


def first_fold(xyz, mine_a, got_a, mine_b, got_b, keep_a, send_a, keep_b, send_b, sum_ref):
    x, y = xyz[0], xyz[1]
    sum_ref[...] = mine_a[...] + got_a[...].astype(F32)
    for other in range(2):
        rows = slice(other * 96, (other + 1) * 96)
        keep_a[rows, :] = sum_ref[block_rows(2 * other + x), :]
        send_a[rows, :] = sum_ref[block_rows(2 * other + 1 - x), :].astype(BF16)
    sum_ref[...] = mine_b[...] + got_b[...].astype(F32)
    for other in range(2):
        rows = slice(other * 96, (other + 1) * 96)
        keep_b[rows, :] = sum_ref[block_rows(2 * y + other), :]
        send_b[rows, :] = sum_ref[block_rows(2 * (1 - y) + other), :].astype(BF16)


def second_fold(xyz, mine_a, got_a, mine_b, got_b, keep_a, send_a, keep_b, send_b, sum_ref):
    x, y = xyz[0], xyz[1]
    sum_ref[...] = mine_a[...] + got_a[...].astype(F32)
    keep_a[...] = sum_ref[block_rows(y), :]
    send_a[...] = sum_ref[block_rows(1 - y), :].astype(BF16)
    sum_ref[...] = mine_b[...] + got_b[...].astype(F32)
    keep_b[...] = sum_ref[block_rows(x), :]
    send_b[...] = sum_ref[block_rows(1 - x), :].astype(BF16)


def third_fold(xyz, mine_a, got_a, mine_b, got_b, keep, send_1, send_2, send_3, sum_ref):
    z = xyz[2]
    width = keep.shape[1]
    for m, (mine, got) in enumerate(((mine_a, got_a), (mine_b, got_b))):
        total = mine[...] + got[...].astype(F32)
        sum_ref[2 * m] = total[:, :width]
        sum_ref[2 * m + 1] = total[:, width:]
    keep[...] = sum_ref[z]
    low, high = lax.rem(z, 2), z // 2
    send_1[...] = sum_ref[2 * high + 1 - low].astype(BF16)
    send_2[...] = sum_ref[2 * (1 - high) + low].astype(BF16)
    send_3[...] = sum_ref[2 * (1 - high) + 1 - low].astype(BF16)


def last_fold(flips, keep, got_1, got_2, got_3, *outs):
    total = keep[...] + got_1[...].astype(F32) + (got_2[...].astype(F32) + got_3[...].astype(F32))
    width = keep.shape[1] // len(outs)
    for m, out in enumerate(outs):
        part = total[:, m * width : (m + 1) * width]
        out[...] = part.T if m in flips else part


def table_fold(mine, got, out):
    out[...] = (mine[...] + got[...].astype(F32)).T


class Reduction:
    def __init__(self, xyz, mine, send):
        self.xyz, self.mine, self.width = xyz, mine, mine.shape[1] // 2
        self.got = swap(send, "dp", 8, 1)

    def first(self):
        ins = [(self.mine, 0), (self.got, 0), (self.mine, 1), (self.got, 1)]
        shape = (192, self.width)
        outs = [whole(shape, F32), whole(shape, BF16)] * 2
        keep_a, send_a, keep_b, send_b = fold_call(first_fold, self.xyz, ins, outs, self.width)
        self.keeps = keep_a, keep_b
        self.gots = swap(send_a, "dp", 8, 2), swap(send_b, "dp", 8, 4)
        return send_a, send_b

    def second(self):
        (keep_a, keep_b), (got_a, got_b) = self.keeps, self.gots
        ins = [(keep_a, 0), (got_a, 0), (keep_b, 0), (got_b, 0)]
        shape = (96, self.width)
        outs = [whole(shape, F32), whole(shape, BF16)] * 2
        keep_a, send_a, keep_b, send_b = fold_call(second_fold, self.xyz, ins, outs, self.width)
        self.keeps = keep_a, keep_b
        self.gots = swap(send_a, "dp", 8, 4), swap(send_b, "dp", 8, 2)
        return send_a, send_b

    def third(self):
        (keep_a, keep_b), (got_a, got_b) = self.keeps, self.gots
        shape = (96, self.width // 2)
        keep, *sends = pl.pallas_call(
            third_fold,
            out_shape=[whole(shape, F32)] + [whole(shape, BF16)] * 3,
            in_specs=[pl.BlockSpec(memory_space=pltpu.SMEM)]
            + [pl.BlockSpec(memory_space=pltpu.VMEM)] * 4,
            out_specs=[pl.BlockSpec(memory_space=pltpu.VMEM)] * 4,
            scratch_shapes=[pltpu.VMEM((4,) + shape, F32)],
        )(self.xyz, keep_a, got_a, keep_b, got_b)
        self.keeps = keep
        self.gots = [swap(send, "tensor", 4, j + 1) for j, send in enumerate(sends)]
        return tuple(sends)

    def last(self, count, flips):
        rows, width = self.keeps.shape
        shape = (rows, width // count)
        outs = [whole(shape[::-1] if m in flips else shape, F32) for m in range(count)]
        return pl.pallas_call(functools.partial(last_fold, flips), out_shape=outs)(
            self.keeps, *self.gots
        )

    def table(self, vocab):
        parts = []
        for keep, got, start in zip(self.keeps, self.gots, (0, self.width)):
            count = min(self.width, vocab - start)
            tile = pl.BlockSpec((96, VTILE), lambda i: (0, i))
            parts.append(
                pl.pallas_call(
                    table_fold,
                    grid=(pl.cdiv(count, VTILE),),
                    out_shape=whole((count, 96), F32),
                    in_specs=[tile] * 2,
                    out_specs=pl.BlockSpec((VTILE, 96), lambda i: (i, 0)),
                )(keep, got)
            )
        return jnp.concatenate(parts, 0)


class WideReduction:
    def __init__(self, xyz, mine, send):
        self.z = xyz[2]
        both = jnp.concatenate([mine, send.astype(F32)], 0)
        self.part = lax.psum_scatter(both, "dp", scatter_dimension=0, tiled=True)

    def first(self):
        return ()

    second = third = first

    def last(self, count, flips):
        rows = self.part.shape[0]
        by_z = self.part.reshape(rows, 4, -1)
        total = lax.psum_scatter(by_z, "tensor", scatter_dimension=1, tiled=True)[:, 0]
        parts = jnp.split(total, count, axis=1)
        return [p.T if m in flips else p for m, p in enumerate(parts)]

    def table(self, vocab):
        return self.part.T


def after(value, *others):
    return lax.optimization_barrier((value,) + others)[0]


def rms_scale(values):
    return lax.rsqrt(jnp.mean(values * values, axis=-1, keepdims=True) + EPS)


def norm_back(values, inv_scale, gain, grad_out):
    weighted = gain * grad_out
    grad_gain = jnp.sum(grad_out * values * inv_scale, axis=0, keepdims=True)
    grad_values = inv_scale * weighted - values * inv_scale * inv_scale * inv_scale * jnp.mean(
        weighted * values, axis=-1, keepdims=True
    )
    return grad_values, grad_gain


def flip(value):
    return value.astype(F32).T


def lane_half(rows, which):
    lane = lax.broadcasted_iota(jnp.int32, (rows, 2 * HDIM), 1)
    return (lane >= HDIM) if which else (lane < HDIM)


def only(value, which):
    return jnp.where(lane_half(value.shape[0], which), value, jnp.zeros_like(value))


def split_rows(flat_ref, mine_ref, send_ref, core, split):
    for block in range(4):
        if split:
            first = pl.multiple_of((2 * block + core) * 96, 96)
            second = pl.multiple_of((2 * block + 1 - core) * 96, 96)
        else:
            first, second = block * 96, HALF_D + block * 96
        mine_ref[block * 96 : (block + 1) * 96, :] = flat_ref[pl.ds(first, 96), :]
        send_ref[block * 96 : (block + 1) * 96, :] = flat_ref[pl.ds(second, 96), :]


def by_shard(left_ref, rights, out_ref, first, per_shard):
    width = 192 * len(rights)
    for z in range(4):
        part = [right[:, z * 192 : (z + 1) * 192] for right in rights]
        right = jnp.concatenate(part, axis=1) if len(part) > 1 else part[0]
        start = z * per_shard + first
        out_ref[:, start : start + width] = dot_nn(left_ref[...], right).astype(out_ref.dtype)


def whole(shape, dtype):
    return jax.ShapeDtypeStruct(shape, dtype)


def local_call(body, outs, scratch, flops, *args):
    smem = pl.BlockSpec(memory_space=pltpu.SMEM)
    vmem = pl.BlockSpec(memory_space=pltpu.VMEM)
    bytes_all = sum(a.size * a.dtype.itemsize for a in args)
    bytes_all += sum(o.size * jnp.dtype(o.dtype).itemsize for o in outs)
    held = sum(math.prod(s.shape) * jnp.dtype(s.dtype).itemsize for s in scratch)
    return pl.pallas_call(
        body,
        out_shape=outs,
        in_specs=[smem] + [vmem] * (len(args) - 1),
        out_specs=[vmem] * len(outs),
        scratch_shapes=scratch,
        cost_estimate=pl.CostEstimate(
            flops=int(flops), bytes_accessed=int(bytes_all), transcendentals=0
        ),
        compiler_params=pltpu.CompilerParams(
            vmem_limit_bytes=min(VMEM_LIMIT, int(bytes_all + held + 16 * 2**20))
        ),
    )(*args)


def self_forward(
    scal, x_own, x_other, gain_self, gain_cross, w_self, w_cq,
    q_out, k_out, v_out, lse_out, att_out, h1_out, q2_out,
    x_ref, n_ref, vt_ref, ot_ref,
):
    half = scal[0]
    live = scal[1]
    own = pl.multiple_of(half * ROWS, ROWS)
    x_ref[pl.ds(own, ROWS), :] = x_own[...].astype(F32)
    x_ref[pl.ds(pl.multiple_of((1 - half) * ROWS, ROWS), ROWS), :] = x_other[...].astype(F32)
    for i in range(2):
        rows = slice(i * ROWS, (i + 1) * ROWS)
        x = x_ref[rows, :]
        n = (x * rms_scale(x) * gain_self[...]).astype(BF16)
        n_ref[rows, :] = n
        q_out[rows, :] = dot_nt(n, w_self[0]).astype(BF16)
        k_out[rows, :] = dot_nt(n, w_self[1]).astype(BF16)
        v_out[rows, :] = dot_nt(n, w_self[2]).astype(BF16)
    vt_ref[...] = dot_nt(w_self[2], n_ref[...]).astype(BF16)
    lse_out[...] = jnp.zeros_like(lse_out)
    key = lax.broadcasted_iota(jnp.int32, (TGT, TGT), 0)
    query = lax.broadcasted_iota(jnp.int32, (TGT, TGT), 1)
    seen = (key <= query) & (key < live)

    @pl.loop(0, PAIRS)
    def _(pair):
        lanes = pl.ds(pl.multiple_of(pair * 128, 128), 128)
        q_pair, k_pair = q_out[:, lanes], k_out[:, lanes]
        for which in range(2):
            head = 2 * pair + which
            feats = pl.ds(pl.multiple_of(head * HDIM, HDIM), HDIM)
            scores = jnp.where(seen, dot_nt(k_pair, only(q_pair, which)) * SCALE, NEG)
            top = jnp.max(scores, axis=0, keepdims=True)
            probs = jnp.exp(scores - top)
            total = jnp.sum(probs, axis=0, keepdims=True)
            lse_out[pl.ds(head, 1), :] = top + jnp.log(total)
            out = dot_nn(vt_ref[feats, :], probs.astype(BF16)) / total
            ot_ref[feats, :] = out

    for i in range(2):
        rows = slice(i * ROWS, (i + 1) * ROWS)
        att = flip(ot_ref[:, rows]).astype(BF16)
        n_ref[rows, :] = att
        h1 = x_ref[rows, :] + dot_nn(att, w_self[3])
        x_ref[rows, :] = h1
        n = (h1 * rms_scale(h1) * gain_cross[...]).astype(BF16)
        q2_out[rows, :] = dot_nt(n, w_cq[...]).astype(BF16)
    att_out[...] = n_ref[pl.ds(own, ROWS), :]
    h1_out[...] = x_ref[pl.ds(own, ROWS), :]


def cross_forward(
    scal, q2, source, w_ck, w_cv, k_out, v_out, own_out, send_out, lse_out, vt_ref, s_ref, ot_ref
):
    half = scal[0]
    live = scal[2] - half * KEYS
    own = pl.multiple_of(half * ROWS, ROWS)
    other = pl.multiple_of((1 - half) * ROWS, ROWS)
    for i in range(KEYS // CHUNK):
        rows = slice(i * CHUNK, (i + 1) * CHUNK)
        src = source[rows, :]
        k_out[rows, :] = dot_nt(src, w_ck[...]).astype(BF16)
        v_out[rows, :] = dot_nt(src, w_cv[...]).astype(BF16)
        vt_ref[:, rows] = dot_nt(w_cv[...], src).astype(BF16)
    lse_out[...] = jnp.zeros_like(lse_out)
    key = lax.broadcasted_iota(jnp.int32, (CHUNK, TGT), 0)

    @pl.loop(0, PAIRS)
    def _(pair):
        lanes = pl.ds(pl.multiple_of(pair * 128, 128), 128)
        q_pair = q2[:, lanes]
        for which in range(2):
            head = 2 * pair + which
            feats = pl.ds(pl.multiple_of(head * HDIM, HDIM), HDIM)
            q_one = only(q_pair, which)
            top = jnp.full((1, TGT), 2 * NEG, F32)
            for i in range(KEYS // CHUNK):
                rows = slice(i * CHUNK, (i + 1) * CHUNK)
                scores = dot_nt(k_out[rows, lanes], q_one) * SCALE
                scores = jnp.where(key < live - i * CHUNK, scores, NEG)
                s_ref[rows, :] = scores
                top = jnp.maximum(top, jnp.max(scores, axis=0, keepdims=True))
            total = jnp.zeros((1, TGT), F32)
            out = jnp.zeros((HDIM, TGT), F32)
            for i in range(KEYS // CHUNK):
                rows = slice(i * CHUNK, (i + 1) * CHUNK)
                probs = jnp.exp(s_ref[rows, :] - top)
                total = total + jnp.sum(probs, axis=0, keepdims=True)
                out = out + dot_nn(vt_ref[feats, rows], probs.astype(BF16))
            lse_out[pl.ds(head, 1), :] = top + jnp.log(total)
            ot_ref[feats, :] = out / total

    own_out[...] = ot_ref[:, pl.ds(own, ROWS)]
    send_out[...] = ot_ref[:, pl.ds(other, ROWS)].astype(BF16)


def ff_forward(
    scal, o_own, o_other, lse_own, lse_other, h1, w_co, gain_ff, gain_final, wg, wu, wd,
    out_ref, fin_ref, h2_ref, att_t_ref, att_ref, lse_ref, mix_ref,
):
    half = scal[0]
    own = pl.multiple_of(half * ROWS, ROWS)
    first, second = lse_own[...], lse_other[...]
    top = jnp.maximum(first, second)
    lse_ref[...] = top + jnp.log(jnp.exp(first - top) + jnp.exp(second - top))
    lse = lse_ref[:, pl.ds(own, ROWS)]
    w_first = jnp.exp(lse_own[:, pl.ds(own, ROWS)] - lse)
    w_second = jnp.exp(lse_other[:, pl.ds(own, ROWS)] - lse)
    for head in range(NHEAD):
        feats = slice(head * HDIM, (head + 1) * HDIM)
        att_t_ref[feats, :] = (
            o_own[feats, :] * w_first[head : head + 1, :]
            + o_other[feats, :].astype(F32) * w_second[head : head + 1, :]
        )
    att = flip(att_t_ref[...]).astype(BF16)
    att_ref[...] = att
    h2 = h1[...] + dot_nn(att, w_co[...])
    h2_ref[...] = h2
    n3 = (h2 * rms_scale(h2) * gain_ff[...]).astype(BF16)

    @pl.loop(0, FF // 512)
    def _(i):
        rows = pl.ds(pl.multiple_of(i * 512, 512), 512)
        gate = dot_nt(n3, wg[rows, :])
        up = dot_nt(n3, wu[rows, :])
        mix_ref[:, rows] = (jax.nn.gelu(gate, approximate=True) * up).astype(BF16)

    out = h2 + dot_nn(mix_ref[...], wd[...])
    out_ref[...] = out
    fin_ref[...] = (out * rms_scale(out) * gain_final[...] * D ** (-0.5)).astype(BF16)


def ff_backward(
    split, scal, gf_own, gf_1, gf_2, gf_3, block_out, h2_in, gain_ff, gain_final, wg, wu, wd,
    w_co, att_t, mine_ref, send_ref, res_ref, rows_ref, gatt_ref, dot_ref, gg_ref,
    flat_ref, nm_ref, ns_ref, gm_ref, gs_ref, gn_ref,
):
    core = scal[3]
    grad = gf_own[...] + gf_1[...].astype(F32)
    grad = grad + (gf_2[...].astype(F32) + gf_3[...].astype(F32))
    out = block_out[...]
    res, gg_final = norm_back(out, rms_scale(out), gain_final[...], grad * D ** (-0.5))
    gg_ref[0:1, :] = gg_final
    rows_b = res.astype(BF16)
    res_ref[...] = res
    flat_ref[...] = flip(rows_b).astype(BF16)
    split_rows(flat_ref, gm_ref, gs_ref, core, split)
    h2 = h2_in[...]
    scale3 = rms_scale(h2)
    n3 = (h2 * scale3 * gain_ff[...]).astype(BF16)
    flat_ref[...] = flip(n3).astype(BF16)
    split_rows(flat_ref, nm_ref, ns_ref, core, split)
    gn_ref[...] = jnp.zeros_like(gn_ref)
    const = (2.0 / 3.141592653589793) ** 0.5

    @pl.loop(0, FF // 512)
    def _(i):
        start = pl.multiple_of(i * 512, 512)
        rows = pl.ds(start, 512)
        gate = dot_nt(n3, wg[rows, :])
        up = dot_nt(n3, wu[rows, :])
        square = gate * gate
        tanh = jnp.tanh(const * (gate + 0.044715 * gate * square))
        gelu = 0.5 * gate * (1.0 + tanh)
        slope = 0.5 * (1.0 + tanh) + 0.5 * gate * (1.0 - tanh * tanh) * const * (
            1.0 + 3.0 * 0.044715 * square
        )
        grad_mixed = dot_nt(rows_b, wd[rows, :])
        g_gate = (grad_mixed * up * slope).astype(BF16)
        g_up = (grad_mixed * gelu).astype(BF16)
        mixed = (gelu * up).astype(BF16)
        gn_ref[...] += dot_nn(g_gate, wg[rows, :]) + dot_nn(g_up, wu[rows, :])
        for m, (mine, send, right) in enumerate(
            ((nm_ref, ns_ref, g_gate), (nm_ref, ns_ref, g_up), (gm_ref, gs_ref, mixed))
        ):
            cols = pl.ds(pl.multiple_of(3 * start + m * 512, 512), 512)
            mine_ref[:, cols] = dot_nn(mine[...], right)
            send_ref[:, cols] = dot_nn(send[...], right).astype(BF16)

    step, gg_ff = norm_back(h2, scale3, gain_ff[...], gn_ref[...])
    gg_ref[1:2, :] = gg_ff
    res = res_ref[...] + step
    res_ref[...] = res
    rows_b = res.astype(BF16)
    rows_ref[...] = rows_b
    gatt_ref[...] = dot_nt(rows_b, w_co[...]).astype(BF16)
    gatt_t = dot_nt(w_co[...], rows_b).astype(BF16).astype(F32)
    dot_ref[...] = jnp.zeros_like(dot_ref)
    for head in range(NHEAD):
        feats = slice(head * HDIM, (head + 1) * HDIM)
        dot_ref[head : head + 1, :] = jnp.sum(gatt_t[feats, :] * att_t[feats, :], 0, keepdims=True)


def both_halves(half, own, other, target):
    target[pl.ds(pl.multiple_of(half * ROWS, ROWS), ROWS), :] = own[...]
    target[pl.ds(pl.multiple_of((1 - half) * ROWS, ROWS), ROWS), :] = other[...]


def cross_backward(
    scal, q2, k2, v2, lse, g_own, g_other, dot_own, dot_other,
    dk_ref, dv_ref, own_out, send_out, g_ref, dot_ref, dq_ref,
):
    half = scal[0]
    live = scal[2] - half * KEYS
    own = pl.multiple_of(half * ROWS, ROWS)
    other = pl.multiple_of((1 - half) * ROWS, ROWS)
    both_halves(half, g_own, g_other, g_ref)
    dot_ref[:, pl.ds(own, ROWS)] = dot_own[...]
    dot_ref[:, pl.ds(other, ROWS)] = dot_other[...]
    key = lax.broadcasted_iota(jnp.int32, (CHUNK, TGT), 0)

    @pl.loop(0, PAIRS)
    def _(pair):
        lanes = pl.ds(pl.multiple_of(pair * 128, 128), 128)
        q_pair, g_pair = q2[:, lanes], g_ref[:, lanes]
        for i in range(KEYS // CHUNK):
            rows = slice(i * CHUNK, (i + 1) * CHUNK)
            k_part, v_part = k2[rows, lanes], v2[rows, lanes]
            k_flip = flip(k_part).astype(BF16)
            grad_k = jnp.zeros((CHUNK, 128), F32)
            grad_v = jnp.zeros((CHUNK, 128), F32)
            for which in range(2):
                head = 2 * pair + which
                feats = pl.ds(pl.multiple_of(head * HDIM, HDIM), HDIM)
                q_one, g_one = only(q_pair, which), only(g_pair, which)
                scores = dot_nt(k_part, q_one) * SCALE
                scores = jnp.where(key < live - i * CHUNK, scores, NEG)
                probs = jnp.exp(scores - lse[pl.ds(head, 1), :])
                grad_p = dot_nt(v_part, g_one)
                grad_s = (probs * (grad_p - dot_ref[pl.ds(head, 1), :])).astype(BF16)
                grad_k = grad_k + dot_nn(grad_s, q_one)
                grad_v = grad_v + dot_nn(probs.astype(BF16), g_one)
                grad_q = dot_nn(k_flip[which * HDIM : (which + 1) * HDIM, :], grad_s)
                if i == 0:
                    dq_ref[feats, :] = grad_q
                else:
                    dq_ref[feats, :] += grad_q
            dk_ref[rows, lanes] = (grad_k * SCALE).astype(BF16)
            dv_ref[rows, lanes] = grad_v.astype(BF16)

    own_out[...] = dq_ref[:, pl.ds(own, ROWS)]
    send_out[...] = dq_ref[:, pl.ds(other, ROWS)].astype(BF16)


def source_backward(
    split, scal, dk, dv, source, w_ck, w_cv, gsrc_ref, mine_ref, send_ref, flat_ref, sm_ref, ss_ref
):
    for i in range(KEYS // CHUNK):
        rows = slice(i * CHUNK, (i + 1) * CHUNK)
        gsrc_ref[rows, :] = dot_nn(dk[rows, :], w_ck[...]) + dot_nn(dv[rows, :], w_cv[...])
        flat_ref[:, rows] = flip(source[rows, :]).astype(BF16)
    split_rows(flat_ref, sm_ref, ss_ref, scal[3], split)
    rights = (dk[...], dv[...])
    by_shard(sm_ref, rights, mine_ref, 0, 384)
    by_shard(ss_ref, rights, send_ref, 0, 384)


def query_backward(
    split, scal, dq_own, dq_other, h1_in, gain_cross, w_cq, res_in, rows_in, att, w_so,
    kv_mine, kv_send, mine_ref, send_ref, res_ref, rows_ref, gatt_ref, gg_ref, flat_ref, a_ref, b_ref,
):
    core = scal[3]
    dq = (flip(dq_own[...] + dq_other[...].astype(F32)) * SCALE).astype(BF16)
    h1 = h1_in[...]
    scale2 = rms_scale(h1)
    n2 = (h1 * scale2 * gain_cross[...]).astype(BF16)
    step, gg = norm_back(h1, scale2, gain_cross[...], dot_nn(dq, w_cq[...]))
    gg_ref[...] = gg
    res = res_in[...] + step
    res_ref[...] = res
    rows_b = res.astype(BF16)
    rows_ref[...] = rows_b
    gatt_ref[...] = dot_nt(rows_b, w_so[...]).astype(BF16)
    for m, (left, right) in enumerate(((n2, dq), (rows_in[...], att[...]))):
        flat_ref[...] = flip(left).astype(BF16)
        split_rows(flat_ref, a_ref, b_ref, core, split)
        by_shard(a_ref, (right,), mine_ref, 576 * m, D)
        by_shard(b_ref, (right,), send_ref, 576 * m, D)
    for z in range(4):
        cols = slice(z * D + 192, z * D + 576)
        mine_ref[:, cols] = kv_mine[:, z * 384 : (z + 1) * 384]
        send_ref[:, cols] = kv_send[:, z * 384 : (z + 1) * 384]


def self_backward(
    split, scal, q1, k1, v1, lse, g_own, g_other, x_own, gain_self, w_self, res_in, rows_in, att,
    mine_ref, send_ref, gin_ref, gg_ref,
    g_ref, dq_ref, dk_ref, dv_ref, flat_ref, a_ref, b_ref,
):
    half = scal[0]
    live = scal[1]
    core = scal[3]
    own = pl.multiple_of(half * ROWS, ROWS)
    both_halves(half, g_own, g_other, g_ref)
    key = lax.broadcasted_iota(jnp.int32, (TGT, TGT), 0)
    query = lax.broadcasted_iota(jnp.int32, (TGT, TGT), 1)
    seen = (key <= query) & (key < live)

    @pl.loop(0, PAIRS)
    def _(pair):
        lanes = pl.ds(pl.multiple_of(pair * 128, 128), 128)
        q_pair, g_pair = q1[:, lanes], g_ref[:, lanes]
        k_pair, v_pair = k1[:, lanes], v1[:, lanes]
        k_flip = flip(k_pair).astype(BF16)
        grad_k = jnp.zeros((TGT, 128), F32)
        grad_v = jnp.zeros((TGT, 128), F32)
        for which in range(2):
            head = 2 * pair + which
            feats = pl.ds(pl.multiple_of(head * HDIM, HDIM), HDIM)
            q_one, g_one = only(q_pair, which), only(g_pair, which)
            scores = jnp.where(seen, dot_nt(k_pair, q_one) * SCALE, NEG)
            probs = jnp.exp(scores - lse[pl.ds(head, 1), :])
            grad_p = dot_nt(v_pair, g_one)
            row_dot = jnp.sum(probs * grad_p, axis=0, keepdims=True)
            grad_s = (probs * (grad_p - row_dot)).astype(BF16)
            grad_k = grad_k + dot_nn(grad_s, q_one)
            grad_v = grad_v + dot_nn(probs.astype(BF16), g_one)
            dq_ref[feats, :] = dot_nn(k_flip[which * HDIM : (which + 1) * HDIM, :], grad_s)
        dk_ref[:, lanes] = (grad_k * SCALE).astype(BF16)
        dv_ref[:, lanes] = grad_v.astype(BF16)

    dq = (flip(dq_ref[:, pl.ds(own, ROWS)]) * SCALE).astype(BF16)
    dk = dk_ref[pl.ds(own, ROWS), :]
    dv = dv_ref[pl.ds(own, ROWS), :]
    x = x_own[...].astype(F32)
    scale1 = rms_scale(x)
    n1 = (x * scale1 * gain_self[...]).astype(BF16)
    grad_n = dot_nn(dq, w_self[0]) + dot_nn(dk, w_self[1]) + dot_nn(dv, w_self[2])
    step, gg = norm_back(x, scale1, gain_self[...], grad_n)
    gg_ref[...] = gg
    gin_ref[...] = res_in[...] + step
    flat_ref[...] = flip(n1).astype(BF16)
    split_rows(flat_ref, a_ref, b_ref, core, split)
    by_shard(a_ref, (dq, dk, dv), mine_ref, 0, D)
    by_shard(b_ref, (dq, dk, dv), send_ref, 0, D)
    flat_ref[...] = flip(rows_in[...]).astype(BF16)
    split_rows(flat_ref, a_ref, b_ref, core, split)
    by_shard(a_ref, (att[...],), mine_ref, 576, D)
    by_shard(b_ref, (att[...],), send_ref, 576, D)


def logits_kernel(vocab, rows_ref, table_ref, target_ref, logits_ref, stats_ref, m_ref, s_ref, p_ref):
    tile = pl.program_id(0)
    count = rows_ref.shape[0]

    @pl.when(tile == 0)
    def _():
        m_ref[...] = jnp.full_like(m_ref, 2 * NEG)
        s_ref[...] = jnp.zeros_like(s_ref)
        p_ref[...] = jnp.zeros_like(p_ref)

    column = tile * VTILE + lax.broadcasted_iota(jnp.int32, (count, VTILE), 1)
    logits = dot_nt(rows_ref[...], table_ref[...])
    logits = jnp.where(column < vocab, logits, 2 * NEG)
    logits_ref[...] = logits
    old = m_ref[:, 0:1]
    new = jnp.maximum(old, jnp.max(logits, axis=1, keepdims=True))
    total = s_ref[:, 0:1] * jnp.exp(old - new) + jnp.sum(
        jnp.exp(logits - new), axis=1, keepdims=True
    )
    hit = jnp.where(column == target_ref[...], logits, 0.0)
    m_ref[...] = jnp.broadcast_to(new, m_ref.shape)
    s_ref[...] = jnp.broadcast_to(total, s_ref.shape)
    p_ref[...] += jnp.broadcast_to(jnp.sum(hit, axis=1, keepdims=True), p_ref.shape)

    @pl.when(tile == pl.num_programs(0) - 1)
    def _():
        lane = lax.broadcasted_iota(jnp.int32, m_ref.shape, 1)
        merged = jnp.where(lane == 0, m_ref[...], jnp.where(lane == 1, s_ref[...], p_ref[...]))
        stats_ref[...] = merged.T[0:8, :]


def head_logits(rows, table, target):
    count = rows.shape[0]
    vocab = table.shape[0]
    tiles = pl.cdiv(vocab, VTILE)
    return pl.pallas_call(
        functools.partial(logits_kernel, vocab),
        grid=(tiles,),
        out_shape=[whole((count, tiles * VTILE), F32), whole((8, count), F32)],
        in_specs=[
            pl.BlockSpec((count, D), lambda i: (0, 0)),
            pl.BlockSpec((VTILE, D), lambda i: (i, 0)),
            pl.BlockSpec((count, 1), lambda i: (0, 0)),
        ],
        out_specs=[
            pl.BlockSpec((count, VTILE), lambda i: (0, i)),
            pl.BlockSpec((8, count), lambda i: (0, 0)),
        ],
        scratch_shapes=[pltpu.VMEM((count, 128), F32)] * 3,
        cost_estimate=pl.CostEstimate(
            flops=2 * count * vocab * D, bytes_accessed=vocab * (2 * D + 4 * count), transcendentals=0
        ),
        compiler_params=pltpu.CompilerParams(vmem_limit_bytes=VMEM_LIMIT),
    )(rows, table, target)


def grads_kernel(vocab, logits_ref, table_ref, target_ref, lse_ref, live_ref, g_ref, gf_ref, acc_ref):
    tile = pl.program_id(0)
    count = logits_ref.shape[0]

    @pl.when(tile == 0)
    def _():
        acc_ref[...] = jnp.zeros_like(acc_ref)

    column = tile * VTILE + lax.broadcasted_iota(jnp.int32, (count, VTILE), 1)
    hit = jnp.where(column == target_ref[...], 1.0, 0.0)
    grad = jnp.where(live_ref[...] > 0, jnp.exp(logits_ref[...] - lse_ref[...]) - hit, 0.0)
    grad = grad.astype(BF16)
    g_ref[...] = grad
    entry = tile * VTILE + lax.broadcasted_iota(jnp.int32, (VTILE, D), 0)
    table = jnp.where(entry < vocab, table_ref[...], jnp.zeros_like(table_ref[...]))
    acc_ref[...] += dot_nn(grad, table)

    @pl.when(tile == pl.num_programs(0) - 1)
    def _():
        gf_ref[...] = acc_ref[...].astype(gf_ref.dtype)


def head_grads(logits, table, target, lse, live, dtype):
    count = logits.shape[0]
    vocab = table.shape[0]
    tiles = pl.cdiv(vocab, VTILE)
    column = pl.BlockSpec((count, 1), lambda i: (0, 0))
    return pl.pallas_call(
        functools.partial(grads_kernel, vocab),
        grid=(tiles,),
        out_shape=[whole((count, tiles * VTILE), BF16), whole((count, D), dtype)],
        in_specs=[
            pl.BlockSpec((count, VTILE), lambda i: (0, i)),
            pl.BlockSpec((VTILE, D), lambda i: (i, 0)),
            column,
            column,
            column,
        ],
        out_specs=[
            pl.BlockSpec((count, VTILE), lambda i: (0, i)),
            pl.BlockSpec((count, D), lambda i: (0, 0)),
        ],
        scratch_shapes=[pltpu.VMEM((count, D), F32)],
        cost_estimate=pl.CostEstimate(
            flops=2 * count * vocab * D, bytes_accessed=vocab * (2 * D + 6 * count), transcendentals=0
        ),
        compiler_params=pltpu.CompilerParams(vmem_limit_bytes=VMEM_LIMIT),
    )(logits, table, target, lse, live)


def table_kernel(fm_a, fm_b, fs_a, fs_b, g_a, g_b, mine_ref, send_ref):
    first, second = g_a[...], g_b[...]
    mine_ref[...] = dot_nn(fm_a[...], first) + dot_nn(fm_b[...], second)
    send_ref[...] = (dot_nn(fs_a[...], first) + dot_nn(fs_b[...], second)).astype(BF16)


def table_grads(flat_a, flat_b, g_a, g_b):
    count, width = g_a.shape
    left = pl.BlockSpec((HALF_D, count), lambda i: (0, 0))
    right = pl.BlockSpec((count, VTILE), lambda i: (0, i))
    out = pl.BlockSpec((HALF_D, VTILE), lambda i: (0, i))
    return pl.pallas_call(
        table_kernel,
        grid=(width // VTILE,),
        out_shape=[whole((HALF_D, width), F32), whole((HALF_D, width), BF16)],
        in_specs=[left] * 4 + [right] * 2,
        out_specs=[out] * 2,
        cost_estimate=pl.CostEstimate(
            flops=4 * count * width * D, bytes_accessed=width * (4 * count + 6 * HALF_D), transcendentals=0
        ),
        compiler_params=pltpu.CompilerParams(vmem_limit_bytes=VMEM_LIMIT),
    )(flat_a[0], flat_b[0], flat_a[1], flat_b[1], g_a, g_b)


def make(mesh):
    dp_size = mesh.shape["dp"]
    split = dp_size == 8

    def on_device(
        block_in,
        source,
        target_len,
        source_len,
        targets,
        gain_self,
        gain_cross,
        gain_ff,
        gain_final,
        self_q,
        self_k,
        self_v,
        self_o,
        cross_q,
        cross_k,
        cross_v,
        cross_o,
        ff_gate,
        ff_up,
        ff_down,
        embed_table,
    ):
        z = lax.axis_index("tensor")
        dp = lax.axis_index("dp")
        half = lax.rem(z, 2)
        seq = z // 2
        core = lax.rem(dp, 2)
        gain_self, gain_cross, gain_ff, gain_final = (
            g.reshape(1, D) for g in (gain_self, gain_cross, gain_ff, gain_final)
        )

        def pair_swap(value):
            return swap(value, "tensor", 4, 1)

        x_other = pair_swap(block_in)
        w_self, w_cross = gather_blocks(
            [
                jnp.concatenate([self_q.T, self_k.T, self_v.T, self_o], 0),
                jnp.concatenate([cross_q.T, cross_k.T, cross_v.T, cross_o], 0),
            ],
            dp_size,
        )
        wg = gather_wide(ff_gate.T, dp_size)
        wu = gather_wide(ff_up.T, dp_size)
        wd = gather_wide(ff_down, dp_size)
        cq, ck, cv, co = (w_cross[i] for i in range(4))
        scal = jnp.stack(
            [
                half,
                lax.dynamic_index_in_dim(target_len, seq, keepdims=False),
                lax.dynamic_index_in_dim(source_len, seq, keepdims=False),
                core,
            ]
        ).astype(jnp.int32)

        def vm(shape, dtype):
            return pltpu.VMEM(shape, dtype)

        pair = (TGT, D)
        q1, k1, v1, lse1, a1, h1, q2 = local_call(
            self_forward,
            [whole(pair, BF16)] * 3
            + [whole((16, TGT), F32), whole((ROWS, D), BF16), whole((ROWS, D), F32), whole(pair, BF16)],
            [vm(pair, F32), vm(pair, BF16), vm((D, TGT), BF16), vm((D, TGT), F32)],
            8e9,
            scal, block_in, x_other, gain_self, gain_cross, w_self, cq,
        )
        k2, v2, o_own, o_send, lse_own = local_call(
            cross_forward,
            [whole((KEYS, D), BF16)] * 2
            + [whole((D, ROWS), F32), whole((D, ROWS), BF16), whole((16, TGT), F32)],
            [vm((D, KEYS), BF16), vm((KEYS, TGT), F32), vm((D, TGT), F32)],
            15e9,
            scal, q2, source, ck, cv,
        )
        block_out, fin, h2, att_t, a2, lse2 = local_call(
            ff_forward,
            [whole((ROWS, D), F32), whole((ROWS, D), BF16), whole((ROWS, D), F32)]
            + [whole((D, ROWS), F32), whole((ROWS, D), BF16), whole((16, TGT), F32)],
            [vm((ROWS, FF), BF16)],
            3e9,
            scal, o_own, pair_swap(o_send), lse_own, pair_swap(lse_own), h1, co,
            gain_ff, gain_final, wg, wu, wd,
        )

        vocab = embed_table.shape[0]

        def block(by_block, j, axis=0):
            return lax.dynamic_index_in_dim(by_block, z ^ j, axis, keepdims=False)

        tgt_local = targets - z * vocab
        tgt_local = jnp.where((tgt_local >= 0) & (tgt_local < vocab), tgt_local, -1)
        tgt_blocks = tgt_local.reshape(4, ROWS)
        position = lax.rem(jnp.arange(4 * ROWS), TGT)
        live = position < jnp.repeat(target_len, TGT, total_repeat_length=4 * ROWS)
        live_blocks = live.astype(jnp.int32).reshape(4, ROWS)
        fin_1, fin_2, fin_3 = (swap(fin, "tensor", 4, j) for j in (1, 2, 3))
        fin_a = jnp.concatenate([fin_2, fin_3], 0)
        fin_b = jnp.concatenate([fin, fin_1], 0)

        def columns(by_block, order):
            return jnp.concatenate([block(by_block, j) for j in order], 0)[:, None]

        tgt_a, tgt_b = columns(tgt_blocks, (2, 3)), columns(tgt_blocks, (0, 1))
        logits_b, stats_b = head_logits(fin_b, embed_table, tgt_b)
        logits_a, stats_a = head_logits(fin_a, embed_table, tgt_a)
        stats = [stats_b[:, :ROWS], stats_b[:, ROWS:], stats_a[:, :ROWS], stats_a[:, ROWS:]]
        stats = jnp.stack(stats, 0)
        stats = jnp.stack([block(stats, j) for j in range(4)], 0)
        others = [stats] + [swap(stats, "tensor", 4, j) for j in (1, 2, 3)]

        def over_z(values, op):
            return op(op(values[0], values[1]), op(values[2], values[3]))

        top = over_z([s[:, 0] for s in others], jnp.maximum)
        total = over_z([s[:, 1] * jnp.exp(s[:, 0] - top) for s in others], jnp.add)
        picked = over_z([s[:, 2] for s in others], jnp.add)
        g_lse = top + jnp.log(total)
        token_loss = jnp.where(live, (g_lse - picked).reshape(-1), 0.0)
        g_a, gf_a = head_grads(
            logits_a, embed_table, tgt_a, columns(g_lse, (2, 3)), columns(live_blocks, (2, 3)), BF16
        )
        g_b, gf_b = head_grads(
            logits_b, embed_table, tgt_b, columns(g_lse, (0, 1)), columns(live_blocks, (0, 1)), F32
        )
        gf_2 = swap(gf_a[:ROWS], "tensor", 4, 2)
        gf_3 = swap(gf_a[ROWS:], "tensor", 4, 3)
        gf_1 = swap(gf_b[ROWS:].astype(BF16), "tensor", 4, 1)

        def halves(rows):
            flat = rows.T
            if not split:
                return flat[:HALF_D], flat[HALF_D:]
            flat = flat.reshape(4, 2, 96, -1)
            return tuple(
                lax.dynamic_index_in_dim(flat, i, 1, keepdims=False).reshape(HALF_D, -1)
                for i in (core, 1 - core)
            )

        reduction = Reduction if split else WideReduction
        xyz = jnp.stack([lax.rem(dp // 2, 2), dp // 4, z]).astype(jnp.int32)
        e_mine, e_send = table_grads(halves(fin_a), halves(fin_b), g_a, g_b)
        if not split:
            e_mine, e_send = e_mine[:, :vocab], e_send[:, :vocab]
        e_sum = reduction(xyz, e_mine, e_send)

        half_t = (HALF_D, ROWS)
        ff_mine, ff_send, res2, rows2, gatt, dots, gg_a = local_call(
            functools.partial(ff_backward, split),
            [whole((HALF_D, 3 * FF), F32), whole((HALF_D, 3 * FF), BF16), whole((ROWS, D), F32)]
            + [whole((ROWS, D), BF16)] * 2
            + [whole((16, ROWS), F32), whole((2, D), F32)],
            [vm((D, ROWS), BF16)] + [vm(half_t, BF16)] * 4
            + [vm((ROWS, D), F32)],
            10e9,
            scal, after(gf_b[:ROWS], e_send), gf_1, gf_2, gf_3, block_out, h2,
            gain_ff, gain_final, wg, wu, wd, co, att_t,
        )
        ff_sum = reduction(xyz, ff_mine, ff_send)
        gatt_other, dots_other = pair_swap(gatt), pair_swap(dots)
        sent = e_sum.first()
        dk2, dv2, dq_own, dq_send = local_call(
            cross_backward,
            [whole((KEYS, D), BF16)] * 2 + [whole((D, ROWS), F32), whole((D, ROWS), BF16)],
            [vm(pair, BF16), vm((16, TGT), F32), vm((D, TGT), F32)],
            20e9,
            scal, q2, k2, v2, lse2, after(gatt, *sent), gatt_other, dots, dots_other,
        )
        dq_other = pair_swap(dq_send)
        sent = ff_sum.first()
        grad_source, kv_mine, kv_send = local_call(
            functools.partial(source_backward, split),
            [whole((KEYS, D), F32), whole((HALF_D, 2 * D), F32), whole((HALF_D, 2 * D), BF16)],
            [vm((D, KEYS), BF16)] + [vm((HALF_D, KEYS), BF16)] * 2,
            5e9,
            scal, after(dk2, *sent), dv2, source, ck, cv,
        )
        sent = e_sum.second()
        c_mine, c_send, res1, rows1, gatt1, gg_b = local_call(
            functools.partial(query_backward, split),
            [whole((HALF_D, 4 * D), F32), whole((HALF_D, 4 * D), BF16), whole((ROWS, D), F32)]
            + [whole((ROWS, D), BF16)] * 2 + [whole((1, D), F32)],
            [vm((D, ROWS), BF16)] + [vm(half_t, BF16)] * 2,
            2e9,
            scal, after(dq_own, *sent), dq_other, h1, gain_cross, cq, res2, rows2, a2, w_self[3],
            kv_mine, kv_send,
        )
        c_sum = reduction(xyz, c_mine, c_send)
        gatt1_other = pair_swap(gatt1)
        sent = ff_sum.second() + c_sum.first()
        s_mine, s_send, grad_block_in, gg_c = local_call(
            functools.partial(self_backward, split),
            [whole((HALF_D, 4 * D), F32), whole((HALF_D, 4 * D), BF16)]
            + [whole((ROWS, D), F32), whole((1, D), F32)],
            [vm(pair, BF16), vm((D, TGT), F32), vm(pair, BF16), vm(pair, BF16)]
            + [vm((D, ROWS), BF16)] + [vm(half_t, BF16)] * 2,
            12e9,
            scal, q1, k1, v1, lse1, after(gatt1, *sent), gatt1_other, block_in, gain_self, w_self,
            res1, rows1, a1,
        )
        s_sum = reduction(xyz, s_mine, s_send)
        gains = jnp.concatenate([gg_a, gg_b, gg_c], 0)
        if split:
            for axis, size, bit in (("dp", 8, 1), ("tensor", 4, 1), ("dp", 8, 2), ("tensor", 4, 2), ("dp", 8, 4)):
                gains = gains + swap(gains, axis, size, bit)
        else:
            gains = lax.psum(gains, ("dp", "tensor"))
        sent = s_sum.first()
        sent = sent + ff_sum.third() + c_sum.second()
        grad_embed = e_sum.table(vocab)
        s_sum.second()
        c_sum.third()
        ff_grads = ff_sum.last(3, (2,))
        s_sum.third()
        c_grads = c_sum.last(4, (3,))
        s_grads = s_sum.last(4, (3,))

        return (
            block_out,
            token_loss,
            grad_block_in,
            grad_source,
            gains[3],
            gains[2],
            gains[1],
            gains[0],
            *s_grads,
            *c_grads,
            *ff_grads,
            grad_embed,
        )

    return on_device


def solution(mesh):
    rows = P(("dp", "tensor"), None)
    wide, tall = P(None, "tensor"), P("tensor", None)
    in_specs = (rows, rows) + (P("dp"),) * 3 + (P(),) * 4
    in_specs += (wide, wide, wide, tall) * 2 + (wide, wide, tall, tall)
    g_in, g_out = P("dp", "tensor"), P("tensor", "dp")
    out_specs = (rows, P("dp"), rows, rows) + (P(),) * 4
    out_specs += (g_in, g_in, g_in, g_out) * 2 + (g_in, g_in, g_out, g_out)
    return jax.shard_map(
        make(mesh), mesh=mesh, in_specs=in_specs, out_specs=out_specs, check_vma=False
    )
```

time: 952 us -> 768 us (0.81)
  Pallas kernels: 148 us -> 404 us
  matrix products: 225 us -> 0 us
  local copies, waits for them, and re-layouts: 202 us -> 96.7 us
  other arithmetic: 116 us -> 13 us
  blocking collectives: 41.3 us -> 0 us
  waiting for transfers between devices: 140 us -> 165 us
  between operations: 2.68 us -> 15.2 us
    pallas_call x1 -> x30, Pallas kernels: 148 us -> 404 us  [the longest x8 109 us: local_call(): pl.pallas_call(body, out_shape=outs, in_specs=[smem] + [vmem] * (len(args...]
    dot_general x48 -> x0, matrix products: 225 us -> none  [the longest x12 47.9 us: dot_nt(): lax.dot_general(left, right, (((1,), (1,)), ((), ())), preferred_element_...]
    concatenate x20 -> x2, local copies, waits for them, and re-layouts: 82.9 us -> 0.05 us  [the longest x1 0.03 us: on_device(): fin_b = jnp.concatenate([fin, fin_1], 0)]
    all_gather x0 -> x3, waiting for transfers between devices: none -> 56.2 us  [gather_wide(): return lax.all_gather(part, ('tensor', 'dp'), axis=0, tiled=True)]
    convert_element_type x29 -> x1, other arithmetic: 52 us -> 0.01 us  [on_device(): live_blocks = live.astype(jnp.int32).reshape(4, ROWS)]
    psum x1 -> x0, blocking collectives: 41.3 us -> none  [on_device(): lax.psum(jnp.stack([gg_self, gg_cross, gg_ff, gg_final]), ('dp', 'tensor'))]
    reduce_sum x8 -> x0, other arithmetic: 32 us -> none  [the longest x1 15 us: on_device(): picked = jnp.sum(jnp.where(hit, logits, 0.0), axis=1)]
    ppermute x45 -> x50, waiting for transfers between devices: 140 us -> 109 us  [swap(): return lax.ppermute(value, axis_name, [(i, i ^ bit) for i in range(size)])]
  transfers between devices with their start and end apart: 45 -> 53, of which waited for: 26 -> 14; matrix products, arithmetic and copies ran while one was open for 35% -> 6% of each run, Pallas kernels for 16% -> 36%
where the time goes in v2:
time: 768 us; the launch traced here: 759 us
  Pallas kernels  404 us (53%)
  waiting for transfers between devices  165 us (21%)
  local copies, waits for them, and re-layouts  96.7 us (13%)
  starting transfers between devices  65.7 us (9%)
  between operations  15.2 us (2%)
  other arithmetic  13 us (2%)
    ppermute x50, waiting for transfers between devices, swap(): return lax.ppermute(value, axis_name, [(i, i ^ bit) for i in range(size)])  109 us
    pallas_call x8, Pallas kernels, local_call(): pl.pallas_call(body, out_shape=outs, in_specs=[smem] + [vmem] * (len(args...  109 us
    pallas_call x1, Pallas kernels, gather_blocks(): pl.pallas_call(functools.partial(gather_kernel, groups), out_shape=[jax.S...  76.4 us
    unnamed x261, local copies, waits for them, and re-layouts  71.9 us
    pallas_call x2, Pallas kernels, head_logits(): pl.pallas_call(functools.partial(logits_kernel, vocab), grid=(tiles,), ou...  70 us
    ppermute x50, starting transfers between devices, swap(): return lax.ppermute(value, axis_name, [(i, i ^ bit) for i in range(size)])  65.6 us
    all_gather x3, waiting for transfers between devices, gather_wide(): return lax.all_gather(part, ('tensor', 'dp'), axis=0, tiled=True)  56.2 us
    pallas_call x8, Pallas kernels, fold_call(): pl.pallas_call(body, grid=(width // tile,), out_shape=outs, in_specs=in_s...  53.9 us
  transfers between devices with their start and end apart: 53, of which 14 were waited for; matrix products, arithmetic and copies ran while one was open for 6% of the time, Pallas kernels for 36%

profile of v2, /device:TPU:0, one launch (start us, length us, event | category | flops | bytes accessed | tf_op | source)
XLA Modules:
  0.0 758.9 jit_solution(6861998081271071854)
XLA Ops:
  10.9 3.1 collective-permute-start
  16.6 3.2 pad_maximum_fusion.1
  21.2 76.4 %shard_map.356 = (bf16[4,768,768]{2,1,0:T(8,128)(2,1)}, bf16[4,768,768]{2,1,0:T(8,128)(2,1)}) custom-call(bf16[768,768]{1,0:T(8,128)(2,1)} %get-tuple-element.352.refs_0_, bf16[768,768]{1,0:T(8,128)(2,1)} %get-tuple-element.353.refs_1_), custom_call_target="tpu_custom_call" | custom-call | tf_op jit(solution)/shard_map/pallas_call | solution.py:158
  97.6 2.8 slice_bitcast_fusion.1
  102.9 11.9 %shard_map.357 = (bf16[512,768]{1,0:T(8,128)(2,1)S(1)}, bf16[512,768]{1,0:T(8,128)(2,1)S(1)}, bf16[512,768]{1,0:T(8,128)(2,1)S(1)}, f32[16,512]{1,0:T(8,128)S(1)...) custom-call(s32[4]{0:T(128)S(1)} %pad_add_fusion.4.scal, ...), custom_call_target="tpu_custom_call" | custom-call | flops 8000000000 | bytes 11048976 | tf_op jit(solution)/shard_map/pallas_call | solution.py:401
  115.8 17.8 %shard_map.358 = (bf16[1024,768]{1,0:T(8,128)(2,1)S(1)}, bf16[1024,768]{1,0:T(8,128)(2,1)S(1)}, f32[768,256]{1,0:T(8,128)S(1)}, bf16[768,256]{1,0:T(8,128)(2,1)}, f32[16,512]{1,0:T(8,128)S(1)}) custom-call(s32[4]{0:T(128)S(1)} %pad_add_fusion.4.scal, bf16[512,768]{1,0:T(8,128)(2,1)S(1)} %get-tuple-element.148.q2, bf16[1024,768]{1,0:T(8,128)(2,1)S(1)} %copy-done.41, ...), custom_call_target="tpu_custom_call" | custom-call | flops 15000000512 | bytes 9076752 | tf_op jit(solution)/shard_map/pallas_call | solution.py:401
  142.8 9.1 %collective-permute-done.2.lse_other = f32[16,512]{1,0:T(8,128)S(1)} collective-permute-done((f32[16,512]{1,0:T(8,128)}, f32[16,512]{1,0:T(8,128)S(1)}, u32[]{:S(2)}, u32[]{:S(2)}) %collective-permute-start.2) | collective-permute-done | bytes 32800 | tf_op jit(solution)/shard_map/ppermute | solution.py:40
  153.3 56.2 %all-gather.8.cloned.1.call-done.wd = bf16[2048,768]{1,0:T(8,128)(2,1)} async-done(((bf16[64,768]{1,0:T(8,128)(2,1)}), bf16[2048,768]{1,0:T(8,128)(2,1)}) %all-gather.8.cloned.1.call-update) | async-done | bytes 3145744 | tf_op jit(solution)/shard_map/all_gather | solution.py:148
  218.8 5.8 shard_map.359
  236.1 6.8 collective-permute-done.3
  243.8 34.9 %shard_map.360 = (f32[512,8192]{1,0:T(8,128)}, f32[8,512]{1,0:T(8,128)}) custom-call(bf16[512,768]{1,0:T(8,128)(2,1)} %copy-done.78, bf16[8032,768]{1,0:T(8,128)(2,1)} %table_ref.7, s32[512,1]{1,0:T(8,128)} %copy.58.target_ref), custom_call_target="tpu_custom_call" | custom-call | flops 6316621824 | bytes 28786688 | tf_op jit(solution)/shard_map/pallas_call | solution.py:792
  280.4 35.1 %shard_map.361 = (f32[512,8192]{1,0:T(8,128)}, f32[8,512]{1,0:T(8,128)}) custom-call(bf16[512,768]{1,0:T(8,128)(2,1)} %copy-done.77, bf16[8032,768]{1,0:T(8,128)(2,1)} %table_ref.7, s32[512,1]{1,0:T(8,128)} %copy.59.target_ref), custom_call_target="tpu_custom_call" | custom-call | flops 6316621824 | bytes 28786688 | tf_op jit(solution)/shard_map/pallas_call | solution.py:792
  316.3 2.7 collective-permute-start.7
  320.7 2.3 copy.71
  331.1 22.8 %shard_map.363 = (bf16[512,8192]{1,0:T(8,128)(2,1)}, bf16[512,768]{1,0:T(8,128)(2,1)}) custom-call(f32[512,8192]{1,0:T(8,128)} %get-tuple-element.166.logits_ref, bf16[8032,768]{1,0:T(8,128)(2,1)} %table_ref.7, s32[512,1]{1,0:T(8,128)} %copy.59.target_ref, f32[512,1]{1,0:T(8,128)} %copy.73.lse_ref, s32[512,1]{1,0:T(8,128)} %copy.74.live_ref), custom_call_target="tpu_custom_call" | custom-call | flops 6316621824 | bytes 37011456 | tf_op jit(solution)/shard_map/pallas_call | solution.py:840
  354.0 23.2 %shard_map.362 = (bf16[512,8192]{1,0:T(8,128)(2,1)}, f32[512,768]{1,0:T(8,128)}) custom-call(f32[512,8192]{1,0:T(8,128)} %get-tuple-element.164.logits_ref, bf16[8032,768]{1,0:T(8,128)(2,1)} %table_ref.7, s32[512,1]{1,0:T(8,128)} %copy.58.target_ref, f32[512,1]{1,0:T(8,128)} %copy.68.lse_ref, s32[512,1]{1,0:T(8,128)} %copy.69.live_ref), custom_call_target="tpu_custom_call" | custom-call | flops 6316621824 | bytes 37011456 | tf_op jit(solution)/shard_map/pallas_call | solution.py:840
  377.2 21.4 %shard_map.364 = (f32[384,8192]{1,0:T(8,128)}, bf16[384,8192]{1,0:T(8,128)(2,1)}) custom-call(bf16[384,512]{1,0:T(8,128)(2,1)} %bitcast.172, bf16[384,512]{1,0:T(8,128)(2,1)} %bitcast.170, bf16[384,512]{1,0:T(8,128)(2,1)} %bitcast.171, bf16[384,512]{1,0:T(8,128)(2,1)} %bitcast.169, bf16[512,8192]{1,0:T(8,128)(2,1)} %get-tuple-element.167.g_a, ...), custom_call_target="tpu_custom_call" | custom-call | flops 12884901888 | bytes 35651584 | tf_op jit(solution)/shard_map/pallas_call | solution.py:874
  402.5 25.2 %collective-permute-done.10.gf_2 = bf16[256,768]{1,0:T(8,128)(2,1)S(1)} collective-permute-done((bf16[256,768]{1,0:T(8,128)(2,1)S(1)}, bf16[256,768]{1,0:T(8,128)(2,1)S(1)}, u32[]{:S(2)}, u32[]{:S(2)}) %collective-permute-start.10) | collective-permute-done | bytes 393248 | tf_op jit(solution)/shard_map/ppermute | solution.py:40
  429.2 18.4 %shard_map.365 = (f32[384,6144]{1,0:T(8,128)}, bf16[384,6144]{1,0:T(8,128)(2,1)}, f32[256,768]{1,0:T(8,128)S(1)}, bf16[256,768]{1,0:T(8,128)(2,1)S(1)}, bf16[256...) custom-call(s32[4]{0:T(128)S(1)} %copy-done.35, f32[256,768]{1,0:T(8,128)S(1)} %slice.128.gf_own, ...), custom_call_target="tpu_custom_call" | custom-call | flops 10000000000 | bytes 30699536 | tf_op jit(solution)/shard_map/pallas_call | solution.py:401
  449.2 7.6 collective-permute-start.13
  458.8 8.8 %shard_map.369 = (f32[192,3072]{1,0:T(8,128)}, bf16[192,3072]{1,0:T(8,128)(2,1)}, f32[192,3072]{1,0:T(8,128)}, bf16[192,3072]{1,0:T(8,128)(2,1)}) custom-call(s32[3]{0:T(128)} %pad_add_fusion.5.xyz, f32[384,6144]{1,0:T(8,128)} %get-tuple-element.191.mine_a.mine_b, bf16[384,6144]{1,0:T(8,128)(2,1)} %collective-permute-done.18.got_a.got_b, ...), custom_call_target="tpu_custom_call" | custom-call | bytes 21233664 | tf_op jit(solution)/shard_map/pallas_call | solution.py:190
  467.6 11.5 %shard_map.366 = (f32[192,4096]{1,0:T(8,128)}, bf16[192,4096]{1,0:T(8,128)(2,1)}, f32[192,4096]{1,0:T(8,128)}, bf16[192,4096]{1,0:T(8,128)(2,1)}) custom-call(s32[3]{0:T(128)} %pad_add_fusion.5.xyz, f32[384,8192]{1,0:T(8,128)} %get-tuple-element.175.mine_a.mine_b, bf16[384,8192]{1,0:T(8,128)(2,1)} %collective-permute-done.12.got_a.got_b, ...), custom_call_target="tpu_custom_call" | custom-call | bytes 28311552 | tf_op jit(solution)/shard_map/pallas_call | solution.py:190
  485.9 25.2 %shard_map.367 = (bf16[1024,768]{1,0:T(8,128)(2,1)S(1)}, bf16[1024,768]{1,0:T(8,128)(2,1)S(1)}, f32[768,256]{1,0:T(8,128)S(1)}, bf16[768,256]{1,0:T(8,128)(2,1)}) custom-call(s32[4]{0:T(128)S(1)} %copy-done.36, bf16[512,768]{1,0:T(8,128)(2,1)S(1)} %copy-done.67, bf16[1024,768]{1,0:T(8,128)(2,1)S(1)} %copy-done.71, bf16[1024,768]{1,0:T(8,128)(2,1)S(1)} %copy-done.73, ...), custom_call_target="tpu_custom_call" | custom-call | flops 20000000000 | bytes 9109520 | tf_op jit(solution)/shard_map/pallas_call | solution.py:401
  511.1 6.1 collective-permute-start.17
  517.2 6.5 shard_map.370
  527.9 8.0 %shard_map.368 = (f32[96,4096]{1,0:T(8,128)}, bf16[96,4096]{1,0:T(8,128)(2,1)}, f32[96,4096]{1,0:T(8,128)}, bf16[96,4096]{1,0:T(8,128)(2,1)}) custom-call(s32[3]{0:T(128)} %pad_add_fusion.5.xyz, f32[192,4096]{1,0:T(8,128)} %get-tuple-element.181.mine_a, bf16[192,4096]{1,0:T(8,128)(2,1)} %copy-done.79, f32[192,4096]{1,0:T(8,128)} %get-tuple-element.182.mine_b, ...), custom_call_target="tpu_custom_call" | custom-call | bytes 14155776 | tf_op jit(solution)/shard_map/pallas_call | solution.py:190
  542.8 5.9 shard_map.371
  554.4 26.3 %collective-permute-done.19.got_a = bf16[192,3072]{1,0:T(8,128)(2,1)S(1)} collective-permute-done((bf16[192,3072]{1,0:T(8,128)(2,1)S(1)}, bf16[192,3072]{1,0:T(8,128)(2,1)S(1)}, u32[]{:S(2)}, u32[]{:S(2)}) %collective-permute-start.19) | collective-permute-done | bytes 1179680 | tf_op jit(solution)/shard_map/ppermute | solution.py:40
  583.0 6.3 shard_map.372
  589.3 5.8 shard_map.373
  595.9 2.3 copy-done.27
  605.6 17.2 %shard_map.374 = (f32[384,3072]{1,0:T(8,128)S(1)}, bf16[384,3072]{1,0:T(8,128)(2,1)S(1)}, f32[256,768]{1,0:T(8,128)}, f32[1,768]{1,0:T(1,128)S(1)}) custom-call(s32[4]{0:T(128)S(1)} %copy-done.38, bf16[512,768]{1,0:T(8,128)(2,1)S(1)} %copy-done.61, bf16[512,768]{1,0:T(8,128)(2,1)S(1)} %copy-done.63, bf16[512,768]{1,0:T(8,128)(2,1)S(1)} %copy-done.65, ...), custom_call_target="tpu_custom_call" | custom-call | flops 12000000000 | bytes 17733648 | tf_op jit(solution)/shard_map/pallas_call | solution.py:401
  626.9 13.8 %collective-permute-done.43.got_a = bf16[96,3072]{1,0:T(8,128)(2,1)S(1)} collective-permute-done((bf16[96,3072]{1,0:T(8,128)(2,1)S(1)}, bf16[96,3072]{1,0:T(8,128)(2,1)S(1)}, u32[]{:S(2)}, u32[]{:S(2)}) %collective-permute-start.43) | collective-permute-done | bytes 589856 | tf_op jit(solution)/shard_map/ppermute | solution.py:40
  641.8 3.4 shard_map.382
  649.7 5.4 shard_map.375
  656.7 3.7 collective-permute-done.24
  661.4 2.7 collective-permute-done.46.got_2
  665.4 7.8 %collective-permute-done.25 = f32[4,768]{1,0:T(4,128)S(1)} collective-permute-done((f32[4,768]{1,0:T(4,128)S(1)}, f32[4,768]{1,0:T(4,128)S(1)}, u32[]{:S(2)}, u32[]{:S(2)}) %collective-permute-start.25) | collective-permute-done | bytes 12320 | tf_op jit(solution)/shard_map/ppermute | solution.py:40
  677.2 4.0 shard_map.379
  685.6 4.1 shard_map.376
  689.7 8.9 %collective-permute-done.38.got_a = bf16[96,1536]{1,0:T(8,128)(2,1)} collective-permute-done((bf16[96,1536]{1,0:T(8,128)(2,1)}, bf16[96,1536]{1,0:T(8,128)(2,1)}, u32[]{:S(2)}, u32[]{:S(2)}) %collective-permute-start.38) | collective-permute-done | bytes 294944 | tf_op jit(solution)/shard_map/ppermute | solution.py:40
  701.5 2.5 shard_map.380
  708.5 2.3 shard_map.383
  712.5 6.3 shard_map.384
  719.7 6.4 shard_map.385
  728.5 2.5 shard_map.377
  735.4 3.9 pad_maximum_fusion
  739.3 5.3 copy.76
  (409 shorter events, 144.5 us)
Async XLA Ops:
  7.2 146.1 %all-gather.4.cloned.1.call-start = ((), (), s32[]{:S(2)}) async-start(), calls=%async_computation | async-start | bytes 3244032 | tf_op jit(solution)/shard_map/all_gather | solution.py:148
  9.3 144.0 %all-gather.6.cloned.1.call-start = ((), (), s32[]{:S(2)}) async-start(), calls=%async_computation.1 | async-start | bytes 3244032 | tf_op jit(solution)/shard_map/all_gather | solution.py:148
  10.2 199.3 %all-gather.8.cloned.1.call-start = ((), (), s32[]{:S(2)}) async-start(), calls=%async_computation.2 | async-start | bytes 3244032 | tf_op jit(solution)/shard_map/all_gather | solution.py:148
  10.9 89.5 %collective-permute-start = (bf16[256,768]{1,0:T(8,128)(2,1)}, bf16[256,768]{1,0:T(8,128)(2,1)S(1)}, u32[]{:S(2)}, u32[]{:S(2)}) collective-permute-start(bf16[256,768]{1,0:T(8,128)(2,1)} %x_own.3), channel_id=1, source_target_pairs={{0,1},{1,0},{2,3},{3,2},{4,5},{5,4},{6,7},{7,6},{8,9},{9,8},{10,11... | collective-permute-start | bytes 1179656 | tf_op jit(solution)/shard_map/ppermute | solution.py:40
  137.4 15.2 %collective-permute-start.1 = (bf16[768,256]{1,0:T(8,128)(2,1)}, bf16[768,256]{1,0:T(8,128)(2,1)S(1)}, u32[]{:S(2)}, u32[]{:S(2)}) collective-permute-start(bf16[768,256]{1,0:T(8,128)(2,1)} %get-tuple-element.150), channel_id=1, source_target_pairs={{0,1},{1,0},{2,3},{3,2},{4,5},{5,4},{6,7},{7,6},{8,9},{9,8},{10,11... | collective-permute-start | bytes 1179656 | tf_op jit(solution)/shard_map/ppermute | solution.py:40
  139.3 12.6 %collective-permute-start.2 = (f32[16,512]{1,0:T(8,128)}, f32[16,512]{1,0:T(8,128)S(1)}, u32[]{:S(2)}, u32[]{:S(2)}) collective-permute-start(f32[16,512]{1,0:T(8,128)} %copy-done.28), channel_id=1, source_target_pairs={{0,1},{1,0},{2,3},{3,2},{4,5},{5,4},{6,7},{7,6},{8,9},{9,8},{10,11... | collective-permute-start | bytes 98312 | tf_op jit(solution)/shard_map/ppermute | solution.py:40
  227.2 15.7 %collective-permute-start.3 = (bf16[256,768]{1,0:T(8,128)(2,1)}, bf16[256,768]{1,0:T(8,128)(2,1)S(1)}, u32[]{:S(2)}, u32[]{:S(2)}) collective-permute-start(bf16[256,768]{1,0:T(8,128)(2,1)} %get-tuple-element.154), channel_id=1, source_target_pairs={{0,1},{1,0},{2,3},{3,2},{4,5},{5,4},{6,7},{7,6},{8,9},{9,8},{10,11... | collective-permute-start | bytes 1179656 | tf_op jit(solution)/shard_map/ppermute | solution.py:40
  231.2 47.5 %collective-permute-start.4 = (bf16[256,768]{1,0:T(8,128)(2,1)}, bf16[256,768]{1,0:T(8,128)(2,1)S(1)}, u32[]{:S(2)}, u32[]{:S(2)}) collective-permute-start(bf16[256,768]{1,0:T(8,128)(2,1)} %get-tuple-element.154), channel_id=1, source_target_pairs={{0,2},{1,3},{2,0},{3,1},{4,6},{5,7},{6,4},{7,5},{8,10},{9,11},{10,... | collective-permute-start | bytes 1179656 | tf_op jit(solution)/shard_map/ppermute | solution.py:40
  233.4 46.1 %collective-permute-start.5 = (bf16[256,768]{1,0:T(8,128)(2,1)}, bf16[256,768]{1,0:T(8,128)(2,1)S(1)}, u32[]{:S(2)}, u32[]{:S(2)}) collective-permute-start(bf16[256,768]{1,0:T(8,128)(2,1)} %get-tuple-element.154), channel_id=1, source_target_pairs={{0,3},{1,2},{2,1},{3,0},{4,7},{5,6},{6,5},{7,4},{8,11},{9,10},{10,... | collective-permute-start | bytes 1179656 | tf_op jit(solution)/shard_map/ppermute | solution.py:40
  316.3 11.2 %collective-permute-start.6 = (f32[4,8,256]{2,0,1:T(4,128)S(1)}, f32[4,8,256]{2,0,1:T(4,128)S(1)}, u32[]{:S(2)}, u32[]{:S(2)}) collective-permute-start(f32[4,8,256]{2,0,1:T(4,128)S(1)} %copy.60), channel_id=1, source_target_pairs={{0,1},{1,0},{2,3},{3,2},{4,5},{5,4},{6,7},{7,6},{8,9},{9,8},{10,11... | collective-permute-start | bytes 98312 | tf_op jit(solution)/shard_map/ppermute | solution.py:40
  316.3 11.8 %collective-permute-start.7 = (f32[4,8,256]{2,0,1:T(4,128)S(1)}, f32[4,8,256]{2,0,1:T(4,128)S(1)}, u32[]{:S(2)}, u32[]{:S(2)}) collective-permute-start(f32[4,8,256]{2,0,1:T(4,128)S(1)} %copy.60), channel_id=1, source_target_pairs={{0,2},{1,3},{2,0},{3,1},{4,6},{5,7},{6,4},{7,5},{8,10},{9,11},{10,... | collective-permute-start | bytes 98312 | tf_op jit(solution)/shard_map/ppermute | solution.py:40
  319.1 9.6 %collective-permute-start.8 = (f32[4,8,256]{2,1,0:T(8,128)S(1)}, f32[4,8,256]{2,1,0:T(8,128)S(1)}, u32[]{:S(2)}, u32[]{:S(2)}) collective-permute-start(f32[4,8,256]{2,1,0:T(8,128)S(1)} %pad_maximum_fusion.4), channel_id=1, source_target_pairs={{0,3},{1,2},{2,1},{3,0},{4,7},{5,6},{6,5},{7,4},{8,11},{9,10},{10,... | collective-permute-start | bytes 98312 | tf_op jit(solution)/shard_map/ppermute | solution.py:40
  398.6 69.0 %collective-permute-start.12 = (bf16[384,8192]{1,0:T(8,128)(2,1)}, bf16[384,8192]{1,0:T(8,128)(2,1)}, u32[]{:S(2)}, u32[]{:S(2)}) collective-permute-start(bf16[384,8192]{1,0:T(8,128)(2,1)} %get-tuple-element.169), channel_id=1, source_target_pairs={{0,4},{4,0},{8,12},{12,8},{16,20},{20,16},{24,28},{28,24},{1,5},{5... | collective-permute-start | bytes 18874376 | tf_op jit(solution)/shard_map/ppermute | solution.py:40
  398.8 28.9 %collective-permute-start.10 = (bf16[256,768]{1,0:T(8,128)(2,1)S(1)}, bf16[256,768]{1,0:T(8,128)(2,1)S(1)}, u32[]{:S(2)}, u32[]{:S(2)}) collective-permute-start(bf16[256,768]{1,0:T(8,128)(2,1)S(1)} %get-tuple-element.309), channel_id=1, source_target_pairs={{0,2},{1,3},{2,0},{3,1},{4,6},{5,7},{6,4},{7,5},{8,10},{9,11},{10,... | collective-permute-start | bytes 1179656 | tf_op jit(solution)/shard_map/ppermute | solution.py:40
  398.9 28.9 %collective-permute-start.11 = (bf16[256,768]{1,0:T(8,128)(2,1)S(1)}, bf16[256,768]{1,0:T(8,128)(2,1)S(1)}, u32[]{:S(2)}, u32[]{:S(2)}) collective-permute-start(bf16[256,768]{1,0:T(8,128)(2,1)S(1)} %get-tuple-element.308), channel_id=1, source_target_pairs={{0,3},{1,2},{2,1},{3,0},{4,7},{5,6},{6,5},{7,4},{8,11},{9,10},{10,... | collective-permute-start | bytes 1179656 | tf_op jit(solution)/shard_map/ppermute | solution.py:40
  401.1 28.0 %collective-permute-start.9 = (bf16[256,768]{1,0:T(8,128)(2,1)S(1)}, bf16[256,768]{1,0:T(8,128)(2,1)S(1)}, u32[]{:S(2)}, u32[]{:S(2)}) collective-permute-start(bf16[256,768]{1,0:T(8,128)(2,1)S(1)} %slice.189), channel_id=1, source_target_pairs={{0,1},{1,0},{2,3},{3,2},{4,5},{5,4},{6,7},{7,6},{8,9},{9,8},{10,11... | collective-permute-start | bytes 1179656 | tf_op jit(solution)/shard_map/ppermute | solution.py:40
  449.2 32.0 %collective-permute-start.13 = (bf16[256,768]{1,0:T(8,128)(2,1)}, bf16[256,768]{1,0:T(8,128)(2,1)}, u32[]{:S(2)}, u32[]{:S(2)}) collective-permute-start(bf16[256,768]{1,0:T(8,128)(2,1)} %get-tuple-element.178.g_own), channel_id=1, source_target_pairs={{0,1},{1,0},{2,3},{3,2},{4,5},{5,4},{6,7},{7,6},{8,9},{9,8},{10,11... | collective-permute-start | bytes 1179656 | tf_op jit(solution)/shard_map/ppermute | solution.py:40
  458.1 23.1 %collective-permute-start.14 = (f32[16,256]{1,0:T(8,128)}, f32[16,256]{1,0:T(8,128)}, u32[]{:S(2)}, u32[]{:S(2)}) collective-permute-start(f32[16,256]{1,0:T(8,128)} %get-tuple-element.179.dot_own), channel_id=1, source_target_pairs={{0,1},{1,0},{2,3},{3,2},{4,5},{5,4},{6,7},{7,6},{8,9},{9,8},{10,11... | collective-permute-start | bytes 49160 | tf_op jit(solution)/shard_map/ppermute | solution.py:40
  479.1 47.0 %collective-permute-start.15 = (bf16[192,4096]{1,0:T(8,128)(2,1)}, bf16[192,4096]{1,0:T(8,128)(2,1)S(1)}, u32[]{:S(2)}, u32[]{:S(2)}) collective-permute-start(bf16[192,4096]{1,0:T(8,128)(2,1)} %get-tuple-element.176), channel_id=1, source_target_pairs={{0,8},{4,12},{8,0},{12,4},{16,24},{20,28},{24,16},{28,20},{1,9},{5... | collective-permute-start | bytes 4718600 | tf_op jit(solution)/shard_map/ppermute | solution.py:40
  480.6 45.6 %collective-permute-start.16 = (bf16[192,4096]{1,0:T(8,128)(2,1)}, bf16[192,4096]{1,0:T(8,128)(2,1)S(1)}, u32[]{:S(2)}, u32[]{:S(2)}) collective-permute-start(bf16[192,4096]{1,0:T(8,128)(2,1)} %get-tuple-element.177), channel_id=1, source_target_pairs={{0,16},{4,20},{8,24},{12,28},{16,0},{20,4},{24,8},{28,12},{1,17},{... | collective-permute-start | bytes 4718600 | tf_op jit(solution)/shard_map/ppermute | solution.py:40
  511.1 24.8 %collective-permute-start.17 = (bf16[768,256]{1,0:T(8,128)(2,1)}, bf16[768,256]{1,0:T(8,128)(2,1)}, u32[]{:S(2)}, u32[]{:S(2)}) collective-permute-start(bf16[768,256]{1,0:T(8,128)(2,1)} %get-tuple-element.186), channel_id=1, source_target_pairs={{0,1},{1,0},{2,3},{3,2},{4,5},{5,4},{6,7},{7,6},{8,9},{9,8},{10,11... | collective-permute-start | bytes 1179656 | tf_op jit(solution)/shard_map/ppermute | solution.py:40
  552.4 36.9 %collective-permute-start.21 = (bf16[384,3072]{1,0:T(8,128)(2,1)}, bf16[384,3072]{1,0:T(8,128)(2,1)}, u32[]{:S(2)}, u32[]{:S(2)}) collective-permute-start(bf16[384,3072]{1,0:T(8,128)(2,1)} %get-tuple-element.205), channel_id=1, source_target_pairs={{0,4},{4,0},{8,12},{12,8},{16,20},{20,16},{24,28},{28,24},{1,5},{5... | collective-permute-start | bytes 7077896 | tf_op jit(solution)/shard_map/ppermute | solution.py:40
  552.4 28.4 %collective-permute-start.19 = (bf16[192,3072]{1,0:T(8,128)(2,1)S(1)}, bf16[192,3072]{1,0:T(8,128)(2,1)S(1)}, u32[]{:S(2)}, u32[]{:S(2)}) collective-permute-start(bf16[192,3072]{1,0:T(8,128)(2,1)S(1)} %copy-done.120), channel_id=1, source_target_pairs={{0,8},{4,12},{8,0},{12,4},{16,24},{20,28},{24,16},{28,20},{1,9},{5... | collective-permute-start | bytes 3538952 | tf_op jit(solution)/shard_map/ppermute | solution.py:40
  553.9 28.1 %collective-permute-start.20 = (bf16[192,3072]{1,0:T(8,128)(2,1)S(1)}, bf16[192,3072]{1,0:T(8,128)(2,1)S(1)}, u32[]{:S(2)}, u32[]{:S(2)}) collective-permute-start(bf16[192,3072]{1,0:T(8,128)(2,1)S(1)} %copy-done.119), channel_id=1, source_target_pairs={{0,16},{4,20},{8,24},{12,28},{16,0},{20,4},{24,8},{28,12},{1,17},{... | collective-permute-start | bytes 3538952 | tf_op jit(solution)/shard_map/ppermute | solution.py:40
  554.4 40.7 %collective-permute-start.22 = (bf16[256,768]{1,0:T(8,128)(2,1)}, bf16[256,768]{1,0:T(8,128)(2,1)S(1)}, u32[]{:S(2)}, u32[]{:S(2)}) collective-permute-start(bf16[256,768]{1,0:T(8,128)(2,1)} %get-tuple-element.208.g_own), channel_id=1, source_target_pairs={{0,1},{1,0},{2,3},{3,2},{4,5},{5,4},{6,7},{7,6},{8,9},{9,8},{10,11... | collective-permute-start | bytes 1179656 | tf_op jit(solution)/shard_map/ppermute | solution.py:40
  624.9 22.5 %collective-permute-start.28 = (bf16[384,3072]{1,0:T(8,128)(2,1)S(1)}, bf16[384,3072]{1,0:T(8,128)(2,1)}, u32[]{:S(2)}, u32[]{:S(2)}) collective-permute-start(bf16[384,3072]{1,0:T(8,128)(2,1)S(1)} %get-tuple-element.218), channel_id=1, source_target_pairs={{0,4},{4,0},{8,12},{12,8},{16,20},{20,16},{24,28},{28,24},{1,5},{5... | collective-permute-start | bytes 7077896 | tf_op jit(solution)/shard_map/ppermute | solution.py:40
  624.9 15.7 %collective-permute-start.43 = (bf16[96,3072]{1,0:T(8,128)(2,1)S(1)}, bf16[96,3072]{1,0:T(8,128)(2,1)S(1)}, u32[]{:S(2)}, u32[]{:S(2)}) collective-permute-start(bf16[96,3072]{1,0:T(8,128)(2,1)S(1)} %copy-done.122), channel_id=1, source_target_pairs={{0,16},{4,20},{8,24},{12,28},{16,0},{20,4},{24,8},{28,12},{1,17},{... | collective-permute-start | bytes 1769480 | tf_op jit(solution)/shard_map/ppermute | solution.py:40
  625.5 15.5 %collective-permute-start.44 = (bf16[96,3072]{1,0:T(8,128)(2,1)S(1)}, bf16[96,3072]{1,0:T(8,128)(2,1)S(1)}, u32[]{:S(2)}, u32[]{:S(2)}) collective-permute-start(bf16[96,3072]{1,0:T(8,128)(2,1)S(1)} %copy-done.121), channel_id=1, source_target_pairs={{0,8},{4,12},{8,0},{12,4},{16,24},{20,28},{24,16},{28,20},{1,9},{5... | collective-permute-start | bytes 1769480 | tf_op jit(solution)/shard_map/ppermute | solution.py:40
  645.2 11.4 %collective-permute-start.45 = (bf16[96,1536]{1,0:T(8,128)(2,1)}, bf16[96,1536]{1,0:T(8,128)(2,1)S(1)}, u32[]{:S(2)}, u32[]{:S(2)}) collective-permute-start(bf16[96,1536]{1,0:T(8,128)(2,1)} %get-tuple-element.252), channel_id=1, source_target_pairs={{0,1},{1,0},{2,3},{3,2},{4,5},{5,4},{6,7},{7,6},{8,9},{9,8},{10,11... | collective-permute-start | bytes 884744 | tf_op jit(solution)/shard_map/ppermute | solution.py:40
  645.2 29.2 %collective-permute-start.36 = (bf16[192,1536]{1,0:T(8,128)(2,1)}, bf16[192,1536]{1,0:T(8,128)(2,1)}, u32[]{:S(2)}, u32[]{:S(2)}) collective-permute-start(bf16[192,1536]{1,0:T(8,128)(2,1)} %get-tuple-element.206), channel_id=1, source_target_pairs={{0,8},{4,12},{8,0},{12,4},{16,24},{20,28},{24,16},{28,20},{1,9},{5... | collective-permute-start | bytes 1769480 | tf_op jit(solution)/shard_map/ppermute | solution.py:40
  646.7 28.5 %collective-permute-start.37 = (bf16[192,1536]{1,0:T(8,128)(2,1)}, bf16[192,1536]{1,0:T(8,128)(2,1)}, u32[]{:S(2)}, u32[]{:S(2)}) collective-permute-start(bf16[192,1536]{1,0:T(8,128)(2,1)} %get-tuple-element.207), channel_id=1, source_target_pairs={{0,16},{4,20},{8,24},{12,28},{16,0},{20,4},{24,8},{28,12},{1,17},{... | collective-permute-start | bytes 1769480 | tf_op jit(solution)/shard_map/ppermute | solution.py:40
  647.5 16.6 %collective-permute-start.46 = (bf16[96,1536]{1,0:T(8,128)(2,1)}, bf16[96,1536]{1,0:T(8,128)(2,1)S(1)}, u32[]{:S(2)}, u32[]{:S(2)}) collective-permute-start(bf16[96,1536]{1,0:T(8,128)(2,1)} %get-tuple-element.253), channel_id=1, source_target_pairs={{0,2},{1,3},{2,0},{3,1},{4,6},{5,7},{6,4},{7,5},{8,10},{9,11},{10,... | collective-permute-start | bytes 884744 | tf_op jit(solution)/shard_map/ppermute | solution.py:40
  655.1 27.4 %collective-permute-start.29 = (bf16[192,1536]{1,0:T(8,128)(2,1)}, bf16[192,1536]{1,0:T(8,128)(2,1)S(1)}, u32[]{:S(2)}, u32[]{:S(2)}) collective-permute-start(bf16[192,1536]{1,0:T(8,128)(2,1)} %get-tuple-element.220), channel_id=1, source_target_pairs={{0,8},{4,12},{8,0},{12,4},{16,24},{20,28},{24,16},{28,20},{1,9},{5... | collective-permute-start | bytes 1769480 | tf_op jit(solution)/shard_map/ppermute | solution.py:40
  660.4 23.0 %collective-permute-start.30 = (bf16[192,1536]{1,0:T(8,128)(2,1)}, bf16[192,1536]{1,0:T(8,128)(2,1)S(1)}, u32[]{:S(2)}, u32[]{:S(2)}) collective-permute-start(bf16[192,1536]{1,0:T(8,128)(2,1)} %get-tuple-element.222), channel_id=1, source_target_pairs={{0,16},{4,20},{8,24},{12,28},{16,0},{20,4},{24,8},{28,12},{1,17},{... | collective-permute-start | bytes 1769480 | tf_op jit(solution)/shard_map/ppermute | solution.py:40
  673.2 31.4 %collective-permute-start.48 = (bf16[96,4096]{1,0:T(8,128)(2,1)}, bf16[96,4096]{1,0:T(8,128)(2,1)S(1)}, u32[]{:S(2)}, u32[]{:S(2)}) collective-permute-start(bf16[96,4096]{1,0:T(8,128)(2,1)} %get-tuple-element.183), channel_id=1, source_target_pairs={{0,16},{4,20},{8,24},{12,28},{16,0},{20,4},{24,8},{28,12},{1,17},{... | collective-permute-start | bytes 2359304 | tf_op jit(solution)/shard_map/ppermute | solution.py:40
  674.4 44.4 %collective-permute-start.49 = (bf16[96,4096]{1,0:T(8,128)(2,1)}, bf16[96,4096]{1,0:T(8,128)(2,1)S(1)}, u32[]{:S(2)}, u32[]{:S(2)}) collective-permute-start(bf16[96,4096]{1,0:T(8,128)(2,1)} %get-tuple-element.184), channel_id=1, source_target_pairs={{0,8},{4,12},{8,0},{12,4},{16,24},{20,28},{24,16},{28,20},{1,9},{5... | collective-permute-start | bytes 2359304 | tf_op jit(solution)/shard_map/ppermute | solution.py:40
  681.2 17.4 %collective-permute-start.38 = (bf16[96,1536]{1,0:T(8,128)(2,1)}, bf16[96,1536]{1,0:T(8,128)(2,1)}, u32[]{:S(2)}, u32[]{:S(2)}) collective-permute-start(bf16[96,1536]{1,0:T(8,128)(2,1)} %get-tuple-element.238), channel_id=1, source_target_pairs={{0,16},{4,20},{8,24},{12,28},{16,0},{20,4},{24,8},{28,12},{1,17},{... | collective-permute-start | bytes 884744 | tf_op jit(solution)/shard_map/ppermute | solution.py:40
  682.5 16.8 %collective-permute-start.39 = (bf16[96,1536]{1,0:T(8,128)(2,1)}, bf16[96,1536]{1,0:T(8,128)(2,1)}, u32[]{:S(2)}, u32[]{:S(2)}) collective-permute-start(bf16[96,1536]{1,0:T(8,128)(2,1)} %get-tuple-element.240), channel_id=1, source_target_pairs={{0,8},{4,12},{8,0},{12,4},{16,24},{20,28},{24,16},{28,20},{1,9},{5... | collective-permute-start | bytes 884744 | tf_op jit(solution)/shard_map/ppermute | solution.py:40
  683.4 20.6 %collective-permute-start.47 = (bf16[96,1536]{1,0:T(8,128)(2,1)}, bf16[96,1536]{1,0:T(8,128)(2,1)}, u32[]{:S(2)}, u32[]{:S(2)}) collective-permute-start(bf16[96,1536]{1,0:T(8,128)(2,1)} %get-tuple-element.254), channel_id=1, source_target_pairs={{0,3},{1,2},{2,1},{3,0},{4,7},{5,6},{6,5},{7,4},{8,11},{9,10},{10,... | collective-permute-start | bytes 884744 | tf_op jit(solution)/shard_map/ppermute | solution.py:40
  698.6 27.7 %collective-permute-start.31 = (bf16[96,1536]{1,0:T(8,128)(2,1)}, bf16[96,1536]{1,0:T(8,128)(2,1)S(1)}, u32[]{:S(2)}, u32[]{:S(2)}) collective-permute-start(bf16[96,1536]{1,0:T(8,128)(2,1)} %get-tuple-element.224), channel_id=1, source_target_pairs={{0,16},{4,20},{8,24},{12,28},{16,0},{20,4},{24,8},{28,12},{1,17},{... | collective-permute-start | bytes 884744 | tf_op jit(solution)/shard_map/ppermute | solution.py:40
  699.3 29.2 %collective-permute-start.32 = (bf16[96,1536]{1,0:T(8,128)(2,1)}, bf16[96,1536]{1,0:T(8,128)(2,1)}, u32[]{:S(2)}, u32[]{:S(2)}) collective-permute-start(bf16[96,1536]{1,0:T(8,128)(2,1)} %get-tuple-element.226), channel_id=1, source_target_pairs={{0,8},{4,12},{8,0},{12,4},{16,24},{20,28},{24,16},{28,20},{1,9},{5... | collective-permute-start | bytes 884744 | tf_op jit(solution)/shard_map/ppermute | solution.py:40
  704.0 28.1 %collective-permute-start.27 = (f32[4,768]{1,0:T(4,128)S(1)}, f32[4,768]{1,0:T(4,128)S(1)}, u32[]{:S(2)}, u32[]{:S(2)}) collective-permute-start(f32[4,768]{1,0:T(4,128)S(1)} %add.171), channel_id=1, source_target_pairs={{0,16},{4,20},{8,24},{12,28},{16,0},{20,4},{24,8},{28,12},{1,17},{... | collective-permute-start | bytes 36872 | tf_op jit(solution)/shard_map/ppermute | solution.py:40
  704.6 28.6 %collective-permute-start.40 = (bf16[96,768]{1,0:T(8,128)(2,1)}, bf16[96,768]{1,0:T(8,128)(2,1)S(1)}, u32[]{:S(2)}, u32[]{:S(2)}) collective-permute-start(bf16[96,768]{1,0:T(8,128)(2,1)} %get-tuple-element.242), channel_id=1, source_target_pairs={{0,1},{1,0},{2,3},{3,2},{4,5},{5,4},{6,7},{7,6},{8,9},{9,8},{10,11... | collective-permute-start | bytes 442376 | tf_op jit(solution)/shard_map/ppermute | solution.py:40
  726.1 19.1 %collective-permute-start.41 = (bf16[96,768]{1,0:T(8,128)(2,1)}, bf16[96,768]{1,0:T(8,128)(2,1)S(1)}, u32[]{:S(2)}, u32[]{:S(2)}) collective-permute-start(bf16[96,768]{1,0:T(8,128)(2,1)} %get-tuple-element.243), channel_id=1, source_target_pairs={{0,2},{1,3},{2,0},{3,1},{4,6},{5,7},{6,4},{7,5},{8,10},{9,11},{10,... | collective-permute-start | bytes 442376 | tf_op jit(solution)/shard_map/ppermute | solution.py:40
  726.3 18.9 %collective-permute-start.42 = (bf16[96,768]{1,0:T(8,128)(2,1)}, bf16[96,768]{1,0:T(8,128)(2,1)S(1)}, u32[]{:S(2)}, u32[]{:S(2)}) collective-permute-start(bf16[96,768]{1,0:T(8,128)(2,1)} %get-tuple-element.244), channel_id=1, source_target_pairs={{0,3},{1,2},{2,1},{3,0},{4,7},{5,6},{6,5},{7,4},{8,11},{9,10},{10,... | collective-permute-start | bytes 442376 | tf_op jit(solution)/shard_map/ppermute | solution.py:40
  731.0 16.9 %collective-permute-start.33 = (bf16[96,768]{1,0:T(8,128)(2,1)}, bf16[96,768]{1,0:T(8,128)(2,1)S(1)}, u32[]{:S(2)}, u32[]{:S(2)}) collective-permute-start(bf16[96,768]{1,0:T(8,128)(2,1)} %get-tuple-element.228), channel_id=1, source_target_pairs={{0,1},{1,0},{2,3},{3,2},{4,5},{5,4},{6,7},{7,6},{8,9},{9,8},{10,11... | collective-permute-start | bytes 442376 | tf_op jit(solution)/shard_map/ppermute | solution.py:40
  732.1 17.2 %collective-permute-start.34 = (bf16[96,768]{1,0:T(8,128)(2,1)}, bf16[96,768]{1,0:T(8,128)(2,1)S(1)}, u32[]{:S(2)}, u32[]{:S(2)}) collective-permute-start(bf16[96,768]{1,0:T(8,128)(2,1)} %get-tuple-element.229), channel_id=1, source_target_pairs={{0,2},{1,3},{2,0},{3,1},{4,6},{5,7},{6,4},{7,5},{8,10},{9,11},{10,... | collective-permute-start | bytes 442376 | tf_op jit(solution)/shard_map/ppermute | solution.py:40
  733.2 16.1 %collective-permute-start.35 = (bf16[96,768]{1,0:T(8,128)(2,1)}, bf16[96,768]{1,0:T(8,128)(2,1)S(1)}, u32[]{:S(2)}, u32[]{:S(2)}) collective-permute-start(bf16[96,768]{1,0:T(8,128)(2,1)} %get-tuple-element.230), channel_id=1, source_target_pairs={{0,3},{1,2},{2,1},{3,0},{4,7},{5,6},{6,5},{7,4},{8,11},{9,10},{10,... | collective-permute-start | bytes 442376 | tf_op jit(solution)/shard_map/ppermute | solution.py:40
  (128 other events, 1491.9 us)
Sparse Core Ops, SparseCore 0:
  11.5 73.7 all-gather.3
  88.7 58.4 all-gather.5
  150.7 58.7 all-gather.7

commit v3 on v2

--- a/solution.py
+++ b/solution.py
@@ -40,105 +40,79 @@
     return lax.ppermute(value, axis_name, [(i, i ^ bit) for i in range(size)])
 
 
-def gather_kernel(groups, *refs):
-    ins, outs = refs[:groups], refs[groups : 2 * groups]
-    send_sem, recv_sem, local_sem = refs[2 * groups :]
-    dp = lax.axis_index("dp")
-    z = lax.axis_index("tensor")
-    core_peer = dp + 1 - 2 * lax.rem(dp, 2)
-    x_peer = dp + 2 - 4 * lax.rem(dp // 2, 2)
-    y_peer = dp + 4 - 8 * (dp // 4)
-    xy_peer = x_peer + y_peer - dp
-    low, high = lax.rem(z, 2), z // 2
-    z_peers = [high * 2 + 1 - low, (1 - high) * 2 + low, (1 - high) * 2 + 1 - low]
-    barrier = pltpu.get_barrier_semaphore()
-    for other in (core_peer, x_peer, y_peer):
-        pl.semaphore_signal(
-            barrier, inc=1, device_id={"dp": other, "tensor": z}, device_id_type=MESH_ID
-        )
-    for other in z_peers:
-        pl.semaphore_signal(
-            barrier, inc=1, device_id={"dp": dp, "tensor": other}, device_id_type=MESH_ID
-        )
-    pl.semaphore_wait(barrier, 6)
-
-    rows, hid = 96, 192
-
-    def piece(g, shard, owner, start=0, count=rows):
-        offset = pl.multiple_of(shard * hid + lax.rem(owner, 2) * rows + start, 16)
-        return outs[g].at[owner // 2, pl.ds(offset, count)]
-
-    used = [0]
-
-    def remote(src, dst, target_dp, target_z):
-        sem = used[0]
-        used[0] += 1
+class Gather:
+    def __init__(self, links, refs, used):
+        self.links, self.refs, self.used = links, refs, used
+        self.last = []
+
+    def piece(self, ref, shard, owner, part=None):
+        if len(ref.shape) == 2:
+            rows = ref.shape[0] // 32
+            base = shard * 8 * rows + owner * rows
+        else:
+            rows = ref.shape[1] // 8
+            base = shard * 2 * rows + lax.rem(owner, 2) * rows
+        start, count = (0, rows) if part is None else (part * rows // 2, rows // 2)
+        where = pl.ds(pl.multiple_of(base + start, 16), count)
+        return ref.at[where] if len(ref.shape) == 2 else ref.at[owner // 2, where]
+
+    def send(self, part, peer):
+        send_sem, recv_sem = self.links["sems"]
+        sem = self.used[0]
+        self.used[0] += 1
         copy = pltpu.make_async_remote_copy(
-            src_ref=src,
-            dst_ref=dst,
+            src_ref=part,
+            dst_ref=part,
             send_sem=send_sem.at[sem],
             recv_sem=recv_sem.at[sem],
-            device_id={"dp": target_dp, "tensor": target_z},
+            device_id={"dp": peer[0], "tensor": peer[1]},
             device_id_type=MESH_ID,
         )
         copy.start()
         return copy
 
-    def along_z(g):
-        offset = pl.multiple_of(dp * rows, 16)
-        return [
-            remote(ins[g].at[pl.ds(offset, rows)], piece(g, z, dp), dp, z_peers[j])
-            for j in range(3)
+    def along_z(self):
+        links = self.links
+        self.z_copies = [
+            self.send(self.piece(ref, links["z"], links["dp"]), peer)
+            for ref in self.refs
+            for peer in links["z_peers"]
         ]
 
-    z_copies, x_copies, y_copies, d_copies, c_copies, own = {}, {}, {}, {}, {}, []
-    z_copies[0] = along_z(0)
-    for g in range(groups):
-        for m in range(4):
-            copy = pltpu.make_async_copy(
-                ins[g].at[pl.ds(m * hid, hid)],
-                outs[g].at[m, pl.ds(pl.multiple_of(z * hid, 16), hid)],
-                local_sem.at[4 * g + m],
-            )
-            copy.start()
-            own.append(copy)
-    for step in range(groups + 2):
-        g = step
-        if g < groups:
-            for copy in z_copies[g]:
-                copy.wait()
-            if g + 1 < groups:
-                z_copies[g + 1] = along_z(g + 1)
-            x_copies[g], y_copies[g], c_copies[g] = [], [], []
-            for peer in z_peers:
-                part = piece(g, peer, dp)
-                x_copies[g].append(remote(part, part, x_peer, z))
-                y_copies[g].append(remote(part, part, y_peer, z))
-                c_copies[g].append(remote(part, part, core_peer, z))
-        g = step - 1
-        if 0 <= g < groups:
-            d_copies[g] = []
-            for j, peer in enumerate(z_peers):
-                x_copies[g][j].wait()
-                part = piece(g, peer, x_peer, 0, rows // 2)
-                d_copies[g].append(remote(part, part, y_peer, z))
-                y_copies[g][j].wait()
-                part = piece(g, peer, y_peer, rows // 2, rows // 2)
-                d_copies[g].append(remote(part, part, x_peer, z))
-                for owner in (x_peer, y_peer):
-                    part = piece(g, peer, owner)
-                    c_copies[g].append(remote(part, part, core_peer, z))
-        g = step - 2
-        if 0 <= g < groups:
-            for j, peer in enumerate(z_peers):
-                d_copies[g][2 * j].wait()
-                d_copies[g][2 * j + 1].wait()
-                part = piece(g, peer, xy_peer)
-                c_copies[g].append(remote(part, part, core_peer, z))
-    for copy in own:
-        copy.wait()
-    for g in range(groups):
-        for copy in c_copies[g]:
+    def along_xy(self):
+        links = self.links
+        for copy in self.z_copies:
+            copy.wait()
+        self.x_copies, self.y_copies = [], []
+        for ref in self.refs:
+            for _, shard in links["z_peers"]:
+                part = self.piece(ref, shard, links["dp"])
+                self.x_copies.append(self.send(part, links["x"]))
+                self.y_copies.append(self.send(part, links["y"]))
+                self.last.append(self.send(part, links["core"]))
+
+    def diagonal(self):
+        links = self.links
+        self.d_copies = []
+        at = 0
+        for ref in self.refs:
+            for _, shard in links["z_peers"]:
+                self.x_copies[at].wait()
+                self.d_copies.append(self.send(self.piece(ref, shard, links["x"][0], 0), links["y"]))
+                self.y_copies[at].wait()
+                self.d_copies.append(self.send(self.piece(ref, shard, links["y"][0], 1), links["x"]))
+                for owner in (links["x"][0], links["y"][0]):
+                    self.last.append(self.send(self.piece(ref, shard, owner), links["core"]))
+                at += 1
+
+    def finish(self):
+        links = self.links
+        for copy in self.d_copies:
+            copy.wait()
+        for ref in self.refs:
+            for _, shard in links["z_peers"]:
+                self.last.append(self.send(self.piece(ref, shard, links["xy"]), links["core"]))
+        for copy in self.last:
             copy.wait()
 
 
@@ -146,27 +120,6 @@
     rows = shard.shape[0] // dp_size
     part = lax.dynamic_slice_in_dim(shard, lax.axis_index("dp") * rows, rows, 0)
     return lax.all_gather(part, ("tensor", "dp"), axis=0, tiled=True)
-
-
-def gather_blocks(shards, dp_size):
-    if dp_size != 8:
-        return [
-            gather_wide(shard, dp_size).reshape(4, 4, D // 4, D).swapaxes(0, 1).reshape(4, D, D)
-            for shard in shards
-        ]
-    groups = len(shards)
-    return pl.pallas_call(
-        functools.partial(gather_kernel, groups),
-        out_shape=[jax.ShapeDtypeStruct((4, D, D), BF16) for _ in shards],
-        in_specs=[pl.BlockSpec(memory_space=pl.ANY)] * groups,
-        out_specs=[pl.BlockSpec(memory_space=pl.ANY)] * groups,
-        scratch_shapes=[
-            pltpu.SemaphoreType.DMA((27 * groups,)),
-            pltpu.SemaphoreType.DMA((27 * groups,)),
-            pltpu.SemaphoreType.DMA((4 * groups,)),
-        ],
-        compiler_params=pltpu.CompilerParams(collective_id=0, has_side_effects=True),
-    )(*shards)
 
 
 def tile_of(width):
@@ -318,7 +271,7 @@
 
 class WideReduction:
     def __init__(self, xyz, mine, send):
-        self.z = xyz[2]
+        self.gots = ()
         both = jnp.concatenate([mine, send.astype(F32)], 0)
         self.part = lax.psum_scatter(both, "dp", scatter_dimension=0, tiled=True)
 
@@ -413,123 +366,235 @@
     )(*args)
 
 
-def self_forward(
-    scal, x_own, x_other, gain_self, gain_cross, w_self, w_cq,
-    q_out, k_out, v_out, lse_out, att_out, h1_out, q2_out,
-    x_ref, n_ref, vt_ref, ot_ref,
-):
-    half = scal[0]
-    live = scal[1]
+def forward_kernel(split, *refs):
+    (scal, x_own, source, gain_self, gain_cross, gain_ff, gain_final), refs = refs[:7], refs[7:]
+    shards, refs = refs[: 11 if split else 5], refs[11 if split else 5 :]
+    (q1, k1, v1, lse1, att1, h1_out, q2, k2, v2), refs = refs[:9], refs[9:]
+    (out_ref, fin_ref, h2_ref, att_t_ref, att2, lse2), refs = refs[:6], refs[6:]
+    if split:
+        copies_out, refs = refs[:11], refs[11:]
+        (ws, wc, wg, wu, wd), refs = refs[:5], refs[5:]
+    else:
+        ws, wc, wg, wu, wd = shards
+    (x_other, x_ref, n_ref, vt_ref, ot_ref, s_ref, o_send, o_other, lse_own, lse_other, mix_ref), refs = (
+        refs[:11],
+        refs[11:],
+    )
+    pair_send, pair_recv = refs[:2]
+    dp = lax.axis_index("dp")
+    z = lax.axis_index("tensor")
+    low, high = lax.rem(z, 2), z // 2
+    half, live, live_src = low, scal[1], scal[2] - low * KEYS
+    z_peers = [(dp, high * 2 + 1 - low)]
+    peers = z_peers
+    if split:
+        z_peers = z_peers + [(dp, (1 - high) * 2 + low), (dp, (1 - high) * 2 + 1 - low)]
+        x_peer = dp + 2 - 4 * lax.rem(dp // 2, 2)
+        y_peer = dp + 4 - 8 * (dp // 4)
+        links = dict(
+            dp=dp,
+            z=z,
+            z_peers=z_peers,
+            x=(x_peer, z),
+            y=(y_peer, z),
+            xy=x_peer + y_peer - dp,
+            core=(dp + 1 - 2 * lax.rem(dp, 2), z),
+            sems=refs[2:4],
+        )
+        out_sem = refs[4]
+        peers = z_peers + [links["x"], links["y"], links["core"]]
+    barrier = pltpu.get_barrier_semaphore()
+    for peer in peers:
+        pl.semaphore_signal(
+            barrier, inc=1, device_id={"dp": peer[0], "tensor": peer[1]}, device_id_type=MESH_ID
+        )
+
+    def exchange(index, src, dst):
+        copy = pltpu.make_async_remote_copy(
+            src_ref=src,
+            dst_ref=dst,
+            send_sem=pair_send.at[index],
+            recv_sem=pair_recv.at[index],
+            device_id={"dp": z_peers[0][0], "tensor": z_peers[0][1]},
+            device_id_type=MESH_ID,
+        )
+        copy.start()
+        return copy
+
+    leaving = []
+    if split:
+        used = [0]
+        groups = [Gather(links, refs_of, used) for refs_of in ([ws], [wc], [wg], [wu], [wd])]
+        of_self, of_cross, of_gate, of_up, of_down = groups
+        hid, fhid = D // 4, FF // 4
+
+        def place_block(target, first):
+            rows = pl.ds(pl.multiple_of(z * hid, 16), hid)
+            for m in range(3):
+                target[m, rows, :] = flip(shards[first + m][...]).astype(BF16)
+            target[3, rows, :] = shards[first + 3][...]
+
+        def place_wide(target, shard, flipped):
+            rows = pl.ds(pl.multiple_of(z * fhid, 16), fhid)
+            target[rows, :] = flip(shard[...]).astype(BF16) if flipped else shard[...]
+
+        def leave(first, parts):
+            for i, part in enumerate(parts):
+                copy = pltpu.make_async_copy(part, copies_out[first + i], out_sem.at[first + i])
+                copy.start()
+                leaving.append(copy)
+
+        place_block(ws, 0)
+        pl.semaphore_wait(barrier, len(peers))
+        of_self.along_z()
+    else:
+        pl.semaphore_wait(barrier, len(peers))
+    x_copy = exchange(0, x_own, x_other)
+    if split:
+        place_block(wc, 4)
+        place_wide(wg, shards[8], True)
+        place_wide(wu, shards[9], True)
+        place_wide(wd, shards[10], False)
+        of_self.along_xy()
+        of_cross.along_z()
+        of_self.diagonal()
+        of_cross.along_xy()
+        of_gate.along_z()
+    x_copy.wait()
     own = pl.multiple_of(half * ROWS, ROWS)
+    other = pl.multiple_of((1 - half) * ROWS, ROWS)
     x_ref[pl.ds(own, ROWS), :] = x_own[...].astype(F32)
-    x_ref[pl.ds(pl.multiple_of((1 - half) * ROWS, ROWS), ROWS), :] = x_other[...].astype(F32)
+    x_ref[pl.ds(other, ROWS), :] = x_other[...].astype(F32)
+    lse1[...] = jnp.zeros_like(lse1)
+    lse_own[...] = jnp.zeros_like(lse_own)
+    if split:
+        of_self.finish()
+        leave(0, [ws.at[m] for m in range(4)])
     for i in range(2):
         rows = slice(i * ROWS, (i + 1) * ROWS)
         x = x_ref[rows, :]
         n = (x * rms_scale(x) * gain_self[...]).astype(BF16)
         n_ref[rows, :] = n
-        q_out[rows, :] = dot_nt(n, w_self[0]).astype(BF16)
-        k_out[rows, :] = dot_nt(n, w_self[1]).astype(BF16)
-        v_out[rows, :] = dot_nt(n, w_self[2]).astype(BF16)
-    vt_ref[...] = dot_nt(w_self[2], n_ref[...]).astype(BF16)
-    lse_out[...] = jnp.zeros_like(lse_out)
+        q1[rows, :] = dot_nt(n, ws[0]).astype(BF16)
+        k1[rows, :] = dot_nt(n, ws[1]).astype(BF16)
+        v1[rows, :] = dot_nt(n, ws[2]).astype(BF16)
+    vt_ref[:, :TGT] = dot_nt(ws[2], n_ref[...]).astype(BF16)
+    if split:
+        of_gate.along_xy()
+        of_up.along_z()
     key = lax.broadcasted_iota(jnp.int32, (TGT, TGT), 0)
     query = lax.broadcasted_iota(jnp.int32, (TGT, TGT), 1)
     seen = (key <= query) & (key < live)
 
-    @pl.loop(0, PAIRS)
-    def _(pair):
-        lanes = pl.ds(pl.multiple_of(pair * 128, 128), 128)
-        q_pair, k_pair = q_out[:, lanes], k_out[:, lanes]
-        for which in range(2):
-            head = 2 * pair + which
-            feats = pl.ds(pl.multiple_of(head * HDIM, HDIM), HDIM)
-            scores = jnp.where(seen, dot_nt(k_pair, only(q_pair, which)) * SCALE, NEG)
-            top = jnp.max(scores, axis=0, keepdims=True)
-            probs = jnp.exp(scores - top)
-            total = jnp.sum(probs, axis=0, keepdims=True)
-            lse_out[pl.ds(head, 1), :] = top + jnp.log(total)
-            out = dot_nn(vt_ref[feats, :], probs.astype(BF16)) / total
-            ot_ref[feats, :] = out
-
+    def self_pairs(first, last):
+        @pl.loop(first, last)
+        def _(pair):
+            lanes = pl.ds(pl.multiple_of(pair * 128, 128), 128)
+            q_pair, k_pair = q1[:, lanes], k1[:, lanes]
+            for which in range(2):
+                head = 2 * pair + which
+                feats = pl.ds(pl.multiple_of(head * HDIM, HDIM), HDIM)
+                scores = jnp.where(seen, dot_nt(k_pair, only(q_pair, which)) * SCALE, NEG)
+                top = jnp.max(scores, axis=0, keepdims=True)
+                probs = jnp.exp(scores - top)
+                total = jnp.sum(probs, axis=0, keepdims=True)
+                lse1[pl.ds(head, 1), :] = top + jnp.log(total)
+                ot_ref[feats, :] = dot_nn(vt_ref[feats, :TGT], probs.astype(BF16)) / total
+
+    self_pairs(0, PAIRS // 2)
+    if split:
+        of_cross.diagonal()
+    self_pairs(PAIRS // 2, PAIRS)
+    if split:
+        of_up.along_xy()
+        of_down.along_z()
+        of_gate.diagonal()
     for i in range(2):
         rows = slice(i * ROWS, (i + 1) * ROWS)
         att = flip(ot_ref[:, rows]).astype(BF16)
         n_ref[rows, :] = att
-        h1 = x_ref[rows, :] + dot_nn(att, w_self[3])
-        x_ref[rows, :] = h1
+        x_ref[rows, :] = x_ref[rows, :] + dot_nn(att, ws[3])
+    att1[...] = n_ref[pl.ds(own, ROWS), :]
+    h1_out[...] = x_ref[pl.ds(own, ROWS), :]
+    if split:
+        of_cross.finish()
+        leave(4, [wc.at[m] for m in range(4)])
+    for i in range(2):
+        rows = slice(i * ROWS, (i + 1) * ROWS)
+        h1 = x_ref[rows, :]
         n = (h1 * rms_scale(h1) * gain_cross[...]).astype(BF16)
-        q2_out[rows, :] = dot_nt(n, w_cq[...]).astype(BF16)
-    att_out[...] = n_ref[pl.ds(own, ROWS), :]
-    h1_out[...] = x_ref[pl.ds(own, ROWS), :]
-
-
-def cross_forward(
-    scal, q2, source, w_ck, w_cv, k_out, v_out, own_out, send_out, lse_out, vt_ref, s_ref, ot_ref
-):
-    half = scal[0]
-    live = scal[2] - half * KEYS
-    own = pl.multiple_of(half * ROWS, ROWS)
-    other = pl.multiple_of((1 - half) * ROWS, ROWS)
+        q2[rows, :] = dot_nt(n, wc[0]).astype(BF16)
     for i in range(KEYS // CHUNK):
         rows = slice(i * CHUNK, (i + 1) * CHUNK)
         src = source[rows, :]
-        k_out[rows, :] = dot_nt(src, w_ck[...]).astype(BF16)
-        v_out[rows, :] = dot_nt(src, w_cv[...]).astype(BF16)
-        vt_ref[:, rows] = dot_nt(w_cv[...], src).astype(BF16)
-    lse_out[...] = jnp.zeros_like(lse_out)
-    key = lax.broadcasted_iota(jnp.int32, (CHUNK, TGT), 0)
-
-    @pl.loop(0, PAIRS)
-    def _(pair):
-        lanes = pl.ds(pl.multiple_of(pair * 128, 128), 128)
-        q_pair = q2[:, lanes]
-        for which in range(2):
-            head = 2 * pair + which
-            feats = pl.ds(pl.multiple_of(head * HDIM, HDIM), HDIM)
-            q_one = only(q_pair, which)
-            top = jnp.full((1, TGT), 2 * NEG, F32)
-            for i in range(KEYS // CHUNK):
-                rows = slice(i * CHUNK, (i + 1) * CHUNK)
-                scores = dot_nt(k_out[rows, lanes], q_one) * SCALE
-                scores = jnp.where(key < live - i * CHUNK, scores, NEG)
-                s_ref[rows, :] = scores
-                top = jnp.maximum(top, jnp.max(scores, axis=0, keepdims=True))
-            total = jnp.zeros((1, TGT), F32)
-            out = jnp.zeros((HDIM, TGT), F32)
-            for i in range(KEYS // CHUNK):
-                rows = slice(i * CHUNK, (i + 1) * CHUNK)
-                probs = jnp.exp(s_ref[rows, :] - top)
-                total = total + jnp.sum(probs, axis=0, keepdims=True)
-                out = out + dot_nn(vt_ref[feats, rows], probs.astype(BF16))
-            lse_out[pl.ds(head, 1), :] = top + jnp.log(total)
-            ot_ref[feats, :] = out / total
-
-    own_out[...] = ot_ref[:, pl.ds(own, ROWS)]
-    send_out[...] = ot_ref[:, pl.ds(other, ROWS)].astype(BF16)
-
-
-def ff_forward(
-    scal, o_own, o_other, lse_own, lse_other, h1, w_co, gain_ff, gain_final, wg, wu, wd,
-    out_ref, fin_ref, h2_ref, att_t_ref, att_ref, lse_ref, mix_ref,
-):
-    half = scal[0]
-    own = pl.multiple_of(half * ROWS, ROWS)
+        k2[rows, :] = dot_nt(src, wc[1]).astype(BF16)
+        v2[rows, :] = dot_nt(src, wc[2]).astype(BF16)
+        vt_ref[:, rows] = dot_nt(wc[2], src).astype(BF16)
+    if split:
+        of_down.along_xy()
+        of_up.diagonal()
+        of_gate.finish()
+        leave(8, [wg])
+    chunk_key = lax.broadcasted_iota(jnp.int32, (CHUNK, TGT), 0)
+
+    def cross_pairs(first, last):
+        @pl.loop(first, last)
+        def _(pair):
+            lanes = pl.ds(pl.multiple_of(pair * 128, 128), 128)
+            q_pair = q2[:, lanes]
+            for which in range(2):
+                head = 2 * pair + which
+                feats = pl.ds(pl.multiple_of(head * HDIM, HDIM), HDIM)
+                q_one = only(q_pair, which)
+                top = jnp.full((1, TGT), 2 * NEG, F32)
+                for i in range(KEYS // CHUNK):
+                    rows = slice(i * CHUNK, (i + 1) * CHUNK)
+                    scores = dot_nt(k2[rows, lanes], q_one) * SCALE
+                    scores = jnp.where(chunk_key < live_src - i * CHUNK, scores, NEG)
+                    s_ref[rows, :] = scores
+                    top = jnp.maximum(top, jnp.max(scores, axis=0, keepdims=True))
+                total = jnp.zeros((1, TGT), F32)
+                out = jnp.zeros((HDIM, TGT), F32)
+                for i in range(KEYS // CHUNK):
+                    rows = slice(i * CHUNK, (i + 1) * CHUNK)
+                    probs = jnp.exp(s_ref[rows, :] - top)
+                    total = total + jnp.sum(probs, axis=0, keepdims=True)
+                    out = out + dot_nn(vt_ref[feats, rows], probs.astype(BF16))
+                lse_own[pl.ds(head, 1), :] = top + jnp.log(total)
+                ot_ref[feats, :] = out / total
+
+    cross_pairs(0, PAIRS // 2)
+    o_send[: D // 2, :] = ot_ref[: D // 2, pl.ds(other, ROWS)].astype(BF16)
+    pair_copies = [exchange(1, o_send.at[: D // 2], o_other.at[: D // 2])]
+    if split:
+        of_down.diagonal()
+        of_up.finish()
+        leave(9, [wu])
+    cross_pairs(PAIRS // 2, PAIRS)
+    o_send[D // 2 :, :] = ot_ref[D // 2 :, pl.ds(other, ROWS)].astype(BF16)
+    pair_copies.append(exchange(2, o_send.at[D // 2 :], o_other.at[D // 2 :]))
+    pair_copies.append(exchange(3, lse_own, lse_other))
+    if split:
+        of_down.finish()
+        leave(10, [wd])
+    for copy in pair_copies:
+        copy.wait()
+
     first, second = lse_own[...], lse_other[...]
     top = jnp.maximum(first, second)
-    lse_ref[...] = top + jnp.log(jnp.exp(first - top) + jnp.exp(second - top))
-    lse = lse_ref[:, pl.ds(own, ROWS)]
+    lse2[...] = top + jnp.log(jnp.exp(first - top) + jnp.exp(second - top))
+    lse = lse2[:, pl.ds(own, ROWS)]
     w_first = jnp.exp(lse_own[:, pl.ds(own, ROWS)] - lse)
     w_second = jnp.exp(lse_other[:, pl.ds(own, ROWS)] - lse)
     for head in range(NHEAD):
         feats = slice(head * HDIM, (head + 1) * HDIM)
         att_t_ref[feats, :] = (
-            o_own[feats, :] * w_first[head : head + 1, :]
+            ot_ref[feats, pl.ds(own, ROWS)] * w_first[head : head + 1, :]
             + o_other[feats, :].astype(F32) * w_second[head : head + 1, :]
         )
     att = flip(att_t_ref[...]).astype(BF16)
-    att_ref[...] = att
-    h2 = h1[...] + dot_nn(att, w_co[...])
+    att2[...] = att
+    h2 = h1_out[...] + dot_nn(att, wc[3])
     h2_ref[...] = h2
     n3 = (h2 * rms_scale(h2) * gain_ff[...]).astype(BF16)
 
@@ -543,6 +608,55 @@
     out = h2 + dot_nn(mix_ref[...], wd[...])
     out_ref[...] = out
     fin_ref[...] = (out * rms_scale(out) * gain_final[...] * D ** (-0.5)).astype(BF16)
+    for copy in leaving:
+        copy.wait()
+
+
+def forward(split, scal, x_own, source, gains, weights):
+    pair = (TGT, D)
+    block = (ROWS, D)
+    outs = [whole(pair, BF16)] * 3 + [whole((16, TGT), F32), whole(block, BF16), whole(block, F32)]
+    outs += [whole(pair, BF16)] + [whole((KEYS, D), BF16)] * 2
+    outs += [whole(block, F32), whole(block, BF16), whole(block, F32), whole((D, ROWS), F32)]
+    outs += [whole(block, BF16), whole((16, TGT), F32)]
+    vmem = pl.BlockSpec(memory_space=pltpu.VMEM)
+    out_specs = [vmem] * len(outs)
+    scratch = []
+    if split:
+        outs += [whole((D, D), BF16)] * 8 + [whole((FF, D), BF16)] * 3
+        out_specs += [pl.BlockSpec(memory_space=pl.ANY)] * 11
+        scratch += [pltpu.VMEM((4, D, D), BF16)] * 2 + [pltpu.VMEM((FF, D), BF16)] * 3
+    scratch += [
+        pltpu.VMEM(block, BF16),
+        pltpu.VMEM(pair, F32),
+        pltpu.VMEM(pair, BF16),
+        pltpu.VMEM((D, KEYS), BF16),
+        pltpu.VMEM((D, TGT), F32),
+        pltpu.VMEM((KEYS, TGT), F32),
+        pltpu.VMEM((D, ROWS), BF16),
+        pltpu.VMEM((D, ROWS), BF16),
+        pltpu.VMEM((16, TGT), F32),
+        pltpu.VMEM((16, TGT), F32),
+        pltpu.VMEM((ROWS, FF), BF16),
+        pltpu.SemaphoreType.DMA((4,)),
+        pltpu.SemaphoreType.DMA((4,)),
+    ]
+    if split:
+        scratch += [pltpu.SemaphoreType.DMA((27 * 5,))] * 2 + [pltpu.SemaphoreType.DMA((11,))]
+    args = (scal, x_own, source, *gains, *weights)
+    return pl.pallas_call(
+        functools.partial(forward_kernel, split),
+        out_shape=outs,
+        in_specs=[pl.BlockSpec(memory_space=pltpu.SMEM)] + [vmem] * (len(args) - 1),
+        out_specs=out_specs,
+        scratch_shapes=scratch,
+        cost_estimate=pl.CostEstimate(
+            flops=int(80e9), bytes_accessed=int(6e7), transcendentals=0
+        ),
+        compiler_params=pltpu.CompilerParams(
+            collective_id=0, has_side_effects=True, vmem_limit_bytes=VMEM_LIMIT
+        ),
+    )(*args)
 
 
 def ff_backward(
@@ -698,7 +812,7 @@
 
 
 def self_backward(
-    split, scal, q1, k1, v1, lse, g_own, g_other, x_own, gain_self, w_self, res_in, rows_in, att,
+    split, scal, q1, k1, v1, lse, g_own, g_other, x_own, gain_self, w_q, w_k, w_v, res_in, rows_in, att,
     mine_ref, send_ref, gin_ref, gg_ref,
     g_ref, dq_ref, dk_ref, dv_ref, flat_ref, a_ref, b_ref,
 ):
@@ -740,7 +854,7 @@
     x = x_own[...].astype(F32)
     scale1 = rms_scale(x)
     n1 = (x * scale1 * gain_self[...]).astype(BF16)
-    grad_n = dot_nn(dq, w_self[0]) + dot_nn(dk, w_self[1]) + dot_nn(dv, w_self[2])
+    grad_n = dot_nn(dq, w_q[...]) + dot_nn(dk, w_k[...]) + dot_nn(dv, w_v[...])
     step, gg = norm_back(x, scale1, gain_self[...], grad_n)
     gg_ref[...] = gg
     gin_ref[...] = res_in[...] + step
@@ -923,18 +1037,6 @@
         def pair_swap(value):
             return swap(value, "tensor", 4, 1)
 
-        x_other = pair_swap(block_in)
-        w_self, w_cross = gather_blocks(
-            [
-                jnp.concatenate([self_q.T, self_k.T, self_v.T, self_o], 0),
-                jnp.concatenate([cross_q.T, cross_k.T, cross_v.T, cross_o], 0),
-            ],
-            dp_size,
-        )
-        wg = gather_wide(ff_gate.T, dp_size)
-        wu = gather_wide(ff_up.T, dp_size)
-        wd = gather_wide(ff_down, dp_size)
-        cq, ck, cv, co = (w_cross[i] for i in range(4))
         scal = jnp.stack(
             [
                 half,
@@ -948,31 +1050,18 @@
             return pltpu.VMEM(shape, dtype)
 
         pair = (TGT, D)
-        q1, k1, v1, lse1, a1, h1, q2 = local_call(
-            self_forward,
-            [whole(pair, BF16)] * 3
-            + [whole((16, TGT), F32), whole((ROWS, D), BF16), whole((ROWS, D), F32), whole(pair, BF16)],
-            [vm(pair, F32), vm(pair, BF16), vm((D, TGT), BF16), vm((D, TGT), F32)],
-            8e9,
-            scal, block_in, x_other, gain_self, gain_cross, w_self, cq,
-        )
-        k2, v2, o_own, o_send, lse_own = local_call(
-            cross_forward,
-            [whole((KEYS, D), BF16)] * 2
-            + [whole((D, ROWS), F32), whole((D, ROWS), BF16), whole((16, TGT), F32)],
-            [vm((D, KEYS), BF16), vm((KEYS, TGT), F32), vm((D, TGT), F32)],
-            15e9,
-            scal, q2, source, ck, cv,
-        )
-        block_out, fin, h2, att_t, a2, lse2 = local_call(
-            ff_forward,
-            [whole((ROWS, D), F32), whole((ROWS, D), BF16), whole((ROWS, D), F32)]
-            + [whole((D, ROWS), F32), whole((ROWS, D), BF16), whole((16, TGT), F32)],
-            [vm((ROWS, FF), BF16)],
-            3e9,
-            scal, o_own, pair_swap(o_send), lse_own, pair_swap(lse_own), h1, co,
-            gain_ff, gain_final, wg, wu, wd,
-        )
+        weights = (
+            self_q, self_k, self_v, self_o, cross_q, cross_k, cross_v, cross_o, ff_gate, ff_up, ff_down,
+        )
+        if not split:
+            wide = [gather_wide(w if i in (3, 7, 10) else w.T, dp_size) for i, w in enumerate(weights)]
+            sq, sk, sv, so, cq, ck, cv, co, wg, wu, wd = wide
+            weights = jnp.stack([sq, sk, sv, so]), jnp.stack([cq, ck, cv, co]), wg, wu, wd
+        gains = gain_self, gain_cross, gain_ff, gain_final
+        results = forward(split, scal, block_in, source, gains, weights)
+        q1, k1, v1, lse1, a1, h1, q2, k2, v2, block_out, fin, h2, att_t, a2, lse2 = results[:15]
+        if split:
+            sq, sk, sv, so, cq, ck, cv, co, wg, wu, wd = results[15:]
 
         vocab = embed_table.shape[0]
 
@@ -1011,10 +1100,11 @@
         g_a, gf_a = head_grads(
             logits_a, embed_table, tgt_a, columns(g_lse, (2, 3)), columns(live_blocks, (2, 3)), BF16
         )
+        gf_2 = swap(gf_a[:ROWS], "tensor", 4, 2)
         g_b, gf_b = head_grads(
             logits_b, embed_table, tgt_b, columns(g_lse, (0, 1)), columns(live_blocks, (0, 1)), F32
         )
-        gf_2 = swap(gf_a[:ROWS], "tensor", 4, 2)
+        g_b, gf_b, gf_2, gf_a = lax.optimization_barrier((g_b, gf_b, gf_2, gf_a))
         gf_3 = swap(gf_a[ROWS:], "tensor", 4, 3)
         gf_1 = swap(gf_b[ROWS:].astype(BF16), "tensor", 4, 1)
 
@@ -1033,6 +1123,7 @@
         e_mine, e_send = table_grads(halves(fin_a), halves(fin_b), g_a, g_b)
         if not split:
             e_mine, e_send = e_mine[:, :vocab], e_send[:, :vocab]
+        e_mine, e_send, gf_1, gf_3 = lax.optimization_barrier((e_mine, e_send, gf_1, gf_3))
         e_sum = reduction(xyz, e_mine, e_send)
 
         half_t = (HALF_D, ROWS)
@@ -1058,6 +1149,7 @@
             scal, q2, k2, v2, lse2, after(gatt, *sent), gatt_other, dots, dots_other,
         )
         dq_other = pair_swap(dq_send)
+        dk2, *e_sum.gots = lax.optimization_barrier((dk2, *e_sum.gots))
         sent = ff_sum.first()
         grad_source, kv_mine, kv_send = local_call(
             functools.partial(source_backward, split),
@@ -1073,7 +1165,7 @@
             + [whole((ROWS, D), BF16)] * 2 + [whole((1, D), F32)],
             [vm((D, ROWS), BF16)] + [vm(half_t, BF16)] * 2,
             2e9,
-            scal, after(dq_own, *sent), dq_other, h1, gain_cross, cq, res2, rows2, a2, w_self[3],
+            scal, after(dq_own, *sent), dq_other, h1, gain_cross, cq, res2, rows2, a2, so,
             kv_mine, kv_send,
         )
         c_sum = reduction(xyz, c_mine, c_send)
@@ -1086,9 +1178,13 @@
             [vm(pair, BF16), vm((D, TGT), F32), vm(pair, BF16), vm(pair, BF16)]
             + [vm((D, ROWS), BF16)] + [vm(half_t, BF16)] * 2,
             12e9,
-            scal, q1, k1, v1, lse1, after(gatt1, *sent), gatt1_other, block_in, gain_self, w_self,
+            scal, q1, k1, v1, lse1, after(gatt1, *sent), gatt1_other, block_in, gain_self, sq, sk, sv,
             res1, rows1, a1,
         )
+        flying = (*e_sum.gots, *ff_sum.gots, *c_sum.gots)
+        s_mine, s_send, *flying = lax.optimization_barrier((s_mine, s_send, *flying))
+        if split:
+            e_sum.gots, ff_sum.gots, c_sum.gots = flying[:2], flying[2:4], flying[4:]
         s_sum = reduction(xyz, s_mine, s_send)
         gains = jnp.concatenate([gg_a, gg_b, gg_c], 0)
         if split:

time: 768 us -> 618 us (0.80)
  waiting for transfers between devices: 165 us -> 71.3 us
  local copies, waits for them, and re-layouts: 96.7 us -> 76.1 us
  between operations: 15.2 us -> 1.8 us
  Pallas kernels: 404 us -> 393 us
  starting transfers between devices: 65.7 us -> 57.3 us
    all_gather x3 -> x0, waiting for transfers between devices: 56.2 us -> none  [gather_wide(): return lax.all_gather(part, ('tensor', 'dp'), axis=0, tiled=True)]
    ppermute x50 -> x47, waiting for transfers between devices: 109 us -> 71.3 us  [swap(): return lax.ppermute(value, axis_name, [(i, i ^ bit) for i in range(size)])]
    pallas_call x8 -> x5, Pallas kernels: 109 us -> 71.4 us  [local_call(): pl.pallas_call(body, out_shape=outs, in_specs=[smem] + [vmem] * (len(args...]
    pallas_call x1, Pallas kernels: 76.4 us -> 104 us  [forward(): pl.pallas_call(functools.partial(forward_kernel, split), out_shape=outs,...]
    unnamed x261 -> x196, local copies, waits for them, and re-layouts: 71.9 us -> 56.9 us
    ppermute x50 -> x47, starting transfers between devices: 65.6 us -> 57.3 us  [swap(): return lax.ppermute(value, axis_name, [(i, i ^ bit) for i in range(size)])]
  transfers between devices with their start and end apart: 53 -> 47, of which waited for: 14 -> 14; matrix products, arithmetic and copies ran while one was open for 6% -> 4% of each run, Pallas kernels for 36% -> 36%
where the time goes in v3:
time: 618 us; the launch traced here: 611 us
  Pallas kernels  393 us (64%)
  local copies, waits for them, and re-layouts  76.1 us (12%)
  waiting for transfers between devices  71.3 us (12%)
  starting transfers between devices  57.3 us (9%)
  other arithmetic  10.7 us (2%)
    pallas_call x1, Pallas kernels, forward(): pl.pallas_call(functools.partial(forward_kernel, split), out_shape=outs,...  104 us
    pallas_call x5, Pallas kernels, local_call(): pl.pallas_call(body, out_shape=outs, in_specs=[smem] + [vmem] * (len(args...  71.4 us
    ppermute x47, waiting for transfers between devices, swap(): return lax.ppermute(value, axis_name, [(i, i ^ bit) for i in range(size)])  71.3 us
    pallas_call x2, Pallas kernels, head_logits(): pl.pallas_call(functools.partial(logits_kernel, vocab), grid=(tiles,), ou...  69.9 us
    ppermute x47, starting transfers between devices, swap(): return lax.ppermute(value, axis_name, [(i, i ^ bit) for i in range(size)])  57.3 us
    unnamed x196, local copies, waits for them, and re-layouts  56.9 us
    pallas_call x8, Pallas kernels, fold_call(): pl.pallas_call(body, grid=(width // tile,), out_shape=outs, in_specs=in_s...  53.6 us
    pallas_call x2, Pallas kernels, head_grads(): pl.pallas_call(functools.partial(grads_kernel, vocab), grid=(tiles,), out...  46 us
  transfers between devices with their start and end apart: 47, of which 14 were waited for; matrix products, arithmetic and copies ran while one was open for 4% of the time, Pallas kernels for 36%

profile of v3, /device:TPU:0, one launch (start us, length us, event | category | flops | bytes accessed | tf_op | source)
XLA Modules:
  0.0 610.6 jit_solution(256967844127792849)
XLA Ops:
  18.7 103.8 %shard_map.356 = (bf16[512,768]{1,0:T(8,128)(2,1)}, bf16[512,768]{1,0:T(8,128)(2,1)}, bf16[512,768]{1,0:T(8,128)(2,1)}, f32[16,512]{1,0:T(8,128)}, bf16[256,768]...) custom-call(s32[4]{0:T(128)} %pad_add_fusion.4.refs_0_.scal, ...), custom_call_target="tpu_custom_call" | custom-call | flops 80000000000 | bytes 60000000 | tf_op jit(solution)/shard_map/pallas_call | solution.py:647
  132.9 8.5 %collective-permute-done = bf16[256,768]{1,0:T(8,128)(2,1)S(1)} collective-permute-done((bf16[256,768]{1,0:T(8,128)(2,1)}, bf16[256,768]{1,0:T(8,128)(2,1)S(1)}, u32[]{:S(2)}, u32[]{:S(2)}) %collective-permute-start) | collective-permute-done | bytes 393248 | tf_op jit(solution)/shard_map/ppermute | solution.py:40
  142.3 34.9 %shard_map.357 = (f32[512,8192]{1,0:T(8,128)}, f32[8,512]{1,0:T(8,128)}) custom-call(bf16[512,768]{1,0:T(8,128)(2,1)} %copy-done.44, bf16[8032,768]{1,0:T(8,128)(2,1)} %table_ref.7, s32[512,1]{1,0:T(8,128)} %copy.66.target_ref), custom_call_target="tpu_custom_call" | custom-call | flops 6316621824 | bytes 28786688 | tf_op jit(solution)/shard_map/pallas_call | solution.py:906
  178.9 35.0 %shard_map.358 = (f32[512,8192]{1,0:T(8,128)}, f32[8,512]{1,0:T(8,128)}) custom-call(bf16[512,768]{1,0:T(8,128)(2,1)} %copy-done.42, bf16[8032,768]{1,0:T(8,128)(2,1)} %table_ref.7, s32[512,1]{1,0:T(8,128)} %copy.67.target_ref), custom_call_target="tpu_custom_call" | custom-call | flops 6316621824 | bytes 28786688 | tf_op jit(solution)/shard_map/pallas_call | solution.py:906
  214.8 2.2 collective-permute-start.4
  217.1 2.1 collective-permute-start.5
  224.9 22.8 %shard_map.360 = (bf16[512,8192]{1,0:T(8,128)(2,1)}, bf16[512,768]{1,0:T(8,128)(2,1)}) custom-call(f32[512,8192]{1,0:T(8,128)} %get-tuple-element.186.logits_ref, bf16[8032,768]{1,0:T(8,128)(2,1)} %table_ref.7, s32[512,1]{1,0:T(8,128)} %copy.67.target_ref, f32[512,1]{1,0:T(8,128)} %copy.79.lse_ref, s32[512,1]{1,0:T(8,128)} %copy.80.live_ref), custom_call_target="tpu_custom_call" | custom-call | flops 6316621824 | bytes 37011456 | tf_op jit(solution)/shard_map/pallas_call | solution.py:954
  249.7 23.2 %shard_map.359 = (bf16[512,8192]{1,0:T(8,128)(2,1)}, f32[512,768]{1,0:T(8,128)}) custom-call(f32[512,8192]{1,0:T(8,128)} %get-tuple-element.183.logits_ref, bf16[8032,768]{1,0:T(8,128)(2,1)} %table_ref.7, s32[512,1]{1,0:T(8,128)} %copy.66.target_ref, f32[512,1]{1,0:T(8,128)} %copy.76.lse_ref, s32[512,1]{1,0:T(8,128)} %copy.77.live_ref), custom_call_target="tpu_custom_call" | custom-call | flops 6316621824 | bytes 37011456 | tf_op jit(solution)/shard_map/pallas_call | solution.py:954
  274.1 2.7 collective-permute-start.7
  278.7 21.5 %shard_map.361 = (f32[384,8192]{1,0:T(8,128)}, bf16[384,8192]{1,0:T(8,128)(2,1)}) custom-call(bf16[384,512]{1,0:T(8,128)(2,1)} %bitcast.151, bf16[384,512]{1,0:T(8,128)(2,1)} %bitcast.150, bf16[384,512]{1,0:T(8,128)(2,1)} %bitcast.152, bf16[384,512]{1,0:T(8,128)(2,1)} %bitcast.149, bf16[512,8192]{1,0:T(8,128)(2,1)} %get-tuple-element.189.g_a, ...), custom_call_target="tpu_custom_call" | custom-call | flops 12884901888 | bytes 35651584 | tf_op jit(solution)/shard_map/pallas_call | solution.py:988
  300.3 18.8 %shard_map.362 = (f32[384,6144]{1,0:T(8,128)}, bf16[384,6144]{1,0:T(8,128)(2,1)}, f32[256,768]{1,0:T(8,128)S(1)}, bf16[256,768]{1,0:T(8,128)(2,1)S(1)}, bf16[256...) custom-call(s32[4]{0:T(128)S(1)} %copy-done.11, f32[256,768]{1,0:T(8,128)S(1)} %slice.110.gf_own, ...), custom_call_target="tpu_custom_call" | custom-call | flops 10000000000 | bytes 30699536 | tf_op jit(solution)/shard_map/pallas_call | solution.py:354
  320.2 2.0 collective-permute-start.11
  322.8 5.3 collective-permute-done.15.got_a.got_b
  328.1 8.8 %shard_map.366 = (f32[192,3072]{1,0:T(8,128)}, bf16[192,3072]{1,0:T(8,128)(2,1)}, f32[192,3072]{1,0:T(8,128)}, bf16[192,3072]{1,0:T(8,128)(2,1)}) custom-call(s32[3]{0:T(128)} %pad_add_fusion.5.xyz, f32[384,6144]{1,0:T(8,128)} %get-tuple-element.228.mine_a.mine_b, bf16[384,6144]{1,0:T(8,128)(2,1)} %collective-permute-done.15.got_a.got_b, ...), custom_call_target="tpu_custom_call" | custom-call | bytes 21233664 | tf_op jit(solution)/shard_map/pallas_call | solution.py:143
  336.9 11.5 %shard_map.363 = (f32[192,4096]{1,0:T(8,128)}, bf16[192,4096]{1,0:T(8,128)(2,1)}, f32[192,4096]{1,0:T(8,128)}, bf16[192,4096]{1,0:T(8,128)(2,1)}) custom-call(s32[3]{0:T(128)} %pad_add_fusion.5.xyz, f32[384,8192]{1,0:T(8,128)} %get-tuple-element.206.mine_a.mine_b, bf16[384,8192]{1,0:T(8,128)(2,1)} %collective-permute-done.9.got_a.got_b, ...), custom_call_target="tpu_custom_call" | custom-call | bytes 28311552 | tf_op jit(solution)/shard_map/pallas_call | solution.py:143
  357.2 24.2 %shard_map.364 = (bf16[1024,768]{1,0:T(8,128)(2,1)S(1)}, bf16[1024,768]{1,0:T(8,128)(2,1)S(1)}, f32[768,256]{1,0:T(8,128)S(1)}, bf16[768,256]{1,0:T(8,128)(2,1)}) custom-call(s32[4]{0:T(128)S(1)} %copy-done.11, bf16[512,768]{1,0:T(8,128)(2,1)S(1)} %copy-done.39, bf16[1024,768]{1,0:T(8,128)(2,1)S(1)} %copy-done.36, bf16[1024,768]{1,0:T(8,128)(2,1)S(1)} %copy-done.37, ...), custom_call_target="tpu_custom_call" | custom-call | flops 20000000000 | bytes 9109520 | tf_op jit(solution)/shard_map/pallas_call | solution.py:354
  387.1 8.1 %shard_map.365 = (f32[96,4096]{1,0:T(8,128)}, bf16[96,4096]{1,0:T(8,128)(2,1)}, f32[96,4096]{1,0:T(8,128)}, bf16[96,4096]{1,0:T(8,128)(2,1)}) custom-call(s32[3]{0:T(128)} %pad_add_fusion.5.xyz, f32[192,4096]{1,0:T(8,128)} %get-tuple-element.212.mine_a, bf16[192,4096]{1,0:T(8,128)(2,1)} %collective-permute-done.12.got_a, ...), custom_call_target="tpu_custom_call" | custom-call | bytes 14155776 | tf_op jit(solution)/shard_map/pallas_call | solution.py:143
  402.0 6.5 %shard_map.367 = (f32[1024,768]{1,0:T(8,128)}, f32[384,1536]{1,0:T(8,128)S(1)}, bf16[384,1536]{1,0:T(8,128)(2,1)S(1)}) custom-call(s32[4]{0:T(128)S(1)} %copy-done.11, bf16[1024,768]{1,0:T(8,128)(2,1)S(1)} %copy-done.23, bf16[1024,768]{1,0:T(8,128)(2,1)S(1)} %copy-done.25, bf16[1024,768]{1,0:T(8,128)(2,1)S(1)} %copy-done.12, ...), custom_call_target="tpu_custom_call" | custom-call | flops 5000000000 | bytes 13762576 | tf_op jit(solution)/shard_map/pallas_call | solution.py:354
  408.6 5.1 shard_map.368
  413.7 2.2 copy-done
  419.6 26.4 %collective-permute-done.16.got_a = bf16[192,3072]{1,0:T(8,128)(2,1)S(1)} collective-permute-done((bf16[192,3072]{1,0:T(8,128)(2,1)S(1)}, bf16[192,3072]{1,0:T(8,128)(2,1)S(1)}, u32[]{:S(2)}, u32[]{:S(2)}) %collective-permute-start.16) | collective-permute-done | bytes 1179680 | tf_op jit(solution)/shard_map/ppermute | solution.py:40
  447.4 6.3 %shard_map.369 = (f32[96,3072]{1,0:T(8,128)}, bf16[96,3072]{1,0:T(8,128)(2,1)}, f32[96,3072]{1,0:T(8,128)}, bf16[96,3072]{1,0:T(8,128)(2,1)}) custom-call(s32[3]{0:T(128)} %pad_add_fusion.5.xyz, f32[192,3072]{1,0:T(8,128)} %get-tuple-element.239.mine_a, bf16[192,3072]{1,0:T(8,128)(2,1)} %copy-done.46, f32[192,3072]{1,0:T(8,128)} %get-tuple-element.240.mine_b, ...), custom_call_target="tpu_custom_call" | custom-call | bytes 10616832 | tf_op jit(solution)/shard_map/pallas_call | solution.py:143
  457.8 5.5 shard_map.370
  463.3 7.0 %collective-permute-done.27.got_a = bf16[96,3072]{1,0:T(8,128)(2,1)} collective-permute-done((bf16[96,3072]{1,0:T(8,128)(2,1)}, bf16[96,3072]{1,0:T(8,128)(2,1)}, u32[]{:S(2)}, u32[]{:S(2)}) %collective-permute-start.27) | collective-permute-done | bytes 589856 | tf_op jit(solution)/shard_map/ppermute | solution.py:40
  480.5 16.8 %shard_map.371 = (f32[384,3072]{1,0:T(8,128)S(1)}, bf16[384,3072]{1,0:T(8,128)(2,1)S(1)}, f32[256,768]{1,0:T(8,128)}, f32[1,768]{1,0:T(1,128)S(1)}) custom-call(s32[4]{0:T(128)S(1)} %copy-done.11, bf16[512,768]{1,0:T(8,128)(2,1)S(1)} %copy-done.33, bf16[512,768]{1,0:T(8,128)(2,1)S(1)} %copy-done.34, bf16[512,768]{1,0:T(8,128)(2,1)S(1)} %copy-done.35, ...), custom_call_target="tpu_custom_call" | custom-call | flops 12000000000 | bytes 16554000 | tf_op jit(solution)/shard_map/pallas_call | solution.py:354
  497.3 2.2 copy-done.1
  500.5 3.7 collective-permute-done.31.got_a.got_b
  504.2 5.4 shard_map.372
  511.7 4.0 shard_map.376
  517.9 8.1 %collective-permute-done.32.got_a = bf16[192,1536]{1,0:T(8,128)(2,1)S(1)} collective-permute-done((bf16[192,1536]{1,0:T(8,128)(2,1)}, bf16[192,1536]{1,0:T(8,128)(2,1)S(1)}, u32[]{:S(2)}, u32[]{:S(2)}) %collective-permute-start.32) | collective-permute-done | bytes 589856 | tf_op jit(solution)/shard_map/ppermute | solution.py:40
  528.3 4.0 shard_map.373
  534.4 2.3 collective-permute-done.21
  538.1 2.3 collective-permute-done.22
  540.4 2.5 collective-permute-start.23
  542.8 2.1 collective-permute-done.23
  547.2 3.5 shard_map.379
  551.7 2.1 collective-permute-start.45
  555.1 2.4 shard_map.377
  561.6 6.3 %shard_map.381 = f32[4096,96]{1,0:T(8,128)} custom-call(f32[96,4096]{1,0:T(8,128)} %get-tuple-element.306.mine, bf16[96,4096]{1,0:T(8,128)(2,1)} %collective-permute-done.25.got), custom_call_target="tpu_custom_call" | custom-call | tf_op jit(solution)/shard_map/pallas_call | solution.py:261
  567.8 6.3 %shard_map.382 = f32[3936,96]{1,0:T(8,128)} custom-call(f32[96,4096]{1,0:T(8,128)} %get-tuple-element.308.mine, bf16[96,4096]{1,0:T(8,128)(2,1)} %collective-permute-done.26.got), custom_call_target="tpu_custom_call" | custom-call | tf_op jit(solution)/shard_map/pallas_call | solution.py:261
  574.2 2.4 collective-permute-start.42
  576.5 2.4 shard_map.374
  580.4 8.0 %collective-permute-start.37 = (bf16[96,768]{1,0:T(8,128)(2,1)}, bf16[96,768]{1,0:T(8,128)(2,1)S(1)}, u32[]{:S(2)}, u32[]{:S(2)}) collective-permute-start(bf16[96,768]{1,0:T(8,128)(2,1)} %get-tuple-element.273), channel_id=1, source_target_pairs={{0,2},{1,3},{2,0},{3,1},{4,6},{5,7},{6,4},{7,5},{8,10},{9,11},{10,... | collective-permute-start | bytes 442376 | tf_op jit(solution)/shard_map/ppermute | solution.py:40
  590.2 4.4 pad_maximum_fusion
  594.7 5.2 copy.84
  600.0 2.3 shard_map.380
  604.7 2.0 shard_map.378
  607.5 2.0 shard_map.375
  (321 shorter events, 111.6 us)
Async XLA Ops:
  18.7 108.3 %copy-start.81 = (pred[1024]{0:T(1024)(128)(4,1)S(1)}, pred[1024]{0:T(1024)(128)(4,1)}, u32[]{:S(2)}) copy-start(pred[1024]{0:T(1024)(128)(4,1)} %constant.232) | copy-start | bytes 3076
  122.5 18.9 %collective-permute-start = (bf16[256,768]{1,0:T(8,128)(2,1)}, bf16[256,768]{1,0:T(8,128)(2,1)S(1)}, u32[]{:S(2)}, u32[]{:S(2)}) collective-permute-start(bf16[256,768]{1,0:T(8,128)(2,1)} %get-tuple-element.172), channel_id=1, source_target_pairs={{0,1},{1,0},{2,3},{3,2},{4,5},{5,4},{6,7},{7,6},{8,9},{9,8},{10,11... | collective-permute-start | bytes 1179656 | tf_op jit(solution)/shard_map/ppermute | solution.py:40
  124.2 53.1 %collective-permute-start.1 = (bf16[256,768]{1,0:T(8,128)(2,1)}, bf16[256,768]{1,0:T(8,128)(2,1)S(1)}, u32[]{:S(2)}, u32[]{:S(2)}) collective-permute-start(bf16[256,768]{1,0:T(8,128)(2,1)} %get-tuple-element.172), channel_id=1, source_target_pairs={{0,2},{1,3},{2,0},{3,1},{4,6},{5,7},{6,4},{7,5},{8,10},{9,11},{10,... | collective-permute-start | bytes 1179656 | tf_op jit(solution)/shard_map/ppermute | solution.py:40
  125.6 52.4 %collective-permute-start.2 = (bf16[256,768]{1,0:T(8,128)(2,1)}, bf16[256,768]{1,0:T(8,128)(2,1)S(1)}, u32[]{:S(2)}, u32[]{:S(2)}) collective-permute-start(bf16[256,768]{1,0:T(8,128)(2,1)} %get-tuple-element.172), channel_id=1, source_target_pairs={{0,3},{1,2},{2,1},{3,0},{4,7},{5,6},{6,5},{7,4},{8,11},{9,10},{10,... | collective-permute-start | bytes 1179656 | tf_op jit(solution)/shard_map/ppermute | solution.py:40
  214.8 6.2 %collective-permute-start.3 = (f32[4,8,256]{2,0,1:T(4,128)S(1)}, f32[4,8,256]{2,0,1:T(4,128)S(1)}, u32[]{:S(2)}, u32[]{:S(2)}) collective-permute-start(f32[4,8,256]{2,0,1:T(4,128)S(1)} %copy.68), channel_id=1, source_target_pairs={{0,1},{1,0},{2,3},{3,2},{4,5},{5,4},{6,7},{7,6},{8,9},{9,8},{10,11... | collective-permute-start | bytes 98312 | tf_op jit(solution)/shard_map/ppermute | solution.py:40
  214.8 6.8 %collective-permute-start.4 = (f32[4,8,256]{2,0,1:T(4,128)S(1)}, f32[4,8,256]{2,0,1:T(4,128)S(1)}, u32[]{:S(2)}, u32[]{:S(2)}) collective-permute-start(f32[4,8,256]{2,0,1:T(4,128)S(1)} %copy.68), channel_id=1, source_target_pairs={{0,2},{1,3},{2,0},{3,1},{4,6},{5,7},{6,4},{7,5},{8,10},{9,11},{10,... | collective-permute-start | bytes 98312 | tf_op jit(solution)/shard_map/ppermute | solution.py:40
  217.1 5.7 collective-permute-start.5
  248.8 24.2 %collective-permute-start.6 = (bf16[256,768]{1,0:T(8,128)(2,1)S(1)}, bf16[256,768]{1,0:T(8,128)(2,1)S(1)}, u32[]{:S(2)}, u32[]{:S(2)}) collective-permute-start(bf16[256,768]{1,0:T(8,128)(2,1)S(1)} %slice.109), channel_id=1, source_target_pairs={{0,2},{1,3},{2,0},{3,1},{4,6},{5,7},{6,4},{7,5},{8,10},{9,11},{10,... | collective-permute-start | bytes 1179656 | tf_op jit(solution)/shard_map/ppermute | solution.py:40
  274.1 26.0 %collective-permute-start.7 = (bf16[256,768]{1,0:T(8,128)(2,1)S(1)}, bf16[256,768]{1,0:T(8,128)(2,1)S(1)}, u32[]{:S(2)}, u32[]{:S(2)}) collective-permute-start(bf16[256,768]{1,0:T(8,128)(2,1)S(1)} %slice.164), channel_id=1, source_target_pairs={{0,1},{1,0},{2,3},{3,2},{4,5},{5,4},{6,7},{7,6},{8,9},{9,8},{10,11... | collective-permute-start | bytes 1179656 | tf_op jit(solution)/shard_map/ppermute | solution.py:40
  276.9 23.2 %collective-permute-start.8 = (bf16[256,768]{1,0:T(8,128)(2,1)S(1)}, bf16[256,768]{1,0:T(8,128)(2,1)S(1)}, u32[]{:S(2)}, u32[]{:S(2)}) collective-permute-start(bf16[256,768]{1,0:T(8,128)(2,1)S(1)} %slice.112), channel_id=1, source_target_pairs={{0,3},{1,2},{2,1},{3,0},{4,7},{5,6},{6,5},{7,4},{8,11},{9,10},{10,... | collective-permute-start | bytes 1179656 | tf_op jit(solution)/shard_map/ppermute | solution.py:40
  300.1 36.8 %collective-permute-start.9 = (bf16[384,8192]{1,0:T(8,128)(2,1)}, bf16[384,8192]{1,0:T(8,128)(2,1)}, u32[]{:S(2)}, u32[]{:S(2)}) collective-permute-start(bf16[384,8192]{1,0:T(8,128)(2,1)} %get-tuple-element.194), channel_id=1, source_target_pairs={{0,4},{4,0},{8,12},{12,8},{16,20},{20,16},{24,28},{28,24},{1,5},{5... | collective-permute-start | bytes 18874376 | tf_op jit(solution)/shard_map/ppermute | solution.py:40
  319.7 8.4 %collective-permute-start.15 = (bf16[384,6144]{1,0:T(8,128)(2,1)}, bf16[384,6144]{1,0:T(8,128)(2,1)}, u32[]{:S(2)}, u32[]{:S(2)}) collective-permute-start(bf16[384,6144]{1,0:T(8,128)(2,1)} %get-tuple-element.229), channel_id=1, source_target_pairs={{0,4},{4,0},{8,12},{12,8},{16,20},{20,16},{24,28},{28,24},{1,5},{5... | collective-permute-start | bytes 14155784 | tf_op jit(solution)/shard_map/ppermute | solution.py:40
  320.2 30.8 %collective-permute-start.10 = (bf16[256,768]{1,0:T(8,128)(2,1)S(1)}, bf16[256,768]{1,0:T(8,128)(2,1)S(1)}, u32[]{:S(2)}, u32[]{:S(2)}) collective-permute-start(bf16[256,768]{1,0:T(8,128)(2,1)S(1)} %get-tuple-element.209.g_own), channel_id=1, source_target_pairs={{0,1},{1,0},{2,3},{3,2},{4,5},{5,4},{6,7},{7,6},{8,9},{9,8},{10,11... | collective-permute-start | bytes 1179656 | tf_op jit(solution)/shard_map/ppermute | solution.py:40
  320.2 30.2 %collective-permute-start.11 = (f32[16,256]{1,0:T(8,128)}, f32[16,256]{1,0:T(8,128)S(1)}, u32[]{:S(2)}, u32[]{:S(2)}) collective-permute-start(f32[16,256]{1,0:T(8,128)} %copy-done.18), channel_id=1, source_target_pairs={{0,1},{1,0},{2,3},{3,2},{4,5},{5,4},{6,7},{7,6},{8,9},{9,8},{10,11... | collective-permute-start | bytes 49160 | tf_op jit(solution)/shard_map/ppermute | solution.py:40
  348.4 37.2 %collective-permute-start.12 = (bf16[192,4096]{1,0:T(8,128)(2,1)}, bf16[192,4096]{1,0:T(8,128)(2,1)}, u32[]{:S(2)}, u32[]{:S(2)}) collective-permute-start(bf16[192,4096]{1,0:T(8,128)(2,1)} %get-tuple-element.207), channel_id=1, source_target_pairs={{0,8},{4,12},{8,0},{12,4},{16,24},{20,28},{24,16},{28,20},{1,9},{5... | collective-permute-start | bytes 4718600 | tf_op jit(solution)/shard_map/ppermute | solution.py:40
  350.4 36.7 %collective-permute-start.13 = (bf16[192,4096]{1,0:T(8,128)(2,1)}, bf16[192,4096]{1,0:T(8,128)(2,1)}, u32[]{:S(2)}, u32[]{:S(2)}) collective-permute-start(bf16[192,4096]{1,0:T(8,128)(2,1)} %get-tuple-element.208), channel_id=1, source_target_pairs={{0,16},{4,20},{8,24},{12,28},{16,0},{20,4},{24,8},{28,12},{1,17},{... | collective-permute-start | bytes 4718600 | tf_op jit(solution)/shard_map/ppermute | solution.py:40
  383.7 24.9 %collective-permute-start.14 = (bf16[768,256]{1,0:T(8,128)(2,1)}, bf16[768,256]{1,0:T(8,128)(2,1)S(1)}, u32[]{:S(2)}, u32[]{:S(2)}) collective-permute-start(bf16[768,256]{1,0:T(8,128)(2,1)} %get-tuple-element.220), channel_id=1, source_target_pairs={{0,1},{1,0},{2,3},{3,2},{4,5},{5,4},{6,7},{7,6},{8,9},{9,8},{10,11... | collective-permute-start | bytes 1179656 | tf_op jit(solution)/shard_map/ppermute | solution.py:40
  417.6 39.6 %collective-permute-start.18 = (bf16[384,3072]{1,0:T(8,128)(2,1)}, bf16[384,3072]{1,0:T(8,128)(2,1)}, u32[]{:S(2)}, u32[]{:S(2)}) collective-permute-start(bf16[384,3072]{1,0:T(8,128)(2,1)} %get-tuple-element.244), channel_id=1, source_target_pairs={{0,4},{4,0},{8,12},{12,8},{16,20},{20,16},{24,28},{28,24},{1,5},{5... | collective-permute-start | bytes 7077896 | tf_op jit(solution)/shard_map/ppermute | solution.py:40
  417.6 28.4 %collective-permute-start.16 = (bf16[192,3072]{1,0:T(8,128)(2,1)S(1)}, bf16[192,3072]{1,0:T(8,128)(2,1)S(1)}, u32[]{:S(2)}, u32[]{:S(2)}) collective-permute-start(bf16[192,3072]{1,0:T(8,128)(2,1)S(1)} %copy-done.84), channel_id=1, source_target_pairs={{0,8},{4,12},{8,0},{12,4},{16,24},{20,28},{24,16},{28,20},{1,9},{5... | collective-permute-start | bytes 3538952 | tf_op jit(solution)/shard_map/ppermute | solution.py:40
  417.9 28.1 %collective-permute-start.17 = (bf16[192,3072]{1,0:T(8,128)(2,1)S(1)}, bf16[192,3072]{1,0:T(8,128)(2,1)S(1)}, u32[]{:S(2)}, u32[]{:S(2)}) collective-permute-start(bf16[192,3072]{1,0:T(8,128)(2,1)S(1)} %copy-done.83), channel_id=1, source_target_pairs={{0,16},{4,20},{8,24},{12,28},{16,0},{20,4},{24,8},{28,12},{1,17},{... | collective-permute-start | bytes 3538952 | tf_op jit(solution)/shard_map/ppermute | solution.py:40
  453.7 16.5 %collective-permute-start.27 = (bf16[96,3072]{1,0:T(8,128)(2,1)}, bf16[96,3072]{1,0:T(8,128)(2,1)}, u32[]{:S(2)}, u32[]{:S(2)}) collective-permute-start(bf16[96,3072]{1,0:T(8,128)(2,1)} %get-tuple-element.241), channel_id=1, source_target_pairs={{0,16},{4,20},{8,24},{12,28},{16,0},{20,4},{24,8},{28,12},{1,17},{... | collective-permute-start | bytes 1769480 | tf_op jit(solution)/shard_map/ppermute | solution.py:40
  455.1 16.6 %collective-permute-start.19 = (bf16[256,768]{1,0:T(8,128)(2,1)S(1)}, bf16[256,768]{1,0:T(8,128)(2,1)S(1)}, u32[]{:S(2)}, u32[]{:S(2)}) collective-permute-start(bf16[256,768]{1,0:T(8,128)(2,1)S(1)} %copy-done.17), channel_id=1, source_target_pairs={{0,1},{1,0},{2,3},{3,2},{4,5},{5,4},{6,7},{7,6},{8,9},{9,8},{10,11... | collective-permute-start | bytes 1179656 | tf_op jit(solution)/shard_map/ppermute | solution.py:40
  455.1 44.3 %collective-permute-start.28 = (bf16[96,3072]{1,0:T(8,128)(2,1)}, bf16[96,3072]{1,0:T(8,128)(2,1)}, u32[]{:S(2)}, u32[]{:S(2)}) collective-permute-start(bf16[96,3072]{1,0:T(8,128)(2,1)} %get-tuple-element.242), channel_id=1, source_target_pairs={{0,8},{4,12},{8,0},{12,4},{16,24},{20,28},{24,16},{28,20},{1,9},{5... | collective-permute-start | bytes 1769480 | tf_op jit(solution)/shard_map/ppermute | solution.py:40
  455.7 43.7 %collective-permute-start.25 = (bf16[96,4096]{1,0:T(8,128)(2,1)}, bf16[96,4096]{1,0:T(8,128)(2,1)}, u32[]{:S(2)}, u32[]{:S(2)}) collective-permute-start(bf16[96,4096]{1,0:T(8,128)(2,1)} %get-tuple-element.217), channel_id=1, source_target_pairs={{0,16},{4,20},{8,24},{12,28},{16,0},{20,4},{24,8},{28,12},{1,17},{... | collective-permute-start | bytes 2359304 | tf_op jit(solution)/shard_map/ppermute | solution.py:40
  457.1 42.3 %collective-permute-start.26 = (bf16[96,4096]{1,0:T(8,128)(2,1)}, bf16[96,4096]{1,0:T(8,128)(2,1)}, u32[]{:S(2)}, u32[]{:S(2)}) collective-permute-start(bf16[96,4096]{1,0:T(8,128)(2,1)} %get-tuple-element.218), channel_id=1, source_target_pairs={{0,8},{4,12},{8,0},{12,4},{16,24},{20,28},{24,16},{28,20},{1,9},{5... | collective-permute-start | bytes 2359304 | tf_op jit(solution)/shard_map/ppermute | solution.py:40
  470.3 29.2 %collective-permute-start.29 = (bf16[192,1536]{1,0:T(8,128)(2,1)}, bf16[192,1536]{1,0:T(8,128)(2,1)S(1)}, u32[]{:S(2)}, u32[]{:S(2)}) collective-permute-start(bf16[192,1536]{1,0:T(8,128)(2,1)} %get-tuple-element.245), channel_id=1, source_target_pairs={{0,8},{4,12},{8,0},{12,4},{16,24},{20,28},{24,16},{28,20},{1,9},{5... | collective-permute-start | bytes 1769480 | tf_op jit(solution)/shard_map/ppermute | solution.py:40
  471.7 27.8 %collective-permute-start.30 = (bf16[192,1536]{1,0:T(8,128)(2,1)}, bf16[192,1536]{1,0:T(8,128)(2,1)S(1)}, u32[]{:S(2)}, u32[]{:S(2)}) collective-permute-start(bf16[192,1536]{1,0:T(8,128)(2,1)} %get-tuple-element.246), channel_id=1, source_target_pairs={{0,16},{4,20},{8,24},{12,28},{16,0},{20,4},{24,8},{28,12},{1,17},{... | collective-permute-start | bytes 1769480 | tf_op jit(solution)/shard_map/ppermute | solution.py:40
  499.5 4.7 collective-permute-start.31
  509.6 16.4 %collective-permute-start.32 = (bf16[192,1536]{1,0:T(8,128)(2,1)}, bf16[192,1536]{1,0:T(8,128)(2,1)S(1)}, u32[]{:S(2)}, u32[]{:S(2)}) collective-permute-start(bf16[192,1536]{1,0:T(8,128)(2,1)} %get-tuple-element.264), channel_id=1, source_target_pairs={{0,8},{4,12},{8,0},{12,4},{16,24},{20,28},{24,16},{28,20},{1,9},{5... | collective-permute-start | bytes 1769480 | tf_op jit(solution)/shard_map/ppermute | solution.py:40
  511.0 16.4 %collective-permute-start.33 = (bf16[192,1536]{1,0:T(8,128)(2,1)}, bf16[192,1536]{1,0:T(8,128)(2,1)S(1)}, u32[]{:S(2)}, u32[]{:S(2)}) collective-permute-start(bf16[192,1536]{1,0:T(8,128)(2,1)} %get-tuple-element.266), channel_id=1, source_target_pairs={{0,16},{4,20},{8,24},{12,28},{16,0},{20,4},{24,8},{28,12},{1,17},{... | collective-permute-start | bytes 1769480 | tf_op jit(solution)/shard_map/ppermute | solution.py:40
  511.7 21.2 %collective-permute-start.20 = (f32[4,768]{1,0:T(4,128)S(1)}, f32[4,768]{1,0:T(4,128)S(1)}, u32[]{:S(2)}, u32[]{:S(2)}) collective-permute-start(f32[4,768]{1,0:T(4,128)S(1)} %pad_maximum_fusion.3), channel_id=1, source_target_pairs={{0,4},{4,0},{8,12},{12,8},{16,20},{20,16},{24,28},{28,24},{1,5},{5... | collective-permute-start | bytes 36872 | tf_op jit(solution)/shard_map/ppermute | solution.py:40
  515.8 35.9 %collective-permute-start.39 = (bf16[96,1536]{1,0:T(8,128)(2,1)}, bf16[96,1536]{1,0:T(8,128)(2,1)S(1)}, u32[]{:S(2)}, u32[]{:S(2)}) collective-permute-start(bf16[96,1536]{1,0:T(8,128)(2,1)} %get-tuple-element.284), channel_id=1, source_target_pairs={{0,16},{4,20},{8,24},{12,28},{16,0},{20,4},{24,8},{28,12},{1,17},{... | collective-permute-start | bytes 884744 | tf_op jit(solution)/shard_map/ppermute | solution.py:40
  517.3 36.6 %collective-permute-start.40 = (bf16[96,1536]{1,0:T(8,128)(2,1)}, bf16[96,1536]{1,0:T(8,128)(2,1)S(1)}, u32[]{:S(2)}, u32[]{:S(2)}) collective-permute-start(bf16[96,1536]{1,0:T(8,128)(2,1)} %get-tuple-element.286), channel_id=1, source_target_pairs={{0,8},{4,12},{8,0},{12,4},{16,24},{20,28},{24,16},{28,20},{1,9},{5... | collective-permute-start | bytes 884744 | tf_op jit(solution)/shard_map/ppermute | solution.py:40
  532.2 25.7 %collective-permute-start.34 = (bf16[96,1536]{1,0:T(8,128)(2,1)}, bf16[96,1536]{1,0:T(8,128)(2,1)S(1)}, u32[]{:S(2)}, u32[]{:S(2)}) collective-permute-start(bf16[96,1536]{1,0:T(8,128)(2,1)} %get-tuple-element.268), channel_id=1, source_target_pairs={{0,16},{4,20},{8,24},{12,28},{16,0},{20,4},{24,8},{28,12},{1,17},{... | collective-permute-start | bytes 884744 | tf_op jit(solution)/shard_map/ppermute | solution.py:40
  532.9 3.8 collective-permute-start.21
  536.7 3.7 collective-permute-start.22
  540.4 4.6 collective-permute-start.23
  545.0 12.5 %collective-permute-start.24 = (f32[4,768]{1,0:T(4,128)S(1)}, f32[4,768]{1,0:T(4,128)S(1)}, u32[]{:S(2)}, u32[]{:S(2)}) collective-permute-start(f32[4,768]{1,0:T(4,128)S(1)} %add.165), channel_id=1, source_target_pairs={{0,16},{4,20},{8,24},{12,28},{16,0},{20,4},{24,8},{28,12},{1,17},{... | collective-permute-start | bytes 36872 | tf_op jit(solution)/shard_map/ppermute | solution.py:40
  550.7 28.3 %collective-permute-start.44 = (bf16[96,1536]{1,0:T(8,128)(2,1)}, bf16[96,1536]{1,0:T(8,128)(2,1)S(1)}, u32[]{:S(2)}, u32[]{:S(2)}) collective-permute-start(bf16[96,1536]{1,0:T(8,128)(2,1)} %get-tuple-element.300), channel_id=1, source_target_pairs={{0,1},{1,0},{2,3},{3,2},{4,5},{5,4},{6,7},{7,6},{8,9},{9,8},{10,11... | collective-permute-start | bytes 884744 | tf_op jit(solution)/shard_map/ppermute | solution.py:40
  551.7 28.6 %collective-permute-start.45 = (bf16[96,1536]{1,0:T(8,128)(2,1)}, bf16[96,1536]{1,0:T(8,128)(2,1)S(1)}, u32[]{:S(2)}, u32[]{:S(2)}) collective-permute-start(bf16[96,1536]{1,0:T(8,128)(2,1)} %get-tuple-element.301), channel_id=1, source_target_pairs={{0,2},{1,3},{2,0},{3,1},{4,6},{5,7},{6,4},{7,5},{8,10},{9,11},{10,... | collective-permute-start | bytes 884744 | tf_op jit(solution)/shard_map/ppermute | solution.py:40
  553.8 26.5 %collective-permute-start.46 = (bf16[96,1536]{1,0:T(8,128)(2,1)}, bf16[96,1536]{1,0:T(8,128)(2,1)S(1)}, u32[]{:S(2)}, u32[]{:S(2)}) collective-permute-start(bf16[96,1536]{1,0:T(8,128)(2,1)} %get-tuple-element.302), channel_id=1, source_target_pairs={{0,3},{1,2},{2,1},{3,0},{4,7},{5,6},{6,5},{7,4},{8,11},{9,10},{10,... | collective-permute-start | bytes 884744 | tf_op jit(solution)/shard_map/ppermute | solution.py:40
  557.5 30.9 %collective-permute-start.41 = (bf16[96,768]{1,0:T(8,128)(2,1)}, bf16[96,768]{1,0:T(8,128)(2,1)S(1)}, u32[]{:S(2)}, u32[]{:S(2)}) collective-permute-start(bf16[96,768]{1,0:T(8,128)(2,1)} %get-tuple-element.288), channel_id=1, source_target_pairs={{0,1},{1,0},{2,3},{3,2},{4,5},{5,4},{6,7},{7,6},{8,9},{9,8},{10,11... | collective-permute-start | bytes 442376 | tf_op jit(solution)/shard_map/ppermute | solution.py:40
  557.9 16.2 %collective-permute-start.35 = (bf16[96,1536]{1,0:T(8,128)(2,1)S(1)}, bf16[96,1536]{1,0:T(8,128)(2,1)S(1)}, u32[]{:S(2)}, u32[]{:S(2)}) collective-permute-start(bf16[96,1536]{1,0:T(8,128)(2,1)S(1)} %copy-done.85), channel_id=1, source_target_pairs={{0,8},{4,12},{8,0},{12,4},{16,24},{20,28},{24,16},{28,20},{1,9},{5... | collective-permute-start | bytes 884744 | tf_op jit(solution)/shard_map/ppermute | solution.py:40
  574.2 29.8 %collective-permute-start.42 = (bf16[96,768]{1,0:T(8,128)(2,1)S(1)}, bf16[96,768]{1,0:T(8,128)(2,1)S(1)}, u32[]{:S(2)}, u32[]{:S(2)}) collective-permute-start(bf16[96,768]{1,0:T(8,128)(2,1)S(1)} %copy-done.87), channel_id=1, source_target_pairs={{0,2},{1,3},{2,0},{3,1},{4,6},{5,7},{6,4},{7,5},{8,10},{9,11},{10,... | collective-permute-start | bytes 442376 | tf_op jit(solution)/shard_map/ppermute | solution.py:40
  579.0 25.0 %collective-permute-start.43 = (bf16[96,768]{1,0:T(8,128)(2,1)S(1)}, bf16[96,768]{1,0:T(8,128)(2,1)S(1)}, u32[]{:S(2)}, u32[]{:S(2)}) collective-permute-start(bf16[96,768]{1,0:T(8,128)(2,1)S(1)} %copy-done.86), channel_id=1, source_target_pairs={{0,3},{1,2},{2,1},{3,0},{4,7},{5,6},{6,5},{7,4},{8,11},{9,10},{10,... | collective-permute-start | bytes 442376 | tf_op jit(solution)/shard_map/ppermute | solution.py:40
  580.3 26.4 %collective-permute-start.36 = (bf16[96,768]{1,0:T(8,128)(2,1)}, bf16[96,768]{1,0:T(8,128)(2,1)S(1)}, u32[]{:S(2)}, u32[]{:S(2)}) collective-permute-start(bf16[96,768]{1,0:T(8,128)(2,1)} %get-tuple-element.272), channel_id=1, source_target_pairs={{0,1},{1,0},{2,3},{3,2},{4,5},{5,4},{6,7},{7,6},{8,9},{9,8},{10,11... | collective-permute-start | bytes 442376 | tf_op jit(solution)/shard_map/ppermute | solution.py:40
  580.4 26.3 %collective-permute-start.37 = (bf16[96,768]{1,0:T(8,128)(2,1)}, bf16[96,768]{1,0:T(8,128)(2,1)S(1)}, u32[]{:S(2)}, u32[]{:S(2)}) collective-permute-start(bf16[96,768]{1,0:T(8,128)(2,1)} %get-tuple-element.273), channel_id=1, source_target_pairs={{0,2},{1,3},{2,0},{3,1},{4,6},{5,7},{6,4},{7,5},{8,10},{9,11},{10,... | collective-permute-start | bytes 442376 | tf_op jit(solution)/shard_map/ppermute | solution.py:40
  588.4 18.3 %collective-permute-start.38 = (bf16[96,768]{1,0:T(8,128)(2,1)}, bf16[96,768]{1,0:T(8,128)(2,1)S(1)}, u32[]{:S(2)}, u32[]{:S(2)}) collective-permute-start(bf16[96,768]{1,0:T(8,128)(2,1)} %get-tuple-element.274), channel_id=1, source_target_pairs={{0,3},{1,2},{2,1},{3,0},{4,7},{5,6},{6,5},{7,4},{8,11},{9,10},{10,... | collective-permute-start | bytes 442376 | tf_op jit(solution)/shard_map/ppermute | solution.py:40
  (87 other events, 814.1 us)

commit v4 on v3

--- a/solution.py
+++ b/solution.py
@@ -19,6 +19,7 @@
 CHUNK = 256
 HALF_D = D // 2
 VTILE = 512
+HTILE = 1024
 F32 = jnp.float32
 BF16 = jnp.bfloat16
 MESH_ID = pl.DeviceIdType.MESH
@@ -868,78 +869,69 @@
     by_shard(b_ref, (att[...],), send_ref, 576, D)
 
 
-def logits_kernel(vocab, rows_ref, table_ref, target_ref, logits_ref, stats_ref, m_ref, s_ref, p_ref):
+def logits_kernel(vocab, flat_ref, table_ref, target_ref, logits_ref, stats_ref):
     tile = pl.program_id(0)
-    count = rows_ref.shape[0]
 
     @pl.when(tile == 0)
     def _():
-        m_ref[...] = jnp.full_like(m_ref, 2 * NEG)
-        s_ref[...] = jnp.zeros_like(s_ref)
-        p_ref[...] = jnp.zeros_like(p_ref)
-
-    column = tile * VTILE + lax.broadcasted_iota(jnp.int32, (count, VTILE), 1)
-    logits = dot_nt(rows_ref[...], table_ref[...])
-    logits = jnp.where(column < vocab, logits, 2 * NEG)
+        row = lax.broadcasted_iota(jnp.int32, stats_ref.shape, 0)
+        stats_ref[...] = jnp.where(row == 0, 2 * NEG, 0.0)
+
+    logits = dot_nn(table_ref[...], flat_ref[...])
+    entry = tile * HTILE + lax.broadcasted_iota(jnp.int32, logits.shape, 0)
+    logits = jnp.where(entry < vocab, logits, 2 * NEG)
     logits_ref[...] = logits
-    old = m_ref[:, 0:1]
-    new = jnp.maximum(old, jnp.max(logits, axis=1, keepdims=True))
-    total = s_ref[:, 0:1] * jnp.exp(old - new) + jnp.sum(
-        jnp.exp(logits - new), axis=1, keepdims=True
+    old = stats_ref[0:1, :]
+    new = jnp.maximum(old, jnp.max(logits, axis=0, keepdims=True))
+    stats_ref[1:2, :] = stats_ref[1:2, :] * jnp.exp(old - new) + jnp.sum(
+        jnp.exp(logits - new), axis=0, keepdims=True
     )
-    hit = jnp.where(column == target_ref[...], logits, 0.0)
-    m_ref[...] = jnp.broadcast_to(new, m_ref.shape)
-    s_ref[...] = jnp.broadcast_to(total, s_ref.shape)
-    p_ref[...] += jnp.broadcast_to(jnp.sum(hit, axis=1, keepdims=True), p_ref.shape)
-
-    @pl.when(tile == pl.num_programs(0) - 1)
-    def _():
-        lane = lax.broadcasted_iota(jnp.int32, m_ref.shape, 1)
-        merged = jnp.where(lane == 0, m_ref[...], jnp.where(lane == 1, s_ref[...], p_ref[...]))
-        stats_ref[...] = merged.T[0:8, :]
-
-
-def head_logits(rows, table, target):
-    count = rows.shape[0]
+    stats_ref[0:1, :] = new
+    hit = jnp.where(entry == target_ref[...], logits, 0.0)
+    stats_ref[2:3, :] += jnp.sum(hit, axis=0, keepdims=True)
+
+
+def head_logits(flat, table, target):
+    count = flat.shape[1]
     vocab = table.shape[0]
-    tiles = pl.cdiv(vocab, VTILE)
+    tiles = pl.cdiv(vocab, HTILE)
     return pl.pallas_call(
         functools.partial(logits_kernel, vocab),
         grid=(tiles,),
-        out_shape=[whole((count, tiles * VTILE), F32), whole((8, count), F32)],
+        out_shape=[whole((tiles * HTILE, count), F32), whole((8, count), F32)],
         in_specs=[
-            pl.BlockSpec((count, D), lambda i: (0, 0)),
-            pl.BlockSpec((VTILE, D), lambda i: (i, 0)),
-            pl.BlockSpec((count, 1), lambda i: (0, 0)),
+            pl.BlockSpec((D, count), lambda i: (0, 0)),
+            pl.BlockSpec((HTILE, D), lambda i: (i, 0)),
+            pl.BlockSpec((1, count), lambda i: (0, 0)),
         ],
         out_specs=[
-            pl.BlockSpec((count, VTILE), lambda i: (0, i)),
+            pl.BlockSpec((HTILE, count), lambda i: (i, 0)),
             pl.BlockSpec((8, count), lambda i: (0, 0)),
         ],
-        scratch_shapes=[pltpu.VMEM((count, 128), F32)] * 3,
         cost_estimate=pl.CostEstimate(
             flops=2 * count * vocab * D, bytes_accessed=vocab * (2 * D + 4 * count), transcendentals=0
         ),
-        compiler_params=pltpu.CompilerParams(vmem_limit_bytes=VMEM_LIMIT),
-    )(rows, table, target)
+        compiler_params=pltpu.CompilerParams(vmem_limit_bytes=VMEM_LIMIT // 2),
+    )(flat, table, target)
 
 
 def grads_kernel(vocab, logits_ref, table_ref, target_ref, lse_ref, live_ref, g_ref, gf_ref, acc_ref):
     tile = pl.program_id(0)
-    count = logits_ref.shape[0]
 
     @pl.when(tile == 0)
     def _():
         acc_ref[...] = jnp.zeros_like(acc_ref)
 
-    column = tile * VTILE + lax.broadcasted_iota(jnp.int32, (count, VTILE), 1)
-    hit = jnp.where(column == target_ref[...], 1.0, 0.0)
+    entry = tile * HTILE + lax.broadcasted_iota(jnp.int32, logits_ref.shape, 0)
+    hit = jnp.where(entry == target_ref[...], 1.0, 0.0)
     grad = jnp.where(live_ref[...] > 0, jnp.exp(logits_ref[...] - lse_ref[...]) - hit, 0.0)
     grad = grad.astype(BF16)
     g_ref[...] = grad
-    entry = tile * VTILE + lax.broadcasted_iota(jnp.int32, (VTILE, D), 0)
+    entry = tile * HTILE + lax.broadcasted_iota(jnp.int32, (HTILE, D), 0)
     table = jnp.where(entry < vocab, table_ref[...], jnp.zeros_like(table_ref[...]))
-    acc_ref[...] += dot_nn(grad, table)
+    acc_ref[...] += lax.dot_general(
+        grad, table, (((0,), (0,)), ((), ())), preferred_element_type=F32
+    )
 
     @pl.when(tile == pl.num_programs(0) - 1)
     def _():
@@ -947,47 +939,47 @@
 
 
 def head_grads(logits, table, target, lse, live, dtype):
-    count = logits.shape[0]
+    count = logits.shape[1]
     vocab = table.shape[0]
-    tiles = pl.cdiv(vocab, VTILE)
-    column = pl.BlockSpec((count, 1), lambda i: (0, 0))
+    tiles = pl.cdiv(vocab, HTILE)
+    row = pl.BlockSpec((1, count), lambda i: (0, 0))
     return pl.pallas_call(
         functools.partial(grads_kernel, vocab),
         grid=(tiles,),
-        out_shape=[whole((count, tiles * VTILE), BF16), whole((count, D), dtype)],
+        out_shape=[whole((tiles * HTILE, count), BF16), whole((count, D), dtype)],
         in_specs=[
-            pl.BlockSpec((count, VTILE), lambda i: (0, i)),
-            pl.BlockSpec((VTILE, D), lambda i: (i, 0)),
-            column,
-            column,
-            column,
+            pl.BlockSpec((HTILE, count), lambda i: (i, 0)),
+            pl.BlockSpec((HTILE, D), lambda i: (i, 0)),
+            row,
+            row,
+            row,
         ],
         out_specs=[
-            pl.BlockSpec((count, VTILE), lambda i: (0, i)),
+            pl.BlockSpec((HTILE, count), lambda i: (i, 0)),
             pl.BlockSpec((count, D), lambda i: (0, 0)),
         ],
         scratch_shapes=[pltpu.VMEM((count, D), F32)],
         cost_estimate=pl.CostEstimate(
             flops=2 * count * vocab * D, bytes_accessed=vocab * (2 * D + 6 * count), transcendentals=0
         ),
-        compiler_params=pltpu.CompilerParams(vmem_limit_bytes=VMEM_LIMIT),
+        compiler_params=pltpu.CompilerParams(vmem_limit_bytes=VMEM_LIMIT // 2),
     )(logits, table, target, lse, live)
 
 
 def table_kernel(fm_a, fm_b, fs_a, fs_b, g_a, g_b, mine_ref, send_ref):
     first, second = g_a[...], g_b[...]
-    mine_ref[...] = dot_nn(fm_a[...], first) + dot_nn(fm_b[...], second)
-    send_ref[...] = (dot_nn(fs_a[...], first) + dot_nn(fs_b[...], second)).astype(BF16)
+    mine_ref[...] = dot_nt(fm_a[...], first) + dot_nt(fm_b[...], second)
+    send_ref[...] = (dot_nt(fs_a[...], first) + dot_nt(fs_b[...], second)).astype(BF16)
 
 
 def table_grads(flat_a, flat_b, g_a, g_b):
-    count, width = g_a.shape
+    width, count = g_a.shape
     left = pl.BlockSpec((HALF_D, count), lambda i: (0, 0))
-    right = pl.BlockSpec((count, VTILE), lambda i: (0, i))
-    out = pl.BlockSpec((HALF_D, VTILE), lambda i: (0, i))
+    right = pl.BlockSpec((HTILE, count), lambda i: (i, 0))
+    out = pl.BlockSpec((HALF_D, HTILE), lambda i: (0, i))
     return pl.pallas_call(
         table_kernel,
-        grid=(width // VTILE,),
+        grid=(width // HTILE,),
         out_shape=[whole((HALF_D, width), F32), whole((HALF_D, width), BF16)],
         in_specs=[left] * 4 + [right] * 2,
         out_specs=[out] * 2,
@@ -1075,11 +1067,11 @@
         live = position < jnp.repeat(target_len, TGT, total_repeat_length=4 * ROWS)
         live_blocks = live.astype(jnp.int32).reshape(4, ROWS)
         fin_1, fin_2, fin_3 = (swap(fin, "tensor", 4, j) for j in (1, 2, 3))
-        fin_a = jnp.concatenate([fin_2, fin_3], 0)
-        fin_b = jnp.concatenate([fin, fin_1], 0)
+        fin_a = jnp.concatenate([fin_2, fin_3], 0).T
+        fin_b = jnp.concatenate([fin, fin_1], 0).T
 
         def columns(by_block, order):
-            return jnp.concatenate([block(by_block, j) for j in order], 0)[:, None]
+            return jnp.concatenate([block(by_block, j) for j in order], 0)[None, :]
 
         tgt_a, tgt_b = columns(tgt_blocks, (2, 3)), columns(tgt_blocks, (0, 1))
         logits_b, stats_b = head_logits(fin_b, embed_table, tgt_b)
@@ -1108,8 +1100,7 @@
         gf_3 = swap(gf_a[ROWS:], "tensor", 4, 3)
         gf_1 = swap(gf_b[ROWS:].astype(BF16), "tensor", 4, 1)
 
-        def halves(rows):
-            flat = rows.T
+        def halves(flat):
             if not split:
                 return flat[:HALF_D], flat[HALF_D:]
             flat = flat.reshape(4, 2, 96, -1)

time: 618 us -> 566 us (0.916)
  Pallas kernels: 393 us -> 331 us
  waiting for transfers between devices: 71.3 us -> 92.4 us
    pallas_call x2, Pallas kernels: 69.9 us -> 26.7 us  [head_logits(): pl.pallas_call(functools.partial(logits_kernel, vocab), grid=(tiles,), ou...]
    ppermute x47, waiting for transfers between devices: 71.3 us -> 92.4 us  [swap(): return lax.ppermute(value, axis_name, [(i, i ^ bit) for i in range(size)])]
    pallas_call x2, Pallas kernels: 46 us -> 30.6 us  [head_grads(): pl.pallas_call(functools.partial(grads_kernel, vocab), grid=(tiles,), out...]
    unnamed x196 -> x177, local copies, waits for them, and re-layouts: 56.9 us -> 60.1 us
  transfers between devices with their start and end apart: 47 -> 47, of which waited for: 14 -> 15; matrix products, arithmetic and copies ran while one was open for 4% -> 3% of each run, Pallas kernels for 36% -> 33%
where the time goes in v4:
time: 566 us; the launch traced here: 559 us
  Pallas kernels  331 us (58%)
  waiting for transfers between devices  92.4 us (16%)
  local copies, waits for them, and re-layouts  71 us (13%)
  starting transfers between devices  52.3 us (9%)
  other arithmetic  10.5 us (2%)
    pallas_call x1, Pallas kernels, forward(): pl.pallas_call(functools.partial(forward_kernel, split), out_shape=outs,...  104 us
    ppermute x47, waiting for transfers between devices, swap(): return lax.ppermute(value, axis_name, [(i, i ^ bit) for i in range(size)])  92.4 us
    pallas_call x5, Pallas kernels, local_call(): pl.pallas_call(body, out_shape=outs, in_specs=[smem] + [vmem] * (len(args...  71.7 us
    unnamed x177, local copies, waits for them, and re-layouts  60.1 us
    pallas_call x8, Pallas kernels, fold_call(): pl.pallas_call(body, grid=(width // tile,), out_shape=outs, in_specs=in_s...  53.7 us
    ppermute x47, starting transfers between devices, swap(): return lax.ppermute(value, axis_name, [(i, i ^ bit) for i in range(size)])  52.3 us
    pallas_call x2, Pallas kernels, head_grads(): pl.pallas_call(functools.partial(grads_kernel, vocab), grid=(tiles,), out...  30.6 us
    pallas_call x2, Pallas kernels, head_logits(): pl.pallas_call(functools.partial(logits_kernel, vocab), grid=(tiles,), ou...  26.7 us
  transfers between devices with their start and end apart: 47, of which 15 were waited for; matrix products, arithmetic and copies ran while one was open for 3% of the time, Pallas kernels for 33%

profile of v4, /device:TPU:0, one launch (start us, length us, event | category | flops | bytes accessed | tf_op | source)
XLA Modules:
  0.0 559.4 jit_solution(761254378615496996)
XLA Ops:
  18.7 103.7 %shard_map.356 = (bf16[512,768]{1,0:T(8,128)(2,1)}, bf16[512,768]{1,0:T(8,128)(2,1)}, bf16[512,768]{1,0:T(8,128)(2,1)}, f32[16,512]{1,0:T(8,128)}, bf16[256,768]...) custom-call(s32[4]{0:T(128)} %pad_add_fusion.4.refs_0_.scal, ...), custom_call_target="tpu_custom_call" | custom-call | flops 80000000000 | bytes 60000000 | tf_op jit(solution)/shard_map/pallas_call | solution.py:648
  129.6 12.8 %collective-permute-done = bf16[256,768]{0,1:T(8,128)(2,1)S(1)} collective-permute-done((bf16[256,768]{0,1:T(8,128)(2,1)S(1)}, bf16[256,768]{0,1:T(8,128)(2,1)S(1)}, u32[]{:S(2)}, u32[]{:S(2)}) %collective-permute-start) | collective-permute-done | bytes 393248 | tf_op jit(solution)/shard_map/ppermute | solution.py:41
  142.5 12.7 %collective-permute-done.1 = bf16[256,768]{0,1:T(8,128)(2,1)S(1)} collective-permute-done((bf16[256,768]{0,1:T(8,128)(2,1)S(1)}, bf16[256,768]{0,1:T(8,128)(2,1)S(1)}, u32[]{:S(2)}, u32[]{:S(2)}) %collective-permute-start.1) | collective-permute-done | bytes 393248 | tf_op jit(solution)/shard_map/ppermute | solution.py:41
  155.2 4.5 copy-done
  159.7 13.4 %shard_map.357 = (f32[8192,512]{1,0:T(8,128)}, f32[8,512]{1,0:T(8,128)S(1)}) custom-call(bf16[768,512]{1,0:T(8,128)(2,1)S(1)} %get-tuple-element.339.flat_ref, bf16[8032,768]{1,0:T(8,128)(2,1)S(1)} %copy-done, s32[1,512]{1,0:T(1,128)S(1)} %bitcast.158), custom_call_target="tpu_custom_call" | custom-call | flops 6316621824 | bytes 28786688 | tf_op jit(solution)/shard_map/pallas_call | solution.py:898
  173.1 13.4 %shard_map.358 = (f32[8192,512]{1,0:T(8,128)}, f32[8,512]{1,0:T(8,128)S(1)}) custom-call(bf16[768,512]{1,0:T(8,128)(2,1)S(1)} %bitcast.156, bf16[8032,768]{1,0:T(8,128)(2,1)S(1)} %copy-done.1, s32[1,512]{1,0:T(1,128)S(1)} %bitcast.160), custom_call_target="tpu_custom_call" | custom-call | flops 6316621824 | bytes 28786688 | tf_op jit(solution)/shard_map/pallas_call | solution.py:898
  186.6 3.3 collective-permute-start.4
  193.3 2.3 collective-permute-done.5
  196.3 14.4 %shard_map.360 = (bf16[8192,512]{1,0:T(8,128)(2,1)S(1)}, bf16[512,768]{1,0:T(8,128)(2,1)S(1)}) custom-call(f32[8192,512]{1,0:T(8,128)} %get-tuple-element.186.logits_ref, bf16[8032,768]{1,0:T(8,128)(2,1)S(1)} %copy-done.1, s32[1,512]{1,0:T(1,128)S(1)} %bitcast.161, f32[1,512]{1,0:T(1,128)S(1)} %bitcast.163, s32[1,512]{1,0:T(1,128)S(1)} %bitcast.165), custom_call_target="tpu_custom_call" | custom-call | flops 6316621824 | bytes 37011456 | tf_op jit(solution)/shard_map/pallas_call | solution.py:946
  210.8 16.2 %shard_map.359 = (bf16[8192,512]{1,0:T(8,128)(2,1)S(1)}, f32[512,768]{1,0:T(8,128)S(1)}) custom-call(f32[8192,512]{1,0:T(8,128)} %get-tuple-element.183.logits_ref, bf16[8032,768]{1,0:T(8,128)(2,1)S(1)} %copy-done.1, s32[1,512]{1,0:T(1,128)S(1)} %bitcast.159, f32[1,512]{1,0:T(1,128)S(1)} %bitcast.162, s32[1,512]{1,0:T(1,128)S(1)} %bitcast.164), custom_call_target="tpu_custom_call" | custom-call | flops 6316621824 | bytes 37011456 | tf_op jit(solution)/shard_map/pallas_call | solution.py:946
  227.1 3.2 copy-done.15
  230.5 2.6 collective-permute-start.8
  233.1 17.9 %shard_map.361 = (f32[384,8192]{1,0:T(8,128)}, bf16[384,8192]{1,0:T(8,128)(2,1)}) custom-call(bf16[384,512]{1,0:T(8,128)(2,1)} %bitcast.169, bf16[384,512]{1,0:T(8,128)(2,1)} %bitcast.168, bf16[384,512]{1,0:T(8,128)(2,1)} %bitcast.170, bf16[384,512]{1,0:T(8,128)(2,1)} %bitcast.167, bf16[8192,512]{1,0:T(8,128)(2,1)} %copy-done.14, bf16[8192,512]{1,0:T(8,128)(2,1)} %copy-done.15), custom_call_target="tpu_custom_call" | custom-call | flops 12884901888 | bytes 35651584 | tf_op jit(solution)/shard_map/pallas_call | solution.py:980
  251.2 18.8 %shard_map.362 = (f32[384,6144]{1,0:T(8,128)}, bf16[384,6144]{1,0:T(8,128)(2,1)}, f32[256,768]{1,0:T(8,128)S(1)}, bf16[256,768]{1,0:T(8,128)(2,1)S(1)}, bf16[256...) custom-call(s32[4]{0:T(128)S(1)} %copy-done.13, f32[256,768]{1,0:T(8,128)S(1)} %slice.110.gf_own, ...), custom_call_target="tpu_custom_call" | custom-call | flops 10000000000 | bytes 30699536 | tf_op jit(solution)/shard_map/pallas_call | solution.py:355
  273.1 5.3 collective-permute-done.15.got_a.got_b
  278.4 8.8 %shard_map.366 = (f32[192,3072]{1,0:T(8,128)}, bf16[192,3072]{1,0:T(8,128)(2,1)}, f32[192,3072]{1,0:T(8,128)}, bf16[192,3072]{1,0:T(8,128)(2,1)}) custom-call(s32[3]{0:T(128)} %pad_add_fusion.5.xyz, f32[384,6144]{1,0:T(8,128)} %get-tuple-element.228.mine_a.mine_b, bf16[384,6144]{1,0:T(8,128)(2,1)} %collective-permute-done.15.got_a.got_b, ...), custom_call_target="tpu_custom_call" | custom-call | bytes 21233664 | tf_op jit(solution)/shard_map/pallas_call | solution.py:144
  287.2 11.5 %shard_map.363 = (f32[192,4096]{1,0:T(8,128)}, bf16[192,4096]{1,0:T(8,128)(2,1)}, f32[192,4096]{1,0:T(8,128)}, bf16[192,4096]{1,0:T(8,128)(2,1)}) custom-call(s32[3]{0:T(128)} %pad_add_fusion.5.xyz, f32[384,8192]{1,0:T(8,128)} %get-tuple-element.206.mine_a.mine_b, bf16[384,8192]{1,0:T(8,128)(2,1)} %collective-permute-done.9.got_a.got_b, ...), custom_call_target="tpu_custom_call" | custom-call | bytes 28311552 | tf_op jit(solution)/shard_map/pallas_call | solution.py:144
  306.4 24.2 %shard_map.364 = (bf16[1024,768]{1,0:T(8,128)(2,1)S(1)}, bf16[1024,768]{1,0:T(8,128)(2,1)S(1)}, f32[768,256]{1,0:T(8,128)S(1)}, bf16[768,256]{1,0:T(8,128)(2,1)}) custom-call(s32[4]{0:T(128)S(1)} %copy-done.13, bf16[512,768]{1,0:T(8,128)(2,1)S(1)} %copy-done.45, bf16[1024,768]{1,0:T(8,128)(2,1)S(1)} %copy-done.42, bf16[1024,768]{1,0:T(8,128)(2,1)S(1)} %copy-done.43, ...), custom_call_target="tpu_custom_call" | custom-call | flops 20000000000 | bytes 9109520 | tf_op jit(solution)/shard_map/pallas_call | solution.py:355
  333.0 2.7 collective-permute-done.12.got_a
  335.9 8.1 %shard_map.365 = (f32[96,4096]{1,0:T(8,128)}, bf16[96,4096]{1,0:T(8,128)(2,1)}, f32[96,4096]{1,0:T(8,128)}, bf16[96,4096]{1,0:T(8,128)(2,1)}) custom-call(s32[3]{0:T(128)} %pad_add_fusion.5.xyz, f32[192,4096]{1,0:T(8,128)} %get-tuple-element.212.mine_a, bf16[192,4096]{1,0:T(8,128)(2,1)} %collective-permute-done.12.got_a, ...), custom_call_target="tpu_custom_call" | custom-call | bytes 14155776 | tf_op jit(solution)/shard_map/pallas_call | solution.py:144
  350.9 6.5 %shard_map.367 = (f32[1024,768]{1,0:T(8,128)}, f32[384,1536]{1,0:T(8,128)S(1)}, bf16[384,1536]{1,0:T(8,128)(2,1)S(1)}) custom-call(s32[4]{0:T(128)S(1)} %copy-done.13, bf16[1024,768]{1,0:T(8,128)(2,1)S(1)} %copy-done.29, bf16[1024,768]{1,0:T(8,128)(2,1)S(1)} %copy-done.31, bf16[1024,768]{1,0:T(8,128)(2,1)S(1)} %copy-done.16, ...), custom_call_target="tpu_custom_call" | custom-call | flops 5000000000 | bytes 13762576 | tf_op jit(solution)/shard_map/pallas_call | solution.py:355
  357.5 5.2 shard_map.368
  362.7 2.2 copy-done.2
  369.5 26.3 %collective-permute-done.16.got_a = bf16[192,3072]{1,0:T(8,128)(2,1)S(1)} collective-permute-done((bf16[192,3072]{1,0:T(8,128)(2,1)S(1)}, bf16[192,3072]{1,0:T(8,128)(2,1)S(1)}, u32[]{:S(2)}, u32[]{:S(2)}) %collective-permute-start.16) | collective-permute-done | bytes 1179680 | tf_op jit(solution)/shard_map/ppermute | solution.py:41
  398.0 6.2 %shard_map.369 = (f32[96,3072]{1,0:T(8,128)}, bf16[96,3072]{1,0:T(8,128)(2,1)}, f32[96,3072]{1,0:T(8,128)}, bf16[96,3072]{1,0:T(8,128)(2,1)}) custom-call(s32[3]{0:T(128)} %pad_add_fusion.5.xyz, f32[192,3072]{1,0:T(8,128)} %get-tuple-element.239.mine_a, bf16[192,3072]{1,0:T(8,128)(2,1)} %copy-done.49, f32[192,3072]{1,0:T(8,128)} %get-tuple-element.240.mine_b, ...), custom_call_target="tpu_custom_call" | custom-call | bytes 10616832 | tf_op jit(solution)/shard_map/pallas_call | solution.py:144
  408.4 5.6 %shard_map.370 = (f32[192,1536]{1,0:T(8,128)}, bf16[192,1536]{1,0:T(8,128)(2,1)}, f32[192,1536]{1,0:T(8,128)}, bf16[192,1536]{1,0:T(8,128)(2,1)}) custom-call(s32[3]{0:T(128)} %pad_add_fusion.5.xyz, f32[384,3072]{1,0:T(8,128)} %copy-done.2, bf16[384,3072]{1,0:T(8,128)(2,1)} %collective-permute-done.18.got_a.got_b, f32[384,3072]{1,0:T(8,128)} %copy-done.2, ...), custom_call_target="tpu_custom_call" | custom-call | bytes 10616832 | tf_op jit(solution)/shard_map/pallas_call | solution.py:144
  414.0 6.9 %collective-permute-done.27.got_a = bf16[96,3072]{1,0:T(8,128)(2,1)} collective-permute-done((bf16[96,3072]{1,0:T(8,128)(2,1)}, bf16[96,3072]{1,0:T(8,128)(2,1)}, u32[]{:S(2)}, u32[]{:S(2)}) %collective-permute-start.27) | collective-permute-done | bytes 589856 | tf_op jit(solution)/shard_map/ppermute | solution.py:41
  431.1 16.9 %shard_map.371 = (f32[384,3072]{1,0:T(8,128)S(1)}, bf16[384,3072]{1,0:T(8,128)(2,1)S(1)}, f32[256,768]{1,0:T(8,128)}, f32[1,768]{1,0:T(1,128)S(1)}) custom-call(s32[4]{0:T(128)S(1)} %copy-done.13, bf16[512,768]{1,0:T(8,128)(2,1)S(1)} %copy-done.39, bf16[512,768]{1,0:T(8,128)(2,1)S(1)} %copy-done.40, bf16[512,768]{1,0:T(8,128)(2,1)S(1)} %copy-done.41, ...), custom_call_target="tpu_custom_call" | custom-call | flops 12000000000 | bytes 16554000 | tf_op jit(solution)/shard_map/pallas_call | solution.py:355
  448.0 2.2 copy-done.3
  451.2 3.7 collective-permute-done.31.got_a.got_b
  455.0 5.4 shard_map.372
  462.5 4.0 shard_map.376
  468.7 8.1 %collective-permute-done.32.got_a = bf16[192,1536]{1,0:T(8,128)(2,1)S(1)} collective-permute-done((bf16[192,1536]{1,0:T(8,128)(2,1)}, bf16[192,1536]{1,0:T(8,128)(2,1)S(1)}, u32[]{:S(2)}, u32[]{:S(2)}) %collective-permute-start.32) | collective-permute-done | bytes 589856 | tf_op jit(solution)/shard_map/ppermute | solution.py:41
  478.5 4.0 shard_map.373
  484.8 2.8 collective-permute-done.21
  488.3 3.0 collective-permute-done.22
  492.2 3.6 collective-permute-done.23
  497.4 3.4 shard_map.379
  502.9 2.2 collective-permute-start.46
  505.2 2.4 shard_map.377
  511.6 6.3 %shard_map.381 = f32[4096,96]{1,0:T(8,128)} custom-call(f32[96,4096]{1,0:T(8,128)} %get-tuple-element.306.mine, bf16[96,4096]{1,0:T(8,128)(2,1)} %collective-permute-done.25.got), custom_call_target="tpu_custom_call" | custom-call | tf_op jit(solution)/shard_map/pallas_call | solution.py:262
  517.8 6.4 %shard_map.382 = f32[3936,96]{1,0:T(8,128)} custom-call(f32[96,4096]{1,0:T(8,128)} %get-tuple-element.308.mine, bf16[96,4096]{1,0:T(8,128)(2,1)} %collective-permute-done.26.got), custom_call_target="tpu_custom_call" | custom-call | tf_op jit(solution)/shard_map/pallas_call | solution.py:262
  526.1 2.4 shard_map.374
  528.5 2.5 collective-permute-start.43
  531.1 6.9 %collective-permute-start.37 = (bf16[96,768]{1,0:T(8,128)(2,1)}, bf16[96,768]{1,0:T(8,128)(2,1)}, u32[]{:S(2)}, u32[]{:S(2)}) collective-permute-start(bf16[96,768]{1,0:T(8,128)(2,1)} %get-tuple-element.273), channel_id=1, source_target_pairs={{0,2},{1,3},{2,0},{3,1},{4,6},{5,7},{6,4},{7,5},{8,10},{9,11},{10,... | collective-permute-start | bytes 442376 | tf_op jit(solution)/shard_map/ppermute | solution.py:41
  539.8 3.9 pad_maximum_fusion
  543.7 5.2 copy.63
  549.0 2.3 shard_map.380
  (295 shorter events, 101.2 us)
Async XLA Ops:
  18.7 109.4 %copy-start.75 = (pred[1024]{0:T(1024)(128)(4,1)S(1)}, pred[1024]{0:T(1024)(128)(4,1)}, u32[]{:S(2)}) copy-start(pred[1024]{0:T(1024)(128)(4,1)} %constant.232) | copy-start | bytes 3076
  123.7 18.7 %collective-permute-start = (bf16[256,768]{0,1:T(8,128)(2,1)S(1)}, bf16[256,768]{0,1:T(8,128)(2,1)S(1)}, u32[]{:S(2)}, u32[]{:S(2)}) collective-permute-start(bf16[256,768]{0,1:T(8,128)(2,1)S(1)} %copy.48), channel_id=1, source_target_pairs={{0,1},{1,0},{2,3},{3,2},{4,5},{5,4},{6,7},{7,6},{8,9},{9,8},{10,11... | collective-permute-start | bytes 1179656 | tf_op jit(solution)/shard_map/ppermute | solution.py:41
  125.3 29.8 %collective-permute-start.1 = (bf16[256,768]{0,1:T(8,128)(2,1)S(1)}, bf16[256,768]{0,1:T(8,128)(2,1)S(1)}, u32[]{:S(2)}, u32[]{:S(2)}) collective-permute-start(bf16[256,768]{0,1:T(8,128)(2,1)S(1)} %copy.48), channel_id=1, source_target_pairs={{0,2},{1,3},{2,0},{3,1},{4,6},{5,7},{6,4},{7,5},{8,10},{9,11},{10,... | collective-permute-start | bytes 1179656 | tf_op jit(solution)/shard_map/ppermute | solution.py:41
  126.7 46.3 %collective-permute-start.2 = (bf16[256,768]{0,1:T(8,128)(2,1)S(1)}, bf16[256,768]{0,1:T(8,128)(2,1)S(1)}, u32[]{:S(2)}, u32[]{:S(2)}) collective-permute-start(bf16[256,768]{0,1:T(8,128)(2,1)S(1)} %copy.48), channel_id=1, source_target_pairs={{0,3},{1,2},{2,1},{3,0},{4,7},{5,6},{6,5},{7,4},{8,11},{9,10},{10,... | collective-permute-start | bytes 1179656 | tf_op jit(solution)/shard_map/ppermute | solution.py:41
  186.5 5.6 %collective-permute-start.3 = (f32[4,8,256]{2,0,1:T(4,128)S(1)}, f32[4,8,256]{2,0,1:T(4,128)S(1)}, u32[]{:S(2)}, u32[]{:S(2)}) collective-permute-start(f32[4,8,256]{2,0,1:T(4,128)S(1)} %copy.51), channel_id=1, source_target_pairs={{0,1},{1,0},{2,3},{3,2},{4,5},{5,4},{6,7},{7,6},{8,9},{9,8},{10,11... | collective-permute-start | bytes 98312 | tf_op jit(solution)/shard_map/ppermute | solution.py:41
  186.6 6.2 %collective-permute-start.4 = (f32[4,8,256]{2,0,1:T(4,128)S(1)}, f32[4,8,256]{2,0,1:T(4,128)S(1)}, u32[]{:S(2)}, u32[]{:S(2)}) collective-permute-start(f32[4,8,256]{2,0,1:T(4,128)S(1)} %copy.51), channel_id=1, source_target_pairs={{0,2},{1,3},{2,0},{3,1},{4,6},{5,7},{6,4},{7,5},{8,10},{9,11},{10,... | collective-permute-start | bytes 98312 | tf_op jit(solution)/shard_map/ppermute | solution.py:41
  189.9 5.7 %collective-permute-start.5 = (f32[4,8,256]{2,1,0:T(8,128)S(1)}, f32[4,8,256]{2,1,0:T(8,128)S(1)}, u32[]{:S(2)}, u32[]{:S(2)}) collective-permute-start(f32[4,8,256]{2,1,0:T(8,128)S(1)} %pad_maximum_fusion.3), channel_id=1, source_target_pairs={{0,3},{1,2},{2,1},{3,0},{4,7},{5,6},{6,5},{7,4},{8,11},{9,10},{10,... | collective-permute-start | bytes 98312 | tf_op jit(solution)/shard_map/ppermute | solution.py:41
  210.7 19.6 %collective-permute-start.6 = (bf16[256,768]{1,0:T(8,128)(2,1)S(1)}, bf16[256,768]{1,0:T(8,128)(2,1)S(1)}, u32[]{:S(2)}, u32[]{:S(2)}) collective-permute-start(bf16[256,768]{1,0:T(8,128)(2,1)S(1)} %slice.109), channel_id=1, source_target_pairs={{0,2},{1,3},{2,0},{3,1},{4,6},{5,7},{6,4},{7,5},{8,10},{9,11},{10,... | collective-permute-start | bytes 1179656 | tf_op jit(solution)/shard_map/ppermute | solution.py:41
  230.4 20.6 %collective-permute-start.7 = (bf16[256,768]{1,0:T(8,128)(2,1)S(1)}, bf16[256,768]{1,0:T(8,128)(2,1)S(1)}, u32[]{:S(2)}, u32[]{:S(2)}) collective-permute-start(bf16[256,768]{1,0:T(8,128)(2,1)S(1)} %slice.164), channel_id=1, source_target_pairs={{0,1},{1,0},{2,3},{3,2},{4,5},{5,4},{6,7},{7,6},{8,9},{9,8},{10,11... | collective-permute-start | bytes 1179656 | tf_op jit(solution)/shard_map/ppermute | solution.py:41
  230.5 20.5 %collective-permute-start.8 = (bf16[256,768]{1,0:T(8,128)(2,1)S(1)}, bf16[256,768]{1,0:T(8,128)(2,1)S(1)}, u32[]{:S(2)}, u32[]{:S(2)}) collective-permute-start(bf16[256,768]{1,0:T(8,128)(2,1)S(1)} %slice.112), channel_id=1, source_target_pairs={{0,3},{1,2},{2,1},{3,0},{4,7},{5,6},{6,5},{7,4},{8,11},{9,10},{10,... | collective-permute-start | bytes 1179656 | tf_op jit(solution)/shard_map/ppermute | solution.py:41
  251.0 36.2 %collective-permute-start.9 = (bf16[384,8192]{1,0:T(8,128)(2,1)}, bf16[384,8192]{1,0:T(8,128)(2,1)}, u32[]{:S(2)}, u32[]{:S(2)}) collective-permute-start(bf16[384,8192]{1,0:T(8,128)(2,1)} %get-tuple-element.194), channel_id=1, source_target_pairs={{0,4},{4,0},{8,12},{12,8},{16,20},{20,16},{24,28},{28,24},{1,5},{5... | collective-permute-start | bytes 18874376 | tf_op jit(solution)/shard_map/ppermute | solution.py:41
  270.0 8.4 %collective-permute-start.15 = (bf16[384,6144]{1,0:T(8,128)(2,1)}, bf16[384,6144]{1,0:T(8,128)(2,1)}, u32[]{:S(2)}, u32[]{:S(2)}) collective-permute-start(bf16[384,6144]{1,0:T(8,128)(2,1)} %get-tuple-element.229), channel_id=1, source_target_pairs={{0,4},{4,0},{8,12},{12,8},{16,20},{20,16},{24,28},{28,24},{1,5},{5... | collective-permute-start | bytes 14155784 | tf_op jit(solution)/shard_map/ppermute | solution.py:41
  270.5 30.2 %collective-permute-start.10 = (bf16[256,768]{1,0:T(8,128)(2,1)S(1)}, bf16[256,768]{1,0:T(8,128)(2,1)S(1)}, u32[]{:S(2)}, u32[]{:S(2)}) collective-permute-start(bf16[256,768]{1,0:T(8,128)(2,1)S(1)} %get-tuple-element.209.g_own), channel_id=1, source_target_pairs={{0,1},{1,0},{2,3},{3,2},{4,5},{5,4},{6,7},{7,6},{8,9},{9,8},{10,11... | collective-permute-start | bytes 1179656 | tf_op jit(solution)/shard_map/ppermute | solution.py:41
  270.5 30.2 %collective-permute-start.11 = (f32[16,256]{1,0:T(8,128)S(1)}, f32[16,256]{1,0:T(8,128)S(1)}, u32[]{:S(2)}, u32[]{:S(2)}) collective-permute-start(f32[16,256]{1,0:T(8,128)S(1)} %get-tuple-element.210.dot_own), channel_id=1, source_target_pairs={{0,1},{1,0},{2,3},{3,2},{4,5},{5,4},{6,7},{7,6},{8,9},{9,8},{10,11... | collective-permute-start | bytes 49160 | tf_op jit(solution)/shard_map/ppermute | solution.py:41
  298.7 37.0 %collective-permute-start.12 = (bf16[192,4096]{1,0:T(8,128)(2,1)}, bf16[192,4096]{1,0:T(8,128)(2,1)}, u32[]{:S(2)}, u32[]{:S(2)}) collective-permute-start(bf16[192,4096]{1,0:T(8,128)(2,1)} %get-tuple-element.207), channel_id=1, source_target_pairs={{0,8},{4,12},{8,0},{12,4},{16,24},{20,28},{24,16},{28,20},{1,9},{5... | collective-permute-start | bytes 4718600 | tf_op jit(solution)/shard_map/ppermute | solution.py:41
  299.2 36.7 %collective-permute-start.13 = (bf16[192,4096]{1,0:T(8,128)(2,1)}, bf16[192,4096]{1,0:T(8,128)(2,1)}, u32[]{:S(2)}, u32[]{:S(2)}) collective-permute-start(bf16[192,4096]{1,0:T(8,128)(2,1)} %get-tuple-element.208), channel_id=1, source_target_pairs={{0,16},{4,20},{8,24},{12,28},{16,0},{20,4},{24,8},{28,12},{1,17},{... | collective-permute-start | bytes 4718600 | tf_op jit(solution)/shard_map/ppermute | solution.py:41
  333.0 24.4 %collective-permute-start.14 = (bf16[768,256]{1,0:T(8,128)(2,1)}, bf16[768,256]{1,0:T(8,128)(2,1)S(1)}, u32[]{:S(2)}, u32[]{:S(2)}) collective-permute-start(bf16[768,256]{1,0:T(8,128)(2,1)} %get-tuple-element.220), channel_id=1, source_target_pairs={{0,1},{1,0},{2,3},{3,2},{4,5},{5,4},{6,7},{7,6},{8,9},{9,8},{10,11... | collective-permute-start | bytes 1179656 | tf_op jit(solution)/shard_map/ppermute | solution.py:41
  367.4 39.7 %collective-permute-start.18 = (bf16[384,3072]{1,0:T(8,128)(2,1)}, bf16[384,3072]{1,0:T(8,128)(2,1)}, u32[]{:S(2)}, u32[]{:S(2)}) collective-permute-start(bf16[384,3072]{1,0:T(8,128)(2,1)} %get-tuple-element.244), channel_id=1, source_target_pairs={{0,4},{4,0},{8,12},{12,8},{16,20},{20,16},{24,28},{28,24},{1,5},{5... | collective-permute-start | bytes 7077896 | tf_op jit(solution)/shard_map/ppermute | solution.py:41
  367.4 28.4 %collective-permute-start.16 = (bf16[192,3072]{1,0:T(8,128)(2,1)S(1)}, bf16[192,3072]{1,0:T(8,128)(2,1)S(1)}, u32[]{:S(2)}, u32[]{:S(2)}) collective-permute-start(bf16[192,3072]{1,0:T(8,128)(2,1)S(1)} %copy-done.78), channel_id=1, source_target_pairs={{0,8},{4,12},{8,0},{12,4},{16,24},{20,28},{24,16},{28,20},{1,9},{5... | collective-permute-start | bytes 3538952 | tf_op jit(solution)/shard_map/ppermute | solution.py:41
  368.9 28.1 %collective-permute-start.17 = (bf16[192,3072]{1,0:T(8,128)(2,1)S(1)}, bf16[192,3072]{1,0:T(8,128)(2,1)S(1)}, u32[]{:S(2)}, u32[]{:S(2)}) collective-permute-start(bf16[192,3072]{1,0:T(8,128)(2,1)S(1)} %copy-done.77), channel_id=1, source_target_pairs={{0,16},{4,20},{8,24},{12,28},{16,0},{20,4},{24,8},{28,12},{1,17},{... | collective-permute-start | bytes 3538952 | tf_op jit(solution)/shard_map/ppermute | solution.py:41
  404.3 16.6 %collective-permute-start.27 = (bf16[96,3072]{1,0:T(8,128)(2,1)}, bf16[96,3072]{1,0:T(8,128)(2,1)}, u32[]{:S(2)}, u32[]{:S(2)}) collective-permute-start(bf16[96,3072]{1,0:T(8,128)(2,1)} %get-tuple-element.241), channel_id=1, source_target_pairs={{0,16},{4,20},{8,24},{12,28},{16,0},{20,4},{24,8},{28,12},{1,17},{... | collective-permute-start | bytes 1769480 | tf_op jit(solution)/shard_map/ppermute | solution.py:41
  405.0 16.6 %collective-permute-start.19 = (bf16[256,768]{1,0:T(8,128)(2,1)S(1)}, bf16[256,768]{1,0:T(8,128)(2,1)S(1)}, u32[]{:S(2)}, u32[]{:S(2)}) collective-permute-start(bf16[256,768]{1,0:T(8,128)(2,1)S(1)} %copy-done.25), channel_id=1, source_target_pairs={{0,1},{1,0},{2,3},{3,2},{4,5},{5,4},{6,7},{7,6},{8,9},{9,8},{10,11... | collective-permute-start | bytes 1179656 | tf_op jit(solution)/shard_map/ppermute | solution.py:41
  405.0 45.1 %collective-permute-start.28 = (bf16[96,3072]{1,0:T(8,128)(2,1)}, bf16[96,3072]{1,0:T(8,128)(2,1)}, u32[]{:S(2)}, u32[]{:S(2)}) collective-permute-start(bf16[96,3072]{1,0:T(8,128)(2,1)} %get-tuple-element.242), channel_id=1, source_target_pairs={{0,8},{4,12},{8,0},{12,4},{16,24},{20,28},{24,16},{28,20},{1,9},{5... | collective-permute-start | bytes 1769480 | tf_op jit(solution)/shard_map/ppermute | solution.py:41
  406.3 43.9 %collective-permute-start.25 = (bf16[96,4096]{1,0:T(8,128)(2,1)}, bf16[96,4096]{1,0:T(8,128)(2,1)}, u32[]{:S(2)}, u32[]{:S(2)}) collective-permute-start(bf16[96,4096]{1,0:T(8,128)(2,1)} %get-tuple-element.217), channel_id=1, source_target_pairs={{0,16},{4,20},{8,24},{12,28},{16,0},{20,4},{24,8},{28,12},{1,17},{... | collective-permute-start | bytes 2359304 | tf_op jit(solution)/shard_map/ppermute | solution.py:41
  407.1 43.1 %collective-permute-start.26 = (bf16[96,4096]{1,0:T(8,128)(2,1)}, bf16[96,4096]{1,0:T(8,128)(2,1)}, u32[]{:S(2)}, u32[]{:S(2)}) collective-permute-start(bf16[96,4096]{1,0:T(8,128)(2,1)} %get-tuple-element.218), channel_id=1, source_target_pairs={{0,8},{4,12},{8,0},{12,4},{16,24},{20,28},{24,16},{28,20},{1,9},{5... | collective-permute-start | bytes 2359304 | tf_op jit(solution)/shard_map/ppermute | solution.py:41
  420.9 29.3 %collective-permute-start.29 = (bf16[192,1536]{1,0:T(8,128)(2,1)}, bf16[192,1536]{1,0:T(8,128)(2,1)S(1)}, u32[]{:S(2)}, u32[]{:S(2)}) collective-permute-start(bf16[192,1536]{1,0:T(8,128)(2,1)} %get-tuple-element.245), channel_id=1, source_target_pairs={{0,8},{4,12},{8,0},{12,4},{16,24},{20,28},{24,16},{28,20},{1,9},{5... | collective-permute-start | bytes 1769480 | tf_op jit(solution)/shard_map/ppermute | solution.py:41
  421.6 28.6 %collective-permute-start.30 = (bf16[192,1536]{1,0:T(8,128)(2,1)}, bf16[192,1536]{1,0:T(8,128)(2,1)S(1)}, u32[]{:S(2)}, u32[]{:S(2)}) collective-permute-start(bf16[192,1536]{1,0:T(8,128)(2,1)} %get-tuple-element.246), channel_id=1, source_target_pairs={{0,16},{4,20},{8,24},{12,28},{16,0},{20,4},{24,8},{28,12},{1,17},{... | collective-permute-start | bytes 1769480 | tf_op jit(solution)/shard_map/ppermute | solution.py:41
  450.2 4.7 collective-permute-start.31
  460.4 16.4 %collective-permute-start.32 = (bf16[192,1536]{1,0:T(8,128)(2,1)}, bf16[192,1536]{1,0:T(8,128)(2,1)S(1)}, u32[]{:S(2)}, u32[]{:S(2)}) collective-permute-start(bf16[192,1536]{1,0:T(8,128)(2,1)} %get-tuple-element.264), channel_id=1, source_target_pairs={{0,8},{4,12},{8,0},{12,4},{16,24},{20,28},{24,16},{28,20},{1,9},{5... | collective-permute-start | bytes 1769480 | tf_op jit(solution)/shard_map/ppermute | solution.py:41
  461.1 16.4 %collective-permute-start.33 = (bf16[192,1536]{1,0:T(8,128)(2,1)}, bf16[192,1536]{1,0:T(8,128)(2,1)S(1)}, u32[]{:S(2)}, u32[]{:S(2)}) collective-permute-start(bf16[192,1536]{1,0:T(8,128)(2,1)} %get-tuple-element.266), channel_id=1, source_target_pairs={{0,16},{4,20},{8,24},{12,28},{16,0},{20,4},{24,8},{28,12},{1,17},{... | collective-permute-start | bytes 1769480 | tf_op jit(solution)/shard_map/ppermute | solution.py:41
  462.5 21.3 %collective-permute-start.20 = (f32[4,768]{1,0:T(4,128)S(1)}, f32[4,768]{1,0:T(4,128)S(1)}, u32[]{:S(2)}, u32[]{:S(2)}) collective-permute-start(f32[4,768]{1,0:T(4,128)S(1)} %pad_maximum_fusion.4), channel_id=1, source_target_pairs={{0,4},{4,0},{8,12},{12,8},{16,20},{20,16},{24,28},{28,24},{1,5},{5... | collective-permute-start | bytes 36872 | tf_op jit(solution)/shard_map/ppermute | solution.py:41
  466.6 35.3 %collective-permute-start.39 = (bf16[96,1536]{1,0:T(8,128)(2,1)}, bf16[96,1536]{1,0:T(8,128)(2,1)S(1)}, u32[]{:S(2)}, u32[]{:S(2)}) collective-permute-start(bf16[96,1536]{1,0:T(8,128)(2,1)} %get-tuple-element.284), channel_id=1, source_target_pairs={{0,16},{4,20},{8,24},{12,28},{16,0},{20,4},{24,8},{28,12},{1,17},{... | collective-permute-start | bytes 884744 | tf_op jit(solution)/shard_map/ppermute | solution.py:41
  467.4 35.5 %collective-permute-start.40 = (bf16[96,1536]{1,0:T(8,128)(2,1)}, bf16[96,1536]{1,0:T(8,128)(2,1)S(1)}, u32[]{:S(2)}, u32[]{:S(2)}) collective-permute-start(bf16[96,1536]{1,0:T(8,128)(2,1)} %get-tuple-element.286), channel_id=1, source_target_pairs={{0,8},{4,12},{8,0},{12,4},{16,24},{20,28},{24,16},{28,20},{1,9},{5... | collective-permute-start | bytes 884744 | tf_op jit(solution)/shard_map/ppermute | solution.py:41
  482.4 25.5 %collective-permute-start.34 = (bf16[96,1536]{1,0:T(8,128)(2,1)}, bf16[96,1536]{1,0:T(8,128)(2,1)S(1)}, u32[]{:S(2)}, u32[]{:S(2)}) collective-permute-start(bf16[96,1536]{1,0:T(8,128)(2,1)} %get-tuple-element.268), channel_id=1, source_target_pairs={{0,16},{4,20},{8,24},{12,28},{16,0},{20,4},{24,8},{28,12},{1,17},{... | collective-permute-start | bytes 884744 | tf_op jit(solution)/shard_map/ppermute | solution.py:41
  483.8 3.8 collective-permute-start.21
  487.5 3.7 collective-permute-start.22
  491.2 4.6 collective-permute-start.23
  495.8 11.8 %collective-permute-start.24 = (f32[4,768]{1,0:T(4,128)S(1)}, f32[4,768]{1,0:T(4,128)S(1)}, u32[]{:S(2)}, u32[]{:S(2)}) collective-permute-start(f32[4,768]{1,0:T(4,128)S(1)} %add.165), channel_id=1, source_target_pairs={{0,16},{4,20},{8,24},{12,28},{16,0},{20,4},{24,8},{28,12},{1,17},{... | collective-permute-start | bytes 36872 | tf_op jit(solution)/shard_map/ppermute | solution.py:41
  500.8 27.8 %collective-permute-start.44 = (bf16[96,1536]{1,0:T(8,128)(2,1)}, bf16[96,1536]{1,0:T(8,128)(2,1)S(1)}, u32[]{:S(2)}, u32[]{:S(2)}) collective-permute-start(bf16[96,1536]{1,0:T(8,128)(2,1)} %get-tuple-element.300), channel_id=1, source_target_pairs={{0,1},{1,0},{2,3},{3,2},{4,5},{5,4},{6,7},{7,6},{8,9},{9,8},{10,11... | collective-permute-start | bytes 884744 | tf_op jit(solution)/shard_map/ppermute | solution.py:41
  501.9 29.1 %collective-permute-start.45 = (bf16[96,1536]{1,0:T(8,128)(2,1)}, bf16[96,1536]{1,0:T(8,128)(2,1)}, u32[]{:S(2)}, u32[]{:S(2)}) collective-permute-start(bf16[96,1536]{1,0:T(8,128)(2,1)} %get-tuple-element.301), channel_id=1, source_target_pairs={{0,2},{1,3},{2,0},{3,1},{4,6},{5,7},{6,4},{7,5},{8,10},{9,11},{10,... | collective-permute-start | bytes 884744 | tf_op jit(solution)/shard_map/ppermute | solution.py:41
  502.9 28.1 %collective-permute-start.46 = (bf16[96,1536]{1,0:T(8,128)(2,1)}, bf16[96,1536]{1,0:T(8,128)(2,1)}, u32[]{:S(2)}, u32[]{:S(2)}) collective-permute-start(bf16[96,1536]{1,0:T(8,128)(2,1)} %get-tuple-element.302), channel_id=1, source_target_pairs={{0,3},{1,2},{2,1},{3,0},{4,7},{5,6},{6,5},{7,4},{8,11},{9,10},{10,... | collective-permute-start | bytes 884744 | tf_op jit(solution)/shard_map/ppermute | solution.py:41
  507.6 30.4 %collective-permute-start.41 = (bf16[96,768]{1,0:T(8,128)(2,1)}, bf16[96,768]{1,0:T(8,128)(2,1)}, u32[]{:S(2)}, u32[]{:S(2)}) collective-permute-start(bf16[96,768]{1,0:T(8,128)(2,1)} %get-tuple-element.288), channel_id=1, source_target_pairs={{0,1},{1,0},{2,3},{3,2},{4,5},{5,4},{6,7},{7,6},{8,9},{9,8},{10,11... | collective-permute-start | bytes 442376 | tf_op jit(solution)/shard_map/ppermute | solution.py:41
  507.9 16.4 %collective-permute-start.35 = (bf16[96,1536]{1,0:T(8,128)(2,1)}, bf16[96,1536]{1,0:T(8,128)(2,1)}, u32[]{:S(2)}, u32[]{:S(2)}) collective-permute-start(bf16[96,1536]{1,0:T(8,128)(2,1)} %get-tuple-element.270), channel_id=1, source_target_pairs={{0,8},{4,12},{8,0},{12,4},{16,24},{20,28},{24,16},{28,20},{1,9},{5... | collective-permute-start | bytes 884744 | tf_op jit(solution)/shard_map/ppermute | solution.py:41
  524.3 28.7 %collective-permute-start.42 = (bf16[96,768]{1,0:T(8,128)(2,1)}, bf16[96,768]{1,0:T(8,128)(2,1)S(1)}, u32[]{:S(2)}, u32[]{:S(2)}) collective-permute-start(bf16[96,768]{1,0:T(8,128)(2,1)} %get-tuple-element.289), channel_id=1, source_target_pairs={{0,2},{1,3},{2,0},{3,1},{4,6},{5,7},{6,4},{7,5},{8,10},{9,11},{10,... | collective-permute-start | bytes 442376 | tf_op jit(solution)/shard_map/ppermute | solution.py:41
  528.5 24.5 %collective-permute-start.43 = (bf16[96,768]{1,0:T(8,128)(2,1)}, bf16[96,768]{1,0:T(8,128)(2,1)}, u32[]{:S(2)}, u32[]{:S(2)}) collective-permute-start(bf16[96,768]{1,0:T(8,128)(2,1)} %get-tuple-element.290), channel_id=1, source_target_pairs={{0,3},{1,2},{2,1},{3,0},{4,7},{5,6},{6,5},{7,4},{8,11},{9,10},{10,... | collective-permute-start | bytes 442376 | tf_op jit(solution)/shard_map/ppermute | solution.py:41
  531.1 24.6 %collective-permute-start.36 = (bf16[96,768]{1,0:T(8,128)(2,1)}, bf16[96,768]{1,0:T(8,128)(2,1)S(1)}, u32[]{:S(2)}, u32[]{:S(2)}) collective-permute-start(bf16[96,768]{1,0:T(8,128)(2,1)} %get-tuple-element.272), channel_id=1, source_target_pairs={{0,1},{1,0},{2,3},{3,2},{4,5},{5,4},{6,7},{7,6},{8,9},{9,8},{10,11... | collective-permute-start | bytes 442376 | tf_op jit(solution)/shard_map/ppermute | solution.py:41
  531.1 24.6 %collective-permute-start.37 = (bf16[96,768]{1,0:T(8,128)(2,1)}, bf16[96,768]{1,0:T(8,128)(2,1)}, u32[]{:S(2)}, u32[]{:S(2)}) collective-permute-start(bf16[96,768]{1,0:T(8,128)(2,1)} %get-tuple-element.273), channel_id=1, source_target_pairs={{0,2},{1,3},{2,0},{3,1},{4,6},{5,7},{6,4},{7,5},{8,10},{9,11},{10,... | collective-permute-start | bytes 442376 | tf_op jit(solution)/shard_map/ppermute | solution.py:41
  538.0 17.7 %collective-permute-start.38 = (bf16[96,768]{1,0:T(8,128)(2,1)}, bf16[96,768]{1,0:T(8,128)(2,1)}, u32[]{:S(2)}, u32[]{:S(2)}) collective-permute-start(bf16[96,768]{1,0:T(8,128)(2,1)} %get-tuple-element.274), channel_id=1, source_target_pairs={{0,3},{1,2},{2,1},{3,0},{4,7},{5,6},{6,5},{7,4},{8,11},{9,10},{10,... | collective-permute-start | bytes 442376 | tf_op jit(solution)/shard_map/ppermute | solution.py:41
  (78 other events, 780.5 us)

commit v5 on v4

--- a/solution.py
+++ b/solution.py
@@ -24,6 +24,7 @@
 BF16 = jnp.bfloat16
 MESH_ID = pl.DeviceIdType.MESH
 VMEM_LIMIT = 56 * 2**20
+FUSED_LIMIT = 62 * 2**20
 NEG = -1000000000.0
 SCALE = HDIM ** (-0.5)
 EPS = 1e-06
@@ -123,163 +124,149 @@
     return lax.all_gather(part, ("tensor", "dp"), axis=0, tiled=True)
 
 
-def tile_of(width):
-    return 512 if width % 512 == 0 else 384
-
-
-def fold_call(body, xyz, ins, outs, width, out_specs=None):
-    tile = tile_of(width)
-
-    def spec(rows, dtype, index):
-        return pl.BlockSpec((rows, tile), index)
-
-    smem = pl.BlockSpec(memory_space=pltpu.SMEM)
-    left, right = (lambda i: (0, i)), (lambda i: (0, i + width // tile))
-    in_specs = [smem] + [
-        spec(a.shape[0], a.dtype, right if second else left) for a, second in ins
-    ]
-    moved = sum(a.shape[0] * width * a.dtype.itemsize for a, _ in ins)
-    moved += sum(o.size * jnp.dtype(o.dtype).itemsize for o in outs)
-    rows = max(a.shape[0] for a, _ in ins)
-    return pl.pallas_call(
-        body,
-        grid=(width // tile,),
-        out_shape=outs,
-        in_specs=in_specs,
-        out_specs=out_specs or [spec(o.shape[0], o.dtype, left) for o in outs],
-        scratch_shapes=[pltpu.VMEM((rows, tile), F32)],
-        cost_estimate=pl.CostEstimate(flops=0, bytes_accessed=moved, transcendentals=0),
-    )(xyz, *[a for a, _ in ins])
-
-
 def block_rows(index):
     return pl.ds(pl.multiple_of(index * 96, 96), 96)
 
 
-def first_fold(xyz, mine_a, got_a, mine_b, got_b, keep_a, send_a, keep_b, send_b, sum_ref):
-    x, y = xyz[0], xyz[1]
-    sum_ref[...] = mine_a[...] + got_a[...].astype(F32)
+class Comm:
+    def __init__(self, send_sem, recv_sem):
+        self.send_sem, self.recv_sem, self.used = send_sem, recv_sem, 0
+        dp, z = lax.axis_index("dp"), lax.axis_index("tensor")
+        self.z = z
+        self.c, self.x, self.y = lax.rem(dp, 2), lax.rem(dp // 2, 2), dp // 4
+        low, high = lax.rem(z, 2), z // 2
+        self.core_peer = (dp + 1 - 2 * self.c, z)
+        self.x_peer = (dp + 2 - 4 * self.x, z)
+        self.y_peer = (dp + 4 - 8 * self.y, z)
+        self.z_shards = (high * 2 + 1 - low, (1 - high) * 2 + low, (1 - high) * 2 + 1 - low)
+        self.z_peers = [(dp, shard) for shard in self.z_shards]
+
+    def barrier(self):
+        barrier = pltpu.get_barrier_semaphore()
+        peers = [self.core_peer, self.x_peer, self.y_peer] + self.z_peers
+        for peer in peers:
+            pl.semaphore_signal(
+                barrier, inc=1, device_id={"dp": peer[0], "tensor": peer[1]}, device_id_type=MESH_ID
+            )
+        pl.semaphore_wait(barrier, len(peers))
+
+    def copy(self, src, dst, peer, index):
+        return pltpu.make_async_remote_copy(
+            src_ref=src,
+            dst_ref=dst,
+            send_sem=self.send_sem.at[index],
+            recv_sem=self.recv_sem.at[index],
+            device_id={"dp": peer[0], "tensor": peer[1]},
+            device_id_type=MESH_ID,
+        )
+
+    def reserve(self, count):
+        self.used += count
+        return self.used - count
+
+    def send(self, src, dst, peer):
+        copy = self.copy(src, dst, peer, self.reserve(1))
+        copy.start()
+        return copy
+
+
+def fold_one(comm, mine, got, keep, send, is_right):
     for other in range(2):
         rows = slice(other * 96, (other + 1) * 96)
-        keep_a[rows, :] = sum_ref[block_rows(2 * other + x), :]
-        send_a[rows, :] = sum_ref[block_rows(2 * other + 1 - x), :].astype(BF16)
-    sum_ref[...] = mine_b[...] + got_b[...].astype(F32)
-    for other in range(2):
-        rows = slice(other * 96, (other + 1) * 96)
-        keep_b[rows, :] = sum_ref[block_rows(2 * y + other), :]
-        send_b[rows, :] = sum_ref[block_rows(2 * (1 - y) + other), :].astype(BF16)
-
-
-def second_fold(xyz, mine_a, got_a, mine_b, got_b, keep_a, send_a, keep_b, send_b, sum_ref):
-    x, y = xyz[0], xyz[1]
-    sum_ref[...] = mine_a[...] + got_a[...].astype(F32)
-    keep_a[...] = sum_ref[block_rows(y), :]
-    send_a[...] = sum_ref[block_rows(1 - y), :].astype(BF16)
-    sum_ref[...] = mine_b[...] + got_b[...].astype(F32)
-    keep_b[...] = sum_ref[block_rows(x), :]
-    send_b[...] = sum_ref[block_rows(1 - x), :].astype(BF16)
-
-
-def third_fold(xyz, mine_a, got_a, mine_b, got_b, keep, send_1, send_2, send_3, sum_ref):
-    z = xyz[2]
-    width = keep.shape[1]
-    for m, (mine, got) in enumerate(((mine_a, got_a), (mine_b, got_b))):
-        total = mine[...] + got[...].astype(F32)
-        sum_ref[2 * m] = total[:, :width]
-        sum_ref[2 * m + 1] = total[:, width:]
-    keep[...] = sum_ref[z]
-    low, high = lax.rem(z, 2), z // 2
-    send_1[...] = sum_ref[2 * high + 1 - low].astype(BF16)
-    send_2[...] = sum_ref[2 * (1 - high) + low].astype(BF16)
-    send_3[...] = sum_ref[2 * (1 - high) + 1 - low].astype(BF16)
-
-
-def last_fold(flips, keep, got_1, got_2, got_3, *outs):
-    total = keep[...] + got_1[...].astype(F32) + (got_2[...].astype(F32) + got_3[...].astype(F32))
-    width = keep.shape[1] // len(outs)
-    for m, out in enumerate(outs):
-        part = total[:, m * width : (m + 1) * width]
-        out[...] = part.T if m in flips else part
-
-
-def table_fold(mine, got, out):
-    out[...] = (mine[...] + got[...].astype(F32)).T
-
-
-class Reduction:
-    def __init__(self, xyz, mine, send):
-        self.xyz, self.mine, self.width = xyz, mine, mine.shape[1] // 2
-        self.got = swap(send, "dp", 8, 1)
-
-    def first(self):
-        ins = [(self.mine, 0), (self.got, 0), (self.mine, 1), (self.got, 1)]
-        shape = (192, self.width)
-        outs = [whole(shape, F32), whole(shape, BF16)] * 2
-        keep_a, send_a, keep_b, send_b = fold_call(first_fold, self.xyz, ins, outs, self.width)
-        self.keeps = keep_a, keep_b
-        self.gots = swap(send_a, "dp", 8, 2), swap(send_b, "dp", 8, 4)
-        return send_a, send_b
-
-    def second(self):
-        (keep_a, keep_b), (got_a, got_b) = self.keeps, self.gots
-        ins = [(keep_a, 0), (got_a, 0), (keep_b, 0), (got_b, 0)]
-        shape = (96, self.width)
-        outs = [whole(shape, F32), whole(shape, BF16)] * 2
-        keep_a, send_a, keep_b, send_b = fold_call(second_fold, self.xyz, ins, outs, self.width)
-        self.keeps = keep_a, keep_b
-        self.gots = swap(send_a, "dp", 8, 4), swap(send_b, "dp", 8, 2)
-        return send_a, send_b
-
-    def third(self):
-        (keep_a, keep_b), (got_a, got_b) = self.keeps, self.gots
-        shape = (96, self.width // 2)
-        keep, *sends = pl.pallas_call(
-            third_fold,
-            out_shape=[whole(shape, F32)] + [whole(shape, BF16)] * 3,
-            in_specs=[pl.BlockSpec(memory_space=pltpu.SMEM)]
-            + [pl.BlockSpec(memory_space=pltpu.VMEM)] * 4,
-            out_specs=[pl.BlockSpec(memory_space=pltpu.VMEM)] * 4,
-            scratch_shapes=[pltpu.VMEM((4,) + shape, F32)],
-        )(self.xyz, keep_a, got_a, keep_b, got_b)
-        self.keeps = keep
-        self.gots = [swap(send, "tensor", 4, j + 1) for j, send in enumerate(sends)]
-        return tuple(sends)
-
-    def last(self, count, flips):
-        rows, width = self.keeps.shape
-        shape = (rows, width // count)
-        outs = [whole(shape[::-1] if m in flips else shape, F32) for m in range(count)]
-        return pl.pallas_call(functools.partial(last_fold, flips), out_shape=outs)(
-            self.keeps, *self.gots
-        )
-
-    def table(self, vocab):
-        parts = []
-        for keep, got, start in zip(self.keeps, self.gots, (0, self.width)):
-            count = min(self.width, vocab - start)
-            tile = pl.BlockSpec((96, VTILE), lambda i: (0, i))
-            parts.append(
-                pl.pallas_call(
-                    table_fold,
-                    grid=(pl.cdiv(count, VTILE),),
-                    out_shape=whole((count, 96), F32),
-                    in_specs=[tile] * 2,
-                    out_specs=pl.BlockSpec((VTILE, 96), lambda i: (i, 0)),
-                )(keep, got)
+        along_x, along_y = 2 * other + comm.x, 2 * comm.y + other
+        stay = along_x * (1 - is_right) + along_y * is_right
+        along_x, along_y = 2 * other + 1 - comm.x, 2 * (1 - comm.y) + other
+        leave = along_x * (1 - is_right) + along_y * is_right
+        stay, leave = block_rows(stay), block_rows(leave)
+        keep[rows, :] = mine[stay, :] + got[stay, :].astype(F32)
+        send[rows, :] = (mine[leave, :] + got[leave, :].astype(F32)).astype(BF16)
+
+
+def fold_two(comm, mine, got, keep, send):
+    for side, bit in enumerate((comm.y, comm.x)):
+        stay, leave = block_rows(bit), block_rows(1 - bit)
+        keep[side] = mine[side, stay, :] + got[side, stay, :].astype(F32)
+        send[side] = (mine[side, leave, :] + got[side, leave, :].astype(F32)).astype(BF16)
+
+
+class Flow:
+    def __init__(self, comm, one, two, three):
+        self.comm, self.one, self.two, self.three = comm, one, two, three
+        self.copies = []
+
+    def wait(self):
+        for copy in self.copies:
+            copy.wait()
+
+    def from_core(self, mine, send, got):
+        comm = self.comm
+        self.copies = [comm.send(send, got, comm.core_peer)]
+        self.mine, self.got = mine, got
+
+    def fold_first(self):
+        self.wait()
+        keep, send, _ = self.one
+        width = keep.shape[2]
+        for side in range(2):
+            cols = pl.ds(side * width, width)
+            fold_one(
+                self.comm, self.mine.at[:, cols], self.got.at[:, cols], keep.at[side], send.at[side], side
             )
-        return jnp.concatenate(parts, 0)
+
+    def send_first(self):
+        comm = self.comm
+        _, send, recv = self.one
+        self.copies = [
+            comm.send(send.at[0], recv.at[0], comm.x_peer),
+            comm.send(send.at[1], recv.at[1], comm.y_peer),
+        ]
+
+    def fold_second(self):
+        self.wait()
+        fold_two(self.comm, self.one[0], self.one[2], self.two[0], self.two[1])
+
+    def send_second(self):
+        comm = self.comm
+        _, send, recv = self.two
+        self.copies = [
+            comm.send(send.at[0], recv.at[0], comm.y_peer),
+            comm.send(send.at[1], recv.at[1], comm.x_peer),
+        ]
+
+    def fold_third(self, shard_ref):
+        self.wait()
+        comm = self.comm
+        (keep, _, recv), (keep3, send3, recv3) = self.two, self.three
+        width = keep3.shape[1]
+        for side in range(2):
+            total = keep[side] + recv[side].astype(F32)
+            shard_ref[2 * side, :, :width] = total[:, :width]
+            shard_ref[2 * side + 1, :, :width] = total[:, width:]
+        keep3[...] = shard_ref[comm.z, :, :width]
+        self.copies = []
+        for j, shard in enumerate(comm.z_shards):
+            send3[j] = shard_ref[shard, :, :width].astype(BF16)
+            self.copies.append(comm.send(send3.at[j], recv3.at[j], comm.z_peers[j]))
+
+    def finish(self, outs, flipped, turn_ref):
+        self.wait()
+        keep, _, recv = self.three
+        width = keep.shape[1] // len(outs)
+        for m, out in enumerate(outs):
+            cols = slice(m * width, (m + 1) * width)
+            part = keep[:, cols] + recv[0, :, cols].astype(F32)
+            part = part + (recv[1, :, cols].astype(F32) + recv[2, :, cols].astype(F32))
+            if m == flipped:
+                turn_ref[:, :width] = part
+                out[...] = turn_ref[:, :width].T
+            else:
+                out[...] = part
 
 
 class WideReduction:
-    def __init__(self, xyz, mine, send):
-        self.gots = ()
+    def __init__(self, z, mine, send):
         both = jnp.concatenate([mine, send.astype(F32)], 0)
         self.part = lax.psum_scatter(both, "dp", scatter_dimension=0, tiled=True)
-
-    def first(self):
-        return ()
-
-    second = third = first
 
     def last(self, count, flips):
         rows = self.part.shape[0]
@@ -292,12 +279,16 @@
         return self.part.T
 
 
-def after(value, *others):
-    return lax.optimization_barrier((value,) + others)[0]
-
-
 def rms_scale(values):
     return lax.rsqrt(jnp.mean(values * values, axis=-1, keepdims=True) + EPS)
+
+
+def spots(scal, split):
+    if split:
+        half, core = lax.rem(lax.axis_index("tensor"), 2), lax.rem(lax.axis_index("dp"), 2)
+    else:
+        half, core = scal[0], scal[3]
+    return half, scal[1], scal[2] - half * KEYS, core
 
 
 def norm_back(values, inv_scale, gain, grad_out):
@@ -663,7 +654,7 @@
 def ff_backward(
     split, scal, gf_own, gf_1, gf_2, gf_3, block_out, h2_in, gain_ff, gain_final, wg, wu, wd,
     w_co, att_t, mine_ref, send_ref, res_ref, rows_ref, gatt_ref, dot_ref, gg_ref,
-    flat_ref, nm_ref, ns_ref, gm_ref, gs_ref, gn_ref,
+    flat_ref, flat_2, nm_ref, ns_ref, gm_ref, gs_ref, gn_ref,
 ):
     core = scal[3]
     grad = gf_own[...] + gf_1[...].astype(F32)
@@ -673,13 +664,15 @@
     gg_ref[0:1, :] = gg_final
     rows_b = res.astype(BF16)
     res_ref[...] = res
-    flat_ref[...] = flip(rows_b).astype(BF16)
+    rows_ref[...] = rows_b
+    flat_ref[...] = flip(rows_ref[...]).astype(BF16)
     split_rows(flat_ref, gm_ref, gs_ref, core, split)
     h2 = h2_in[...]
     scale3 = rms_scale(h2)
     n3 = (h2 * scale3 * gain_ff[...]).astype(BF16)
-    flat_ref[...] = flip(n3).astype(BF16)
-    split_rows(flat_ref, nm_ref, ns_ref, core, split)
+    rows_ref[...] = n3
+    flat_2[...] = flip(rows_ref[...]).astype(BF16)
+    split_rows(flat_2, nm_ref, ns_ref, core, split)
     gn_ref[...] = jnp.zeros_like(gn_ref)
     const = (2.0 / 3.141592653589793) ** 0.5
 
@@ -727,11 +720,10 @@
 
 
 def cross_backward(
-    scal, q2, k2, v2, lse, g_own, g_other, dot_own, dot_other,
+    split, scal, q2, k2, v2, lse, g_own, g_other, dot_own, dot_other,
     dk_ref, dv_ref, own_out, send_out, g_ref, dot_ref, dq_ref,
 ):
-    half = scal[0]
-    live = scal[2] - half * KEYS
+    half, _, live, _ = spots(scal, split)
     own = pl.multiple_of(half * ROWS, ROWS)
     other = pl.multiple_of((1 - half) * ROWS, ROWS)
     both_halves(half, g_own, g_other, g_ref)
@@ -779,21 +771,27 @@
         rows = slice(i * CHUNK, (i + 1) * CHUNK)
         gsrc_ref[rows, :] = dot_nn(dk[rows, :], w_ck[...]) + dot_nn(dv[rows, :], w_cv[...])
         flat_ref[:, rows] = flip(source[rows, :]).astype(BF16)
-    split_rows(flat_ref, sm_ref, ss_ref, scal[3], split)
+    split_rows(flat_ref, sm_ref, ss_ref, spots(scal, split)[3], split)
     rights = (dk[...], dv[...])
-    by_shard(sm_ref, rights, mine_ref, 0, 384)
-    by_shard(ss_ref, rights, send_ref, 0, 384)
+    first, per_shard = (192, D) if split else (0, 384)
+    by_shard(sm_ref, rights, mine_ref, first, per_shard)
+    by_shard(ss_ref, rights, send_ref, first, per_shard)
 
 
 def query_backward(
     split, scal, dq_own, dq_other, h1_in, gain_cross, w_cq, res_in, rows_in, att, w_so,
-    kv_mine, kv_send, mine_ref, send_ref, res_ref, rows_ref, gatt_ref, gg_ref, flat_ref, a_ref, b_ref,
+    kv_mine, kv_send, mine_ref, send_ref, res_ref, rows_ref, gatt_ref, gg_ref, flat_ref, flat_2, a_ref, b_ref, turn_ref,
 ):
-    core = scal[3]
-    dq = (flip(dq_own[...] + dq_other[...].astype(F32)) * SCALE).astype(BF16)
+    core = spots(scal, split)[3]
+    turn_ref[...] = dq_own[...] + dq_other[...].astype(F32)
+    dq = (turn_ref[...].T * SCALE).astype(BF16)
     h1 = h1_in[...]
     scale2 = rms_scale(h1)
-    n2 = (h1 * scale2 * gain_cross[...]).astype(BF16)
+    rows_ref[...] = (h1 * scale2 * gain_cross[...]).astype(BF16)
+    flat_ref[...] = flip(rows_ref[...]).astype(BF16)
+    split_rows(flat_ref, a_ref, b_ref, core, split)
+    by_shard(a_ref, (dq,), mine_ref, 0, D)
+    by_shard(b_ref, (dq,), send_ref, 0, D)
     step, gg = norm_back(h1, scale2, gain_cross[...], dot_nn(dq, w_cq[...]))
     gg_ref[...] = gg
     res = res_in[...] + step
@@ -801,12 +799,11 @@
     rows_b = res.astype(BF16)
     rows_ref[...] = rows_b
     gatt_ref[...] = dot_nt(rows_b, w_so[...]).astype(BF16)
-    for m, (left, right) in enumerate(((n2, dq), (rows_in[...], att[...]))):
-        flat_ref[...] = flip(left).astype(BF16)
-        split_rows(flat_ref, a_ref, b_ref, core, split)
-        by_shard(a_ref, (right,), mine_ref, 576 * m, D)
-        by_shard(b_ref, (right,), send_ref, 576 * m, D)
-    for z in range(4):
+    flat_2[...] = flip(rows_in[...]).astype(BF16)
+    split_rows(flat_2, a_ref, b_ref, core, split)
+    by_shard(a_ref, (att[...],), mine_ref, 576, D)
+    by_shard(b_ref, (att[...],), send_ref, 576, D)
+    for z in range(0 if split else 4):
         cols = slice(z * D + 192, z * D + 576)
         mine_ref[:, cols] = kv_mine[:, z * 384 : (z + 1) * 384]
         send_ref[:, cols] = kv_send[:, z * 384 : (z + 1) * 384]
@@ -815,11 +812,9 @@
 def self_backward(
     split, scal, q1, k1, v1, lse, g_own, g_other, x_own, gain_self, w_q, w_k, w_v, res_in, rows_in, att,
     mine_ref, send_ref, gin_ref, gg_ref,
-    g_ref, dq_ref, dk_ref, dv_ref, flat_ref, a_ref, b_ref,
+    g_ref, dq_ref, dk_ref, dv_ref, flat_ref, flat_2, a_ref, b_ref,
 ):
-    half = scal[0]
-    live = scal[1]
-    core = scal[3]
+    half, live, _, core = spots(scal, split)
     own = pl.multiple_of(half * ROWS, ROWS)
     both_halves(half, g_own, g_other, g_ref)
     key = lax.broadcasted_iota(jnp.int32, (TGT, TGT), 0)
@@ -854,19 +849,472 @@
     dv = dv_ref[pl.ds(own, ROWS), :]
     x = x_own[...].astype(F32)
     scale1 = rms_scale(x)
-    n1 = (x * scale1 * gain_self[...]).astype(BF16)
     grad_n = dot_nn(dq, w_q[...]) + dot_nn(dk, w_k[...]) + dot_nn(dv, w_v[...])
     step, gg = norm_back(x, scale1, gain_self[...], grad_n)
     gg_ref[...] = gg
     gin_ref[...] = res_in[...] + step
-    flat_ref[...] = flip(n1).astype(BF16)
+    g_ref[:ROWS, :] = (x * scale1 * gain_self[...]).astype(BF16)
+    flat_ref[...] = flip(g_ref[:ROWS, :]).astype(BF16)
     split_rows(flat_ref, a_ref, b_ref, core, split)
     by_shard(a_ref, (dq, dk, dv), mine_ref, 0, D)
     by_shard(b_ref, (dq, dk, dv), send_ref, 0, D)
-    flat_ref[...] = flip(rows_in[...]).astype(BF16)
-    split_rows(flat_ref, a_ref, b_ref, core, split)
+    flat_2[...] = flip(rows_in[...]).astype(BF16)
+    split_rows(flat_2, a_ref, b_ref, core, split)
     by_shard(a_ref, (att[...],), mine_ref, 576, D)
     by_shard(b_ref, (att[...],), send_ref, 576, D)
+
+
+def table_ff_kernel(*refs):
+    (scal, g_a, g_b, fm_a, fm_b, fs_a, fs_b, gf_a, gf_b, gf_2), refs = refs[:10], refs[10:]
+    (block_out, h2_in, gain_ff, gain_final, wg, wu, wd, w_co, att_t), refs = refs[:9], refs[9:]
+    (e_keep, e_send, f_keep, f_send, res_ref, rows_ref), refs = refs[:6], refs[6:]
+    (gatt_ref, gatt_other, dot_ref, dot_other, gg_ref), refs = refs[:5], refs[5:]
+    (ga_ring, gb_ring, w_ring, mine_ring, send_ring, got, e_keep1, e_send1, e_recv1), refs = (
+        refs[:9],
+        refs[9:],
+    )
+    (flat_ref, flat_2, nm_ref, ns_ref, gm_ref, gs_ref, gn_ref, gf_send, gf_recv), refs = refs[:9], refs[9:]
+    send_sem, recv_sem, load_sem, w_sem = refs
+    comm = Comm(send_sem, recv_sem)
+    core = comm.c
+
+    def load(step):
+        tile = lax.rem(step, 2) * 4 + step // 2
+        rows = pl.ds(pl.multiple_of(tile * HTILE, HTILE), HTILE)
+        slot = lax.rem(step, 2)
+        return [
+            pltpu.make_async_copy(src.at[rows], dst.at[slot], load_sem.at[slot, i])
+            for i, (src, dst) in enumerate(((g_a, ga_ring), (g_b, gb_ring)))
+        ]
+
+    def load_weights(step):
+        shard = lax.rem(step, 2) * 2 + step // 2
+        rows = pl.ds(pl.multiple_of(shard * 512, 512), 512)
+        slot = lax.rem(step, 2)
+        return [
+            pltpu.make_async_copy(src.at[rows], w_ring.at[slot, i], w_sem.at[slot, i])
+            for i, src in enumerate((wg, wu, wd))
+        ]
+
+    for copy in load(0) + load_weights(0):
+        copy.start()
+    comm.barrier()
+    gf_send[...] = gf_b[ROWS:, :].astype(BF16)
+    gf_copies = [
+        comm.send(gf_send, gf_recv.at[0], comm.z_peers[0]),
+        comm.send(gf_a.at[ROWS:], gf_recv.at[1], comm.z_peers[2]),
+    ]
+    e_core, e_line, f_core = comm.reserve(8), comm.reserve(8), comm.reserve(4)
+
+    def core_copy(step):
+        tile = lax.rem(step, 2) * 4 + step // 2
+        return comm.copy(
+            send_ring.at[lax.rem(step, 2), pl.ds(0, 2)],
+            got.at[pl.ds(2 * tile, 2)],
+            comm.core_peer,
+            e_core + step,
+        )
+
+    def line_copy(step):
+        side, column = lax.rem(step, 2), step // 2
+        cols = pl.ds(pl.multiple_of(column * HTILE, HTILE), HTILE)
+        peer = comm.x_peer[0] * (1 - side) + comm.y_peer[0] * side
+        return comm.copy(
+            e_send1.at[side, :, cols], e_recv1.at[side, :, cols], (peer, comm.z), e_line + step
+        )
+
+    @pl.loop(0, 9)
+    def _(step):
+        @pl.when(step < 8)
+        def _():
+            slot = lax.rem(step, 2)
+            for copy in load(step):
+                copy.wait()
+
+            @pl.when(step < 7)
+            def _():
+                for copy in load(step + 1):
+                    copy.start()
+
+            @pl.when(step >= 2)
+            def _():
+                core_copy(step - 2).wait_send()
+
+            for part in range(2):
+                rows = slice(part * 512, (part + 1) * 512)
+                first, second = ga_ring[slot, rows, :], gb_ring[slot, rows, :]
+                mine_ring[slot, part] = dot_nt(fm_a[...], first) + dot_nt(fm_b[...], second)
+                send_ring[slot, part] = (
+                    dot_nt(fs_a[...], first) + dot_nt(fs_b[...], second)
+                ).astype(BF16)
+            core_copy(step).start()
+
+        @pl.when(step > 0)
+        def _():
+            last = step - 1
+            slot, side = lax.rem(last, 2), lax.rem(last, 2)
+            tile = side * 4 + last // 2
+            core_copy(last).wait_recv()
+            for part in range(2):
+                start = pl.multiple_of((last // 2) * HTILE + part * 512, 512)
+                cols = pl.ds(start, 512)
+                fold_one(
+                    comm,
+                    mine_ring.at[slot, part],
+                    got.at[2 * tile + part],
+                    e_keep1.at[side, :, cols],
+                    e_send1.at[side, :, cols],
+                    side,
+                )
+            line_copy(last).start()
+
+    for step in (6, 7):
+        core_copy(step).wait_send()
+    for copy in gf_copies:
+        copy.wait()
+
+    grad = gf_b[:ROWS, :] + gf_recv[0].astype(F32)
+    grad = grad + (gf_2[...].astype(F32) + gf_recv[1].astype(F32))
+    out = block_out[...]
+    res, gg_final = norm_back(out, rms_scale(out), gain_final[...], grad * D ** (-0.5))
+    gg_ref[0:1, :] = gg_final
+    res_ref[...] = res
+    gatt_ref[...] = res.astype(BF16)
+    flat_ref[...] = flip(gatt_ref[...]).astype(BF16)
+    split_rows(flat_ref, gm_ref, gs_ref, core, True)
+    h2 = h2_in[...]
+    rows_ref[...] = (h2 * rms_scale(h2) * gain_ff[...]).astype(BF16)
+    flat_2[...] = flip(rows_ref[...]).astype(BF16)
+    split_rows(flat_2, nm_ref, ns_ref, core, True)
+    gn_ref[...] = jnp.zeros_like(gn_ref)
+
+    def ff_copy(step):
+        return comm.copy(
+            send_ring.at[lax.rem(step, 2)],
+            got.at[pl.ds(3 * step, 3)],
+            comm.core_peer,
+            f_core + step,
+        )
+
+    @pl.loop(0, 5)
+    def _(step):
+        @pl.when(step < 4)
+        def _():
+            slot = lax.rem(step, 2)
+            for copy in load_weights(step):
+                copy.wait()
+
+            @pl.when(step < 3)
+            def _():
+                for copy in load_weights(step + 1):
+                    copy.start()
+
+            @pl.when(step >= 2)
+            def _():
+                ff_copy(step - 2).wait_send()
+
+            g_gate, g_up, mixed = ff_block(rows_ref, gatt_ref, gn_ref, w_ring.at[slot])
+            for m, (mine, send, right) in enumerate(
+                ((nm_ref, ns_ref, g_gate), (nm_ref, ns_ref, g_up), (gm_ref, gs_ref, mixed))
+            ):
+                mine_ring[slot, m] = dot_nn(mine[...], right)
+                send_ring[slot, m] = dot_nn(send[...], right).astype(BF16)
+            ff_copy(step).start()
+
+        @pl.when(step > 0)
+        def _():
+            last = step - 1
+            slot, side = lax.rem(last, 2), lax.rem(last, 2)
+            ff_copy(last).wait_recv()
+            for m in range(3):
+                cols = pl.ds(pl.multiple_of((last // 2) * 1536 + m * 512, 512), 512)
+                fold_one(
+                    comm,
+                    mine_ring.at[slot, m],
+                    got.at[3 * last + m],
+                    f_keep.at[side, :, cols],
+                    f_send.at[side, :, cols],
+                    side,
+                )
+
+    step, gg_ff = norm_back(h2_in[...], rms_scale(h2_in[...]), gain_ff[...], gn_ref[...])
+    gg_ref[1:2, :] = gg_ff
+    res = res_ref[...] + step
+    res_ref[...] = res
+    rows_b = res.astype(BF16)
+    rows_ref[...] = rows_b
+    gatt_ref[...] = dot_nt(rows_b, w_co[...]).astype(BF16)
+    gatt_t = dot_nt(w_co[...], rows_b).astype(BF16).astype(F32)
+    dot_ref[...] = jnp.zeros_like(dot_ref)
+    for head in range(NHEAD):
+        feats = slice(head * HDIM, (head + 1) * HDIM)
+        dot_ref[head : head + 1, :] = jnp.sum(gatt_t[feats, :] * att_t[feats, :], 0, keepdims=True)
+    pair_copies = [
+        comm.send(gatt_ref, gatt_other, comm.z_peers[0]),
+        comm.send(dot_ref, dot_other, comm.z_peers[0]),
+    ]
+    for step in (2, 3):
+        ff_copy(step).wait_send()
+    for step in range(8):
+        line_copy(step).wait()
+    fold_two(comm, e_keep1, e_recv1, e_keep, e_send)
+    for copy in pair_copies:
+        copy.wait()
+
+
+def ff_block(n3_ref, grad_ref, gn_ref, weights):
+    const = (2.0 / 3.141592653589793) ** 0.5
+    wg, wu, wd = weights[0], weights[1], weights[2]
+    n3 = n3_ref[...]
+    gate = dot_nt(n3, wg)
+    up = dot_nt(n3, wu)
+    square = gate * gate
+    tanh = jnp.tanh(const * (gate + 0.044715 * gate * square))
+    gelu = 0.5 * gate * (1.0 + tanh)
+    slope = 0.5 * (1.0 + tanh) + 0.5 * gate * (1.0 - tanh * tanh) * const * (
+        1.0 + 3.0 * 0.044715 * square
+    )
+    grad_mixed = dot_nt(grad_ref[...], wd)
+    g_gate = (grad_mixed * up * slope).astype(BF16)
+    g_up = (grad_mixed * gelu).astype(BF16)
+    gn_ref[...] += dot_nn(g_gate, wg) + dot_nn(g_up, wu)
+    return g_gate, g_up, (gelu * up).astype(BF16)
+
+
+def cross_kernel(*refs):
+    (scal, q2, k2, v2, lse2, g_own, g_other, dot_own, dot_oth, source), refs = refs[:10], refs[10:]
+    (w_ck, w_cv, w_cq, w_so, h1, gain_cross, res_in, rows_in, att), refs = refs[:9], refs[9:]
+    (e_send, f_keep, f_send), refs = refs[:3], refs[3:]
+    (gsrc, res_ref, rows_ref, gatt1, gatt1_other, gg_ref), refs = refs[:6], refs[6:]
+    (c_keep, c_send, f_keep2, f_send2, e_recv), refs = refs[:5], refs[5:]
+    (g_ref, dot_ref, dq_ref, dk_ref, dv_ref, flat_ref, sm_ref, ss_ref), refs = refs[:8], refs[8:]
+    (mine, send, got, f_recv, own_ref, go_ref, come_ref, flat2, a_ref, b_ref), refs = (
+        refs[:10],
+        refs[10:],
+    )
+    comm = Comm(*refs)
+    comm.barrier()
+    ff = Flow(comm, (f_keep, f_send, f_recv), (f_keep2, f_send2, None), None)
+    ff.send_first()
+    e_copies = [
+        comm.send(e_send.at[0], e_recv.at[0], comm.y_peer),
+        comm.send(e_send.at[1], e_recv.at[1], comm.x_peer),
+    ]
+    cross_backward(
+        True, scal, q2, k2, v2, lse2, g_own, g_other, dot_own, dot_oth,
+        dk_ref, dv_ref, own_ref, go_ref, g_ref, dot_ref, dq_ref,
+    )
+    dq_copy = comm.send(go_ref, come_ref, comm.z_peers[0])
+    source_backward(
+        True, scal, dk_ref, dv_ref, source, w_ck, w_cv, gsrc, mine, send, flat_ref, sm_ref, ss_ref
+    )
+    dq_copy.wait()
+    query_backward(
+        True, scal, own_ref, come_ref, h1, gain_cross, w_cq, res_in, rows_in, att, w_so,
+        None, None, mine, send, res_ref, rows_ref, gatt1, gg_ref, flat2, go_ref, a_ref, b_ref, dq_ref.at[:, :ROWS],
+    )
+    pair_copy = comm.send(gatt1, gatt1_other, comm.z_peers[0])
+    cross = Flow(comm, (c_keep, c_send, None), None, None)
+    cross.from_core(mine, send, got)
+    cross.fold_first()
+    ff.fold_second()
+    pair_copy.wait()
+    for copy in e_copies:
+        copy.wait()
+
+
+def self_kernel(vocab, *refs):
+    (scal, q1, k1, v1, lse1, g_own, g_other, x_own, gain_self, w_q, w_k, w_v), refs = (
+        refs[:12],
+        refs[12:],
+    )
+    (res_in, rows_in, att, gg_a, gg_b), refs = refs[:5], refs[5:]
+    (e_keep, e_recv, f_keep, f_send, c_keep, c_send), refs = refs[:6], refs[6:]
+    (gin_ref, gains_ref, e_out), refs = refs[:3], refs[3:]
+    s_outs, c_outs, f_outs, refs = refs[:4], refs[4:8], refs[8:11], refs[11:]
+    (g_ref, dq_ref, dk_ref, dv_ref, flat_ref, flat_2, a_ref, b_ref, gain_ref), refs = refs[:9], refs[9:]
+    (mine, send, got, shard_ref, f_recv), refs = refs[:5], refs[5:]
+    f_three, (c_recv1, c_keep2, c_send2, c_recv2), refs = refs[:3], refs[3:7], refs[7:]
+    c_three, s_one, s_two, s_three, refs = refs[:3], refs[3:6], refs[6:9], refs[9:12], refs[12:]
+    gain_send, gain_recv, turn_ref, refs = refs[0], refs[1], refs[2], refs[3:]
+    comm = Comm(*refs)
+    comm.barrier()
+    cross = Flow(comm, (c_keep, c_send, c_recv1), (c_keep2, c_send2, c_recv2), c_three)
+    ff = Flow(comm, None, (f_keep, f_send, f_recv), f_three)
+    own = Flow(comm, s_one, s_two, s_three)
+    ff.send_second()
+    cross.send_first()
+    self_backward(
+        True, scal, q1, k1, v1, lse1, g_own, g_other, x_own, gain_self, w_q, w_k, w_v,
+        res_in, rows_in, att, mine, send, gin_ref, gain_ref,
+        g_ref, dq_ref, dk_ref, dv_ref, flat_ref, flat_2, a_ref, b_ref,
+    )
+    own.from_core(mine, send, got)
+    gains_ref[...] = jnp.zeros_like(gains_ref)
+    gains_ref[0:2, :] = gg_a[...]
+    gains_ref[2:3, :] = gg_b[...]
+    gains_ref[3:4, :] = gain_ref[...]
+
+    def gain_step(step, peer):
+        gain_send[step] = gains_ref[...]
+        return comm.send(gain_send.at[step], gain_recv.at[step], peer)
+
+    def gain_done(step, copy):
+        copy.wait()
+        gains_ref[...] = gains_ref[...] + gain_recv[step]
+
+    copy = gain_step(0, comm.core_peer)
+    own.fold_first()
+    own.send_first()
+    gain_done(0, copy)
+    copy = gain_step(1, comm.z_peers[0])
+    ff.fold_third(shard_ref)
+    cross.fold_second()
+    cross.send_second()
+    gain_done(1, copy)
+    copy = gain_step(2, comm.x_peer)
+    width = e_keep.shape[2]
+    for start in range(0, vocab, 512):
+        side, column = start // width, start % width
+        count = min(512, vocab - start)
+        cols = slice(column, column + 512)
+        turn_ref[...] = e_keep[side, :, cols] + e_recv[side, :, cols].astype(F32)
+        e_out[start : start + count, :] = turn_ref[...].T[:count, :]
+    gain_done(2, copy)
+    copy = gain_step(3, comm.y_peer)
+    own.fold_second()
+    own.send_second()
+    cross.fold_third(shard_ref)
+    gain_done(3, copy)
+    copy = gain_step(4, comm.z_peers[1])
+    ff.finish(f_outs, 2, turn_ref)
+    own.fold_third(shard_ref)
+    gain_done(4, copy)
+    cross.finish(c_outs, 3, turn_ref)
+    own.finish(s_outs, 3, turn_ref)
+
+
+def fused_call(body, collective_id, ins, outs, scratch, copies, flops):
+    hbm, vmem = pl.BlockSpec(memory_space=pl.ANY), pl.BlockSpec(memory_space=pltpu.VMEM)
+    moved = sum(a.size * a.dtype.itemsize for a, _ in ins)
+    return pl.pallas_call(
+        body,
+        out_shape=[shape for shape, _ in outs],
+        in_specs=[pl.BlockSpec(memory_space=pltpu.SMEM)] + [hbm if far else vmem for _, far in ins[1:]],
+        out_specs=[hbm if far else vmem for _, far in outs],
+        scratch_shapes=scratch(copies),
+        cost_estimate=pl.CostEstimate(
+            flops=int(flops), bytes_accessed=int(moved), transcendentals=0
+        ),
+        compiler_params=pltpu.CompilerParams(
+            collective_id=collective_id, has_side_effects=True, vmem_limit_bytes=FUSED_LIMIT
+        ),
+    )(*[a for a, _ in ins])
+
+
+def fused_backward(
+    scal, flats_a, flats_b, g_a, g_b, gf_a, gf_b, gf_2, saved, weights, gains, block_in, source, vocab
+):
+    (q1, k1, v1, lse1, a1, h1, q2, k2, v2, block_out, h2, att_t, a2, lse2) = saved
+    (sq, sk, sv, so, cq, ck, cv, co, wg, wu, wd) = weights
+    gain_self, gain_cross, gain_ff, gain_final = gains
+
+    def vm(*shape, dtype=BF16):
+        return pltpu.VMEM(shape, dtype)
+
+    def sems(copies):
+        return [pltpu.SemaphoreType.DMA((copies,))] * 2
+
+    def near(*arrays):
+        return [(a, False) for a in arrays]
+
+    def far(*arrays):
+        return [(a, True) for a in arrays]
+
+    block, pair = (ROWS, D), (TGT, D)
+    half_t = (HALF_D, ROWS)
+    e_half, f_half, c_half = 4096, 3 * FF // 2, 2 * D
+
+    def scratch_1(copies):
+        return [
+            vm(2, HTILE, TGT), vm(2, HTILE, TGT), vm(2, 3, 512, D), vm(2, 3, HALF_D, 512, dtype=F32),
+            vm(2, 3, HALF_D, 512), vm(16, HALF_D, 512), vm(2, 192, e_half, dtype=F32),
+            vm(2, 192, e_half), vm(2, 192, e_half), vm(D, ROWS), vm(D, ROWS),
+            vm(*half_t), vm(*half_t), vm(*half_t), vm(*half_t), vm(*block, dtype=F32),
+            vm(*block), vm(2, *block), *sems(copies),
+            pltpu.SemaphoreType.DMA((2, 2)), pltpu.SemaphoreType.DMA((2, 3)),
+        ]
+
+    outs = near(
+        whole((2, 96, e_half), F32), whole((2, 96, e_half), BF16),
+        whole((2, 192, f_half), F32), whole((2, 192, f_half), BF16),
+        whole(block, F32), whole(block, BF16), whole(block, BF16), whole(block, BF16),
+        whole((16, ROWS), F32), whole((16, ROWS), F32), whole((2, D), F32),
+    )
+    e_keep, e_send, f_keep, f_send, res2, rows2, gatt, gatt_o, dots, dots_o, gg_a = fused_call(
+        table_ff_kernel, 1,
+        near(scal) + far(g_a, g_b)
+        + near(flats_a[0], flats_b[0], flats_a[1], flats_b[1], gf_a, gf_b, gf_2)
+        + near(block_out, h2, gain_ff, gain_final) + far(wg, wu, wd) + near(co, att_t),
+        outs, scratch_1, 24, 40e9,
+    )
+
+    def scratch_2(copies):
+        return [
+            vm(*pair), vm(16, TGT, dtype=F32), vm(D, TGT, dtype=F32), vm(KEYS, D), vm(KEYS, D),
+            vm(D, KEYS), vm(HALF_D, KEYS), vm(HALF_D, KEYS),
+            vm(HALF_D, 4 * D, dtype=F32), vm(HALF_D, 4 * D), vm(HALF_D, 4 * D),
+            vm(2, 192, f_half), vm(D, ROWS, dtype=F32), vm(D, ROWS), vm(D, ROWS),
+            vm(D, ROWS), vm(*half_t), vm(*half_t), *sems(copies),
+        ]
+
+    outs = near(
+        whole((KEYS, D), F32), whole(block, F32), whole(block, BF16), whole(block, BF16),
+        whole(block, BF16), whole((1, D), F32),
+        whole((2, 192, c_half), F32), whole((2, 192, c_half), BF16),
+        whole((2, 96, f_half), F32), whole((2, 96, f_half), BF16),
+    ) + far(whole((2, 96, e_half), BF16))
+    (
+        grad_source, res1, rows1, gatt1, gatt1_o, gg_b, c_keep, c_send, f_keep, f_send, e_recv,
+    ) = fused_call(
+        cross_kernel, 2,
+        near(scal, q2, k2, v2, lse2, gatt, gatt_o, dots, dots_o, source, ck, cv, cq, so)
+        + near(h1, gain_cross, res2, rows2, a2) + far(e_send) + near(f_keep) + far(f_send),
+        outs, scratch_2, 8, 40e9,
+    )
+
+    def scratch_3(copies):
+        def three(width):
+            return [vm(96, width, dtype=F32), vm(3, 96, width), vm(3, 96, width)]
+
+        def two(width):
+            return [vm(2, 96, width, dtype=F32), vm(2, 96, width), vm(2, 96, width)]
+
+        return [
+            vm(*pair), vm(D, TGT, dtype=F32), vm(*pair), vm(*pair), vm(D, ROWS), vm(D, ROWS),
+            vm(*half_t), vm(*half_t), vm(1, D, dtype=F32),
+            vm(HALF_D, 4 * D, dtype=F32), vm(HALF_D, 4 * D), vm(HALF_D, 4 * D),
+            vm(4, 96, f_half // 2, dtype=F32), vm(2, 96, f_half), *three(f_half // 2),
+            vm(2, 192, c_half), *two(c_half), *three(c_half // 2),
+            vm(2, 192, c_half, dtype=F32), vm(2, 192, c_half), vm(2, 192, c_half),
+            *two(c_half), *three(c_half // 2),
+            vm(5, 8, D, dtype=F32), vm(5, 8, D, dtype=F32), vm(96, 512, dtype=F32), *sems(copies),
+        ]
+
+    wide, tall = whole((96, 192), F32), whole((192, 96), F32)
+    ff_wide, ff_tall = whole((96, 512), F32), whole((512, 96), F32)
+    outs = near(
+        whole(block, F32), whole((8, D), F32), whole((vocab, 96), F32),
+        wide, wide, wide, tall, wide, wide, wide, tall, ff_wide, ff_wide, ff_tall,
+    )
+    grad_in, gain_sums, grad_embed, *grads = fused_call(
+        functools.partial(self_kernel, vocab), 3,
+        near(scal, q1, k1, v1, lse1, gatt1, gatt1_o, block_in, gain_self, sq, sk, sv)
+        + near(res1, rows1, a1, gg_a, gg_b, e_keep, e_recv, f_keep) + far(f_send)
+        + near(c_keep) + far(c_send),
+        outs, scratch_3, 32, 20e9,
+    )
+    return grad_in, grad_source, gain_sums, grads, grad_embed
 
 
 def logits_kernel(vocab, flat_ref, table_ref, target_ref, logits_ref, stats_ref):
@@ -1097,9 +1545,6 @@
             logits_b, embed_table, tgt_b, columns(g_lse, (0, 1)), columns(live_blocks, (0, 1)), F32
         )
         g_b, gf_b, gf_2, gf_a = lax.optimization_barrier((g_b, gf_b, gf_2, gf_a))
-        gf_3 = swap(gf_a[ROWS:], "tensor", 4, 3)
-        gf_1 = swap(gf_b[ROWS:].astype(BF16), "tensor", 4, 1)
-
         def halves(flat):
             if not split:
                 return flat[:HALF_D], flat[HALF_D:]
@@ -1109,13 +1554,22 @@
                 for i in (core, 1 - core)
             )
 
-        reduction = Reduction if split else WideReduction
-        xyz = jnp.stack([lax.rem(dp // 2, 2), dp // 4, z]).astype(jnp.int32)
+        if split:
+            saved = (q1, k1, v1, lse1, a1, h1, q2, k2, v2, block_out, h2, att_t, a2, lse2)
+            grad_block_in, grad_source, gains, grads, grad_embed = fused_backward(
+                scal, halves(fin_a), halves(fin_b), g_a, g_b, gf_a, gf_b, gf_2, saved,
+                (sq, sk, sv, so, cq, ck, cv, co, wg, wu, wd),
+                (gain_self, gain_cross, gain_ff, gain_final), block_in, source, vocab,
+            )
+            return (
+                block_out, token_loss, grad_block_in, grad_source,
+                gains[3], gains[2], gains[1], gains[0], *grads, grad_embed,
+            )
+
+        gf_3 = swap(gf_a[ROWS:], "tensor", 4, 3)
+        gf_1 = swap(gf_b[ROWS:].astype(BF16), "tensor", 4, 1)
         e_mine, e_send = table_grads(halves(fin_a), halves(fin_b), g_a, g_b)
-        if not split:
-            e_mine, e_send = e_mine[:, :vocab], e_send[:, :vocab]
-        e_mine, e_send, gf_1, gf_3 = lax.optimization_barrier((e_mine, e_send, gf_1, gf_3))
-        e_sum = reduction(xyz, e_mine, e_send)
+        e_sum = WideReduction(z, e_mine[:, :vocab], e_send[:, :vocab])
 
         half_t = (HALF_D, ROWS)
         ff_mine, ff_send, res2, rows2, gatt, dots, gg_a = local_call(
@@ -1123,73 +1577,55 @@
             [whole((HALF_D, 3 * FF), F32), whole((HALF_D, 3 * FF), BF16), whole((ROWS, D), F32)]
             + [whole((ROWS, D), BF16)] * 2
             + [whole((16, ROWS), F32), whole((2, D), F32)],
-            [vm((D, ROWS), BF16)] + [vm(half_t, BF16)] * 4
+            [vm((D, ROWS), BF16)] * 2 + [vm(half_t, BF16)] * 4
             + [vm((ROWS, D), F32)],
             10e9,
-            scal, after(gf_b[:ROWS], e_send), gf_1, gf_2, gf_3, block_out, h2,
+            scal, gf_b[:ROWS], gf_1, gf_2, gf_3, block_out, h2,
             gain_ff, gain_final, wg, wu, wd, co, att_t,
         )
-        ff_sum = reduction(xyz, ff_mine, ff_send)
+        ff_sum = WideReduction(z, ff_mine, ff_send)
         gatt_other, dots_other = pair_swap(gatt), pair_swap(dots)
-        sent = e_sum.first()
         dk2, dv2, dq_own, dq_send = local_call(
-            cross_backward,
+            functools.partial(cross_backward, split),
             [whole((KEYS, D), BF16)] * 2 + [whole((D, ROWS), F32), whole((D, ROWS), BF16)],
             [vm(pair, BF16), vm((16, TGT), F32), vm((D, TGT), F32)],
             20e9,
-            scal, q2, k2, v2, lse2, after(gatt, *sent), gatt_other, dots, dots_other,
+            scal, q2, k2, v2, lse2, gatt, gatt_other, dots, dots_other,
         )
         dq_other = pair_swap(dq_send)
-        dk2, *e_sum.gots = lax.optimization_barrier((dk2, *e_sum.gots))
-        sent = ff_sum.first()
         grad_source, kv_mine, kv_send = local_call(
             functools.partial(source_backward, split),
             [whole((KEYS, D), F32), whole((HALF_D, 2 * D), F32), whole((HALF_D, 2 * D), BF16)],
             [vm((D, KEYS), BF16)] + [vm((HALF_D, KEYS), BF16)] * 2,
             5e9,
-            scal, after(dk2, *sent), dv2, source, ck, cv,
-        )
-        sent = e_sum.second()
+            scal, dk2, dv2, source, ck, cv,
+        )
         c_mine, c_send, res1, rows1, gatt1, gg_b = local_call(
             functools.partial(query_backward, split),
             [whole((HALF_D, 4 * D), F32), whole((HALF_D, 4 * D), BF16), whole((ROWS, D), F32)]
             + [whole((ROWS, D), BF16)] * 2 + [whole((1, D), F32)],
-            [vm((D, ROWS), BF16)] + [vm(half_t, BF16)] * 2,
+            [vm((D, ROWS), BF16)] * 2 + [vm(half_t, BF16)] * 2 + [vm((D, ROWS), F32)],
             2e9,
-            scal, after(dq_own, *sent), dq_other, h1, gain_cross, cq, res2, rows2, a2, so,
+            scal, dq_own, dq_other, h1, gain_cross, cq, res2, rows2, a2, so,
             kv_mine, kv_send,
         )
-        c_sum = reduction(xyz, c_mine, c_send)
+        c_sum = WideReduction(z, c_mine, c_send)
         gatt1_other = pair_swap(gatt1)
-        sent = ff_sum.second() + c_sum.first()
         s_mine, s_send, grad_block_in, gg_c = local_call(
             functools.partial(self_backward, split),
             [whole((HALF_D, 4 * D), F32), whole((HALF_D, 4 * D), BF16)]
             + [whole((ROWS, D), F32), whole((1, D), F32)],
             [vm(pair, BF16), vm((D, TGT), F32), vm(pair, BF16), vm(pair, BF16)]
-            + [vm((D, ROWS), BF16)] + [vm(half_t, BF16)] * 2,
+            + [vm((D, ROWS), BF16)] * 2 + [vm(half_t, BF16)] * 2,
             12e9,
-            scal, q1, k1, v1, lse1, after(gatt1, *sent), gatt1_other, block_in, gain_self, sq, sk, sv,
+            scal, q1, k1, v1, lse1, gatt1, gatt1_other, block_in, gain_self, sq, sk, sv,
             res1, rows1, a1,
         )
-        flying = (*e_sum.gots, *ff_sum.gots, *c_sum.gots)
-        s_mine, s_send, *flying = lax.optimization_barrier((s_mine, s_send, *flying))
-        if split:
-            e_sum.gots, ff_sum.gots, c_sum.gots = flying[:2], flying[2:4], flying[4:]
-        s_sum = reduction(xyz, s_mine, s_send)
+        s_sum = WideReduction(z, s_mine, s_send)
         gains = jnp.concatenate([gg_a, gg_b, gg_c], 0)
-        if split:
-            for axis, size, bit in (("dp", 8, 1), ("tensor", 4, 1), ("dp", 8, 2), ("tensor", 4, 2), ("dp", 8, 4)):
-                gains = gains + swap(gains, axis, size, bit)
-        else:
-            gains = lax.psum(gains, ("dp", "tensor"))
-        sent = s_sum.first()
-        sent = sent + ff_sum.third() + c_sum.second()
+        gains = lax.psum(gains, ("dp", "tensor"))
         grad_embed = e_sum.table(vocab)
-        s_sum.second()
-        c_sum.third()
         ff_grads = ff_sum.last(3, (2,))
-        s_sum.third()
         c_grads = c_sum.last(4, (3,))
         s_grads = s_sum.last(4, (3,))
 

time: 566 us -> 457 us (0.81)
  waiting for transfers between devices: 92.4 us -> 27 us
  starting transfers between devices: 52.3 us -> 14.7 us
  Pallas kernels: 331 us -> 357 us
  local copies, waits for them, and re-layouts: 71 us -> 46.7 us
    ppermute x47 -> x7, waiting for transfers between devices: 92.4 us -> 27 us  [swap(): return lax.ppermute(value, axis_name, [(i, i ^ bit) for i in range(size)])]
    ppermute x47 -> x7, starting transfers between devices: 52.3 us -> 14.7 us  [swap(): return lax.ppermute(value, axis_name, [(i, i ^ bit) for i in range(size)])]
    pallas_call x22 -> x3, Pallas kernels: 170 us -> 196 us  [fused_call(): pl.pallas_call(body, out_shape=[shape for shape, _ in outs], in_specs=[pl...]
    unnamed x177 -> x83, local copies, waits for them, and re-layouts: 60.1 us -> 35 us
  transfers between devices with their start and end apart: 47 -> 7, of which waited for: 15 -> 3; matrix products, arithmetic and copies ran while one was open for 3% -> 1% of each run, Pallas kernels for 33% -> 7%
where the time goes in v5:
time: 457 us; the launch traced here: 452 us
  Pallas kernels  357 us (78%)
  local copies, waits for them, and re-layouts  46.7 us (10%)
  waiting for transfers between devices  27 us (6%)
  starting transfers between devices  14.7 us (3%)
  other arithmetic  5.3 us (1%)
    pallas_call x3, Pallas kernels, fused_call(): pl.pallas_call(body, out_shape=[shape for shape, _ in outs], in_specs=[pl...  196 us
    pallas_call x1, Pallas kernels, forward(): pl.pallas_call(functools.partial(forward_kernel, split), out_shape=outs,...  104 us
    unnamed x83, local copies, waits for them, and re-layouts  35 us
    pallas_call x2, Pallas kernels, head_grads(): pl.pallas_call(functools.partial(grads_kernel, vocab), grid=(tiles,), out...  30.7 us
    ppermute x7, waiting for transfers between devices, swap(): return lax.ppermute(value, axis_name, [(i, i ^ bit) for i in range(size)])  27 us
    pallas_call x2, Pallas kernels, head_logits(): pl.pallas_call(functools.partial(logits_kernel, vocab), grid=(tiles,), ou...  26.7 us
    ppermute x7, starting transfers between devices, swap(): return lax.ppermute(value, axis_name, [(i, i ^ bit) for i in range(size)])  14.7 us
  transfers between devices with their start and end apart: 7, of which 3 were waited for; matrix products, arithmetic and copies ran while one was open for 1% of the time, Pallas kernels for 7%

profile of v5, /device:TPU:0, one launch (start us, length us, event | category | flops | bytes accessed | tf_op | source)
XLA Modules:
  0.0 452.2 jit_solution(16184505485226523548)
XLA Ops:
  0.7 1.3 dynamic_slice.72
  2.0 1.4 fusion.22
  3.4 1.3 reshape.180.refs_3_.refs_8_
  4.6 1.3 reshape.181.refs_4_.refs_15_
  5.9 1.3 reshape.182.refs_5_.refs_12_
  7.2 1.3 reshape.183.refs_6_.refs_13_
  8.4 1.9 copy.41.refs_7_
  10.4 1.9 copy.42.refs_8_
  12.2 0.9 copy.43.refs_9_
  13.2 0.9 copy.44.refs_11_
  14.1 0.9 copy.45.refs_12_
  15.0 0.9 copy.46.refs_13_
  15.9 1.9 pad_add_fusion.4.refs_0_
  17.8 103.8 %shard_map.356 = (bf16[512,768]{1,0:T(8,128)(2,1)}, bf16[512,768]{1,0:T(8,128)(2,1)}, bf16[512,768]{1,0:T(8,128)(2,1)}, f32[16,512]{1,0:T(8,128)}, bf16[256,768]...) custom-call(s32[4]{0:T(128)} %pad_add_fusion.4.refs_0_, ...), custom_call_target="tpu_custom_call" | custom-call | flops 80000000000 | bytes 60000000 | tf_op jit(solution)/shard_map/pallas_call | solution.py:639
  121.6 1.2 copy.48
  122.8 3.0 collective-permute-start.1
  125.7 1.0 collective-permute-start.2
  126.8 1.3 broadcast_select_fusion
  128.3 24.3 %collective-permute-done.1 = bf16[256,768]{0,1:T(8,128)(2,1)S(1)} collective-permute-done((bf16[256,768]{0,1:T(8,128)(2,1)S(1)}, bf16[256,768]{0,1:T(8,128)(2,1)S(1)}, u32[]{:S(2)}, u32[]{:S(2)}) %collective-permute-start.1) | collective-permute-done | bytes 393248 | tf_op jit(solution)/shard_map/ppermute | solution.py:42
  152.6 4.5 copy-done
  157.1 13.3 %shard_map.358 = (f32[8192,512]{1,0:T(8,128)}, f32[8,512]{1,0:T(8,128)S(1)}) custom-call(bf16[768,512]{1,0:T(8,128)(2,1)S(1)} %bitcast.153, bf16[8032,768]{1,0:T(8,128)(2,1)S(1)} %copy-done, s32[1,512]{1,0:T(1,128)S(1)} %bitcast.157), custom_call_target="tpu_custom_call" | custom-call | flops 6316621824 | bytes 28786688 | tf_op jit(solution)/shard_map/pallas_call | solution.py:1346
  170.6 13.3 %shard_map.357 = (f32[8192,512]{1,0:T(8,128)}, f32[8,512]{1,0:T(8,128)S(1)}) custom-call(bf16[768,512]{1,0:T(8,128)(2,1)S(1)} %get-tuple-element.209.flat_ref, bf16[8032,768]{1,0:T(8,128)(2,1)S(1)} %copy-done.1, s32[1,512]{1,0:T(1,128)S(1)} %bitcast.155), custom_call_target="tpu_custom_call" | custom-call | flops 6316621824 | bytes 28786688 | tf_op jit(solution)/shard_map/pallas_call | solution.py:1346
  184.0 2.2 collective-permute-start.5
  186.2 7.6 %collective-permute-start.4 = (f32[4,8,256]{2,0,1:T(4,128)S(1)}, f32[4,8,256]{2,0,1:T(4,128)S(1)}, u32[]{:S(2)}, u32[]{:S(2)}) collective-permute-start(f32[4,8,256]{2,0,1:T(4,128)S(1)} %copy.51), channel_id=1, source_target_pairs={{0,2},{1,3},{2,0},{3,1},{4,6},{5,7},{6,4},{7,5},{8,10},{9,11},{10,... | collective-permute-start | bytes 98312 | tf_op jit(solution)/shard_map/ppermute | solution.py:42
  193.7 1.2 constant_dynamic-slice_fusion
  194.9 1.0 collective-permute-done.4
  195.9 1.8 collective-permute-done.3
  197.7 14.6 %shard_map.359 = (bf16[8192,512]{1,0:T(8,128)(2,1)S(1)}, bf16[512,768]{1,0:T(8,128)(2,1)S(1)}) custom-call(f32[8192,512]{1,0:T(8,128)} %get-tuple-element.118.logits_ref, bf16[8032,768]{1,0:T(8,128)(2,1)S(1)} %copy-done.1, s32[1,512]{1,0:T(1,128)S(1)} %bitcast.158, f32[1,512]{1,0:T(1,128)S(1)} %bitcast.160, s32[1,512]{1,0:T(1,128)S(1)} %bitcast.162), custom_call_target="tpu_custom_call" | custom-call | flops 6316621824 | bytes 37011456 | tf_op jit(solution)/shard_map/pallas_call | solution.py:1394
  212.4 1.0 collective-permute-start.6
  213.3 16.2 %shard_map.360 = (bf16[8192,512]{1,0:T(8,128)(2,1)S(1)}, f32[512,768]{1,0:T(8,128)S(1)}) custom-call(f32[8192,512]{1,0:T(8,128)} %get-tuple-element.120.logits_ref, bf16[8032,768]{1,0:T(8,128)(2,1)S(1)} %copy-done.1, s32[1,512]{1,0:T(1,128)S(1)} %bitcast.156, f32[1,512]{1,0:T(1,128)S(1)} %bitcast.159, s32[1,512]{1,0:T(1,128)S(1)} %bitcast.161), custom_call_target="tpu_custom_call" | custom-call | flops 6316621824 | bytes 37011456 | tf_op jit(solution)/shard_map/pallas_call | solution.py:1394
  229.6 3.3 copy-done.4
  232.8 1.1 copy-done.5
  234.0 1.9 subtract_select_fusion
  235.9 0.7 copy-done.25
  236.7 54.1 %shard_map.361 = (f32[2,96,4096]{2,1,0:T(8,128)}, bf16[2,96,4096]{2,1,0:T(8,128)(2,1)}, f32[2,192,3072]{2,1,0:T(8,128)}, bf16[2,192,3072]{2,1,0:T(8,128)(2,1)}, ...) custom-call(s32[4]{0:T(128)} %pad_add_fusion.4.refs_0_, ...), custom_call_target="tpu_custom_call" | custom-call | flops 40000000000 | bytes 34084880 | tf_op jit(solution)/shard_map/pallas_call | solution.py:1200
  290.8 57.8 %shard_map.362 = (f32[1024,768]{1,0:T(8,128)}, f32[256,768]{1,0:T(8,128)}, bf16[256,768]{1,0:T(8,128)(2,1)}, bf16[256,768]{1,0:T(8,128)(2,1)}, bf16[256,768]{1,0...) custom-call(s32[4]{0:T(128)} %pad_add_fusion.4.refs_0_, ...), custom_call_target="tpu_custom_call" | custom-call | flops 40000000000 | bytes 22088720 | tf_op jit(solution)/shard_map/pallas_call | solution.py:1200
  348.6 84.0 %shard_map.363 = (f32[256,768]{1,0:T(8,128)}, f32[8,768]{1,0:T(8,128)}, f32[8032,96]{1,0:T(8,128)}, f32[96,192]{1,0:T(8,128)}, f32[96,192]{1,0:T(8,128)}, /*inde...) custom-call(s32[4]{0:T(128)} %pad_add_fusion.4.refs_0_, ...), custom_call_target="tpu_custom_call" | custom-call | flops 20000000000 | bytes 20492304 | tf_op jit(solution)/shard_map/pallas_call | solution.py:1200
  432.6 1.5 slice_reduce_fusion
  434.1 1.8 copy.62
  435.8 5.4 %copy.63 = f32[8032,96]{0,1:T(8,128)} copy(f32[8032,96]{1,0:T(8,128)} %get-tuple-element.199) | data formatting | bytes 6168576
  441.2 0.9 copy.96
  442.1 0.9 copy.97
  443.0 0.7 copy-done.6
  443.7 1.7 copy.98
  445.4 0.6 copy.99
  448.6 0.6 copy.104
  450.5 0.7 copy.107
  451.2 0.7 copy.108
  (91 shorter events, 4.4 us)
Async XLA Ops:
  0.7 11.6 %copy-start.9 = (bf16[768,192]{0,1:T(8,128)(2,1)S(1)}, bf16[768,192]{0,1:T(8,128)(2,1)}, u32[]{:S(2)}) copy-start(bf16[768,192]{0,1:T(8,128)(2,1)} %param.34) | copy-start | bytes 884740
  0.7 12.5 %copy-start.10 = (bf16[768,192]{0,1:T(8,128)(2,1)S(1)}, bf16[768,192]{0,1:T(8,128)(2,1)}, u32[]{:S(2)}) copy-start(bf16[768,192]{0,1:T(8,128)(2,1)} %param.36) | copy-start | bytes 884740
  0.7 13.4 %copy-start.11 = (bf16[768,192]{0,1:T(8,128)(2,1)S(1)}, bf16[768,192]{0,1:T(8,128)(2,1)}, u32[]{:S(2)}) copy-start(bf16[768,192]{0,1:T(8,128)(2,1)} %param.37) | copy-start | bytes 884740
  8.4 6.6 %copy-start.12 = (bf16[768,192]{0,1:T(8,128)(2,1)S(1)}, bf16[768,192]{0,1:T(8,128)(2,1)}, u32[]{:S(2)}) copy-start(bf16[768,192]{0,1:T(8,128)(2,1)} %param.38) | copy-start | bytes 884740
  17.8 109.0 %copy-start.23 = (s32[1024]{0:T(1024)S(1)}, s32[1024]{0:T(1024)}, u32[]{:S(2)}) copy-start(s32[1024]{0:T(1024)} %param.27) | copy-start | bytes 12292
  17.8 109.0 %copy-start.24 = (pred[1024]{0:T(1024)(128)(4,1)S(1)}, pred[1024]{0:T(1024)(128)(4,1)}, u32[]{:S(2)}) copy-start(pred[1024]{0:T(1024)(128)(4,1)} %constant.216) | copy-start | bytes 3076
  122.8 29.8 %collective-permute-start.1 = (bf16[256,768]{0,1:T(8,128)(2,1)S(1)}, bf16[256,768]{0,1:T(8,128)(2,1)S(1)}, u32[]{:S(2)}, u32[]{:S(2)}) collective-permute-start(bf16[256,768]{0,1:T(8,128)(2,1)S(1)} %copy.48), channel_id=1, source_target_pairs={{0,2},{1,3},{2,0},{3,1},{4,6},{5,7},{6,4},{7,5},{8,10},{9,11},{10,... | collective-permute-start | bytes 1179656 | tf_op jit(solution)/shard_map/ppermute | solution.py:42
  125.7 26.8 %collective-permute-start.2 = (bf16[256,768]{0,1:T(8,128)(2,1)S(1)}, bf16[256,768]{0,1:T(8,128)(2,1)S(1)}, u32[]{:S(2)}, u32[]{:S(2)}) collective-permute-start(bf16[256,768]{0,1:T(8,128)(2,1)S(1)} %copy.48), channel_id=1, source_target_pairs={{0,3},{1,2},{2,1},{3,0},{4,7},{5,6},{6,5},{7,4},{8,11},{9,10},{10,... | collective-permute-start | bytes 1179656 | tf_op jit(solution)/shard_map/ppermute | solution.py:42
  126.8 43.7 %collective-permute-start = (bf16[256,768]{0,1:T(8,128)(2,1)S(1)}, bf16[256,768]{0,1:T(8,128)(2,1)S(1)}, u32[]{:S(2)}, u32[]{:S(2)}) collective-permute-start(bf16[256,768]{0,1:T(8,128)(2,1)S(1)} %copy.48), channel_id=1, source_target_pairs={{0,1},{1,0},{2,3},{3,2},{4,5},{5,4},{6,7},{7,6},{8,9},{9,8},{10,11... | collective-permute-start | bytes 1179656 | tf_op jit(solution)/shard_map/ppermute | solution.py:42
  152.6 4.5 copy-start
  157.1 13.5 %copy-start.1 = (bf16[8032,768]{1,0:T(8,128)(2,1)S(1)}, bf16[8032,768]{1,0:T(8,128)(2,1)}, u32[]{:S(2)}) copy-start(bf16[8032,768]{1,0:T(8,128)(2,1)} %table_ref.7) | copy-start | bytes 37011460
  184.0 13.7 %collective-permute-start.5 = (f32[4,8,256]{2,1,0:T(8,128)S(1)}, f32[4,8,256]{2,1,0:T(8,128)S(1)}, u32[]{:S(2)}, u32[]{:S(2)}) collective-permute-start(f32[4,8,256]{2,1,0:T(8,128)S(1)} %pad_maximum_fusion.2), channel_id=1, source_target_pairs={{0,3},{1,2},{2,1},{3,0},{4,7},{5,6},{6,5},{7,4},{8,11},{9,10},{10,... | collective-permute-start | bytes 98312 | tf_op jit(solution)/shard_map/ppermute | solution.py:42
  186.2 9.7 %collective-permute-start.4 = (f32[4,8,256]{2,0,1:T(4,128)S(1)}, f32[4,8,256]{2,0,1:T(4,128)S(1)}, u32[]{:S(2)}, u32[]{:S(2)}) collective-permute-start(f32[4,8,256]{2,0,1:T(4,128)S(1)} %copy.51), channel_id=1, source_target_pairs={{0,2},{1,3},{2,0},{3,1},{4,6},{5,7},{6,4},{7,5},{8,10},{9,11},{10,... | collective-permute-start | bytes 98312 | tf_op jit(solution)/shard_map/ppermute | solution.py:42
  193.7 3.9 collective-permute-start.3
  212.3 17.2 %copy-start.2 = (bf16[512,768]{1,0:T(8,128)(2,1)}, bf16[512,768]{1,0:T(8,128)(2,1)S(1)}, u32[]{:S(2)}) copy-start(bf16[512,768]{1,0:T(8,128)(2,1)S(1)} %get-tuple-element.125.refs_7_) | copy-start | bytes 2359300
  212.3 17.2 %copy-start.3 = (bf16[8192,512]{1,0:T(8,128)(2,1)}, bf16[8192,512]{1,0:T(8,128)(2,1)S(1)}, u32[]{:S(2)}) copy-start(bf16[8192,512]{1,0:T(8,128)(2,1)S(1)} %get-tuple-element.119.refs_1_) | copy-start | bytes 25165828
  212.4 23.6 %collective-permute-start.6 = (bf16[256,768]{1,0:T(8,128)(2,1)S(1)}, bf16[256,768]{1,0:T(8,128)(2,1)S(1)}, u32[]{:S(2)}, u32[]{:S(2)}) collective-permute-start(bf16[256,768]{1,0:T(8,128)(2,1)S(1)} %slice.99), channel_id=1, source_target_pairs={{0,2},{1,3},{2,0},{3,1},{4,6},{5,7},{6,4},{7,5},{8,10},{9,11},{10,... | collective-permute-start | bytes 1179656 | tf_op jit(solution)/shard_map/ppermute | solution.py:42
  229.5 3.3 copy-start.4
  232.8 1.1 copy-start.5
  235.9 0.7 copy-start.25
  435.8 5.4 %copy-start.7 = (f32[256,768]{1,0:T(8,128)S(1)}, f32[256,768]{1,0:T(8,128)}, u32[]{:S(2)}) copy-start(f32[256,768]{1,0:T(8,128)} %get-tuple-element.270.refs_10_) | copy-start | bytes 2359300
  435.8 6.2 %copy-start.8 = (f32[256,768]{1,0:T(8,128)S(1)}, f32[256,768]{1,0:T(8,128)}, u32[]{:S(2)}) copy-start(f32[256,768]{1,0:T(8,128)} %get-tuple-element.272) | copy-start | bytes 2359300
  441.2 2.5 copy-start.6
  443.7 1.7 copy-start.22
  443.7 2.4 copy-start.21
  443.7 3.0 copy-start.20
  443.7 3.6 copy-start.19
  443.7 4.3 copy-start.18
  443.7 4.9 %copy-start.17 = (f32[96,192]{1,0:T(8,128)S(1)}, f32[96,192]{1,0:T(8,128)}, u32[]{:S(2)}) copy-start(f32[96,192]{1,0:T(8,128)} %get-tuple-element.283) | copy-start | bytes 221188
  443.7 5.6 %copy-start.16 = (f32[96,192]{1,0:T(8,128)S(1)}, f32[96,192]{1,0:T(8,128)}, u32[]{:S(2)}) copy-start(f32[96,192]{1,0:T(8,128)} %get-tuple-element.284) | copy-start | bytes 221188
  443.7 6.2 %copy-start.15 = (f32[192,96]{1,0:T(8,128)S(1)}, f32[192,96]{1,0:T(8,128)}, u32[]{:S(2)}) copy-start(f32[192,96]{1,0:T(8,128)} %get-tuple-element.285) | copy-start | bytes 221188
  445.4 5.2 %copy-start.14 = (f32[96,512]{1,0:T(8,128)S(1)}, f32[96,512]{1,0:T(8,128)}, u32[]{:S(2)}) copy-start(f32[96,512]{1,0:T(8,128)} %get-tuple-element.286) | copy-start | bytes 589828
  445.4 5.8 %copy-start.13 = (f32[96,512]{1,0:T(8,128)S(1)}, f32[96,512]{1,0:T(8,128)}, u32[]{:S(2)}) copy-start(f32[96,512]{1,0:T(8,128)} %get-tuple-element.287) | copy-start | bytes 589828

commit v6 on v5

--- a/solution.py
+++ b/solution.py
@@ -248,19 +248,27 @@
             send3[j] = shard_ref[shard, :, :width].astype(BF16)
             self.copies.append(comm.send(send3.at[j], recv3.at[j], comm.z_peers[j]))
 
-    def finish(self, outs, flipped, turn_ref):
-        self.wait()
-        keep, _, recv = self.three
+
+def finish_kernel(vocab, e_keep, e_recv, f_keep, f_recv, c_keep, c_recv, s_keep, s_recv, gin, *refs):
+    e_out, gin_out, refs, turn_ref = refs[0], refs[1], refs[2:-1], refs[-1]
+    gin_out[...] = gin[...]
+    width = e_keep.shape[2]
+    for side in range(2):
+        count = min(width, vocab - side * width)
+        e_out[:, side * width : side * width + count] = e_keep[side, :, :count] + e_recv[
+            side, :, :count
+        ].astype(F32)
+    for keep, recv, outs in ((f_keep, f_recv, refs[8:]), (c_keep, c_recv, refs[4:8]), (s_keep, s_recv, refs[:4])):
         width = keep.shape[1] // len(outs)
         for m, out in enumerate(outs):
             cols = slice(m * width, (m + 1) * width)
             part = keep[:, cols] + recv[0, :, cols].astype(F32)
             part = part + (recv[1, :, cols].astype(F32) + recv[2, :, cols].astype(F32))
-            if m == flipped:
-                turn_ref[:, :width] = part
-                out[...] = turn_ref[:, :width].T
+            if out.shape[0] == 96:
+                out[...] = part
             else:
-                out[...] = part
+                turn_ref[...] = part
+                out[...] = turn_ref[...].T
 
 
 class WideReduction:
@@ -285,9 +293,10 @@
 
 def spots(scal, split):
     if split:
-        half, core = lax.rem(lax.axis_index("tensor"), 2), lax.rem(lax.axis_index("dp"), 2)
-    else:
-        half, core = scal[0], scal[3]
+        z = lax.axis_index("tensor")
+        half, core = lax.rem(z, 2), lax.rem(lax.axis_index("dp"), 2)
+        return half, scal[z // 2], scal[2 + z // 2] - half * KEYS, core
+    half, core = scal[0], scal[3]
     return half, scal[1], scal[2] - half * KEYS, core
 
 
@@ -359,7 +368,8 @@
 
 
 def forward_kernel(split, *refs):
-    (scal, x_own, source, gain_self, gain_cross, gain_ff, gain_final), refs = refs[:7], refs[7:]
+    (scal, x_own, source, gains), refs = refs[:4], refs[4:]
+    gain_self, gain_cross, gain_ff, gain_final = (gains.at[i : i + 1] for i in range(4))
     shards, refs = refs[: 11 if split else 5], refs[11 if split else 5 :]
     (q1, k1, v1, lse1, att1, h1_out, q2, k2, v2), refs = refs[:9], refs[9:]
     (out_ref, fin_ref, h2_ref, att_t_ref, att2, lse2), refs = refs[:6], refs[6:]
@@ -376,7 +386,9 @@
     dp = lax.axis_index("dp")
     z = lax.axis_index("tensor")
     low, high = lax.rem(z, 2), z // 2
-    half, live, live_src = low, scal[1], scal[2] - low * KEYS
+    half = low
+    live = scal[high] if split else scal[1]
+    live_src = (scal[2 + high] if split else scal[2]) - low * KEYS
     z_peers = [(dp, high * 2 + 1 - low)]
     peers = z_peers
     if split:
@@ -423,7 +435,7 @@
         def place_block(target, first):
             rows = pl.ds(pl.multiple_of(z * hid, 16), hid)
             for m in range(3):
-                target[m, rows, :] = flip(shards[first + m][...]).astype(BF16)
+                target[m, rows, :] = shards[first + m][...]
             target[3, rows, :] = shards[first + 3][...]
 
         def place_wide(target, shard, flipped):
@@ -599,7 +611,8 @@
 
     out = h2 + dot_nn(mix_ref[...], wd[...])
     out_ref[...] = out
-    fin_ref[...] = (out * rms_scale(out) * gain_final[...] * D ** (-0.5)).astype(BF16)
+    x_ref[:ROWS, :] = out * rms_scale(out) * gain_final[...] * D ** (-0.5)
+    fin_ref[...] = x_ref[:ROWS, :].T.astype(BF16)
     for copy in leaving:
         copy.wait()
 
@@ -609,7 +622,7 @@
     block = (ROWS, D)
     outs = [whole(pair, BF16)] * 3 + [whole((16, TGT), F32), whole(block, BF16), whole(block, F32)]
     outs += [whole(pair, BF16)] + [whole((KEYS, D), BF16)] * 2
-    outs += [whole(block, F32), whole(block, BF16), whole(block, F32), whole((D, ROWS), F32)]
+    outs += [whole(block, F32), whole((D, ROWS), BF16), whole(block, F32), whole((D, ROWS), F32)]
     outs += [whole(block, BF16), whole((16, TGT), F32)]
     vmem = pl.BlockSpec(memory_space=pltpu.VMEM)
     out_specs = [vmem] * len(outs)
@@ -635,7 +648,7 @@
     ]
     if split:
         scratch += [pltpu.SemaphoreType.DMA((27 * 5,))] * 2 + [pltpu.SemaphoreType.DMA((11,))]
-    args = (scal, x_own, source, *gains, *weights)
+    args = (scal, x_own, source, gains, *weights)
     return pl.pallas_call(
         functools.partial(forward_kernel, split),
         out_shape=outs,
@@ -865,15 +878,17 @@
 
 
 def table_ff_kernel(*refs):
-    (scal, g_a, g_b, fm_a, fm_b, fs_a, fs_b, gf_a, gf_b, gf_2), refs = refs[:10], refs[10:]
-    (block_out, h2_in, gain_ff, gain_final, wg, wu, wd, w_co, att_t), refs = refs[:9], refs[9:]
+    (scal, g_a, g_b, fin_a, fin_b, gf_sum, gf_3), refs = refs[:7], refs[7:]
+    (block_out, h2_in, gains, wg, wu, wd, w_co, att_t), refs = refs[:8], refs[8:]
+    gain_ff, gain_final = gains.at[2:3], gains.at[3:4]
     (e_keep, e_send, f_keep, f_send, res_ref, rows_ref), refs = refs[:6], refs[6:]
     (gatt_ref, gatt_other, dot_ref, dot_other, gg_ref), refs = refs[:5], refs[5:]
     (ga_ring, gb_ring, w_ring, mine_ring, send_ring, got, e_keep1, e_send1, e_recv1), refs = (
         refs[:9],
         refs[9:],
     )
-    (flat_ref, flat_2, nm_ref, ns_ref, gm_ref, gs_ref, gn_ref, gf_send, gf_recv), refs = refs[:9], refs[9:]
+    (flat_ref, flat_2, nm_ref, ns_ref, gm_ref, gs_ref, gn_ref, gf_recv), refs = refs[:8], refs[8:]
+    (fm_a, fm_b, fs_a, fs_b), refs = refs[:4], refs[4:]
     send_sem, recv_sem, load_sem, w_sem = refs
     comm = Comm(send_sem, recv_sem)
     core = comm.c
@@ -899,11 +914,9 @@
     for copy in load(0) + load_weights(0):
         copy.start()
     comm.barrier()
-    gf_send[...] = gf_b[ROWS:, :].astype(BF16)
-    gf_copies = [
-        comm.send(gf_send, gf_recv.at[0], comm.z_peers[0]),
-        comm.send(gf_a.at[ROWS:], gf_recv.at[1], comm.z_peers[2]),
-    ]
+    gf_copies = [comm.send(gf_3, gf_recv, comm.z_peers[2])]
+    split_rows(fin_a, fm_a, fs_a, core, True)
+    split_rows(fin_b, fm_b, fs_b, core, True)
     e_core, e_line, f_core = comm.reserve(8), comm.reserve(8), comm.reserve(4)
 
     def core_copy(step):
@@ -973,8 +986,7 @@
     for copy in gf_copies:
         copy.wait()
 
-    grad = gf_b[:ROWS, :] + gf_recv[0].astype(F32)
-    grad = grad + (gf_2[...].astype(F32) + gf_recv[1].astype(F32))
+    grad = gf_sum[...] + gf_recv[...].astype(F32)
     out = block_out[...]
     res, gg_final = norm_back(out, rms_scale(out), gain_final[...], grad * D ** (-0.5))
     gg_ref[0:1, :] = gg_final
@@ -1083,7 +1095,8 @@
 
 def cross_kernel(*refs):
     (scal, q2, k2, v2, lse2, g_own, g_other, dot_own, dot_oth, source), refs = refs[:10], refs[10:]
-    (w_ck, w_cv, w_cq, w_so, h1, gain_cross, res_in, rows_in, att), refs = refs[:9], refs[9:]
+    (w_ck, w_cv, w_cq, w_so, h1, gains, res_in, rows_in, att), refs = refs[:9], refs[9:]
+    gain_cross = gains.at[1:2]
     (e_send, f_keep, f_send), refs = refs[:3], refs[3:]
     (gsrc, res_ref, rows_ref, gatt1, gatt1_other, gg_ref), refs = refs[:6], refs[6:]
     (c_keep, c_send, f_keep2, f_send2, e_recv), refs = refs[:5], refs[5:]
@@ -1123,20 +1136,23 @@
         copy.wait()
 
 
-def self_kernel(vocab, *refs):
-    (scal, q1, k1, v1, lse1, g_own, g_other, x_own, gain_self, w_q, w_k, w_v), refs = (
+def self_kernel(*refs):
+    (scal, q1, k1, v1, lse1, g_own, g_other, x_own, gains, w_q, w_k, w_v), refs = (
         refs[:12],
         refs[12:],
     )
+    gain_self = gains.at[0:1]
     (res_in, rows_in, att, gg_a, gg_b), refs = refs[:5], refs[5:]
-    (e_keep, e_recv, f_keep, f_send, c_keep, c_send), refs = refs[:6], refs[6:]
-    (gin_ref, gains_ref, e_out), refs = refs[:3], refs[3:]
-    s_outs, c_outs, f_outs, refs = refs[:4], refs[4:8], refs[8:11], refs[11:]
+    (f_keep, f_send, c_keep, c_send), refs = refs[:4], refs[4:]
+    (gin_ref, gains_ref, f_keep3, f_recv3, c_keep3, c_recv3, s_keep3, s_recv3), refs = refs[:8], refs[8:]
     (g_ref, dq_ref, dk_ref, dv_ref, flat_ref, flat_2, a_ref, b_ref, gain_ref), refs = refs[:9], refs[9:]
     (mine, send, got, shard_ref, f_recv), refs = refs[:5], refs[5:]
-    f_three, (c_recv1, c_keep2, c_send2, c_recv2), refs = refs[:3], refs[3:7], refs[7:]
-    c_three, s_one, s_two, s_three, refs = refs[:3], refs[3:6], refs[6:9], refs[9:12], refs[12:]
-    gain_send, gain_recv, turn_ref, refs = refs[0], refs[1], refs[2], refs[3:]
+    (c_recv1, c_keep2, c_send2, c_recv2), refs = refs[:4], refs[4:]
+    s_one, s_two, refs = refs[:3], refs[3:6], refs[6:]
+    (f_send3, c_send3, s_send3, gain_send, gain_recv), refs = refs[:5], refs[5:]
+    f_three = f_keep3, f_send3, f_recv3
+    c_three = c_keep3, c_send3, c_recv3
+    s_three = s_keep3, s_send3, s_recv3
     comm = Comm(*refs)
     comm.barrier()
     cross = Flow(comm, (c_keep, c_send, c_recv1), (c_keep2, c_send2, c_recv2), c_three)
@@ -1173,13 +1189,6 @@
     cross.send_second()
     gain_done(1, copy)
     copy = gain_step(2, comm.x_peer)
-    width = e_keep.shape[2]
-    for start in range(0, vocab, 512):
-        side, column = start // width, start % width
-        count = min(512, vocab - start)
-        cols = slice(column, column + 512)
-        turn_ref[...] = e_keep[side, :, cols] + e_recv[side, :, cols].astype(F32)
-        e_out[start : start + count, :] = turn_ref[...].T[:count, :]
     gain_done(2, copy)
     copy = gain_step(3, comm.y_peer)
     own.fold_second()
@@ -1187,11 +1196,160 @@
     cross.fold_third(shard_ref)
     gain_done(3, copy)
     copy = gain_step(4, comm.z_peers[1])
-    ff.finish(f_outs, 2, turn_ref)
+    ff.wait()
     own.fold_third(shard_ref)
     gain_done(4, copy)
-    cross.finish(c_outs, 3, turn_ref)
-    own.finish(s_outs, 3, turn_ref)
+    cross.wait()
+    own.wait()
+
+
+def head_kernel(vocab, *refs):
+    (lens, fin_own, table, targets), refs = refs[:4], refs[4:]
+    (g_a, g_b, gf_sum, gf_3, loss_ref, fin_a, fin_b), refs = refs[:7], refs[7:]
+    (e_ref, l_ref, fin_recv, stats, stats_recv, ring, acc_ref, gf_send, gf_recv), refs = (
+        refs[:9],
+        refs[9:],
+    )
+    send_sem, recv_sem, e_sem, ring_sem = refs
+    comm = Comm(send_sem, recv_sem)
+    z = comm.z
+    shards = (z,) + comm.z_shards
+    load = pltpu.make_async_copy(table, e_ref.at[:vocab], e_sem.at[0])
+    load.start()
+    barrier = pltpu.get_barrier_semaphore()
+    for peer in comm.z_peers:
+        pl.semaphore_signal(
+            barrier, inc=1, device_id={"dp": peer[0], "tensor": peer[1]}, device_id_type=MESH_ID
+        )
+    pl.semaphore_wait(barrier, 3)
+    fin_copies = [comm.send(fin_own, fin_recv.at[j], comm.z_peers[j]) for j in range(3)]
+    padded = e_ref.shape[0]
+    if padded > vocab:
+        e_ref[vocab:, :] = jnp.zeros((padded - vocab, D), BF16)
+    load.wait()
+    tiles = padded // HTILE
+    local = []
+    for shard in shards:
+        target = targets[pl.ds(shard, 1), :] - z * vocab
+        local.append(jnp.where(target < vocab, target, -1))
+    entry = lax.broadcasted_iota(jnp.int32, (HTILE, ROWS), 0)
+
+    for i in range(4):
+        if i > 0:
+            fin_copies[i - 1].wait()
+        fin = fin_own if i == 0 else fin_recv.at[i - 1]
+        lanes = slice((i % 2) * ROWS, (i % 2 + 1) * ROWS)
+        (fin_b if i < 2 else fin_a)[:, lanes] = fin[...]
+        row = lax.broadcasted_iota(jnp.int32, (8, ROWS), 0)
+        stats[i] = jnp.where(row == 0, 2 * NEG, 0.0)
+
+        @pl.loop(0, tiles)
+        def _(tile):
+            start = pl.multiple_of(tile * HTILE, HTILE)
+            logits = dot_nn(e_ref[pl.ds(start, HTILE), :], fin[...])
+            logits = jnp.where(entry < vocab - start, logits, 2 * NEG)
+            l_ref[i, pl.ds(start, HTILE), :] = logits
+            old = stats[i, 0:1, :]
+            new = jnp.maximum(old, jnp.max(logits, axis=0, keepdims=True))
+            stats[i, 1:2, :] = stats[i, 1:2, :] * jnp.exp(old - new) + jnp.sum(
+                jnp.exp(logits - new), axis=0, keepdims=True
+            )
+            stats[i, 0:1, :] = new
+            hit = jnp.where(entry == local[i] - start, logits, 0.0)
+            stats[i, 2:3, :] += jnp.sum(hit, axis=0, keepdims=True)
+
+    copies = [comm.send(stats, stats_recv.at[j], comm.z_peers[j]) for j in range(3)]
+    for copy in copies:
+        copy.wait()
+
+    def over_z(values, op):
+        return op(op(values[0], values[1]), op(values[2], values[3]))
+
+    lse, live = [], []
+    for i in range(4):
+        parts = [stats.at[i]] + [stats_recv.at[k - 1, i ^ k] for k in (1, 2, 3)]
+        top = over_z([p[0:1, :] for p in parts], jnp.maximum)
+        total = over_z([p[1:2, :] * jnp.exp(p[0:1, :] - top) for p in parts], jnp.add)
+        picked = over_z([p[2:3, :] for p in parts], jnp.add)
+        lse.append(top + jnp.log(total))
+        lane = lax.broadcasted_iota(jnp.int32, (1, ROWS), 1)
+        live.append(lax.rem(shards[i], 2) * ROWS + lane < lens[shards[i] // 2])
+        loss_ref[pl.ds(shards[i], 1), :] = jnp.where(live[i], lse[i] - picked, 0.0)
+
+    gf_copies = []
+    for i in (2, 1, 3, 0):
+        target = g_b if i < 2 else g_a
+        acc_ref[...] = jnp.zeros_like(acc_ref)
+
+        def leave(tile):
+            rows = pl.ds(pl.multiple_of(tile * HTILE, HTILE), HTILE)
+            slot = lax.rem(tile, 2)
+            return pltpu.make_async_copy(
+                ring.at[slot], target.at[rows, pl.ds((i % 2) * ROWS, ROWS)], ring_sem.at[slot]
+            )
+
+        @pl.loop(0, tiles)
+        def _(tile):
+            start = pl.multiple_of(tile * HTILE, HTILE)
+
+            @pl.when(tile >= 2)
+            def _():
+                leave(tile - 2).wait()
+
+            hit = jnp.where(entry == local[i] - start, 1.0, 0.0)
+            grad = jnp.exp(l_ref[i, pl.ds(start, HTILE), :] - lse[i]) - hit
+            grad = jnp.where(live[i], grad, 0.0).astype(BF16)
+            ring[lax.rem(tile, 2)] = grad
+            leave(tile).start()
+            acc_ref[...] += lax.dot_general(
+                grad, e_ref[pl.ds(start, HTILE), :], (((0,), (0,)), ((), ())), preferred_element_type=F32
+            )
+
+        for tile in (tiles - 2, tiles - 1):
+            leave(tile).wait()
+        if i == 3:
+            gf_3[...] = acc_ref[...].astype(BF16)
+        elif i > 0:
+            gf_send[i - 1] = acc_ref[...].astype(BF16)
+            gf_copies.append(comm.send(gf_send.at[i - 1], gf_recv.at[i - 1], comm.z_peers[i - 1]))
+    for copy in gf_copies:
+        copy.wait()
+    gf_sum[...] = acc_ref[...] + (gf_recv[0].astype(F32) + gf_recv[1].astype(F32))
+
+
+def fused_head(lens, fin_t, table, targets):
+    vocab = table.shape[0]
+    padded = pl.cdiv(vocab, HTILE) * HTILE
+    hbm, vmem = pl.BlockSpec(memory_space=pl.ANY), pl.BlockSpec(memory_space=pltpu.VMEM)
+    grad = whole((padded, TGT), BF16)
+    block = (ROWS, D)
+    return pl.pallas_call(
+        functools.partial(head_kernel, vocab),
+        out_shape=[
+            grad, grad, whole(block, F32), whole(block, BF16), whole((4, ROWS), F32),
+            whole((D, TGT), BF16), whole((D, TGT), BF16),
+        ],
+        in_specs=[pl.BlockSpec(memory_space=pltpu.SMEM), vmem, hbm, vmem],
+        out_specs=[hbm, hbm] + [vmem] * 5,
+        scratch_shapes=[
+            pltpu.VMEM((padded, D), BF16),
+            pltpu.VMEM((4, padded, ROWS), F32),
+            pltpu.VMEM((3, D, ROWS), BF16),
+            pltpu.VMEM((4, 8, ROWS), F32),
+            pltpu.VMEM((3, 4, 8, ROWS), F32),
+            pltpu.VMEM((2, HTILE, ROWS), BF16),
+            pltpu.VMEM(block, F32),
+            pltpu.VMEM((2,) + block, BF16),
+            pltpu.VMEM((2,) + block, BF16),
+            pltpu.SemaphoreType.DMA((8,)),
+            pltpu.SemaphoreType.DMA((8,)),
+            pltpu.SemaphoreType.DMA((1,)),
+            pltpu.SemaphoreType.DMA((2,)),
+        ],
+        compiler_params=pltpu.CompilerParams(
+            collective_id=4, has_side_effects=True, vmem_limit_bytes=FUSED_LIMIT
+        ),
+    )(lens, fin_t, table, targets)
 
 
 def fused_call(body, collective_id, ins, outs, scratch, copies, flops):
@@ -1213,11 +1371,10 @@
 
 
 def fused_backward(
-    scal, flats_a, flats_b, g_a, g_b, gf_a, gf_b, gf_2, saved, weights, gains, block_in, source, vocab
+    scal, fin_a, fin_b, g_a, g_b, gf_sum, gf_3, saved, weights, gains, block_in, source, vocab
 ):
     (q1, k1, v1, lse1, a1, h1, q2, k2, v2, block_out, h2, att_t, a2, lse2) = saved
     (sq, sk, sv, so, cq, ck, cv, co, wg, wu, wd) = weights
-    gain_self, gain_cross, gain_ff, gain_final = gains
 
     def vm(*shape, dtype=BF16):
         return pltpu.VMEM(shape, dtype)
@@ -1241,7 +1398,7 @@
             vm(2, 3, HALF_D, 512), vm(16, HALF_D, 512), vm(2, 192, e_half, dtype=F32),
             vm(2, 192, e_half), vm(2, 192, e_half), vm(D, ROWS), vm(D, ROWS),
             vm(*half_t), vm(*half_t), vm(*half_t), vm(*half_t), vm(*block, dtype=F32),
-            vm(*block), vm(2, *block), *sems(copies),
+            vm(*block), *[vm(HALF_D, TGT)] * 4, *sems(copies),
             pltpu.SemaphoreType.DMA((2, 2)), pltpu.SemaphoreType.DMA((2, 3)),
         ]
 
@@ -1253,9 +1410,8 @@
     )
     e_keep, e_send, f_keep, f_send, res2, rows2, gatt, gatt_o, dots, dots_o, gg_a = fused_call(
         table_ff_kernel, 1,
-        near(scal) + far(g_a, g_b)
-        + near(flats_a[0], flats_b[0], flats_a[1], flats_b[1], gf_a, gf_b, gf_2)
-        + near(block_out, h2, gain_ff, gain_final) + far(wg, wu, wd) + near(co, att_t),
+        near(scal) + far(g_a, g_b) + near(fin_a, fin_b, gf_sum, gf_3)
+        + near(block_out, h2, gains) + far(wg, wu, wd) + near(co, att_t),
         outs, scratch_1, 24, 40e9,
     )
 
@@ -1279,14 +1435,11 @@
     ) = fused_call(
         cross_kernel, 2,
         near(scal, q2, k2, v2, lse2, gatt, gatt_o, dots, dots_o, source, ck, cv, cq, so)
-        + near(h1, gain_cross, res2, rows2, a2) + far(e_send) + near(f_keep) + far(f_send),
+        + near(h1, gains, res2, rows2, a2) + far(e_send) + near(f_keep) + far(f_send),
         outs, scratch_2, 8, 40e9,
     )
 
     def scratch_3(copies):
-        def three(width):
-            return [vm(96, width, dtype=F32), vm(3, 96, width), vm(3, 96, width)]
-
         def two(width):
             return [vm(2, 96, width, dtype=F32), vm(2, 96, width), vm(2, 96, width)]
 
@@ -1294,26 +1447,39 @@
             vm(*pair), vm(D, TGT, dtype=F32), vm(*pair), vm(*pair), vm(D, ROWS), vm(D, ROWS),
             vm(*half_t), vm(*half_t), vm(1, D, dtype=F32),
             vm(HALF_D, 4 * D, dtype=F32), vm(HALF_D, 4 * D), vm(HALF_D, 4 * D),
-            vm(4, 96, f_half // 2, dtype=F32), vm(2, 96, f_half), *three(f_half // 2),
-            vm(2, 192, c_half), *two(c_half), *three(c_half // 2),
+            vm(4, 96, f_half // 2, dtype=F32), vm(2, 96, f_half),
+            vm(2, 192, c_half), *two(c_half),
             vm(2, 192, c_half, dtype=F32), vm(2, 192, c_half), vm(2, 192, c_half),
-            *two(c_half), *three(c_half // 2),
-            vm(5, 8, D, dtype=F32), vm(5, 8, D, dtype=F32), vm(96, 512, dtype=F32), *sems(copies),
+            *two(c_half),
+            vm(3, 96, f_half // 2), vm(3, 96, c_half // 2), vm(3, 96, c_half // 2),
+            vm(5, 8, D, dtype=F32), vm(5, 8, D, dtype=F32), *sems(copies),
         ]
 
-    wide, tall = whole((96, 192), F32), whole((192, 96), F32)
-    ff_wide, ff_tall = whole((96, 512), F32), whole((512, 96), F32)
-    outs = near(
-        whole(block, F32), whole((8, D), F32), whole((vocab, 96), F32),
-        wide, wide, wide, tall, wide, wide, wide, tall, ff_wide, ff_wide, ff_tall,
+    def three(width):
+        return whole((96, width), F32), whole((3, 96, width), BF16)
+
+    grad_in, gain_sums, *threes = fused_call(
+        self_kernel, 3,
+        near(scal, q1, k1, v1, lse1, gatt1, gatt1_o, block_in, gains, sq, sk, sv)
+        + near(res1, rows1, a1, gg_a, gg_b, f_keep) + far(f_send) + near(c_keep) + far(c_send),
+        near(
+            whole(block, F32), whole((8, D), F32),
+            *three(f_half // 2), *three(c_half // 2), *three(c_half // 2),
+        ),
+        scratch_3, 32, 20e9,
     )
-    grad_in, gain_sums, grad_embed, *grads = fused_call(
-        functools.partial(self_kernel, vocab), 3,
-        near(scal, q1, k1, v1, lse1, gatt1, gatt1_o, block_in, gain_self, sq, sk, sv)
-        + near(res1, rows1, a1, gg_a, gg_b, e_keep, e_recv, f_keep) + far(f_send)
-        + near(c_keep) + far(c_send),
-        outs, scratch_3, 32, 20e9,
-    )
+    wide, tall, ff_wide = whole((96, 192), F32), whole((192, 96), F32), whole((96, 512), F32)
+    grad_embed, grad_in, *grads = pl.pallas_call(
+        functools.partial(finish_kernel, vocab),
+        out_shape=[
+            whole((96, vocab), F32), whole(block, F32), wide, wide, wide, tall, wide, wide, wide, tall,
+            ff_wide, ff_wide, ff_wide,
+        ],
+        scratch_shapes=[pltpu.VMEM((96, 192), F32)],
+        compiler_params=pltpu.CompilerParams(vmem_limit_bytes=VMEM_LIMIT // 2),
+    )(e_keep, e_recv, *threes, grad_in)
+    grads[-1] = grads[-1].T
+    grad_embed = grad_embed.T
     return grad_in, grad_source, gain_sums, grads, grad_embed
 
 
@@ -1470,9 +1636,8 @@
         half = lax.rem(z, 2)
         seq = z // 2
         core = lax.rem(dp, 2)
-        gain_self, gain_cross, gain_ff, gain_final = (
-            g.reshape(1, D) for g in (gain_self, gain_cross, gain_ff, gain_final)
-        )
+        gains = jnp.stack([gain_self, gain_cross, gain_ff, gain_final])
+        gain_self, gain_cross, gain_ff, gain_final = (gains[i : i + 1] for i in range(4))
 
         def pair_swap(value):
             return swap(value, "tensor", 4, 1)
@@ -1491,17 +1656,33 @@
 
         pair = (TGT, D)
         weights = (
-            self_q, self_k, self_v, self_o, cross_q, cross_k, cross_v, cross_o, ff_gate, ff_up, ff_down,
-        )
-        if not split:
-            wide = [gather_wide(w if i in (3, 7, 10) else w.T, dp_size) for i, w in enumerate(weights)]
-            sq, sk, sv, so, cq, ck, cv, co, wg, wu, wd = wide
-            weights = jnp.stack([sq, sk, sv, so]), jnp.stack([cq, ck, cv, co]), wg, wu, wd
-        gains = gain_self, gain_cross, gain_ff, gain_final
-        results = forward(split, scal, block_in, source, gains, weights)
-        q1, k1, v1, lse1, a1, h1, q2, k2, v2, block_out, fin, h2, att_t, a2, lse2 = results[:15]
+            self_q.T, self_k.T, self_v.T, self_o, cross_q.T, cross_k.T, cross_v.T, cross_o,
+            ff_gate, ff_up, ff_down,
+        )
+        vocab = embed_table.shape[0]
         if split:
-            sq, sk, sv, so, cq, ck, cv, co, wg, wu, wd = results[15:]
+            lens = jnp.concatenate([target_len, source_len])
+            results = forward(True, lens, block_in, source, gains, weights)
+            q1, k1, v1, lse1, a1, h1, q2, k2, v2, block_out, fin_t, h2, att_t, a2, lse2 = results[:15]
+            g_a, g_b, gf_sum, gf_3, losses, fin_a, fin_b = fused_head(
+                lens, fin_t, embed_table, targets.reshape(4, ROWS)
+            )
+            saved = (q1, k1, v1, lse1, a1, h1, q2, k2, v2, block_out, h2, att_t, a2, lse2)
+            grad_block_in, grad_source, gain_sums, grads, grad_embed = fused_backward(
+                lens, fin_a, fin_b, g_a, g_b, gf_sum, gf_3, saved, results[15:], gains,
+                block_in, source, vocab,
+            )
+            return (
+                block_out, losses.reshape(-1), grad_block_in, grad_source,
+                gain_sums[3], gain_sums[2], gain_sums[1], gain_sums[0], *grads, grad_embed,
+            )
+
+        wide = [gather_wide(w.T if i in (8, 9) else w, dp_size) for i, w in enumerate(weights)]
+        sq, sk, sv, so, cq, ck, cv, co, wg, wu, wd = wide
+        weights = jnp.stack([sq, sk, sv, so]), jnp.stack([cq, ck, cv, co]), wg, wu, wd
+        results = forward(False, scal, block_in, source, gains, weights)
+        q1, k1, v1, lse1, a1, h1, q2, k2, v2, block_out, fin, h2, att_t, a2, lse2 = results
+        fin = fin.T
 
         vocab = embed_table.shape[0]
 
@@ -1546,25 +1727,7 @@
         )
         g_b, gf_b, gf_2, gf_a = lax.optimization_barrier((g_b, gf_b, gf_2, gf_a))
         def halves(flat):
-            if not split:
-                return flat[:HALF_D], flat[HALF_D:]
-            flat = flat.reshape(4, 2, 96, -1)
-            return tuple(
-                lax.dynamic_index_in_dim(flat, i, 1, keepdims=False).reshape(HALF_D, -1)
-                for i in (core, 1 - core)
-            )
-
-        if split:
-            saved = (q1, k1, v1, lse1, a1, h1, q2, k2, v2, block_out, h2, att_t, a2, lse2)
-            grad_block_in, grad_source, gains, grads, grad_embed = fused_backward(
-                scal, halves(fin_a), halves(fin_b), g_a, g_b, gf_a, gf_b, gf_2, saved,
-                (sq, sk, sv, so, cq, ck, cv, co, wg, wu, wd),
-                (gain_self, gain_cross, gain_ff, gain_final), block_in, source, vocab,
-            )
-            return (
-                block_out, token_loss, grad_block_in, grad_source,
-                gains[3], gains[2], gains[1], gains[0], *grads, grad_embed,
-            )
+            return flat[:HALF_D], flat[HALF_D:]
 
         gf_3 = swap(gf_a[ROWS:], "tensor", 4, 3)
         gf_1 = swap(gf_b[ROWS:].astype(BF16), "tensor", 4, 1)
@@ -1573,7 +1736,7 @@
 
         half_t = (HALF_D, ROWS)
         ff_mine, ff_send, res2, rows2, gatt, dots, gg_a = local_call(
-            functools.partial(ff_backward, split),
+            functools.partial(ff_backward, False),
             [whole((HALF_D, 3 * FF), F32), whole((HALF_D, 3 * FF), BF16), whole((ROWS, D), F32)]
             + [whole((ROWS, D), BF16)] * 2
             + [whole((16, ROWS), F32), whole((2, D), F32)],

time: 457 us -> 402 us (0.88)
  local copies, waits for them, and re-layouts: 46.7 us -> 16.3 us
  waiting for transfers between devices: 27 us -> 0 us
  Pallas kernels: 357 us -> 379 us
  starting transfers between devices: 14.7 us -> 0 us
    ppermute x7 -> x0, waiting for transfers between devices: 27 us -> none  [swap(): return lax.ppermute(value, axis_name, [(i, i ^ bit) for i in range(size)])]
    pallas_call x4 -> x2, Pallas kernels: 57.4 us -> 82.9 us  [the longest x1 80.1 us: fused_head(): pl.pallas_call(functools.partial(head_kernel, vocab), out_shape=[grad, gr...]
    unnamed x83 -> x31, local copies, waits for them, and re-layouts: 35 us -> 12.4 us
    ppermute x7 -> x0, starting transfers between devices: 14.7 us -> none  [swap(): return lax.ppermute(value, axis_name, [(i, i ^ bit) for i in range(size)])]
  transfers between devices with their start and end apart: 7 -> 0, of which waited for: 3 -> 0; matrix products, arithmetic and copies ran while one was open for 1% -> 0% of each run, Pallas kernels for 7% -> 0%
where the time goes in v6:
time: 402 us; the launch traced here: 398 us
  Pallas kernels  379 us (94%)
  local copies, waits for them, and re-layouts  16.3 us (4%)
    pallas_call x3, Pallas kernels, fused_call(): pl.pallas_call(body, out_shape=[shape for shape, _ in outs], in_specs=[pl...  192 us
    pallas_call x1, Pallas kernels, forward(): pl.pallas_call(functools.partial(forward_kernel, split), out_shape=outs,...  103 us
    pallas_call x1, Pallas kernels, fused_head(): pl.pallas_call(functools.partial(head_kernel, vocab), out_shape=[grad, gr...  80.1 us
    unnamed x31, local copies, waits for them, and re-layouts  12.4 us

profile of v6, /device:TPU:0, one launch (start us, length us, event | category | flops | bytes accessed | tf_op | source)
XLA Modules:
  0.0 397.8 jit_solution(281838193099539842)
XLA Ops:
  0.7 1.3 pad_add_fusion.refs_0_
  1.9 0.7 stack.15
  2.6 0.7 stack.16
  3.3 0.7 stack.17
  4.0 0.7 stack.18
  4.7 0.6 pad_maximum_fusion.refs_3_.refs_9_.refs_15_.refs_8_
  5.3 0.0 copy-start.12
  5.3 103.4 %shard_map.356 = (bf16[512,768]{1,0:T(8,128)(2,1)}, bf16[512,768]{1,0:T(8,128)(2,1)}, bf16[512,768]{1,0:T(8,128)(2,1)}, f32[16,512]{1,0:T(8,128)}, bf16[256,768]...) custom-call(s32[4]{0:T(128)} %pad_add_fusion.refs_0_, ...), custom_call_target="tpu_custom_call" | custom-call | flops 80000000000 | bytes 60000000 | tf_op jit(solution)/shard_map/pallas_call | solution.py:652
  108.7 0.0 copy-done.12
  108.7 0.6 reshape.46.refs_3_
  109.3 80.1 %shard_map.357 = (bf16[8192,512]{1,0:T(8,128)(2,1)}, bf16[8192,512]{1,0:T(8,128)(2,1)}, f32[256,768]{1,0:T(8,128)}, bf16[256,768]{1,0:T(8,128)(2,1)}, f32[4,256]...) custom-call(s32[4]{0:T(128)} %pad_add_fusion.refs_0_, bf16[768,256]{1,0:T(8,128)(2,1)} %get-tuple-element.97.refs_1_, ...), custom_call_target="tpu_custom_call" | custom-call | tf_op jit(solution)/shard_map/pallas_call | solution.py:1326
  189.3 53.4 %shard_map.358 = (f32[2,96,4096]{2,1,0:T(8,128)}, bf16[2,96,4096]{2,1,0:T(8,128)(2,1)}, f32[2,192,3072]{2,1,0:T(8,128)}, bf16[2,192,3072]{2,1,0:T(8,128)(2,1)}, ...) custom-call(s32[4]{0:T(128)} %pad_add_fusion.refs_0_, ...), custom_call_target="tpu_custom_call" | custom-call | flops 40000000000 | bytes 32518160 | tf_op jit(solution)/shard_map/pallas_call | solution.py:1358
  242.7 57.8 %shard_map.359 = (f32[1024,768]{1,0:T(8,128)}, f32[256,768]{1,0:T(8,128)}, bf16[256,768]{1,0:T(8,128)(2,1)}, bf16[256,768]{1,0:T(8,128)(2,1)}, bf16[256,768]{1,0...) custom-call(s32[4]{0:T(128)} %pad_add_fusion.refs_0_, ...), custom_call_target="tpu_custom_call" | custom-call | flops 40000000000 | bytes 22097936 | tf_op jit(solution)/shard_map/pallas_call | solution.py:1358
  300.6 0.0 copy-start.1
  300.6 81.2 %shard_map.360 = (f32[256,768]{1,0:T(8,128)}, f32[8,768]{1,0:T(8,128)}, f32[96,1536]{1,0:T(8,128)}, bf16[3,96,1536]{2,1,0:T(8,128)(2,1)}, f32[96,768]{1,0:T(8,12...) custom-call(s32[4]{0:T(128)} %pad_add_fusion.refs_0_, ...), custom_call_target="tpu_custom_call" | custom-call | flops 20000000000 | bytes 15782928 | tf_op jit(solution)/shard_map/pallas_call | solution.py:1358
  381.7 0.0 copy-done.1
  381.8 0.0 copy-start
  381.8 1.9 copy-done
  383.6 0.0 copy-start.2
  383.6 1.2 copy-done.2
  384.8 0.0 copy-start.3
  384.8 1.1 copy-done.3
  385.9 0.0 copy-start.4
  385.9 1.1 copy-done.4
  387.0 0.0 copy-start.5
  387.0 1.0 copy-done.5
  388.0 0.0 copy-start.6
  388.0 1.0 copy-done.6
  389.0 0.0 copy-start.7
  389.0 1.0 copy-done.7
  390.0 0.0 copy-start.8
  390.0 1.0 copy-done.8
  391.0 0.0 copy-start.11
  391.0 0.0 copy-start.13
  391.0 0.0 copy-start.10
  391.0 0.0 copy-start.9
  391.0 2.8 shard_map.361
  393.8 0.0 copy-done.11
  393.8 0.6 slice_reduce_fusion
  394.4 0.0 copy-done.13
  394.4 0.6 copy.41
  395.0 0.0 copy-done.10
  395.0 0.9 copy.44
  395.9 0.0 copy-done.9
  395.9 1.7 copy.45
Async XLA Ops:
  5.3 103.4 %copy-start.12 = (s32[1024]{0:T(1024)S(1)}, s32[1024]{0:T(1024)}, u32[]{:S(2)}) copy-start(s32[1024]{0:T(1024)} %param.25) | copy-start | bytes 12292
  300.6 81.2 %copy-start.1 = (bf16[2,96,4096]{2,1,0:T(8,128)(2,1)S(1)}, bf16[2,96,4096]{2,1,0:T(8,128)(2,1)}, u32[]{:S(2)}) copy-start(bf16[2,96,4096]{2,1,0:T(8,128)(2,1)} %get-tuple-element.131.e_recv) | copy-start | bytes 4718596
  381.8 1.9 copy-start
  383.6 1.2 copy-start.2
  384.8 1.1 copy-start.3
  385.9 1.1 copy-start.4
  387.0 1.0 copy-start.5
  388.0 1.0 copy-start.6
  389.0 1.0 copy-start.7
  390.0 1.0 copy-start.8
  391.0 2.8 copy-start.11
  391.0 3.5 copy-start.13
  391.0 4.1 %copy-start.10 = (f32[256,768]{1,0:T(8,128)S(1)}, f32[256,768]{1,0:T(8,128)}, u32[]{:S(2)}) copy-start(f32[256,768]{1,0:T(8,128)} %get-tuple-element.196.refs_7_) | copy-start | bytes 2359300
  391.0 4.9 %copy-start.9 = (f32[1024,768]{1,0:T(8,128)S(1)}, f32[1024,768]{1,0:T(8,128)}, u32[]{:S(2)}) copy-start(f32[1024,768]{1,0:T(8,128)} %get-tuple-element.199) | copy-start | bytes 9437188

commit v7 on v6

--- a/solution.py
+++ b/solution.py
@@ -236,21 +236,31 @@
     def fold_third(self, shard_ref):
         self.wait()
         comm = self.comm
-        (keep, _, recv), (keep3, send3, recv3) = self.two, self.three
+        (keep, _, recv), (keep3, send3, _) = self.two, self.three
         width = keep3.shape[1]
         for side in range(2):
             total = keep[side] + recv[side].astype(F32)
             shard_ref[2 * side, :, :width] = total[:, :width]
             shard_ref[2 * side + 1, :, :width] = total[:, width:]
         keep3[...] = shard_ref[comm.z, :, :width]
-        self.copies = []
         for j, shard in enumerate(comm.z_shards):
             send3[j] = shard_ref[shard, :, :width].astype(BF16)
-            self.copies.append(comm.send(send3.at[j], recv3.at[j], comm.z_peers[j]))
-
-
-def finish_kernel(vocab, e_keep, e_recv, f_keep, f_recv, c_keep, c_recv, s_keep, s_recv, gin, *refs):
-    e_out, gin_out, refs, turn_ref = refs[0], refs[1], refs[2:-1], refs[-1]
+
+    def send_third(self):
+        _, send3, recv3 = self.three
+        peers = self.comm.z_peers
+        self.copies = [self.comm.send(send3.at[j], recv3.at[j], peers[j]) for j in range(3)]
+
+
+def finish_kernel(vocab, *refs):
+    sources, (e_out, gin_out), refs = refs[:9], refs[9:11], refs[11:]
+    refs, held, (sem, turn_ref) = refs[:11], refs[11:20], refs[20:]
+    copies = [pltpu.make_async_copy(src, dst, sem.at[i]) for i, (src, dst) in enumerate(zip(sources, held))]
+    for copy in copies:
+        copy.start()
+    for copy in copies:
+        copy.wait()
+    e_keep, e_recv, f_keep, f_recv, c_keep, c_recv, s_keep, s_recv, gin = held
     gin_out[...] = gin[...]
     width = e_keep.shape[2]
     for side in range(2):
@@ -825,7 +835,7 @@
 def self_backward(
     split, scal, q1, k1, v1, lse, g_own, g_other, x_own, gain_self, w_q, w_k, w_v, res_in, rows_in, att,
     mine_ref, send_ref, gin_ref, gg_ref,
-    g_ref, dq_ref, dk_ref, dv_ref, flat_ref, flat_2, a_ref, b_ref,
+    g_ref, dq_ref, dk_ref, dv_ref, flat_ref, flat_2, a_ref, b_ref, midway=None,
 ):
     half, live, _, core = spots(scal, split)
     own = pl.multiple_of(half * ROWS, ROWS)
@@ -857,6 +867,8 @@
         dk_ref[:, lanes] = (grad_k * SCALE).astype(BF16)
         dv_ref[:, lanes] = grad_v.astype(BF16)
 
+    if midway is not None:
+        midway()
     dq = (flip(dq_ref[:, pl.ds(own, ROWS)]) * SCALE).astype(BF16)
     dk = dk_ref[pl.ds(own, ROWS), :]
     dv = dv_ref[pl.ds(own, ROWS), :]
@@ -1097,27 +1109,26 @@
     (scal, q2, k2, v2, lse2, g_own, g_other, dot_own, dot_oth, source), refs = refs[:10], refs[10:]
     (w_ck, w_cv, w_cq, w_so, h1, gains, res_in, rows_in, att), refs = refs[:9], refs[9:]
     gain_cross = gains.at[1:2]
-    (e_send, f_keep, f_send), refs = refs[:3], refs[3:]
+    (f_keep, f_send), refs = refs[:2], refs[2:]
     (gsrc, res_ref, rows_ref, gatt1, gatt1_other, gg_ref), refs = refs[:6], refs[6:]
-    (c_keep, c_send, f_keep2, f_send2, e_recv), refs = refs[:5], refs[5:]
+    (c_keep, c_send, f_keep3, f_send3), refs = refs[:4], refs[4:]
     (g_ref, dot_ref, dq_ref, dk_ref, dv_ref, flat_ref, sm_ref, ss_ref), refs = refs[:8], refs[8:]
     (mine, send, got, f_recv, own_ref, go_ref, come_ref, flat2, a_ref, b_ref), refs = (
         refs[:10],
         refs[10:],
     )
+    f_two, shard_ref, refs = refs[:3], refs[3], refs[4:]
     comm = Comm(*refs)
     comm.barrier()
-    ff = Flow(comm, (f_keep, f_send, f_recv), (f_keep2, f_send2, None), None)
+    ff = Flow(comm, (f_keep, f_send, f_recv), f_two, (f_keep3, f_send3, None))
     ff.send_first()
-    e_copies = [
-        comm.send(e_send.at[0], e_recv.at[0], comm.y_peer),
-        comm.send(e_send.at[1], e_recv.at[1], comm.x_peer),
-    ]
     cross_backward(
         True, scal, q2, k2, v2, lse2, g_own, g_other, dot_own, dot_oth,
         dk_ref, dv_ref, own_ref, go_ref, g_ref, dot_ref, dq_ref,
     )
     dq_copy = comm.send(go_ref, come_ref, comm.z_peers[0])
+    ff.fold_second()
+    ff.send_second()
     source_backward(
         True, scal, dk_ref, dv_ref, source, w_ck, w_cv, gsrc, mine, send, flat_ref, sm_ref, ss_ref
     )
@@ -1130,10 +1141,8 @@
     cross = Flow(comm, (c_keep, c_send, None), None, None)
     cross.from_core(mine, send, got)
     cross.fold_first()
-    ff.fold_second()
+    ff.fold_third(shard_ref)
     pair_copy.wait()
-    for copy in e_copies:
-        copy.wait()
 
 
 def self_kernel(*refs):
@@ -1143,27 +1152,31 @@
     )
     gain_self = gains.at[0:1]
     (res_in, rows_in, att, gg_a, gg_b), refs = refs[:5], refs[5:]
-    (f_keep, f_send, c_keep, c_send), refs = refs[:4], refs[4:]
-    (gin_ref, gains_ref, f_keep3, f_recv3, c_keep3, c_recv3, s_keep3, s_recv3), refs = refs[:8], refs[8:]
+    (f_send3, e_send, c_keep, c_send), refs = refs[:4], refs[4:]
+    (gin_ref, gains_ref, f_recv3, c_keep3, c_recv3, s_keep3, s_recv3, e_recv), refs = refs[:8], refs[8:]
     (g_ref, dq_ref, dk_ref, dv_ref, flat_ref, flat_2, a_ref, b_ref, gain_ref), refs = refs[:9], refs[9:]
-    (mine, send, got, shard_ref, f_recv), refs = refs[:5], refs[5:]
+    (mine, send, got, shard_ref, shard_2), refs = refs[:5], refs[5:]
     (c_recv1, c_keep2, c_send2, c_recv2), refs = refs[:4], refs[4:]
     s_one, s_two, refs = refs[:3], refs[3:6], refs[6:]
-    (f_send3, c_send3, s_send3, gain_send, gain_recv), refs = refs[:5], refs[5:]
-    f_three = f_keep3, f_send3, f_recv3
+    (c_send3, s_send3, gain_send, gain_recv), refs = refs[:4], refs[4:]
     c_three = c_keep3, c_send3, c_recv3
     s_three = s_keep3, s_send3, s_recv3
     comm = Comm(*refs)
     comm.barrier()
     cross = Flow(comm, (c_keep, c_send, c_recv1), (c_keep2, c_send2, c_recv2), c_three)
-    ff = Flow(comm, None, (f_keep, f_send, f_recv), f_three)
+    ff = Flow(comm, None, None, (None, f_send3, f_recv3))
     own = Flow(comm, s_one, s_two, s_three)
-    ff.send_second()
     cross.send_first()
+    ff.send_third()
+
+    def midway():
+        cross.fold_second()
+        cross.send_second()
+
     self_backward(
         True, scal, q1, k1, v1, lse1, g_own, g_other, x_own, gain_self, w_q, w_k, w_v,
         res_in, rows_in, att, mine, send, gin_ref, gain_ref,
-        g_ref, dq_ref, dk_ref, dv_ref, flat_ref, flat_2, a_ref, b_ref,
+        g_ref, dq_ref, dk_ref, dv_ref, flat_ref, flat_2, a_ref, b_ref, midway,
     )
     own.from_core(mine, send, got)
     gains_ref[...] = jnp.zeros_like(gains_ref)
@@ -1184,23 +1197,28 @@
     own.send_first()
     gain_done(0, copy)
     copy = gain_step(1, comm.z_peers[0])
-    ff.fold_third(shard_ref)
-    cross.fold_second()
-    cross.send_second()
+    cross.fold_third(shard_ref)
+    cross.send_third()
     gain_done(1, copy)
     copy = gain_step(2, comm.x_peer)
+    own.fold_second()
+    own.send_second()
+    e_copies = [
+        comm.send(e_send.at[0], e_recv.at[0], comm.y_peer),
+        comm.send(e_send.at[1], e_recv.at[1], comm.x_peer),
+    ]
     gain_done(2, copy)
     copy = gain_step(3, comm.y_peer)
-    own.fold_second()
-    own.send_second()
-    cross.fold_third(shard_ref)
+    own.fold_third(shard_2)
+    own.send_third()
     gain_done(3, copy)
     copy = gain_step(4, comm.z_peers[1])
     ff.wait()
-    own.fold_third(shard_ref)
+    cross.wait()
     gain_done(4, copy)
-    cross.wait()
     own.wait()
+    for copy in e_copies:
+        copy.wait()
 
 
 def head_kernel(vocab, *refs):
@@ -1421,21 +1439,23 @@
             vm(D, KEYS), vm(HALF_D, KEYS), vm(HALF_D, KEYS),
             vm(HALF_D, 4 * D, dtype=F32), vm(HALF_D, 4 * D), vm(HALF_D, 4 * D),
             vm(2, 192, f_half), vm(D, ROWS, dtype=F32), vm(D, ROWS), vm(D, ROWS),
-            vm(D, ROWS), vm(*half_t), vm(*half_t), *sems(copies),
+            vm(D, ROWS), vm(*half_t), vm(*half_t),
+            vm(2, 96, f_half, dtype=F32), vm(2, 96, f_half), vm(2, 96, f_half),
+            vm(4, 96, f_half // 2, dtype=F32), *sems(copies),
         ]
 
     outs = near(
         whole((KEYS, D), F32), whole(block, F32), whole(block, BF16), whole(block, BF16),
         whole(block, BF16), whole((1, D), F32),
         whole((2, 192, c_half), F32), whole((2, 192, c_half), BF16),
-        whole((2, 96, f_half), F32), whole((2, 96, f_half), BF16),
-    ) + far(whole((2, 96, e_half), BF16))
+        whole((96, f_half // 2), F32), whole((3, 96, f_half // 2), BF16),
+    )
     (
-        grad_source, res1, rows1, gatt1, gatt1_o, gg_b, c_keep, c_send, f_keep, f_send, e_recv,
+        grad_source, res1, rows1, gatt1, gatt1_o, gg_b, c_keep, c_send, f_keep, f_send,
     ) = fused_call(
         cross_kernel, 2,
         near(scal, q2, k2, v2, lse2, gatt, gatt_o, dots, dots_o, source, ck, cv, cq, so)
-        + near(h1, gains, res2, rows2, a2) + far(e_send) + near(f_keep) + far(f_send),
+        + near(h1, gains, res2, rows2, a2) + near(f_keep) + far(f_send),
         outs, scratch_2, 8, 40e9,
     )
 
@@ -1447,27 +1467,29 @@
             vm(*pair), vm(D, TGT, dtype=F32), vm(*pair), vm(*pair), vm(D, ROWS), vm(D, ROWS),
             vm(*half_t), vm(*half_t), vm(1, D, dtype=F32),
             vm(HALF_D, 4 * D, dtype=F32), vm(HALF_D, 4 * D), vm(HALF_D, 4 * D),
-            vm(4, 96, f_half // 2, dtype=F32), vm(2, 96, f_half),
+            vm(4, 96, c_half // 2, dtype=F32), vm(4, 96, c_half // 2, dtype=F32),
             vm(2, 192, c_half), *two(c_half),
             vm(2, 192, c_half, dtype=F32), vm(2, 192, c_half), vm(2, 192, c_half),
             *two(c_half),
-            vm(3, 96, f_half // 2), vm(3, 96, c_half // 2), vm(3, 96, c_half // 2),
+            vm(3, 96, c_half // 2), vm(3, 96, c_half // 2),
             vm(5, 8, D, dtype=F32), vm(5, 8, D, dtype=F32), *sems(copies),
         ]
 
     def three(width):
         return whole((96, width), F32), whole((3, 96, width), BF16)
 
-    grad_in, gain_sums, *threes = fused_call(
+    grad_in, gain_sums, f_recv, c_keep, c_recv, s_keep, s_recv, e_recv = fused_call(
         self_kernel, 3,
         near(scal, q1, k1, v1, lse1, gatt1, gatt1_o, block_in, gains, sq, sk, sv)
-        + near(res1, rows1, a1, gg_a, gg_b, f_keep) + far(f_send) + near(c_keep) + far(c_send),
+        + near(res1, rows1, a1, gg_a, gg_b) + far(f_send, e_send) + near(c_keep) + far(c_send),
         near(
-            whole(block, F32), whole((8, D), F32),
-            *three(f_half // 2), *three(c_half // 2), *three(c_half // 2),
-        ),
+            whole(block, F32), whole((8, D), F32), whole((3, 96, f_half // 2), BF16),
+            *three(c_half // 2), *three(c_half // 2),
+        )
+        + far(whole((2, 96, e_half), BF16)),
         scratch_3, 32, 20e9,
     )
+    parts = e_keep, e_recv, f_keep, f_recv, c_keep, c_recv, s_keep, s_recv, grad_in
     wide, tall, ff_wide = whole((96, 192), F32), whole((192, 96), F32), whole((96, 512), F32)
     grad_embed, grad_in, *grads = pl.pallas_call(
         functools.partial(finish_kernel, vocab),
@@ -1475,9 +1497,11 @@
             whole((96, vocab), F32), whole(block, F32), wide, wide, wide, tall, wide, wide, wide, tall,
             ff_wide, ff_wide, ff_wide,
         ],
-        scratch_shapes=[pltpu.VMEM((96, 192), F32)],
-        compiler_params=pltpu.CompilerParams(vmem_limit_bytes=VMEM_LIMIT // 2),
-    )(e_keep, e_recv, *threes, grad_in)
+        in_specs=[pl.BlockSpec(memory_space=pl.ANY)] * 9,
+        scratch_shapes=[pltpu.VMEM(part.shape, part.dtype) for part in parts]
+        + [pltpu.SemaphoreType.DMA((9,)), pltpu.VMEM((96, 192), F32)],
+        compiler_params=pltpu.CompilerParams(vmem_limit_bytes=FUSED_LIMIT),
+    )(*parts)
     grads[-1] = grads[-1].T
     grad_embed = grad_embed.T
     return grad_in, grad_source, gain_sums, grads, grad_embed

time: 402 us -> 390 us (0.970)
  local copies, waits for them, and re-layouts: 16.3 us -> 9.23 us
    pallas_call x3, Pallas kernels: 192 us -> 185 us  [fused_call(): pl.pallas_call(body, out_shape=[shape for shape, _ in outs], in_specs=[pl...]
    unnamed x31 -> x11, local copies, waits for them, and re-layouts: 12.4 us -> 5.25 us
where the time goes in v7:
time: 390 us; the launch traced here: 387 us
  Pallas kernels  375 us (96%)
  local copies, waits for them, and re-layouts  9.23 us (2%)
    pallas_call x3, Pallas kernels, fused_call(): pl.pallas_call(body, out_shape=[shape for shape, _ in outs], in_specs=[pl...  185 us
    pallas_call x1, Pallas kernels, forward(): pl.pallas_call(functools.partial(forward_kernel, split), out_shape=outs,...  103 us
    pallas_call x1, Pallas kernels, fused_head(): pl.pallas_call(functools.partial(head_kernel, vocab), out_shape=[grad, gr...  80 us

profile of v7, /device:TPU:0, one launch (start us, length us, event | category | flops | bytes accessed | tf_op | source)
XLA Modules:
  0.0 386.7 jit_solution(7973291753336300340)
XLA Ops:
  0.7 1.3 pad_add_fusion.refs_0_
  1.9 0.7 stack.15
  2.6 0.7 stack.16
  3.3 0.7 stack.17
  4.0 0.7 stack.18
  4.7 0.6 pad_maximum_fusion.refs_3_.refs_9_.refs_15_.refs_8_
  5.3 0.0 copy-start.2
  5.3 103.4 %shard_map.356 = (bf16[512,768]{1,0:T(8,128)(2,1)}, bf16[512,768]{1,0:T(8,128)(2,1)}, bf16[512,768]{1,0:T(8,128)(2,1)}, f32[16,512]{1,0:T(8,128)}, bf16[256,768]...) custom-call(s32[4]{0:T(128)} %pad_add_fusion.refs_0_, ...), custom_call_target="tpu_custom_call" | custom-call | flops 80000000000 | bytes 60000000 | tf_op jit(solution)/shard_map/pallas_call | solution.py:662
  108.7 0.0 copy-done.2
  108.7 0.6 reshape.46.refs_3_
  109.3 80.0 %shard_map.357 = (bf16[8192,512]{1,0:T(8,128)(2,1)}, bf16[8192,512]{1,0:T(8,128)(2,1)}, f32[256,768]{1,0:T(8,128)}, bf16[256,768]{1,0:T(8,128)(2,1)}, f32[4,256]...) custom-call(s32[4]{0:T(128)} %pad_add_fusion.refs_0_, bf16[768,256]{1,0:T(8,128)(2,1)} %get-tuple-element.96.refs_1_, ...), custom_call_target="tpu_custom_call" | custom-call | tf_op jit(solution)/shard_map/pallas_call | solution.py:1344
  189.3 53.4 %shard_map.358 = (f32[2,96,4096]{2,1,0:T(8,128)}, bf16[2,96,4096]{2,1,0:T(8,128)(2,1)}, f32[2,192,3072]{2,1,0:T(8,128)}, bf16[2,192,3072]{2,1,0:T(8,128)(2,1)}, ...) custom-call(s32[4]{0:T(128)} %pad_add_fusion.refs_0_, ...), custom_call_target="tpu_custom_call" | custom-call | flops 40000000000 | bytes 32518160 | tf_op jit(solution)/shard_map/pallas_call | solution.py:1376
  242.7 57.9 %shard_map.359 = (f32[1024,768]{1,0:T(8,128)}, f32[256,768]{1,0:T(8,128)}, bf16[256,768]{1,0:T(8,128)(2,1)}, bf16[256,768]{1,0:T(8,128)(2,1)}, bf16[256,768]{1,0...) custom-call(s32[4]{0:T(128)} %pad_add_fusion.refs_0_, ...), custom_call_target="tpu_custom_call" | custom-call | flops 40000000000 | bytes 20525072 | tf_op jit(solution)/shard_map/pallas_call | solution.py:1376
  300.7 73.7 %shard_map.360 = (f32[256,768]{1,0:T(8,128)}, f32[8,768]{1,0:T(8,128)}, bf16[3,96,1536]{2,1,0:T(8,128)(2,1)}, f32[96,768]{1,0:T(8,128)}, bf16[3,96,768]{2,1,0:T(...) custom-call(s32[4]{0:T(128)} %pad_add_fusion.refs_0_, ...), custom_call_target="tpu_custom_call" | custom-call | flops 20000000000 | bytes 14701584 | tf_op jit(solution)/shard_map/pallas_call | solution.py:1376
  374.4 0.0 copy-start.1
  374.4 0.0 copy-start.3
  374.4 0.0 copy-start
  374.4 6.2 %shard_map.361 = (f32[96,8032]{1,0:T(8,128)}, f32[256,768]{1,0:T(8,128)}, f32[96,192]{1,0:T(8,128)}, f32[96,192]{1,0:T(8,128)}, f32[96,192]{1,0:T(8,128)}, /*ind...) custom-call(f32[2,96,4096]{2,1,0:T(8,128)} %get-tuple-element.110.re, ...), custom_call_target="tpu_custom_call" | custom-call | tf_op jit(solution)/shard_map/pallas_call | solution.py:1494
  380.6 0.0 copy-done.1
  380.6 0.6 slice_reduce_fusion
  381.3 0.0 copy-done.3
  381.3 0.6 copy.41
  381.9 0.0 copy-done
  381.9 0.9 copy.44
  382.8 3.8 copy.45
Async XLA Ops:
  5.3 103.4 %copy-start.2 = (s32[1024]{0:T(1024)S(1)}, s32[1024]{0:T(1024)}, u32[]{:S(2)}) copy-start(s32[1024]{0:T(1024)} %param.25) | copy-start | bytes 12292
  374.4 6.2 %copy-start.1 = (f32[8,768]{1,0:T(8,128)S(1)}, f32[8,768]{1,0:T(8,128)}, u32[]{:S(2)}) copy-start(f32[8,768]{1,0:T(8,128)} %get-tuple-element.157) | copy-start | bytes 73732
  374.4 6.9 %copy-start.3 = (f32[4,256]{1,0:T(4,128)S(1)}, f32[4,256]{1,0:T(4,128)}, u32[]{:S(2)}) copy-start(f32[4,256]{1,0:T(4,128)} %get-tuple-element.97) | copy-start | bytes 12292
  374.4 7.5 %copy-start = (f32[256,768]{1,0:T(8,128)S(1)}, f32[256,768]{1,0:T(8,128)}, u32[]{:S(2)}) copy-start(f32[256,768]{1,0:T(8,128)} %get-tuple-element.194.refs_7_) | copy-start | bytes 2359300

commit v8 on v7

--- a/solution.py
+++ b/solution.py
@@ -253,14 +253,15 @@
 
 
 def finish_kernel(vocab, *refs):
-    sources, (e_out, gin_out), refs = refs[:9], refs[9:11], refs[11:]
+    sources, (e_out, gin_out, gsrc_out, block_ref), refs = refs[:11], refs[11:15], refs[15:]
     refs, held, (sem, turn_ref) = refs[:11], refs[11:20], refs[20:]
+    held = held + (gsrc_out, block_ref)
     copies = [pltpu.make_async_copy(src, dst, sem.at[i]) for i, (src, dst) in enumerate(zip(sources, held))]
     for copy in copies:
         copy.start()
     for copy in copies:
         copy.wait()
-    e_keep, e_recv, f_keep, f_recv, c_keep, c_recv, s_keep, s_recv, gin = held
+    e_keep, e_recv, f_keep, f_recv, c_keep, c_recv, s_keep, s_recv, gin = held[:9]
     gin_out[...] = gin[...]
     width = e_keep.shape[2]
     for side in range(2):
@@ -545,7 +546,6 @@
         v2[rows, :] = dot_nt(src, wc[2]).astype(BF16)
         vt_ref[:, rows] = dot_nt(wc[2], src).astype(BF16)
     if split:
-        of_down.along_xy()
         of_up.diagonal()
         of_gate.finish()
         leave(8, [wg])
@@ -581,7 +581,7 @@
     o_send[: D // 2, :] = ot_ref[: D // 2, pl.ds(other, ROWS)].astype(BF16)
     pair_copies = [exchange(1, o_send.at[: D // 2], o_other.at[: D // 2])]
     if split:
-        of_down.diagonal()
+        of_down.along_xy()
         of_up.finish()
         leave(9, [wu])
     cross_pairs(PAIRS // 2, PAIRS)
@@ -589,8 +589,7 @@
     pair_copies.append(exchange(2, o_send.at[D // 2 :], o_other.at[D // 2 :]))
     pair_copies.append(exchange(3, lse_own, lse_other))
     if split:
-        of_down.finish()
-        leave(10, [wd])
+        of_down.diagonal()
     for copy in pair_copies:
         copy.wait()
 
@@ -619,7 +618,10 @@
         up = dot_nt(n3, wu[rows, :])
         mix_ref[:, rows] = (jax.nn.gelu(gate, approximate=True) * up).astype(BF16)
 
-    out = h2 + dot_nn(mix_ref[...], wd[...])
+    if split:
+        of_down.finish()
+        leave(10, [wd])
+    out = h2_ref[...] + dot_nn(mix_ref[...], wd[...])
     out_ref[...] = out
     x_ref[:ROWS, :] = out * rms_scale(out) * gain_final[...] * D ** (-0.5)
     fin_ref[...] = x_ref[:ROWS, :].T.astype(BF16)
@@ -1490,21 +1492,23 @@
         scratch_3, 32, 20e9,
     )
     parts = e_keep, e_recv, f_keep, f_recv, c_keep, c_recv, s_keep, s_recv, grad_in
+    through = grad_source, block_out
     wide, tall, ff_wide = whole((96, 192), F32), whole((192, 96), F32), whole((96, 512), F32)
-    grad_embed, grad_in, *grads = pl.pallas_call(
+    grad_embed, grad_in, grad_source, block_out, *grads = pl.pallas_call(
         functools.partial(finish_kernel, vocab),
         out_shape=[
-            whole((96, vocab), F32), whole(block, F32), wide, wide, wide, tall, wide, wide, wide, tall,
+            whole((96, vocab), F32), whole(block, F32), whole((KEYS, D), F32), whole(block, F32),
+            wide, wide, wide, tall, wide, wide, wide, tall,
             ff_wide, ff_wide, ff_wide,
         ],
-        in_specs=[pl.BlockSpec(memory_space=pl.ANY)] * 9,
+        in_specs=[pl.BlockSpec(memory_space=pl.ANY)] * 11,
         scratch_shapes=[pltpu.VMEM(part.shape, part.dtype) for part in parts]
-        + [pltpu.SemaphoreType.DMA((9,)), pltpu.VMEM((96, 192), F32)],
+        + [pltpu.SemaphoreType.DMA((11,)), pltpu.VMEM((96, 192), F32)],
         compiler_params=pltpu.CompilerParams(vmem_limit_bytes=FUSED_LIMIT),
-    )(*parts)
+    )(*parts, *through)
     grads[-1] = grads[-1].T
     grad_embed = grad_embed.T
-    return grad_in, grad_source, gain_sums, grads, grad_embed
+    return block_out, grad_in, grad_source, gain_sums, grads, grad_embed
 
 
 def logits_kernel(vocab, flat_ref, table_ref, target_ref, logits_ref, stats_ref):
@@ -1660,7 +1664,7 @@
         half = lax.rem(z, 2)
         seq = z // 2
         core = lax.rem(dp, 2)
-        gains = jnp.stack([gain_self, gain_cross, gain_ff, gain_final])
+        gains = jnp.concatenate([gain_self, gain_cross, gain_ff, gain_final]).reshape(4, D)
         gain_self, gain_cross, gain_ff, gain_final = (gains[i : i + 1] for i in range(4))
 
         def pair_swap(value):
@@ -1692,7 +1696,7 @@
                 lens, fin_t, embed_table, targets.reshape(4, ROWS)
             )
             saved = (q1, k1, v1, lse1, a1, h1, q2, k2, v2, block_out, h2, att_t, a2, lse2)
-            grad_block_in, grad_source, gain_sums, grads, grad_embed = fused_backward(
+            block_out, grad_block_in, grad_source, gain_sums, grads, grad_embed = fused_backward(
                 lens, fin_a, fin_b, g_a, g_b, gf_sum, gf_3, saved, results[15:], gains,
                 block_in, source, vocab,
             )

time: 390 us -> 386 us (0.990)
  local copies, waits for them, and re-layouts: 9.23 us -> 3.13 us
    unnamed x11 -> x5, local copies, waits for them, and re-layouts: 5.25 us -> 0.6 us
where the time goes in v8:
time: 386 us; the launch traced here: 383 us
  Pallas kernels  377 us (98%)
    pallas_call x3, Pallas kernels, fused_call(): pl.pallas_call(body, out_shape=[shape for shape, _ in outs], in_specs=[pl...  185 us
    pallas_call x1, Pallas kernels, forward(): pl.pallas_call(functools.partial(forward_kernel, split), out_shape=outs,...  103 us
    pallas_call x1, Pallas kernels, fused_head(): pl.pallas_call(functools.partial(head_kernel, vocab), out_shape=[grad, gr...  80.1 us
    pallas_call x1, Pallas kernels, fused_backward(): pl.pallas_call(functools.partial(finish_kernel, vocab), out_shape=[whole(...  8.16 us

profile of v8, /device:TPU:0, one launch (start us, length us, event | category | flops | bytes accessed | tf_op | source)
XLA Modules:
  0.0 382.8 jit_solution(3451741635246086371)
XLA Ops:
  0.7 1.3 pad_add_fusion.refs_0_
  1.9 1.3 reshape.50.refs_3_
  3.2 0.7 pad_maximum_fusion
  3.9 0.6 reshape.49.refs_3_.refs_9_.refs_15_.refs_8_
  4.6 103.0 %shard_map.356 = (bf16[512,768]{1,0:T(8,128)(2,1)}, bf16[512,768]{1,0:T(8,128)(2,1)}, bf16[512,768]{1,0:T(8,128)(2,1)}, f32[16,512]{1,0:T(8,128)}, bf16[256,768]...) custom-call(s32[4]{0:T(128)} %pad_add_fusion.refs_0_, ...), custom_call_target="tpu_custom_call" | custom-call | flops 80000000000 | bytes 60000000 | tf_op jit(solution)/shard_map/pallas_call | solution.py:664
  107.6 80.1 %shard_map.357 = (bf16[8192,512]{1,0:T(8,128)(2,1)}, bf16[8192,512]{1,0:T(8,128)(2,1)}, f32[256,768]{1,0:T(8,128)}, bf16[256,768]{1,0:T(8,128)(2,1)}, f32[4,256]...) custom-call(s32[4]{0:T(128)} %pad_add_fusion.refs_0_, bf16[768,256]{1,0:T(8,128)(2,1)} %get-tuple-element.97.refs_1_, ...), custom_call_target="tpu_custom_call" | custom-call | tf_op jit(solution)/shard_map/pallas_call | solution.py:1346
  187.7 0.0 copy-start.1
  187.7 53.8 %shard_map.358 = (f32[2,96,4096]{2,1,0:T(8,128)}, bf16[2,96,4096]{2,1,0:T(8,128)(2,1)}, f32[2,192,3072]{2,1,0:T(8,128)}, bf16[2,192,3072]{2,1,0:T(8,128)(2,1)}, ...) custom-call(s32[4]{0:T(128)} %pad_add_fusion.refs_0_, ...), custom_call_target="tpu_custom_call" | custom-call | flops 40000000000 | bytes 32518160 | tf_op jit(solution)/shard_map/pallas_call | solution.py:1378
  241.5 0.0 copy-done.1
  241.5 0.6 copy.41
  242.1 57.9 %shard_map.359 = (f32[1024,768]{1,0:T(8,128)}, f32[256,768]{1,0:T(8,128)}, bf16[256,768]{1,0:T(8,128)(2,1)}, bf16[256,768]{1,0:T(8,128)(2,1)}, bf16[256,768]{1,0...) custom-call(s32[4]{0:T(128)} %pad_add_fusion.refs_0_, ...), custom_call_target="tpu_custom_call" | custom-call | flops 40000000000 | bytes 20525072 | tf_op jit(solution)/shard_map/pallas_call | solution.py:1378
  300.0 73.7 %shard_map.360 = (f32[256,768]{1,0:T(8,128)}, f32[8,768]{1,0:T(8,128)}, bf16[3,96,1536]{2,1,0:T(8,128)(2,1)}, f32[96,768]{1,0:T(8,128)}, bf16[3,96,768]{2,1,0:T(...) custom-call(s32[4]{0:T(128)} %pad_add_fusion.refs_0_, ...), custom_call_target="tpu_custom_call" | custom-call | flops 20000000000 | bytes 14701584 | tf_op jit(solution)/shard_map/pallas_call | solution.py:1378
  373.7 0.0 copy-start
  373.7 8.2 %shard_map.361 = (f32[96,8032]{1,0:T(8,128)}, f32[256,768]{1,0:T(8,128)}, f32[1024,768]{1,0:T(8,128)}, f32[256,768]{1,0:T(8,128)}, f32[96,192]{1,0:T(8,128)}, /*...) custom-call(f32[2,96,4096]{2,1,0:T(8,128)} %get-tuple-element.111.re, ...), custom_call_target="tpu_custom_call" | custom-call | tf_op jit(solution)/shard_map/pallas_call | solution.py:1497
  381.9 0.0 copy-done
  381.9 0.6 slice_reduce_fusion
Async XLA Ops:
  187.7 53.8 %copy-start.1 = (f32[4,256]{1,0:T(4,128)S(1)}, f32[4,256]{1,0:T(4,128)}, u32[]{:S(2)}) copy-start(f32[4,256]{1,0:T(4,128)} %get-tuple-element.158) | copy-start | bytes 12292
  373.7 8.2 %copy-start = (f32[8,768]{1,0:T(8,128)S(1)}, f32[8,768]{1,0:T(8,128)}, u32[]{:S(2)}) copy-start(f32[8,768]{1,0:T(8,128)} %get-tuple-element.161) | copy-start | bytes 73732
